TPU v7x, 128 devices: a whole 4x4x4 slice. The times are simulated.
128 devices in a mesh: grid: 32 (over y, x, z_lo), ipts: 4 (over z_hi, core).
Axes of the slice: x: 4, y: 4, z: 4 (z_hi: 2, z_lo: 2; z = z_hi * 2 + z_lo), core: 2. Of those that a mesh axis runs over, the one named last changes fastest.
Arguments:
- orbitals: bfloat16 [65536, 1024], P(('grid', 'ipts')), may hold values from -1.1953125 to 1.1953125
- targets: bfloat16 [65536, 256], P(('grid', 'ipts')), may hold values from -6 to 6
- points: int32 [4, 4096], P('ipts', 'grid'), may hold values from 0 to 65535, as said below
- potential: bfloat16 [65536, 16384], P('grid', 'ipts'), may hold values from -0.046875 to 0.046875
Outputs:
- exchanged: bfloat16 [65536, 256], P(('grid', 'ipts'))
Inputs may be any that keep to these rules, and one draw needn't show every extreme that they name: Indices are distinct over all groups; each row of points rises strictly, and its entries k * 128 to (k + 1) * 128 - 1 lie in grid rows k * 2048 to (k + 1) * 2048 - 1.
All inputs are finite; a program needn't handle non-finite values.
Results may differ from a plain program's by a relative error of at most 0.0049.
Values may be sent and summed in bfloat16 or wider, within the bound.
No kernel may reach another device: no remote copies, remote signals or barrier semaphores. Data moves between devices by JAX's collectives and lax.ppermute only.
A program may use at most 128 MiB of HBM per device.

v0:
```python
import jax
import jax.numpy as jnp
from jax import lax
from jax.sharding import Mesh
from jax.sharding import PartitionSpec as P

IPTS = ("ipts_0", "ipts_1")
GRID_IPTS = ("grid", "ipts_0", "ipts_1")


def in_order(pieces, dim):
    dims = list(pieces.shape[1:])
    dims[dim] *= pieces.shape[0]
    return jnp.moveaxis(pieces, 0, dim).reshape(dims)


def gather_in_order(value, axes, turns):
    pieces = value
    for k in turns:
        pieces = lax.all_gather(pieces, axes[k])
    done = turns[::-1]
    back = [done.index(k) for k in range(len(axes))]
    pieces = pieces.transpose(*back, *range(len(axes), pieces.ndim))
    return pieces.reshape(-1, *value.shape)


def whole_of(value, axes, turns, dim):
    return in_order(gather_in_order(value, axes, turns), dim)


def split_up(value, dim, length):
    before, after = (value.shape[:dim], value.shape[dim + 1 :])
    return jnp.moveaxis(value.reshape(*before, length, -1, *after), dim, 0)


def sum_at_owner(value, axis, dim):
    pieces = split_up(value, dim, lax.axis_size(axis))
    arrived = lax.all_to_all(pieces, axis, split_axis=0, concat_axis=0, tiled=True)
    return arrived.astype(jnp.float32).sum(axis=0)


def sent_together(arrays, axis, dim, along):
    both = jnp.concatenate(arrays, axis=along)
    whole, at, finished = (lax.all_gather(both, axis, axis=dim, tiled=True), 0, [])
    for a in arrays:
        finished.append(lax.slice_in_dim(whole, at, at + a.shape[along], axis=along))
        at += a.shape[along]
    return tuple(finished)


def summed_on_arrival(value, axis, dim):
    length = lax.axis_size(axis)
    pieces = lax.all_to_all(split_up(value, dim, length), axis, 0, 0, tiled=True)
    return jnp.sum(pieces, axis=0)


def local(orbitals, targets, points, potential):
    groups = lax.axis_size(IPTS)
    own_rows = orbitals.shape[0]
    slab_length = own_rows * groups
    slab_start = lax.axis_index("grid") * slab_length
    whole_slab = lax.all_gather(orbitals, IPTS, axis=0, tiled=True)
    every_group = whole_of(points, IPTS, (0, 1), 0)
    orbital_values = jnp.take(whole_slab, points[0] - slab_start, axis=0)
    offset = every_group - (slab_start + lax.axis_index(IPTS) * own_rows)
    inside = (offset >= 0) & (offset < own_rows)
    clipped = jnp.clip(offset, 0, own_rows - 1)
    picked = jnp.take(targets, clipped, axis=0) * inside[:, :, None].astype(targets.dtype)
    summed = sum_at_owner(picked, IPTS, 0)
    target_values = summed[0].astype(jnp.bfloat16)
    orbital_piece, target_piece = sent_together((orbital_values, target_values), "grid", 0, 1)
    products = lax.dot_general(
        whole_slab, orbital_piece, (((1,), (1,)), ((), ())), preferred_element_type=jnp.float32
    )
    weighted = (potential * products).astype(jnp.bfloat16)
    group_total = jnp.dot(weighted, target_piece, preferred_element_type=jnp.float32)
    summed_rows = summed_on_arrival(group_total, IPTS, 0)
    return (-summed_rows).astype(jnp.bfloat16)


def solution(mesh):
    torus = Mesh(mesh.devices.reshape(mesh.shape["grid"], 2, 2), ("grid", "ipts_0", "ipts_1"))
    placed = (P(GRID_IPTS, None), P(GRID_IPTS, None), P(IPTS, "grid"), P("grid", IPTS))
    return jax.shard_map(
        local, mesh=torus, in_specs=placed, out_specs=P(GRID_IPTS, None), check_vma=False
    )
```

profile of v0, /device:TPU:1, one launch (start us, length us, event | category | flops | bytes accessed | tf_op | source)
XLA Modules:
  0.0 362.0 jit_solution(10757572754428285465)
XLA Ops:
  6.5 0.0 copy-start
  6.5 0.0 all-gather.7.cloned.1.call-start
  6.5 0.7 all-gather.7.cloned.1.call-update
  7.3 6.2 %all-gather.2 = s32[2,1,128]{2,1,0:T(1,128)S(1)} all-gather(s32[1,1,128]{2,1,0:T(1,128)} %bitcast.38), channel_id=2, replica_groups=mesh['grid'=32,'ipts_0'=2,'ipts_1'=2] {'ipts_0'}, dimensions={0}, use_global_device_ids=true | all-gather | bytes 1536 | tf_op jit(solution)/shard_map/all_gather | solution.py:20
  13.5 3.0 all-gather.3
  16.5 0.0 copy-done
  16.5 2.0 gather_fusion.1
  18.5 0.9 select_multiply_fusion
  19.4 5.1 %all-to-all-start = ((bf16[4,1,128,256]{3,2,1,0:T(8,128)(2,1)}), bf16[4,1,128,256]{3,2,1,0:T(8,128)(2,1)S(1)}, u32[]{:S(2)}, u32[]{:S(2)}) async-start(bf16[4,1,128,256]{3,2,1,0:T(8,128)(2,1)} %select_multiply_fusion), calls=%async_computation | async-start | bytes 524288 | tf_op jit(solution)/shard_map/all_to_all | solution.py:38
  24.5 0.0 all-gather.9.cloned.1.call-start
  24.5 0.7 fusion.8
  25.2 0.7 compare_and_fusion.1
  25.8 8.4 %all-to-all-done = bf16[4,1,128,256]{3,2,1,0:T(8,128)(2,1)S(1)} async-done(((bf16[4,1,128,256]{3,2,1,0:T(8,128)(2,1)}), bf16[4,1,128,256]{3,2,1,0:T(8,128)(2,1)S(1)}, u32[]{:S(2)}, u32[]{:S(2)}) %all-to-all-start) | async-done | bytes 262176 | tf_op jit(solution)/shard_map/all_to_all | solution.py:38
  34.3 19.9 %all-gather.7.cloned.1.call-done = bf16[2048,1024]{1,0:T(8,128)(2,1)} async-done(((bf16[512,1024]{1,0:T(8,128)(2,1)}), bf16[2048,1024]{1,0:T(8,128)(2,1)}) %all-gather.7.cloned.1.call-update) | async-done | bytes 4194320 | tf_op jit(solution)/shard_map/all_gather | solution.py:62
  54.2 3.8 %gather_fusion = bf16[128,1024]{1,0:T(8,128)(2,1)S(1)} fusion(bf16[2048,1024]{1,0:T(8,128)(2,1)} %all-gather.7.cloned.1.call-done, s32[1024]{0:T(1024)S(1)} %pad_clamp_fusion.1), kind=kCustom, calls=%fused_computation | custom fusion | bytes 524800 | tf_op jit(solution)/shard_map/jit(_take)/gather | solution.py:64
  57.9 0.1 broadcast_select_fusion
  58.0 0.8 pad_maximum_fusion
  58.8 0.0 all-gather.9.cloned.1.call-update
  58.8 22.6 %copy.8 = bf16[2048,4096]{0,1:T(8,128)(2,1)} copy(bf16[2048,4096]{1,0:T(8,128)(2,1)} %param.7) | data formatting | bytes 33554432 | tf_op args[3]
  81.4 207.0 %all-gather.9.cloned.1.call-done = bf16[4096,1280]{1,0:T(8,128)(2,1)} async-done(((bf16[128,1280]{1,0:T(8,128)(2,1)}), bf16[4096,1280]{1,0:T(8,128)(2,1)}) %all-gather.9.cloned.1.call-update) | async-done | bytes 10485776 | tf_op jit(solution)/shard_map/all_gather | solution.py:44
  288.4 34.1 %fusion.3 = f32[2048,256]{1,0:T(8,128)} fusion(bf16[2048,4096]{0,1:T(8,128)(2,1)} %copy.8, bf16[2048,1024]{1,0:T(8,128)(2,1)} %all-gather.7.cloned.1.call-done, bf16[4096,1280]{1,0:T(8,128)(2,1)} %all-gather.9.cloned.1.call-done), kind=kOutput, calls=%fused_computation.5 | convolution fusion | flops 21500002304 | bytes 33554432 | tf_op jit(solution)/shard_map/dot_general | solution.py:76
  322.5 31.8 %all_to_all.10 = f32[4,512,256]{2,1,0:T(8,128)S(1)} all-to-all(f32[4,512,256]{2,1,0:T(8,128)} %bitcast.32), channel_id=1, replica_groups=mesh['grid'=32,'ipts_0'=2,'ipts_1'=2] {'ipts_0','ipts_1'}, dimensions={0} | all-to-all | bytes 4194304 | tf_op jit(solution)/shard_map/all_to_all | solution.py:53
  354.3 0.2 reduce_sum.22
  354.4 0.7 negate_convert_fusion
  (9 shorter events, 0.1 us)
Async XLA Ops:
  6.5 10.0 %copy-start = (bf16[512,256]{1,0:T(8,128)(2,1)S(1)}, bf16[512,256]{1,0:T(8,128)(2,1)}, u32[]{:S(2)}) copy-start(bf16[512,256]{1,0:T(8,128)(2,1)} %param.5) | copy-start | bytes 786436
  6.5 47.6 %all-gather.7.cloned.1.call-start = ((), (), s32[]{:S(2)}) async-start(), calls=%async_computation.2 | async-start | bytes 5242880 | tf_op jit(solution)/shard_map/all_gather | solution.py:62
  19.4 14.8 %all-to-all-start = ((bf16[4,1,128,256]{3,2,1,0:T(8,128)(2,1)}), bf16[4,1,128,256]{3,2,1,0:T(8,128)(2,1)S(1)}, u32[]{:S(2)}, u32[]{:S(2)}) async-start(bf16[4,1,128,256]{3,2,1,0:T(8,128)(2,1)} %select_multiply_fusion), calls=%async_computation | async-start | bytes 524288 | tf_op jit(solution)/shard_map/all_to_all | solution.py:38
  24.5 263.9 %all-gather.9.cloned.1.call-start = ((), (), s32[]{:S(2)}) async-start(), calls=%async_computation.3 | async-start | bytes 10813440 | tf_op jit(solution)/shard_map/all_gather | solution.py:44
Sparse Core Ops, SparseCore 0:
  9.0 45.0 all-gather.6
  59.0 229.4 all-gather.8
where the time goes:
time: 363 us; the launch traced here: 362 us
  waiting for transfers between devices  236 us (65%)
  blocking collectives  41 us (11%)
  matrix products  34.1 us (9%)
  local copies, waits for them, and re-layouts  28.3 us (8%)
  between operations  13.5 us (4%)
  starting transfers between devices  5.07 us (1%)
  other arithmetic  4.09 us (1%)
    all_gather x1, waiting for transfers between devices, sent_together(): lax.all_gather(both, axis, axis=dim, tiled=True)  207 us
    dot_general x1, matrix products, local(): jnp.dot(weighted, target_piece, preferred_element_type=jnp.float32)  34.1 us
    all_to_all x1, blocking collectives, summed_on_arrival(): lax.all_to_all(split_up(value, dim, length), axis, 0, 0, tiled=True)  31.8 us
    unnamed x3, local copies, waits for them, and re-layouts  22.6 us
    all_gather x1, waiting for transfers between devices, local(): whole_slab = lax.all_gather(orbitals, IPTS, axis=0, tiled=True)  19.9 us
    all_gather x2, blocking collectives, gather_in_order(): pieces = lax.all_gather(pieces, axes[k])  9.21 us
    all_to_all x1, waiting for transfers between devices, sum_at_owner(): lax.all_to_all(pieces, axis, split_axis=0, concat_axis=0, tiled=True)  8.39 us
  transfers between devices with their start and end apart: 3, of which 3 were waited for; matrix products, arithmetic and copies ran while one was open for 7% of the time, Pallas kernels for 0%

commit v1 on v0

v1 whole, which is shorter than its diff:
```python
import jax
import jax.numpy as jnp
from jax import lax
from jax.experimental import pallas as pl
from jax.experimental.pallas import tpu as pltpu
from jax.sharding import Mesh
from jax.sharding import PartitionSpec as P

AXES = ("y", "x", "zl", "zh", "c")
SLABS = ("y", "x", "zl")
IPTS = ("zh", "c")
RING = 4

ROUNDS = (
    (((0, 1), "x", 1), ((0, 3), "x", -1), ((1, 0), "y", 1), ((3, 0), "y", -1)),
    (((1, 1), "x", 1), ((3, 3), "x", -1), ((1, 3), "y", 1), ((3, 1), "y", -1)),
    (((0, 2), "x", 1), ((1, 2), "x", -1), ((2, 0), "y", 1), ((2, 1), "y", -1)),
    (((2, 2), "x", 1), ((3, 2), "x", -1), ((2, 3), "y", -1)),
)


def from_neighbour(value, axis, side):
    n = lax.axis_size(axis)
    return lax.ppermute(value, axis, [((i + side) % n, i) for i in range(n)])


def source_offset(block, axis, side):
    dy, dx = block
    return ((dy - side) % RING, dx) if axis == "y" else (dy, (dx - side) % RING)


def pick_kernel(bases, ids, own_orb, sib_orb, own_tgt, sib_tgt, mine, theirs):
    rows = own_orb.shape[0]
    norb = own_orb.shape[1]
    for k, out in ((0, mine), (1, theirs)):
        row = lax.broadcasted_iota(jnp.int32, (rows, out.shape[0]), 0)
        at = ids[k : k + 1, :]
        own = (row + bases[0] == at).astype(jnp.bfloat16)
        sib = (row + bases[1] == at).astype(jnp.bfloat16)
        dims = (((0,), (0,)), ((), ()))

        def select(hot, values):
            return lax.dot_general(hot, values, dims, preferred_element_type=jnp.float32)

        out[:, :norb] = (select(own, own_orb[...]) + select(sib, sib_orb[...])).astype(out.dtype)
        out[:, norb:] = (select(own, own_tgt[...]) + select(sib, sib_tgt[...])).astype(out.dtype)


def pick(bases, ids, own_orb, sib_orb, own_tgt, sib_tgt):
    points = ids.shape[1]
    width = own_orb.shape[1] + own_tgt.shape[1]
    out = jax.ShapeDtypeStruct((points, width), own_orb.dtype)
    whole = pl.BlockSpec(memory_space=pltpu.VMEM)
    return pl.pallas_call(
        pick_kernel,
        out_shape=(out, out),
        in_specs=[pl.BlockSpec(memory_space=pltpu.SMEM)] + [whole] * 5,
        out_specs=(whole, whole),
        compiler_params=pltpu.CompilerParams(vmem_limit_bytes=32 << 20),
        name="pick",
    )(bases, ids, own_orb, sib_orb, own_tgt, sib_tgt)


def apply_kernel(count, first, rows, cols, *refs):
    slab = refs[0]
    pairs = refs[1 : 1 + count]
    pots = refs[1 + count : 1 + 2 * count]
    out = refs[-1]
    norb = slab.shape[1]
    total = None if first else refs[1 + 2 * count][...]
    for pair, pot in zip(pairs, pots):
        products = lax.dot_general(
            slab[...], pair[:, :norb], (((1,), (1,)), ((), ())), preferred_element_type=jnp.float32
        )
        weighted = (pot[...].astype(jnp.float32) * products).astype(jnp.bfloat16)
        term = jnp.dot(weighted, pair[:, norb:], preferred_element_type=jnp.float32)
        total = term if total is None else total + term
    out[...] = total


def apply_pairs(slab, pairs, potential, rows, cols, total):
    count = len(pairs)
    tile = slab.shape[0] // 4
    norb = slab.shape[1]
    points, width = pairs[0].shape
    nj = width - norb
    acc = pl.BlockSpec((tile, nj), lambda i, r, c: (i, 0))

    def pot_spec(k):
        return pl.BlockSpec((tile, points), lambda i, r, c: (r[i], c[k]))

    first = total is None
    specs = [pl.BlockSpec((tile, norb), lambda i, r, c: (i, 0))]
    specs += [pl.BlockSpec((points, width), lambda i, r, c: (0, 0))] * count
    specs += [pot_spec(k) for k in range(count)]
    args = [slab, *pairs] + [potential] * count
    if not first:
        specs.append(acc)
        args.append(total)
    flops = 2 * slab.shape[0] * points * count * width
    moved = slab.size * 2 + count * (slab.shape[0] * points + points * width) * 2 + slab.shape[0] * nj * 8

    def body(r, c, *refs):
        apply_kernel(count, first, r, c, *refs)

    return pl.pallas_call(
        body,
        out_shape=jax.ShapeDtypeStruct((slab.shape[0], nj), jnp.float32),
        grid_spec=pltpu.PrefetchScalarGridSpec(
            num_scalar_prefetch=2, grid=(4,), in_specs=specs, out_specs=acc
        ),
        input_output_aliases={} if first else {len(args) + 1: 0},
        cost_estimate=pl.CostEstimate(flops=flops, bytes_accessed=moved, transcendentals=0),
        compiler_params=pltpu.CompilerParams(vmem_limit_bytes=40 << 20),
        name="apply",
    )(rows, cols, *args)


def after(value, *others):
    return lax.optimization_barrier((value, others))[0]


def local(orbitals, targets, points, potential):
    own_rows = orbitals.shape[0]
    zl, zh, c = (lax.axis_index(a) for a in ("zl", "zh", "c"))
    y, x = lax.axis_index("y"), lax.axis_index("x")
    slab_start = ((y * RING + x) * 2 + zl) * own_rows * 4

    sib_orb = from_neighbour(orbitals, "c", 1)
    sib_tgt = from_neighbour(targets, "c", 1)
    far_points = from_neighbour(points, "zh", 1)
    bases = jnp.stack([slab_start + (zh * 2 + c) * own_rows, slab_start + (zh * 2 + 1 - c) * own_rows])
    ids = jnp.concatenate([points, far_points], axis=0)
    mine, theirs = pick(bases.astype(jnp.int32), ids, orbitals, sib_orb, targets, sib_tgt)
    block = mine + from_neighbour(theirs, "zh", 1)
    near = from_neighbour(block, "zl", 1)
    low = jnp.where(zl == 0, block, near)
    high = jnp.where(zl == 0, near, block)
    pair = jnp.concatenate([low, high], axis=0)

    far_orb = from_neighbour(after(orbitals, near), "zh", 1)
    far_sib = from_neighbour(far_orb, "c", 1)
    slab = jnp.concatenate([orbitals, far_orb, sib_orb, far_sib], axis=0)
    rows = jnp.stack([zh * 2 + c, (1 - zh) * 2 + c, zh * 2 + 1 - c, (1 - zh) * 2 + 1 - c]).astype(jnp.int32)

    have = {(0, 0): pair}
    total = None
    pending = [(0, 0)]

    def columns(blocks):
        return jnp.stack([(y + dy) % RING * RING + (x + dx) % RING for dy, dx in blocks]).astype(jnp.int32)

    for moves in ROUNDS:
        new = {}
        for block_at, axis, side in moves:
            new[block_at] = from_neighbour(have[source_offset(block_at, axis, side)], axis, side)
        total = apply_pairs(slab, [have[k] for k in pending], potential, rows, columns(pending), total)
        have.update(new)
        pending = list(new)
    total = apply_pairs(slab, [have[k] for k in pending], potential, rows, columns(pending), total)

    half = 2 * own_rows
    both = total[:half] + from_neighbour(total[half:], "c", 1)
    away = from_neighbour(both[own_rows:].astype(jnp.bfloat16), "zh", 1)
    return (-(both[:own_rows] + away.astype(jnp.float32))).astype(jnp.bfloat16)


def solution(mesh):
    torus = Mesh(mesh.devices.reshape(RING, RING, 2, 2, 2), AXES)
    placed = (P(AXES, None), P(AXES, None), P(IPTS, SLABS), P(SLABS, IPTS))
    return jax.shard_map(local, mesh=torus, in_specs=placed, out_specs=P(AXES, None), check_vma=False)
```

time: 363 us -> 153 us (0.42)
  waiting for transfers between devices: 236 us -> 49.2 us
  Pallas kernels: 0 us -> 48.5 us
  blocking collectives: 41 us -> 0 us
  starting transfers between devices: 5.07 us -> 41.2 us
  matrix products: 34.1 us -> 0 us
  local copies, waits for them, and re-layouts: 28.3 us -> 11.1 us
  between operations: 13.5 us -> 0.17 us
    all_gather x2 -> x0, waiting for transfers between devices: 227 us -> none  [the longest x1 207 us: sent_together(): lax.all_gather(both, axis, axis=dim, tiled=True)]
    ppermute x0 -> x24, waiting for transfers between devices: none -> 49.2 us  [from_neighbour(): return lax.ppermute(value, axis, [((i + side) % n, i) for i in range(n)])]
    pallas_call x0 -> x6, Pallas kernels: none -> 48.5 us  [the longest x5 47.1 us: apply_pairs(): pl.pallas_call(body, out_shape=jax.ShapeDtypeStruct((slab.shape[0], nj),...]
    ppermute x0 -> x24, starting transfers between devices: none -> 41.2 us  [from_neighbour(): return lax.ppermute(value, axis, [((i + side) % n, i) for i in range(n)])]
    dot_general x1 -> x0, matrix products: 34.1 us -> none  [local(): jnp.dot(weighted, target_piece, preferred_element_type=jnp.float32)]
    all_to_all x1 -> x0, blocking collectives: 31.8 us -> none  [summed_on_arrival(): lax.all_to_all(split_up(value, dim, length), axis, 0, 0, tiled=True)]
    unnamed x3 -> x11, local copies, waits for them, and re-layouts: 22.6 us -> 8.73 us
    all_gather x2 -> x0, blocking collectives: 9.21 us -> none  [gather_in_order(): pieces = lax.all_gather(pieces, axes[k])]
  transfers between devices with their start and end apart: 3 -> 24, of which waited for: 3 -> 9; matrix products, arithmetic and copies ran while one was open for 7% -> 5% of each run, Pallas kernels for 0% -> 25%
where the time goes in v1:
time: 153 us; the launch traced here: 152 us
  waiting for transfers between devices  49.2 us (32%)
  Pallas kernels  48.5 us (32%)
  starting transfers between devices  41.2 us (27%)
  local copies, waits for them, and re-layouts  11.1 us (7%)
  other arithmetic  2.14 us (1%)
    ppermute x24, waiting for transfers between devices, from_neighbour(): return lax.ppermute(value, axis, [((i + side) % n, i) for i in range(n)])  49.2 us
    pallas_call x5, Pallas kernels, apply_pairs(): pl.pallas_call(body, out_shape=jax.ShapeDtypeStruct((slab.shape[0], nj),...  47.1 us
    ppermute x24, starting transfers between devices, from_neighbour(): return lax.ppermute(value, axis, [((i + side) % n, i) for i in range(n)])  41.2 us
    unnamed x11, local copies, waits for them, and re-layouts  8.73 us
  transfers between devices with their start and end apart: 24, of which 9 were waited for; matrix products, arithmetic and copies ran while one was open for 5% of the time, Pallas kernels for 25%

profile of v1, /device:TPU:1, one launch (start us, length us, event | category | flops | bytes accessed | tf_op | source)
XLA Modules:
  0.0 152.3 jit_solution(10437806654539463145)
XLA Ops:
  0.0 1.4 collective-permute-start.1
  1.4 3.7 %collective-permute-start = (s32[1,128]{1,0:T(1,128)}, s32[1,128]{1,0:T(1,128)S(1)}, u32[]{:S(2)}, u32[]{:S(2)}) collective-permute-start(s32[1,128]{1,0:T(1,128)} %param.6), channel_id=1, source_target_pairs={{2,0},{0,2},{3,1},{1,3},{6,4},{4,6},{7,5},{5,7},{10,8},{8,10},{11,... | collective-permute-start | bytes 1544 | tf_op jit(solution)/shard_map/ppermute | solution.py:24
  6.9 1.2 copy-done.1
  9.0 1.4 pick.1
  10.5 3.0 %collective-permute-start.3 = (bf16[128,1280]{1,0:T(8,128)(2,1)S(1)}, bf16[128,1280]{1,0:T(8,128)(2,1)S(1)}, u32[]{:S(2)}, u32[]{:S(2)}) collective-permute-start(bf16[128,1280]{1,0:T(8,128)(2,1)S(1)} %get-tuple-element.9), channel_id=1, source_target_pairs={{2,0},{0,2},{3,1},{1,3},{6,4},{4,6},{7,5},{5,7},{10,8},{8,10},{11,... | collective-permute-start | bytes 983048 | tf_op jit(solution)/shard_map/ppermute | solution.py:24
  13.5 6.4 %collective-permute-done.3 = bf16[128,1280]{1,0:T(8,128)(2,1)S(1)} collective-permute-done((bf16[128,1280]{1,0:T(8,128)(2,1)S(1)}, bf16[128,1280]{1,0:T(8,128)(2,1)S(1)}, u32[]{:S(2)}, u32[]{:S(2)}) %collective-permute-start.3) | collective-permute-done | bytes 327712 | tf_op jit(solution)/shard_map/ppermute | solution.py:24
  20.8 6.2 %collective-permute-done.4 = bf16[128,1280]{1,0:T(8,128)(2,1)S(1)} collective-permute-done((bf16[128,1280]{1,0:T(8,128)(2,1)S(1)}, bf16[128,1280]{1,0:T(8,128)(2,1)S(1)}, u32[]{:S(2)}, u32[]{:S(2)}) %collective-permute-start.4) | collective-permute-done | bytes 327712 | tf_op jit(solution)/shard_map/ppermute | solution.py:24
  26.9 2.4 %collective-permute-start.5 = (bf16[512,1024]{1,0:T(8,128)(2,1)}, bf16[512,1024]{1,0:T(8,128)(2,1)}, u32[]{:S(2)}, u32[]{:S(2)}) collective-permute-start(bf16[512,1024]{1,0:T(8,128)(2,1)} %own_orb.1), channel_id=1, source_target_pairs={{2,0},{0,2},{3,1},{1,3},{6,4},{4,6},{7,5},{5,7},{10,8},{8,10},{11,... | collective-permute-start | bytes 3145736 | tf_op jit(solution)/shard_map/ppermute | solution.py:24
  29.5 2.6 %collective-permute-start.7 = (bf16[256,1280]{1,0:T(8,128)(2,1)S(1)}, bf16[256,1280]{1,0:T(8,128)(2,1)S(1)}, u32[]{:S(2)}, u32[]{:S(2)}) collective-permute-start(bf16[256,1280]{1,0:T(8,128)(2,1)S(1)} %pad_maximum_fusion.refs_1_), channel_id=1, source_target_pairs={{8,0},{16,8},{24,16},{0,24},{9,1},{17,9},{25,17},{1,25},{10,2},{18... | collective-permute-start | bytes 1966088 | tf_op jit(solution)/shard_map/ppermute | solution.py:24
  32.0 1.3 collective-permute-start.11
  33.3 18.8 %collective-permute-done.5 = bf16[512,1024]{1,0:T(8,128)(2,1)} collective-permute-done((bf16[512,1024]{1,0:T(8,128)(2,1)}, bf16[512,1024]{1,0:T(8,128)(2,1)}, u32[]{:S(2)}, u32[]{:S(2)}) %collective-permute-start.5) | collective-permute-done | bytes 1048608 | tf_op jit(solution)/shard_map/ppermute | solution.py:24
  52.1 3.2 %collective-permute-start.6 = (bf16[512,1024]{1,0:T(8,128)(2,1)}, bf16[512,1024]{1,0:T(8,128)(2,1)}, u32[]{:S(2)}, u32[]{:S(2)}) collective-permute-start(bf16[512,1024]{1,0:T(8,128)(2,1)} %collective-permute-done.5), channel_id=1, source_target_pairs={{1,0},{0,1},{3,2},{2,3},{5,4},{4,5},{7,6},{6,7},{9,8},{8,9},{11,10... | collective-permute-start | bytes 3145736 | tf_op jit(solution)/shard_map/ppermute | solution.py:24
  55.4 2.7 %collective-permute-start.19 = (bf16[256,1280]{1,0:T(8,128)(2,1)S(1)}, bf16[256,1280]{1,0:T(8,128)(2,1)}, u32[]{:S(2)}, u32[]{:S(2)}) collective-permute-start(bf16[256,1280]{1,0:T(8,128)(2,1)S(1)} %pad_maximum_fusion.refs_1_), channel_id=1, source_target_pairs={{32,0},{64,32},{96,64},{0,96},{33,1},{65,33},{97,65},{1,97},{34,2}... | collective-permute-start | bytes 1966088 | tf_op jit(solution)/shard_map/ppermute | solution.py:24
  59.3 1.2 collective-permute-start.12
  60.5 2.7 %collective-permute-start.17 = (bf16[256,1280]{1,0:T(8,128)(2,1)}, bf16[256,1280]{1,0:T(8,128)(2,1)}, u32[]{:S(2)}, u32[]{:S(2)}) collective-permute-start(bf16[256,1280]{1,0:T(8,128)(2,1)} %collective-permute-done.16.refs_2_), channel_id=1, source_target_pairs={{32,0},{64,32},{96,64},{0,96},{33,1},{65,33},{97,65},{1,97},{34,2}... | collective-permute-start | bytes 1966088 | tf_op jit(solution)/shard_map/ppermute | solution.py:24
  63.3 2.3 %constant_dynamic-update-slice_fusion.2 = bf16[2048,1024]{1,0:T(8,128)(2,1)} fusion(bf16[2048,1024]{1,0:T(8,128)(2,1)} %constant_dynamic-update-slice_fusion.3, bf16[512,1024]{1,0:T(8,128)(2,1)} %collective-permute-done.5), kind=kLoop, calls=%fused_computation.10 | loop fusion | bytes 2097152
  66.6 5.7 %collective-permute-done.19.refs_3_ = bf16[256,1280]{1,0:T(8,128)(2,1)} collective-permute-done((bf16[256,1280]{1,0:T(8,128)(2,1)S(1)}, bf16[256,1280]{1,0:T(8,128)(2,1)}, u32[]{:S(2)}, u32[]{:S(2)}) %collective-permute-start.19) | collective-permute-done | bytes 655392 | tf_op jit(solution)/shard_map/ppermute | solution.py:24
  72.3 2.5 %collective-permute-start.15 = (bf16[256,1280]{1,0:T(8,128)(2,1)S(1)}, bf16[256,1280]{1,0:T(8,128)(2,1)S(1)}, u32[]{:S(2)}, u32[]{:S(2)}) collective-permute-start(bf16[256,1280]{1,0:T(8,128)(2,1)S(1)} %collective-permute-done.7.refs_1_), channel_id=1, source_target_pairs={{8,0},{16,8},{24,16},{0,24},{9,1},{17,9},{25,17},{1,25},{10,2},{18... | collective-permute-start | bytes 1966088 | tf_op jit(solution)/shard_map/ppermute | solution.py:24
  75.5 2.5 %collective-permute-start.21 = (bf16[256,1280]{1,0:T(8,128)(2,1)}, bf16[256,1280]{1,0:T(8,128)(2,1)S(1)}, u32[]{:S(2)}, u32[]{:S(2)}) collective-permute-start(bf16[256,1280]{1,0:T(8,128)(2,1)} %collective-permute-done.19.refs_3_), channel_id=1, source_target_pairs={{8,0},{16,8},{24,16},{0,24},{9,1},{17,9},{25,17},{1,25},{10,2},{18... | collective-permute-start | bytes 1966088 | tf_op jit(solution)/shard_map/ppermute | solution.py:24
  78.0 2.3 %constant_dynamic-update-slice_fusion.refs_0_ = bf16[2048,1024]{1,0:T(8,128)(2,1)} fusion(bf16[2048,1024]{1,0:T(8,128)(2,1)} %constant_dynamic-update-slice_fusion.1, bf16[512,1024]{1,0:T(8,128)(2,1)} %collective-permute-done.6), kind=kLoop, calls=%fused_computation.8 | loop fusion | bytes 2097152 | tf_op jit(solution)/shard_map/concatenate | solution.py:143
  80.3 2.2 %copy-done = bf16[2048,1024]{1,0:T(8,128)(2,1)S(1)} copy-done((bf16[2048,1024]{1,0:T(8,128)(2,1)S(1)}, bf16[2048,1024]{1,0:T(8,128)(2,1)}, u32[]{:S(2)}) %copy-start) | copy-done | bytes 4194328
  82.4 4.5 %apply.5.refs_9_ = f32[2048,256]{1,0:T(8,128)S(1)} custom-call(s32[4]{0:T(128)S(1)} %get-tuple-element.13.r, s32[1]{0:T(128)} %bitcast.21.c, bf16[2048,1024]{1,0:T(8,128)(2,1)S(1)} %copy-done, bf16[256,1280]{1,0:T(8,128)(2,1)S(1)} %pad_maximum_fusion.refs_1_, bf16[2048,4096]{1,0:T(8,128)(2,1)} %refs_6_.7), custom_call_target="tpu_custom_call" | custom-call | flops 1342177280 | bytes 10092544 | tf_op jit(solution)/shard_map/apply/pallas_call | solution.py:106
  86.9 2.7 %collective-permute-start.20 = (bf16[256,1280]{1,0:T(8,128)(2,1)}, bf16[256,1280]{1,0:T(8,128)(2,1)S(1)}, u32[]{:S(2)}, u32[]{:S(2)}) collective-permute-start(bf16[256,1280]{1,0:T(8,128)(2,1)} %collective-permute-done.19.refs_3_), channel_id=1, source_target_pairs={{32,0},{64,32},{96,64},{0,96},{33,1},{65,33},{97,65},{1,97},{34,2}... | collective-permute-start | bytes 1966088 | tf_op jit(solution)/shard_map/ppermute | solution.py:24
  89.7 11.5 %apply.6.refs_9_ = f32[2048,256]{1,0:T(8,128)S(1)} custom-call(s32[4]{0:T(128)S(1)} %get-tuple-element.13.r, s32[4]{0:T(128)S(1)} %pad_add_fusion.6.c, bf16[2048,1024]{1,0:T(8,128)(2,1)S(1)} %copy-done, bf16[256,1280]{1,0:T(8,128)(2,1)S(1)} %collective-permute-done.7.refs_1_, ...), custom_call_target="tpu_custom_call", output_to_operand_aliasing={{}: (11, {})} | custom-call | flops 5368709120 | bytes 15204352 | tf_op jit(solution)/shard_map/apply/pallas_call | solution.py:106
  103.5 2.5 %collective-permute-start.10 = (bf16[256,1280]{1,0:T(8,128)(2,1)S(1)}, bf16[256,1280]{1,0:T(8,128)(2,1)S(1)}, u32[]{:S(2)}, u32[]{:S(2)}) collective-permute-start(bf16[256,1280]{1,0:T(8,128)(2,1)S(1)} %collective-permute-done.9.refs_4_), channel_id=1, source_target_pairs={{8,0},{16,8},{24,16},{0,24},{9,1},{17,9},{25,17},{1,25},{10,2},{18... | collective-permute-start | bytes 1966088 | tf_op jit(solution)/shard_map/ppermute | solution.py:24
  106.0 11.4 %apply.7.refs_9_ = f32[2048,256]{1,0:T(8,128)S(1)} custom-call(s32[4]{0:T(128)S(1)} %get-tuple-element.13.r, s32[4]{0:T(128)S(1)} %pad_add_fusion.5.c, bf16[2048,1024]{1,0:T(8,128)(2,1)S(1)} %copy-done, bf16[256,1280]{1,0:T(8,128)(2,1)S(1)} %collective-permute-done.21.refs_1_, ...), custom_call_target="tpu_custom_call", output_to_operand_aliasing={{}: (11, {})} | custom-call | flops 5368709120 | bytes 15204352 | tf_op jit(solution)/shard_map/apply/pallas_call | solution.py:106
  117.4 10.8 %apply.8.refs_7_ = f32[2048,256]{1,0:T(8,128)S(1)} custom-call(s32[4]{0:T(128)S(1)} %get-tuple-element.13.r, s32[4]{0:T(128)S(1)} %get-tuple-element.14.c, bf16[2048,1024]{1,0:T(8,128)(2,1)S(1)} %copy-done, bf16[256,1280]{1,0:T(8,128)(2,1)S(1)} %collective-permute-done.15.refs_1_, ...), custom_call_target="tpu_custom_call", output_to_operand_aliasing={{}: (11, {})} | custom-call | flops 5368709120 | bytes 15204352 | tf_op jit(solution)/shard_map/apply/pallas_call | solution.py:106
  128.2 8.9 %apply.9 = f32[2048,256]{1,0:T(8,128)S(1)} custom-call(s32[4]{0:T(128)S(1)} %get-tuple-element.13.r, s32[3]{0:T(128)S(1)} %pad_add_fusion.2.c, bf16[2048,1024]{1,0:T(8,128)(2,1)S(1)} %copy-done, bf16[256,1280]{1,0:T(8,128)(2,1)S(1)} %collective-permute-done.10.refs_1_, ...), custom_call_target="tpu_custom_call", output_to_operand_aliasing={{}: (9, {})} | custom-call | flops 4026531840 | bytes 13500416 | tf_op jit(solution)/shard_map/apply/pallas_call | solution.py:106
  137.2 2.7 %collective-permute-start.22 = (f32[1024,256]{1,0:T(8,128)S(1)}, f32[1024,256]{1,0:T(8,128)S(1)}, u32[]{:S(2)}, u32[]{:S(2)}) collective-permute-start(f32[1024,256]{1,0:T(8,128)S(1)} %slice.18), channel_id=1, source_target_pairs={{1,0},{0,1},{3,2},{2,3},{5,4},{4,5},{7,6},{6,7},{9,8},{8,9},{11,10... | collective-permute-start | bytes 3145736 | tf_op jit(solution)/shard_map/ppermute | solution.py:24
  140.0 2.3 %collective-permute-done.22 = f32[1024,256]{1,0:T(8,128)S(1)} collective-permute-done((f32[1024,256]{1,0:T(8,128)S(1)}, f32[1024,256]{1,0:T(8,128)S(1)}, u32[]{:S(2)}, u32[]{:S(2)}) %collective-permute-start.22) | collective-permute-done | bytes 1048608 | tf_op jit(solution)/shard_map/ppermute | solution.py:24
  142.4 1.5 collective-permute-start.23
  143.9 7.6 %collective-permute-done.23 = bf16[512,256]{1,0:T(8,128)(2,1)S(1)} collective-permute-done((bf16[512,256]{1,0:T(8,128)(2,1)S(1)}, bf16[512,256]{1,0:T(8,128)(2,1)S(1)}, u32[]{:S(2)}, u32[]{:S(2)}) %collective-permute-start.23) | collective-permute-done | bytes 262176 | tf_op jit(solution)/shard_map/ppermute | solution.py:24
  (47 shorter events, 10.2 us)
Async XLA Ops:
  0.0 6.8 %collective-permute-start.1 = (bf16[512,1024]{1,0:T(8,128)(2,1)}, bf16[512,1024]{1,0:T(8,128)(2,1)S(1)}, u32[]{:S(2)}, u32[]{:S(2)}) collective-permute-start(bf16[512,1024]{1,0:T(8,128)(2,1)} %own_orb.1), channel_id=1, source_target_pairs={{1,0},{0,1},{3,2},{2,3},{5,4},{4,5},{7,6},{6,7},{9,8},{8,9},{11,10... | collective-permute-start | bytes 3145736 | tf_op jit(solution)/shard_map/ppermute | solution.py:24
  1.4 5.4 %collective-permute-start.2 = (bf16[512,256]{1,0:T(8,128)(2,1)}, bf16[512,256]{1,0:T(8,128)(2,1)S(1)}, u32[]{:S(2)}, u32[]{:S(2)}) collective-permute-start(bf16[512,256]{1,0:T(8,128)(2,1)} %own_tgt.1), channel_id=1, source_target_pairs={{1,0},{0,1},{3,2},{2,3},{5,4},{4,5},{7,6},{6,7},{9,8},{8,9},{11,10... | collective-permute-start | bytes 786440 | tf_op jit(solution)/shard_map/ppermute | solution.py:24
  1.4 4.7 %collective-permute-start = (s32[1,128]{1,0:T(1,128)}, s32[1,128]{1,0:T(1,128)S(1)}, u32[]{:S(2)}, u32[]{:S(2)}) collective-permute-start(s32[1,128]{1,0:T(1,128)} %param.6), channel_id=1, source_target_pairs={{2,0},{0,2},{3,1},{1,3},{6,4},{4,6},{7,5},{5,7},{10,8},{8,10},{11,... | collective-permute-start | bytes 1544 | tf_op jit(solution)/shard_map/ppermute | solution.py:24
  6.8 1.2 copy-start.1
  8.1 0.9 copy-start.3
  9.0 49.2 %copy-start.2 = (bf16[512,1024]{1,0:T(8,128)(2,1)S(1)}, bf16[512,1024]{1,0:T(8,128)(2,1)}, u32[]{:S(2)}) copy-start(bf16[512,1024]{1,0:T(8,128)(2,1)} %own_orb.1) | copy-start | bytes 3145732
  10.5 9.4 %collective-permute-start.3 = (bf16[128,1280]{1,0:T(8,128)(2,1)S(1)}, bf16[128,1280]{1,0:T(8,128)(2,1)S(1)}, u32[]{:S(2)}, u32[]{:S(2)}) collective-permute-start(bf16[128,1280]{1,0:T(8,128)(2,1)S(1)} %get-tuple-element.9), channel_id=1, source_target_pairs={{2,0},{0,2},{3,1},{1,3},{6,4},{4,6},{7,5},{5,7},{10,8},{8,10},{11,... | collective-permute-start | bytes 983048 | tf_op jit(solution)/shard_map/ppermute | solution.py:24
  20.0 7.0 %collective-permute-start.4 = (bf16[128,1280]{1,0:T(8,128)(2,1)S(1)}, bf16[128,1280]{1,0:T(8,128)(2,1)S(1)}, u32[]{:S(2)}, u32[]{:S(2)}) collective-permute-start(bf16[128,1280]{1,0:T(8,128)(2,1)S(1)} %add.187), channel_id=1, source_target_pairs={{4,0},{0,4},{5,1},{1,5},{6,2},{2,6},{7,3},{3,7},{12,8},{8,12},{13,... | collective-permute-start | bytes 983048 | tf_op jit(solution)/shard_map/ppermute | solution.py:24
  26.9 25.2 %collective-permute-start.5 = (bf16[512,1024]{1,0:T(8,128)(2,1)}, bf16[512,1024]{1,0:T(8,128)(2,1)}, u32[]{:S(2)}, u32[]{:S(2)}) collective-permute-start(bf16[512,1024]{1,0:T(8,128)(2,1)} %own_orb.1), channel_id=1, source_target_pairs={{2,0},{0,2},{3,1},{1,3},{6,4},{4,6},{7,5},{5,7},{10,8},{8,10},{11,... | collective-permute-start | bytes 3145736 | tf_op jit(solution)/shard_map/ppermute | solution.py:24
  29.5 28.7 %collective-permute-start.7 = (bf16[256,1280]{1,0:T(8,128)(2,1)S(1)}, bf16[256,1280]{1,0:T(8,128)(2,1)S(1)}, u32[]{:S(2)}, u32[]{:S(2)}) collective-permute-start(bf16[256,1280]{1,0:T(8,128)(2,1)S(1)} %pad_maximum_fusion.refs_1_), channel_id=1, source_target_pairs={{8,0},{16,8},{24,16},{0,24},{9,1},{17,9},{25,17},{1,25},{10,2},{18... | collective-permute-start | bytes 1966088 | tf_op jit(solution)/shard_map/ppermute | solution.py:24
  32.0 27.3 %collective-permute-start.11 = (bf16[256,1280]{1,0:T(8,128)(2,1)S(1)}, bf16[256,1280]{1,0:T(8,128)(2,1)}, u32[]{:S(2)}, u32[]{:S(2)}) collective-permute-start(bf16[256,1280]{1,0:T(8,128)(2,1)S(1)} %pad_maximum_fusion.refs_1_), channel_id=1, source_target_pairs={{96,0},{0,32},{32,64},{64,96},{97,1},{1,33},{33,65},{65,97},{98,2}... | collective-permute-start | bytes 1966088 | tf_op jit(solution)/shard_map/ppermute | solution.py:24
  33.3 27.2 %collective-permute-start.16 = (bf16[256,1280]{1,0:T(8,128)(2,1)S(1)}, bf16[256,1280]{1,0:T(8,128)(2,1)}, u32[]{:S(2)}, u32[]{:S(2)}) collective-permute-start(bf16[256,1280]{1,0:T(8,128)(2,1)S(1)} %pad_maximum_fusion.refs_1_), channel_id=1, source_target_pairs={{24,0},{0,8},{8,16},{16,24},{25,1},{1,9},{9,17},{17,25},{26,2},{2,... | collective-permute-start | bytes 1966088 | tf_op jit(solution)/shard_map/ppermute | solution.py:24
  52.1 25.9 %collective-permute-start.6 = (bf16[512,1024]{1,0:T(8,128)(2,1)}, bf16[512,1024]{1,0:T(8,128)(2,1)}, u32[]{:S(2)}, u32[]{:S(2)}) collective-permute-start(bf16[512,1024]{1,0:T(8,128)(2,1)} %collective-permute-done.5), channel_id=1, source_target_pairs={{1,0},{0,1},{3,2},{2,3},{5,4},{4,5},{7,6},{6,7},{9,8},{8,9},{11,10... | collective-permute-start | bytes 3145736 | tf_op jit(solution)/shard_map/ppermute | solution.py:24
  55.4 16.9 %collective-permute-start.19 = (bf16[256,1280]{1,0:T(8,128)(2,1)S(1)}, bf16[256,1280]{1,0:T(8,128)(2,1)}, u32[]{:S(2)}, u32[]{:S(2)}) collective-permute-start(bf16[256,1280]{1,0:T(8,128)(2,1)S(1)} %pad_maximum_fusion.refs_1_), channel_id=1, source_target_pairs={{32,0},{64,32},{96,64},{0,96},{33,1},{65,33},{97,65},{1,97},{34,2}... | collective-permute-start | bytes 1966088 | tf_op jit(solution)/shard_map/ppermute | solution.py:24
  58.1 17.4 %collective-permute-start.8 = (bf16[256,1280]{1,0:T(8,128)(2,1)S(1)}, bf16[256,1280]{1,0:T(8,128)(2,1)}, u32[]{:S(2)}, u32[]{:S(2)}) collective-permute-start(bf16[256,1280]{1,0:T(8,128)(2,1)S(1)} %collective-permute-done.7.refs_1_), channel_id=1, source_target_pairs={{96,0},{0,32},{32,64},{64,96},{97,1},{1,33},{33,65},{65,97},{98,2}... | collective-permute-start | bytes 1966088 | tf_op jit(solution)/shard_map/ppermute | solution.py:24
  59.3 27.6 %collective-permute-start.12 = (bf16[256,1280]{1,0:T(8,128)(2,1)}, bf16[256,1280]{1,0:T(8,128)(2,1)S(1)}, u32[]{:S(2)}, u32[]{:S(2)}) collective-permute-start(bf16[256,1280]{1,0:T(8,128)(2,1)} %collective-permute-done.11.refs_4_), channel_id=1, source_target_pairs={{24,0},{0,8},{8,16},{16,24},{25,1},{1,9},{9,17},{17,25},{26,2},{2,... | collective-permute-start | bytes 1966088 | tf_op jit(solution)/shard_map/ppermute | solution.py:24
  60.5 29.2 %collective-permute-start.17 = (bf16[256,1280]{1,0:T(8,128)(2,1)}, bf16[256,1280]{1,0:T(8,128)(2,1)}, u32[]{:S(2)}, u32[]{:S(2)}) collective-permute-start(bf16[256,1280]{1,0:T(8,128)(2,1)} %collective-permute-done.16.refs_2_), channel_id=1, source_target_pairs={{32,0},{64,32},{96,64},{0,96},{33,1},{65,33},{97,65},{1,97},{34,2}... | collective-permute-start | bytes 1966088 | tf_op jit(solution)/shard_map/ppermute | solution.py:24
  72.3 30.3 %collective-permute-start.15 = (bf16[256,1280]{1,0:T(8,128)(2,1)S(1)}, bf16[256,1280]{1,0:T(8,128)(2,1)S(1)}, u32[]{:S(2)}, u32[]{:S(2)}) collective-permute-start(bf16[256,1280]{1,0:T(8,128)(2,1)S(1)} %collective-permute-done.7.refs_1_), channel_id=1, source_target_pairs={{8,0},{16,8},{24,16},{0,24},{9,1},{17,9},{25,17},{1,25},{10,2},{18... | collective-permute-start | bytes 1966088 | tf_op jit(solution)/shard_map/ppermute | solution.py:24
  75.5 26.3 %collective-permute-start.21 = (bf16[256,1280]{1,0:T(8,128)(2,1)}, bf16[256,1280]{1,0:T(8,128)(2,1)S(1)}, u32[]{:S(2)}, u32[]{:S(2)}) collective-permute-start(bf16[256,1280]{1,0:T(8,128)(2,1)} %collective-permute-done.19.refs_3_), channel_id=1, source_target_pairs={{8,0},{16,8},{24,16},{0,24},{9,1},{17,9},{25,17},{1,25},{10,2},{18... | collective-permute-start | bytes 1966088 | tf_op jit(solution)/shard_map/ppermute | solution.py:24
  78.0 25.5 %collective-permute-start.9 = (bf16[256,1280]{1,0:T(8,128)(2,1)}, bf16[256,1280]{1,0:T(8,128)(2,1)S(1)}, u32[]{:S(2)}, u32[]{:S(2)}) collective-permute-start(bf16[256,1280]{1,0:T(8,128)(2,1)} %collective-permute-done.8.refs_4_), channel_id=1, source_target_pairs={{96,0},{0,32},{32,64},{64,96},{97,1},{1,33},{33,65},{65,97},{98,2}... | collective-permute-start | bytes 1966088 | tf_op jit(solution)/shard_map/ppermute | solution.py:24
  80.2 2.2 %copy-start = (bf16[2048,1024]{1,0:T(8,128)(2,1)S(1)}, bf16[2048,1024]{1,0:T(8,128)(2,1)}, u32[]{:S(2)}) copy-start(bf16[2048,1024]{1,0:T(8,128)(2,1)} %constant_dynamic-update-slice_fusion.refs_0_) | copy-start | bytes 12582916
  86.9 30.4 %collective-permute-start.20 = (bf16[256,1280]{1,0:T(8,128)(2,1)}, bf16[256,1280]{1,0:T(8,128)(2,1)S(1)}, u32[]{:S(2)}, u32[]{:S(2)}) collective-permute-start(bf16[256,1280]{1,0:T(8,128)(2,1)} %collective-permute-done.19.refs_3_), channel_id=1, source_target_pairs={{32,0},{64,32},{96,64},{0,96},{33,1},{65,33},{97,65},{1,97},{34,2}... | collective-permute-start | bytes 1966088 | tf_op jit(solution)/shard_map/ppermute | solution.py:24
  89.7 27.7 %collective-permute-start.18 = (bf16[256,1280]{1,0:T(8,128)(2,1)}, bf16[256,1280]{1,0:T(8,128)(2,1)S(1)}, u32[]{:S(2)}, u32[]{:S(2)}) collective-permute-start(bf16[256,1280]{1,0:T(8,128)(2,1)} %collective-permute-done.17.refs_3_), channel_id=1, source_target_pairs={{24,0},{0,8},{8,16},{16,24},{25,1},{1,9},{9,17},{17,25},{26,2},{2,... | collective-permute-start | bytes 1966088 | tf_op jit(solution)/shard_map/ppermute | solution.py:24
  101.8 26.4 %collective-permute-start.13 = (bf16[256,1280]{1,0:T(8,128)(2,1)S(1)}, bf16[256,1280]{1,0:T(8,128)(2,1)S(1)}, u32[]{:S(2)}, u32[]{:S(2)}) collective-permute-start(bf16[256,1280]{1,0:T(8,128)(2,1)S(1)} %collective-permute-done.12.refs_2_), channel_id=1, source_target_pairs={{24,0},{0,8},{8,16},{16,24},{25,1},{1,9},{9,17},{17,25},{26,2},{2,... | collective-permute-start | bytes 1966088 | tf_op jit(solution)/shard_map/ppermute | solution.py:24
  102.6 25.6 %collective-permute-start.14 = (bf16[256,1280]{1,0:T(8,128)(2,1)S(1)}, bf16[256,1280]{1,0:T(8,128)(2,1)S(1)}, u32[]{:S(2)}, u32[]{:S(2)}) collective-permute-start(bf16[256,1280]{1,0:T(8,128)(2,1)S(1)} %collective-permute-done.12.refs_2_), channel_id=1, source_target_pairs={{96,0},{0,32},{32,64},{64,96},{97,1},{1,33},{33,65},{65,97},{98,2}... | collective-permute-start | bytes 1966088 | tf_op jit(solution)/shard_map/ppermute | solution.py:24
  103.5 24.7 %collective-permute-start.10 = (bf16[256,1280]{1,0:T(8,128)(2,1)S(1)}, bf16[256,1280]{1,0:T(8,128)(2,1)S(1)}, u32[]{:S(2)}, u32[]{:S(2)}) collective-permute-start(bf16[256,1280]{1,0:T(8,128)(2,1)S(1)} %collective-permute-done.9.refs_4_), channel_id=1, source_target_pairs={{8,0},{16,8},{24,16},{0,24},{9,1},{17,9},{25,17},{1,25},{10,2},{18... | collective-permute-start | bytes 1966088 | tf_op jit(solution)/shard_map/ppermute | solution.py:24
  137.2 5.0 %collective-permute-start.22 = (f32[1024,256]{1,0:T(8,128)S(1)}, f32[1024,256]{1,0:T(8,128)S(1)}, u32[]{:S(2)}, u32[]{:S(2)}) collective-permute-start(f32[1024,256]{1,0:T(8,128)S(1)} %slice.18), channel_id=1, source_target_pairs={{1,0},{0,1},{3,2},{2,3},{5,4},{4,5},{7,6},{6,7},{9,8},{8,9},{11,10... | collective-permute-start | bytes 3145736 | tf_op jit(solution)/shard_map/ppermute | solution.py:24
  142.4 9.1 %collective-permute-start.23 = (bf16[512,256]{1,0:T(8,128)(2,1)S(1)}, bf16[512,256]{1,0:T(8,128)(2,1)S(1)}, u32[]{:S(2)}, u32[]{:S(2)}) collective-permute-start(bf16[512,256]{1,0:T(8,128)(2,1)S(1)} %slice.28), channel_id=1, source_target_pairs={{2,0},{0,2},{3,1},{1,3},{6,4},{4,6},{7,5},{5,7},{10,8},{8,10},{11,... | collective-permute-start | bytes 786440 | tf_op jit(solution)/shard_map/ppermute | solution.py:24

commit v2 on v0

v2 whole, which is shorter than its diff:
```python
import jax
import jax.numpy as jnp
from jax import lax
from jax.experimental import pallas as pl
from jax.experimental.pallas import tpu as pltpu
from jax.sharding import Mesh
from jax.sharding import PartitionSpec as P

AXES = ("y", "x", "zl", "zh", "c")
SLABS = ("y", "x", "zl")
IPTS = ("zh", "c")
RING = 4
NEXT = (((0, 1), "x", 1), ((0, 3), "x", -1), ((1, 0), "y", 1), ((3, 0), "y", -1))


def take_from(value, axis, side):
    n = lax.axis_size(axis)
    return lax.ppermute(value, axis, [((i + side) % n, i) for i in range(n)])


def after(value, *others):
    return lax.optimization_barrier((value, others))[0]


def pick_kernel(bases, ids, orb, tgt, mine, theirs):
    rows, norb = orb.shape
    half = rows // 2
    for k, out in ((0, mine), (1, theirs)):
        row = lax.broadcasted_iota(jnp.int32, (rows, out.shape[0]), 0)
        row = row + jnp.where(row < half, bases[0], bases[1] - half)
        hot = (row == ids[k : k + 1, :]).astype(jnp.bfloat16)
        dims = (((0,), (0,)), ((), ()))
        out[:, :norb] = lax.dot_general(hot, orb[...], dims, preferred_element_type=jnp.float32).astype(out.dtype)
        out[:, norb:] = lax.dot_general(hot, tgt[...], dims, preferred_element_type=jnp.float32).astype(out.dtype)


def pick(bases, ids, orb, tgt):
    out = jax.ShapeDtypeStruct((ids.shape[1], orb.shape[1] + tgt.shape[1]), orb.dtype)
    whole = pl.BlockSpec(memory_space=pltpu.VMEM)
    return pl.pallas_call(
        pick_kernel,
        out_shape=(out, out),
        in_specs=[pl.BlockSpec(memory_space=pltpu.SMEM)] + [whole] * 3,
        out_specs=(whole, whole),
        compiler_params=pltpu.CompilerParams(vmem_limit_bytes=32 << 20),
        name="pick",
    )(bases, ids, orb, tgt)


def apply_parts(slab, parts, potential, rows, cols, total):
    count = len(cols)
    tile = slab.shape[0] // 2
    norb = slab.shape[1]
    points = sum(p.shape[0] for p in parts) // count
    width = parts[0].shape[1]
    nj = width - norb
    first = total is None

    def body(r, c, slab_ref, *refs):
        ours, pots, out = refs[: len(parts)], refs[len(parts) : len(parts) + count], refs[-1]
        here = pl.ds(pl.multiple_of(pl.program_id(0) * tile, tile), tile)
        orb = jnp.concatenate([p[:, :norb] for p in ours], axis=0)
        tgt = jnp.concatenate([p[:, norb:] for p in ours], axis=0)
        products = lax.dot_general(
            slab_ref[here, :], orb, (((1,), (1,)), ((), ())), preferred_element_type=jnp.float32
        )
        pot = jnp.concatenate([p[...] for p in pots], axis=1)
        weighted = (pot.astype(jnp.float32) * products).astype(jnp.bfloat16)
        term = jnp.dot(weighted, tgt, preferred_element_type=jnp.float32)
        out[here, :] = term if first else refs[len(parts) + count][here, :] + term

    def pot_spec(k):
        return pl.BlockSpec((tile, points), lambda i, r, c: (r[i], c[k]))

    whole = pl.BlockSpec(memory_space=pltpu.VMEM)
    specs = [whole] * (1 + len(parts)) + [pot_spec(k) for k in range(count)]
    args = [slab, *parts] + [potential] * count
    if not first:
        specs.append(whole)
        args.append(total)
    flops = 2 * slab.shape[0] * points * count * width
    return pl.pallas_call(
        body,
        out_shape=jax.ShapeDtypeStruct((slab.shape[0], nj), jnp.float32),
        grid_spec=pltpu.PrefetchScalarGridSpec(
            num_scalar_prefetch=2, grid=(2,), in_specs=specs, out_specs=whole
        ),
        input_output_aliases={} if first else {len(args) + 1: 0},
        cost_estimate=pl.CostEstimate(
            flops=flops, bytes_accessed=count * slab.shape[0] * points * 2, transcendentals=0
        ),
        compiler_params=pltpu.CompilerParams(vmem_limit_bytes=24 << 20),
        name="apply",
    )(rows, jnp.stack(cols).astype(jnp.int32), *args)


def local(orbitals, targets, points, potential):
    own_rows = orbitals.shape[0]
    potential = pltpu.with_memory_space_constraint(potential, pltpu.HBM)
    count = points.shape[1]
    y, x, zl, zh, c = (lax.axis_index(a) for a in AXES)
    slab_start = ((y * RING + x) * 2 + zl) * own_rows * 4

    sib_orb = take_from(orbitals, "c", 1)
    sib_tgt = take_from(targets, "c", 1)
    far_points = take_from(points, "zh", 1)
    near_slab = jnp.concatenate([orbitals, sib_orb], axis=0)
    near_tgt = jnp.concatenate([targets, sib_tgt], axis=0)
    near_rows = jnp.stack([zh * 2 + c, zh * 2 + 1 - c]).astype(jnp.int32)
    far_rows = jnp.stack([(1 - zh) * 2 + c, (1 - zh) * 2 + 1 - c]).astype(jnp.int32)
    ids = jnp.concatenate([points, far_points], axis=0)
    mine, theirs = pick((slab_start + near_rows * own_rows).astype(jnp.int32), ids, near_slab, near_tgt)
    block = mine + take_from(theirs, "zh", 1)

    def in_order(own, other):
        low, high = jnp.where(zl == 0, own, other), jnp.where(zl == 0, other, own)
        return jnp.concatenate([low, high], axis=0)

    def column(at):
        return (y + at[0]) % RING * RING + (x + at[1]) % RING

    def near_apply(parts, ats, total):
        return apply_parts(near_slab, parts, potential, near_rows, [column(at) for at in ats], total)

    def far_apply(parts, ats, total):
        return apply_parts(far_slab, parts, potential, far_rows, [column(at) for at in ats], total)

    own = {at: take_from(block, axis, side) for at, axis, side in NEXT}
    other = take_from(block, "zl", 1)
    others = {at: take_from(other, axis, side) for at, axis, side in NEXT}
    far_orb = take_from(after(orbitals, other, *own.values()), "zh", 1)
    pair = {at: in_order(own[at], others[at]) for at in own}
    pair[0, 0] = in_order(block, other)
    near = near_apply([pair[0, 0]], [(0, 0)], None)

    left, down, up, right = (after(pair[at], near) for at in ((3, 0), (0, 1), (1, 0), (0, 3)))
    own[0, 1], own[1, 0] = after(own[0, 1], near), after(own[1, 0], near)
    col = {(0, 2): take_from(own[0, 1], "x", 1), (2, 0): take_from(own[1, 0], "y", 1)}
    pair[3, 3] = take_from(left, "x", -1)
    pair[3, 1] = take_from(down, "y", -1)
    first = tuple(own)
    near = near_apply([pair[at] for at in first], first, near)
    pair[1, 1] = take_from(after(up, near, *col.values()), "x", 1)
    pair[1, 3] = take_from(after(right, near, *col.values()), "y", 1)
    for at in col:
        pair[at] = in_order(col[at], take_from(after(col[at], near), "zl", 1))
    far_sib = take_from(after(far_orb, pair[3, 3]), "c", 1)
    far_slab = jnp.concatenate([far_orb, far_sib], axis=0)
    pair[3, 2] = take_from(pair[3, 3], "x", -1)
    pair[2, 1] = take_from(pair[3, 1], "y", -1)
    far = far_apply([pair[0, 0]] + [pair[at] for at in first], ((0, 0),) + first, None)

    pair[2, 3] = take_from(after(pair[1, 3], far), "y", 1)
    edge = take_from(after(pair[1, 1][:count], far), "x", 1)
    second = ((3, 3), (3, 1), (1, 1), (1, 3))
    near = near_apply([pair[at] for at in second], second, near)

    edge = [edge, take_from(after(pair[1, 3][count:], near), "x", -1)]
    corner = [
        take_from(after(pair[2, 1][:count], near), "x", 1),
        take_from(after(pair[3, 2][count:], near), "y", -1),
    ]
    far = far_apply([pair[at] for at in second], second, far)
    third = ((0, 2), (2, 0), (3, 2), (2, 1))
    near = near_apply([pair[at] for at in third], third, after(near, far))
    far = far_apply([pair[at] for at in third], third, after(far, near))
    last = [pair[2, 3], *edge, *corner]
    ats = ((2, 3), (1, 2), (2, 2))
    far = far_apply(last, ats, far)
    near = near_apply(last, ats, after(near, far))

    far = far[:own_rows] + take_from(far[own_rows:], "c", 1)
    away = take_from(far.astype(jnp.bfloat16), "zh", 1)
    near = near[:own_rows] + take_from(near[own_rows:], "c", 1)
    return (-(near + away.astype(jnp.float32))).astype(jnp.bfloat16)


def solution(mesh):
    torus = Mesh(mesh.devices.reshape(RING, RING, 2, 2, 2), AXES)
    placed = (P(AXES, None), P(AXES, None), P(IPTS, SLABS), P(SLABS, IPTS))
    return jax.shard_map(local, mesh=torus, in_specs=placed, out_specs=P(AXES, None), check_vma=False)
```

time: 363 us -> 144 us (0.40)
  waiting for transfers between devices: 236 us -> 41.6 us
  Pallas kernels: 0 us -> 46 us
  starting transfers between devices: 5.07 us -> 50.7 us
  blocking collectives: 41 us -> 0 us
  matrix products: 34.1 us -> 0 us
  local copies, waits for them, and re-layouts: 28.3 us -> 1.76 us
  between operations: 13.5 us -> 0.48 us
    all_gather x2 -> x0, waiting for transfers between devices: 227 us -> none  [the longest x1 207 us: sent_together(): lax.all_gather(both, axis, axis=dim, tiled=True)]
    ppermute x0 -> x33, starting transfers between devices: none -> 50.7 us  [take_from(): return lax.ppermute(value, axis, [((i + side) % n, i) for i in range(n)])]
    pallas_call x0 -> x10, Pallas kernels: none -> 46 us  [the longest x9 44.6 us: apply_parts(): pl.pallas_call(body, out_shape=jax.ShapeDtypeStruct((slab.shape[0], nj),...]
    ppermute x0 -> x33, waiting for transfers between devices: none -> 41.6 us  [take_from(): return lax.ppermute(value, axis, [((i + side) % n, i) for i in range(n)])]
    dot_general x1 -> x0, matrix products: 34.1 us -> none  [local(): jnp.dot(weighted, target_piece, preferred_element_type=jnp.float32)]
    all_to_all x1 -> x0, blocking collectives: 31.8 us -> none  [summed_on_arrival(): lax.all_to_all(split_up(value, dim, length), axis, 0, 0, tiled=True)]
    unnamed x3 -> x8, local copies, waits for them, and re-layouts: 22.6 us -> 1.38 us
    all_gather x2 -> x0, blocking collectives: 9.21 us -> none  [gather_in_order(): pieces = lax.all_gather(pieces, axes[k])]
  transfers between devices with their start and end apart: 3 -> 33, of which waited for: 3 -> 11; matrix products, arithmetic and copies ran while one was open for 7% -> 3% of each run, Pallas kernels for 0% -> 28%
where the time goes in v2:
time: 144 us
  starting transfers between devices  50.7 us (35%)
  Pallas kernels  46 us (32%)
  waiting for transfers between devices  41.6 us (29%)
  other arithmetic  3.07 us (2%)
  local copies, waits for them, and re-layouts  1.76 us (1%)
    ppermute x33, starting transfers between devices, take_from(): return lax.ppermute(value, axis, [((i + side) % n, i) for i in range(n)])  50.7 us
    pallas_call x9, Pallas kernels, apply_parts(): pl.pallas_call(body, out_shape=jax.ShapeDtypeStruct((slab.shape[0], nj),...  44.6 us
    ppermute x33, waiting for transfers between devices, take_from(): return lax.ppermute(value, axis, [((i + side) % n, i) for i in range(n)])  41.6 us
  transfers between devices with their start and end apart: 33, of which 11 were waited for; matrix products, arithmetic and copies ran while one was open for 3% of the time, Pallas kernels for 28%

profile of v2, /device:TPU:1, one launch (start us, length us, event | category | flops | bytes accessed | tf_op | source)
XLA Modules:
  0.0 143.6 jit_solution(5941333303991677940)
XLA Ops:
  0.0 1.4 collective-permute-start
  1.4 3.8 %collective-permute-start.1 = (s32[1,128]{1,0:T(1,128)}, s32[1,128]{1,0:T(1,128)S(1)}, u32[]{:S(2)}, u32[]{:S(2)}) collective-permute-start(s32[1,128]{1,0:T(1,128)} %param.6), channel_id=1, source_target_pairs={{2,0},{0,2},{3,1},{1,3},{6,4},{4,6},{7,5},{5,7},{10,8},{8,10},{11,... | collective-permute-start | bytes 1544 | tf_op jit(solution)/shard_map/ppermute | solution.py:18
  7.7 1.5 %pick.1 = (bf16[128,1280]{1,0:T(8,128)(2,1)S(1)}, bf16[128,1280]{1,0:T(8,128)(2,1)S(1)}) custom-call(s32[2]{0:T(128)S(1)} %get-tuple-element.49.bases, s32[2,128]{1,0:T(2,128)S(1)} %pad_add_fusion.ids, bf16[1024,1024]{1,0:T(8,128)(2,1)S(1)} %constant_dynamic-update-slice_fusion.orb.slab_ref, bf16[1024,256]{1,0:T(8,128)(2,1)S(1)} %pad_maximum_fusion.7.tgt), custom_call_target="tpu_custom_call" | custom-call | tf_op jit(solution)/shard_map/pick/pallas_call | solution.py:40
  9.2 2.7 %collective-permute-start.3 = (bf16[128,1280]{1,0:T(8,128)(2,1)S(1)}, bf16[128,1280]{1,0:T(8,128)(2,1)S(1)}, u32[]{:S(2)}, u32[]{:S(2)}) collective-permute-start(bf16[128,1280]{1,0:T(8,128)(2,1)S(1)} %get-tuple-element.28), channel_id=1, source_target_pairs={{2,0},{0,2},{3,1},{1,3},{6,4},{4,6},{7,5},{5,7},{10,8},{8,10},{11,... | collective-permute-start | bytes 983048 | tf_op jit(solution)/shard_map/ppermute | solution.py:18
  11.9 7.1 %collective-permute-done.3 = bf16[128,1280]{1,0:T(8,128)(2,1)S(1)} collective-permute-done((bf16[128,1280]{1,0:T(8,128)(2,1)S(1)}, bf16[128,1280]{1,0:T(8,128)(2,1)S(1)}, u32[]{:S(2)}, u32[]{:S(2)}) %collective-permute-start.3) | collective-permute-done | bytes 327712 | tf_op jit(solution)/shard_map/ppermute | solution.py:18
  19.6 2.5 %collective-permute-start.7 = (bf16[128,1280]{1,0:T(8,128)(2,1)S(1)}, bf16[128,1280]{1,0:T(8,128)(2,1)S(1)}, u32[]{:S(2)}, u32[]{:S(2)}) collective-permute-start(bf16[128,1280]{1,0:T(8,128)(2,1)S(1)} %add.258), channel_id=1, source_target_pairs={{8,0},{16,8},{24,16},{0,24},{9,1},{17,9},{25,17},{1,25},{10,2},{18... | collective-permute-start | bytes 983048 | tf_op jit(solution)/shard_map/ppermute | solution.py:18
  22.0 2.7 %collective-permute-start.9 = (bf16[128,1280]{1,0:T(8,128)(2,1)S(1)}, bf16[128,1280]{1,0:T(8,128)(2,1)S(1)}, u32[]{:S(2)}, u32[]{:S(2)}) collective-permute-start(bf16[128,1280]{1,0:T(8,128)(2,1)S(1)} %add.258), channel_id=1, source_target_pairs={{32,0},{64,32},{96,64},{0,96},{33,1},{65,33},{97,65},{1,97},{34,2}... | collective-permute-start | bytes 983048 | tf_op jit(solution)/shard_map/ppermute | solution.py:18
  24.8 1.7 %collective-permute-done.5 = bf16[128,1280]{1,0:T(8,128)(2,1)S(1)} collective-permute-done((bf16[128,1280]{1,0:T(8,128)(2,1)S(1)}, bf16[128,1280]{1,0:T(8,128)(2,1)S(1)}, u32[]{:S(2)}, u32[]{:S(2)}) %collective-permute-start.5) | collective-permute-done | bytes 327712 | tf_op jit(solution)/shard_map/ppermute | solution.py:18
  27.9 2.9 %apply.9.refs_8_ = f32[1024,256]{1,0:T(8,128)S(1)} custom-call(s32[2]{0:T(128)S(1)} %get-tuple-element.50.r, s32[1]{0:T(128)} %bitcast.5.c, bf16[1024,1024]{1,0:T(8,128)(2,1)S(1)} %constant_dynamic-update-slice_fusion.orb.slab_ref, bf16[256,1280]{1,0:T(8,128)(2,1)S(1)} %pad_maximum_fusion.1.refs_0_, bf16[2048,4096]{1,0:T(8,128)(2,1)} %refs_7_.15), custom_call_target="tpu_custom_call" | custom-call | flops 671088640 | bytes 524288 | tf_op jit(solution)/shard_map/apply/pallas_call | solution.py:82
  30.8 2.5 %collective-permute-start.13 = (bf16[128,1280]{1,0:T(8,128)(2,1)S(1)}, bf16[128,1280]{1,0:T(8,128)(2,1)S(1)}, u32[]{:S(2)}, u32[]{:S(2)}) collective-permute-start(bf16[128,1280]{1,0:T(8,128)(2,1)S(1)} %collective-permute-done.7), channel_id=1, source_target_pairs={{8,0},{16,8},{24,16},{0,24},{9,1},{17,9},{25,17},{1,25},{10,2},{18... | collective-permute-start | bytes 983048 | tf_op jit(solution)/shard_map/ppermute | solution.py:18
  33.3 1.4 %collective-permute-start.14 = (bf16[128,1280]{1,0:T(8,128)(2,1)S(1)}, bf16[128,1280]{1,0:T(8,128)(2,1)S(1)}, u32[]{:S(2)}, u32[]{:S(2)}) collective-permute-start(bf16[128,1280]{1,0:T(8,128)(2,1)S(1)} %collective-permute-done.9), channel_id=1, source_target_pairs={{32,0},{64,32},{96,64},{0,96},{33,1},{65,33},{97,65},{1,97},{34,2}... | collective-permute-start | bytes 983048 | tf_op jit(solution)/shard_map/ppermute | solution.py:18
  34.8 1.7 %collective-permute-start.16 = (bf16[512,1024]{1,0:T(8,128)(2,1)S(1)}, bf16[512,1024]{1,0:T(8,128)(2,1)S(1)}, u32[]{:S(2)}, u32[]{:S(2)}) collective-permute-start(bf16[512,1024]{1,0:T(8,128)(2,1)S(1)} %copy-done), channel_id=1, source_target_pairs={{2,0},{0,2},{3,1},{1,3},{6,4},{4,6},{7,5},{5,7},{10,8},{8,10},{11,... | collective-permute-start | bytes 3145736 | tf_op jit(solution)/shard_map/ppermute | solution.py:18
  36.7 2.3 %collective-permute-done.12 = bf16[128,1280]{1,0:T(8,128)(2,1)S(1)} collective-permute-done((bf16[128,1280]{1,0:T(8,128)(2,1)S(1)}, bf16[128,1280]{1,0:T(8,128)(2,1)S(1)}, u32[]{:S(2)}, u32[]{:S(2)}) %collective-permute-start.12) | collective-permute-done | bytes 327712 | tf_op jit(solution)/shard_map/ppermute | solution.py:18
  39.1 4.6 %collective-permute-done.6 = bf16[128,1280]{1,0:T(8,128)(2,1)S(1)} collective-permute-done((bf16[128,1280]{1,0:T(8,128)(2,1)S(1)}, bf16[128,1280]{1,0:T(8,128)(2,1)S(1)}, u32[]{:S(2)}, u32[]{:S(2)}) %collective-permute-start.6) | collective-permute-done | bytes 327712 | tf_op jit(solution)/shard_map/ppermute | solution.py:18
  44.1 2.9 %collective-permute-done.10 = bf16[128,1280]{1,0:T(8,128)(2,1)S(1)} collective-permute-done((bf16[128,1280]{1,0:T(8,128)(2,1)S(1)}, bf16[128,1280]{1,0:T(8,128)(2,1)S(1)}, u32[]{:S(2)}, u32[]{:S(2)}) %collective-permute-start.10) | collective-permute-done | bytes 327712 | tf_op jit(solution)/shard_map/ppermute | solution.py:18
  47.1 2.8 %collective-permute-done.8 = bf16[128,1280]{1,0:T(8,128)(2,1)S(1)} collective-permute-done((bf16[128,1280]{1,0:T(8,128)(2,1)S(1)}, bf16[128,1280]{1,0:T(8,128)(2,1)S(1)}, u32[]{:S(2)}, u32[]{:S(2)}) %collective-permute-start.8) | collective-permute-done | bytes 327712 | tf_op jit(solution)/shard_map/ppermute | solution.py:18
  50.1 5.3 %apply.10.refs_8_ = f32[1024,256]{1,0:T(8,128)S(1)} custom-call(s32[2]{0:T(128)S(1)} %get-tuple-element.50.r, s32[4]{0:T(128)S(1)} %pad_add_fusion.3.c, bf16[1024,1024]{1,0:T(8,128)(2,1)S(1)} %constant_dynamic-update-slice_fusion.orb.slab_ref, bf16[256,1280]{1,0:T(8,128)(2,1)S(1)} %pad_maximum_fusion.2.refs_0_.refs_1_, ...), custom_call_target="tpu_custom_call", output_to_operand_aliasing={{}: (11, {})} | custom-call | flops 2684354560 | bytes 2097152 | tf_op jit(solution)/shard_map/apply/pallas_call | solution.py:82
  58.0 2.6 %collective-permute-start.20 = (bf16[256,1280]{1,0:T(8,128)(2,1)S(1)}, bf16[256,1280]{1,0:T(8,128)(2,1)S(1)}, u32[]{:S(2)}, u32[]{:S(2)}) collective-permute-start(bf16[256,1280]{1,0:T(8,128)(2,1)S(1)} %pad_maximum_fusion.3.refs_2_.refs_3_), channel_id=1, source_target_pairs={{8,0},{16,8},{24,16},{0,24},{9,1},{17,9},{25,17},{1,25},{10,2},{18... | collective-permute-start | bytes 1966088 | tf_op jit(solution)/shard_map/ppermute | solution.py:18
  60.6 3.1 %collective-permute-start.15 = (bf16[256,1280]{1,0:T(8,128)(2,1)S(1)}, bf16[256,1280]{1,0:T(8,128)(2,1)S(1)}, u32[]{:S(2)}, u32[]{:S(2)}) collective-permute-start(bf16[256,1280]{1,0:T(8,128)(2,1)S(1)} %pad_maximum_fusion.refs_1_.refs_2_), channel_id=1, source_target_pairs={{32,0},{64,32},{96,64},{0,96},{33,1},{65,33},{97,65},{1,97},{34,2}... | collective-permute-start | bytes 1966088 | tf_op jit(solution)/shard_map/ppermute | solution.py:18
  64.3 10.4 %collective-permute-start.18 = (bf16[512,1024]{1,0:T(8,128)(2,1)S(1)}, bf16[512,1024]{1,0:T(8,128)(2,1)S(1)}, u32[]{:S(2)}, u32[]{:S(2)}) collective-permute-start(bf16[512,1024]{1,0:T(8,128)(2,1)S(1)} %collective-permute-done.16), channel_id=1, source_target_pairs={{1,0},{0,1},{3,2},{2,3},{5,4},{4,5},{7,6},{6,7},{9,8},{8,9},{11,10... | collective-permute-start | bytes 3145736 | tf_op jit(solution)/shard_map/ppermute | solution.py:18
  75.3 5.3 %apply.12.refs_8_ = f32[1024,256]{1,0:T(8,128)S(1)} custom-call(s32[2]{0:T(128)S(1)} %get-tuple-element.50.r, s32[4]{0:T(128)S(1)} %pad_add_fusion.5.c, bf16[1024,1024]{1,0:T(8,128)(2,1)S(1)} %constant_dynamic-update-slice_fusion.orb.slab_ref, bf16[256,1280]{1,0:T(8,128)(2,1)S(1)} %collective-permute-done.17.refs_0_, ...), custom_call_target="tpu_custom_call", output_to_operand_aliasing={{}: (11, {})} | custom-call | flops 2684354560 | bytes 2097152 | tf_op jit(solution)/shard_map/apply/pallas_call | solution.py:82
  80.8 9.8 %collective-permute-done.26.refs_2_ = bf16[256,1280]{1,0:T(8,128)(2,1)S(1)} collective-permute-done((bf16[256,1280]{1,0:T(8,128)(2,1)S(1)}, bf16[256,1280]{1,0:T(8,128)(2,1)S(1)}, u32[]{:S(2)}, u32[]{:S(2)}) %collective-permute-start.26) | collective-permute-done | bytes 655392 | tf_op jit(solution)/shard_map/ppermute | solution.py:18
  91.2 6.1 %apply.11.refs_8_ = f32[1024,256]{1,0:T(8,128)S(1)} custom-call(s32[2]{0:T(128)S(1)} %pad_add_fusion.4.r, s32[5]{0:T(128)S(1)} %stack.116.c, bf16[1024,1024]{1,0:T(8,128)(2,1)S(1)} %constant_dynamic-update-slice_fusion.2.slab_ref, bf16[256,1280]{1,0:T(8,128)(2,1)S(1)} %pad_maximum_fusion.1.refs_0_, bf16[256,1280]{1,0:T(8,128)(2,1)S(1)} %pad_maximum_fusion.2.refs_0_.refs_1_, ...), custom_call_target="tpu_custom_call" | custom-call | flops 3355443200 | bytes 2621440 | tf_op jit(solution)/shard_map/apply/pallas_call | solution.py:82
  97.3 2.7 %collective-permute-start.19 = (bf16[256,1280]{1,0:T(8,128)(2,1)S(1)}, bf16[256,1280]{1,0:T(8,128)(2,1)S(1)}, u32[]{:S(2)}, u32[]{:S(2)}) collective-permute-start(bf16[256,1280]{1,0:T(8,128)(2,1)S(1)} %collective-permute-done.15.refs_3_), channel_id=1, source_target_pairs={{32,0},{64,32},{96,64},{0,96},{33,1},{65,33},{97,65},{1,97},{34,2}... | collective-permute-start | bytes 1966088 | tf_op jit(solution)/shard_map/ppermute | solution.py:18
  99.9 5.3 %apply.13.refs_8_ = f32[1024,256]{1,0:T(8,128)S(1)} custom-call(s32[2]{0:T(128)S(1)} %pad_add_fusion.4.r, s32[4]{0:T(128)S(1)} %pad_add_fusion.5.c, bf16[1024,1024]{1,0:T(8,128)(2,1)S(1)} %constant_dynamic-update-slice_fusion.2.slab_ref, bf16[256,1280]{1,0:T(8,128)(2,1)S(1)} %collective-permute-done.17.refs_0_, ...), custom_call_target="tpu_custom_call", output_to_operand_aliasing={{}: (11, {})} | custom-call | flops 2684354560 | bytes 2097152 | tf_op jit(solution)/shard_map/apply/pallas_call | solution.py:82
  105.8 5.3 %apply.14.refs_8_ = f32[1024,256]{1,0:T(8,128)S(1)} custom-call(s32[2]{0:T(128)S(1)} %get-tuple-element.50.r, s32[4]{0:T(128)S(1)} %pad_add_fusion.6.c, bf16[1024,1024]{1,0:T(8,128)(2,1)S(1)} %constant_dynamic-update-slice_fusion.orb.slab_ref, bf16[256,1280]{1,0:T(8,128)(2,1)S(1)} %pad_maximum_fusion.5.refs_0_, ...), custom_call_target="tpu_custom_call", output_to_operand_aliasing={{}: (11, {})} | custom-call | flops 2684354560 | bytes 2097152 | tf_op jit(solution)/shard_map/apply/pallas_call | solution.py:82
  111.1 5.3 %apply.15.refs_8_ = f32[1024,256]{1,0:T(8,128)S(1)} custom-call(s32[2]{0:T(128)S(1)} %pad_add_fusion.4.r, s32[4]{0:T(128)S(1)} %pad_add_fusion.6.c, bf16[1024,1024]{1,0:T(8,128)(2,1)S(1)} %constant_dynamic-update-slice_fusion.2.slab_ref, bf16[256,1280]{1,0:T(8,128)(2,1)S(1)} %pad_maximum_fusion.5.refs_0_, ...), custom_call_target="tpu_custom_call", output_to_operand_aliasing={{}: (11, {})} | custom-call | flops 2684354560 | bytes 2097152 | tf_op jit(solution)/shard_map/apply/pallas_call | solution.py:82
  116.5 4.5 %apply.16 = f32[1024,256]{1,0:T(8,128)S(1)} custom-call(s32[2]{0:T(128)S(1)} %pad_add_fusion.4.r, s32[3]{0:T(128)S(1)} %pad_add_fusion.2.c, bf16[1024,1024]{1,0:T(8,128)(2,1)S(1)} %constant_dynamic-update-slice_fusion.2.slab_ref, bf16[256,1280]{1,0:T(8,128)(2,1)S(1)} %collective-permute-done.19.refs_0_, ...), custom_call_target="tpu_custom_call", output_to_operand_aliasing={{}: (11, {})} | custom-call | flops 2013265920 | bytes 1572864 | tf_op jit(solution)/shard_map/apply/pallas_call | solution.py:82
  121.1 8.0 %collective-permute-start.31 = (f32[512,256]{1,0:T(8,128)S(1)}, f32[512,256]{1,0:T(8,128)S(1)}, u32[]{:S(2)}, u32[]{:S(2)}) collective-permute-start(f32[512,256]{1,0:T(8,128)S(1)} %slice.39), channel_id=1, source_target_pairs={{1,0},{0,1},{3,2},{2,3},{5,4},{4,5},{7,6},{6,7},{9,8},{8,9},{11,10... | collective-permute-start | bytes 1572872 | tf_op jit(solution)/shard_map/ppermute | solution.py:18
  129.1 4.6 %apply.17 = f32[1024,256]{1,0:T(8,128)S(1)} custom-call(s32[2]{0:T(128)S(1)} %get-tuple-element.50.r, s32[3]{0:T(128)S(1)} %pad_add_fusion.2.c, bf16[1024,1024]{1,0:T(8,128)(2,1)S(1)} %constant_dynamic-update-slice_fusion.orb.slab_ref, bf16[256,1280]{1,0:T(8,128)(2,1)S(1)} %collective-permute-done.19.refs_0_, ...), custom_call_target="tpu_custom_call", output_to_operand_aliasing={{}: (11, {})} | custom-call | flops 2013265920 | bytes 1572864 | tf_op jit(solution)/shard_map/apply/pallas_call | solution.py:82
  133.9 1.7 %collective-permute-done.30 = f32[512,256]{1,0:T(8,128)S(1)} collective-permute-done((f32[512,256]{1,0:T(8,128)S(1)}, f32[512,256]{1,0:T(8,128)S(1)}, u32[]{:S(2)}, u32[]{:S(2)}) %collective-permute-start.30) | collective-permute-done | bytes 524320 | tf_op jit(solution)/shard_map/ppermute | solution.py:18
  135.7 7.2 %collective-permute-done.32 = bf16[512,256]{1,0:T(8,128)(2,1)S(1)} collective-permute-done((bf16[512,256]{1,0:T(8,128)(2,1)S(1)}, bf16[512,256]{1,0:T(8,128)(2,1)S(1)}, u32[]{:S(2)}, u32[]{:S(2)}) %collective-permute-start.32) | collective-permute-done | bytes 262176 | tf_op jit(solution)/shard_map/ppermute | solution.py:18
  (85 shorter events, 11.5 us)
Async XLA Ops:
  0.0 7.6 %collective-permute-start = (bf16[512,1024]{1,0:T(8,128)(2,1)}, bf16[512,1024]{1,0:T(8,128)(2,1)S(1)}, u32[]{:S(2)}, u32[]{:S(2)}) collective-permute-start(bf16[512,1024]{1,0:T(8,128)(2,1)} %param.4), channel_id=1, source_target_pairs={{1,0},{0,1},{3,2},{2,3},{5,4},{4,5},{7,6},{6,7},{9,8},{8,9},{11,10... | collective-permute-start | bytes 3145736 | tf_op jit(solution)/shard_map/ppermute | solution.py:18
  1.4 5.2 %collective-permute-start.2 = (bf16[512,256]{1,0:T(8,128)(2,1)}, bf16[512,256]{1,0:T(8,128)(2,1)}, u32[]{:S(2)}, u32[]{:S(2)}) collective-permute-start(bf16[512,256]{1,0:T(8,128)(2,1)} %param.5), channel_id=1, source_target_pairs={{1,0},{0,1},{3,2},{2,3},{5,4},{4,5},{7,6},{6,7},{9,8},{8,9},{11,10... | collective-permute-start | bytes 786440 | tf_op jit(solution)/shard_map/ppermute | solution.py:18
  1.4 5.2 %collective-permute-start.1 = (s32[1,128]{1,0:T(1,128)}, s32[1,128]{1,0:T(1,128)S(1)}, u32[]{:S(2)}, u32[]{:S(2)}) collective-permute-start(s32[1,128]{1,0:T(1,128)} %param.6), channel_id=1, source_target_pairs={{2,0},{0,2},{3,1},{1,3},{6,4},{4,6},{7,5},{5,7},{10,8},{8,10},{11,... | collective-permute-start | bytes 1544 | tf_op jit(solution)/shard_map/ppermute | solution.py:18
  9.2 9.8 %collective-permute-start.3 = (bf16[128,1280]{1,0:T(8,128)(2,1)S(1)}, bf16[128,1280]{1,0:T(8,128)(2,1)S(1)}, u32[]{:S(2)}, u32[]{:S(2)}) collective-permute-start(bf16[128,1280]{1,0:T(8,128)(2,1)S(1)} %get-tuple-element.28), channel_id=1, source_target_pairs={{2,0},{0,2},{3,1},{1,3},{6,4},{4,6},{7,5},{5,7},{10,8},{8,10},{11,... | collective-permute-start | bytes 983048 | tf_op jit(solution)/shard_map/ppermute | solution.py:18
  19.1 7.4 %collective-permute-start.5 = (bf16[128,1280]{1,0:T(8,128)(2,1)S(1)}, bf16[128,1280]{1,0:T(8,128)(2,1)S(1)}, u32[]{:S(2)}, u32[]{:S(2)}) collective-permute-start(bf16[128,1280]{1,0:T(8,128)(2,1)S(1)} %add.258), channel_id=1, source_target_pairs={{4,0},{0,4},{5,1},{1,5},{6,2},{2,6},{7,3},{3,7},{12,8},{8,12},{13,... | collective-permute-start | bytes 983048 | tf_op jit(solution)/shard_map/ppermute | solution.py:18
  19.6 11.2 %collective-permute-start.7 = (bf16[128,1280]{1,0:T(8,128)(2,1)S(1)}, bf16[128,1280]{1,0:T(8,128)(2,1)S(1)}, u32[]{:S(2)}, u32[]{:S(2)}) collective-permute-start(bf16[128,1280]{1,0:T(8,128)(2,1)S(1)} %add.258), channel_id=1, source_target_pairs={{8,0},{16,8},{24,16},{0,24},{9,1},{17,9},{25,17},{1,25},{10,2},{18... | collective-permute-start | bytes 983048 | tf_op jit(solution)/shard_map/ppermute | solution.py:18
  22.0 8.8 %collective-permute-start.9 = (bf16[128,1280]{1,0:T(8,128)(2,1)S(1)}, bf16[128,1280]{1,0:T(8,128)(2,1)S(1)}, u32[]{:S(2)}, u32[]{:S(2)}) collective-permute-start(bf16[128,1280]{1,0:T(8,128)(2,1)S(1)} %add.258), channel_id=1, source_target_pairs={{32,0},{64,32},{96,64},{0,96},{33,1},{65,33},{97,65},{1,97},{34,2}... | collective-permute-start | bytes 983048 | tf_op jit(solution)/shard_map/ppermute | solution.py:18
  24.8 10.0 %collective-permute-start.4 = (bf16[128,1280]{1,0:T(8,128)(2,1)S(1)}, bf16[128,1280]{1,0:T(8,128)(2,1)S(1)}, u32[]{:S(2)}, u32[]{:S(2)}) collective-permute-start(bf16[128,1280]{1,0:T(8,128)(2,1)S(1)} %add.258), channel_id=1, source_target_pairs={{24,0},{0,8},{8,16},{16,24},{25,1},{1,9},{9,17},{17,25},{26,2},{2,... | collective-permute-start | bytes 983048 | tf_op jit(solution)/shard_map/ppermute | solution.py:18
  24.8 10.0 %collective-permute-start.11 = (bf16[128,1280]{1,0:T(8,128)(2,1)S(1)}, bf16[128,1280]{1,0:T(8,128)(2,1)S(1)}, u32[]{:S(2)}, u32[]{:S(2)}) collective-permute-start(bf16[128,1280]{1,0:T(8,128)(2,1)S(1)} %add.258), channel_id=1, source_target_pairs={{96,0},{0,32},{32,64},{64,96},{97,1},{1,33},{33,65},{65,97},{98,2}... | collective-permute-start | bytes 983048 | tf_op jit(solution)/shard_map/ppermute | solution.py:18
  26.5 12.4 %collective-permute-start.12 = (bf16[128,1280]{1,0:T(8,128)(2,1)S(1)}, bf16[128,1280]{1,0:T(8,128)(2,1)S(1)}, u32[]{:S(2)}, u32[]{:S(2)}) collective-permute-start(bf16[128,1280]{1,0:T(8,128)(2,1)S(1)} %collective-permute-done.5), channel_id=1, source_target_pairs={{96,0},{0,32},{32,64},{64,96},{97,1},{1,33},{33,65},{65,97},{98,2}... | collective-permute-start | bytes 983048 | tf_op jit(solution)/shard_map/ppermute | solution.py:18
  30.8 24.5 %collective-permute-start.13 = (bf16[128,1280]{1,0:T(8,128)(2,1)S(1)}, bf16[128,1280]{1,0:T(8,128)(2,1)S(1)}, u32[]{:S(2)}, u32[]{:S(2)}) collective-permute-start(bf16[128,1280]{1,0:T(8,128)(2,1)S(1)} %collective-permute-done.7), channel_id=1, source_target_pairs={{8,0},{16,8},{24,16},{0,24},{9,1},{17,9},{25,17},{1,25},{10,2},{18... | collective-permute-start | bytes 983048 | tf_op jit(solution)/shard_map/ppermute | solution.py:18
  33.3 22.0 %collective-permute-start.14 = (bf16[128,1280]{1,0:T(8,128)(2,1)S(1)}, bf16[128,1280]{1,0:T(8,128)(2,1)S(1)}, u32[]{:S(2)}, u32[]{:S(2)}) collective-permute-start(bf16[128,1280]{1,0:T(8,128)(2,1)S(1)} %collective-permute-done.9), channel_id=1, source_target_pairs={{32,0},{64,32},{96,64},{0,96},{33,1},{65,33},{97,65},{1,97},{34,2}... | collective-permute-start | bytes 983048 | tf_op jit(solution)/shard_map/ppermute | solution.py:18
  34.8 25.8 %collective-permute-start.16 = (bf16[512,1024]{1,0:T(8,128)(2,1)S(1)}, bf16[512,1024]{1,0:T(8,128)(2,1)S(1)}, u32[]{:S(2)}, u32[]{:S(2)}) collective-permute-start(bf16[512,1024]{1,0:T(8,128)(2,1)S(1)} %copy-done), channel_id=1, source_target_pairs={{2,0},{0,2},{3,1},{1,3},{6,4},{4,6},{7,5},{5,7},{10,8},{8,10},{11,... | collective-permute-start | bytes 3145736 | tf_op jit(solution)/shard_map/ppermute | solution.py:18
  36.5 7.1 %collective-permute-start.6 = (bf16[128,1280]{1,0:T(8,128)(2,1)S(1)}, bf16[128,1280]{1,0:T(8,128)(2,1)S(1)}, u32[]{:S(2)}, u32[]{:S(2)}) collective-permute-start(bf16[128,1280]{1,0:T(8,128)(2,1)S(1)} %collective-permute-done.5), channel_id=1, source_target_pairs={{24,0},{0,8},{8,16},{16,24},{25,1},{1,9},{9,17},{17,25},{26,2},{2,... | collective-permute-start | bytes 983048 | tf_op jit(solution)/shard_map/ppermute | solution.py:18
  39.0 8.0 %collective-permute-start.10 = (bf16[128,1280]{1,0:T(8,128)(2,1)S(1)}, bf16[128,1280]{1,0:T(8,128)(2,1)S(1)}, u32[]{:S(2)}, u32[]{:S(2)}) collective-permute-start(bf16[128,1280]{1,0:T(8,128)(2,1)S(1)} %collective-permute-done.5), channel_id=1, source_target_pairs={{32,0},{64,32},{96,64},{0,96},{33,1},{65,33},{97,65},{1,97},{34,2}... | collective-permute-start | bytes 983048 | tf_op jit(solution)/shard_map/ppermute | solution.py:18
  43.7 6.2 %collective-permute-start.8 = (bf16[128,1280]{1,0:T(8,128)(2,1)S(1)}, bf16[128,1280]{1,0:T(8,128)(2,1)S(1)}, u32[]{:S(2)}, u32[]{:S(2)}) collective-permute-start(bf16[128,1280]{1,0:T(8,128)(2,1)S(1)} %collective-permute-done.5), channel_id=1, source_target_pairs={{8,0},{16,8},{24,16},{0,24},{9,1},{17,9},{25,17},{1,25},{10,2},{18... | collective-permute-start | bytes 983048 | tf_op jit(solution)/shard_map/ppermute | solution.py:18
  47.0 11.1 %collective-permute-start.17 = (bf16[256,1280]{1,0:T(8,128)(2,1)S(1)}, bf16[256,1280]{1,0:T(8,128)(2,1)S(1)}, u32[]{:S(2)}, u32[]{:S(2)}) collective-permute-start(bf16[256,1280]{1,0:T(8,128)(2,1)S(1)} %pad_maximum_fusion.4.refs_3_.refs_4_), channel_id=1, source_target_pairs={{24,0},{0,8},{8,16},{16,24},{25,1},{1,9},{9,17},{17,25},{26,2},{2,... | collective-permute-start | bytes 1966088 | tf_op jit(solution)/shard_map/ppermute | solution.py:18
  55.4 8.9 %collective-permute-start.28 = (bf16[128,1280]{1,0:T(8,128)(2,1)S(1)}, bf16[128,1280]{1,0:T(8,128)(2,1)S(1)}, u32[]{:S(2)}, u32[]{:S(2)}) collective-permute-start(bf16[128,1280]{1,0:T(8,128)(2,1)S(1)} %collective-permute-done.13), channel_id=1, source_target_pairs={{4,0},{0,4},{5,1},{1,5},{6,2},{2,6},{7,3},{3,7},{12,8},{8,12},{13,... | collective-permute-start | bytes 983048 | tf_op jit(solution)/shard_map/ppermute | solution.py:18
  56.0 18.7 %collective-permute-start.29 = (bf16[128,1280]{1,0:T(8,128)(2,1)S(1)}, bf16[128,1280]{1,0:T(8,128)(2,1)S(1)}, u32[]{:S(2)}, u32[]{:S(2)}) collective-permute-start(bf16[128,1280]{1,0:T(8,128)(2,1)S(1)} %collective-permute-done.14), channel_id=1, source_target_pairs={{4,0},{0,4},{5,1},{1,5},{6,2},{2,6},{7,3},{3,7},{12,8},{8,12},{13,... | collective-permute-start | bytes 983048 | tf_op jit(solution)/shard_map/ppermute | solution.py:18
  57.1 18.0 %collective-permute-start.22 = (bf16[256,1280]{1,0:T(8,128)(2,1)S(1)}, bf16[256,1280]{1,0:T(8,128)(2,1)S(1)}, u32[]{:S(2)}, u32[]{:S(2)}) collective-permute-start(bf16[256,1280]{1,0:T(8,128)(2,1)S(1)} %pad_maximum_fusion.2.refs_0_.refs_1_), channel_id=1, source_target_pairs={{96,0},{0,32},{32,64},{64,96},{97,1},{1,33},{33,65},{65,97},{98,2}... | collective-permute-start | bytes 1966088 | tf_op jit(solution)/shard_map/ppermute | solution.py:18
  58.0 17.2 %collective-permute-start.20 = (bf16[256,1280]{1,0:T(8,128)(2,1)S(1)}, bf16[256,1280]{1,0:T(8,128)(2,1)S(1)}, u32[]{:S(2)}, u32[]{:S(2)}) collective-permute-start(bf16[256,1280]{1,0:T(8,128)(2,1)S(1)} %pad_maximum_fusion.3.refs_2_.refs_3_), channel_id=1, source_target_pairs={{8,0},{16,8},{24,16},{0,24},{9,1},{17,9},{25,17},{1,25},{10,2},{18... | collective-permute-start | bytes 1966088 | tf_op jit(solution)/shard_map/ppermute | solution.py:18
  60.6 14.6 %collective-permute-start.15 = (bf16[256,1280]{1,0:T(8,128)(2,1)S(1)}, bf16[256,1280]{1,0:T(8,128)(2,1)S(1)}, u32[]{:S(2)}, u32[]{:S(2)}) collective-permute-start(bf16[256,1280]{1,0:T(8,128)(2,1)S(1)} %pad_maximum_fusion.refs_1_.refs_2_), channel_id=1, source_target_pairs={{32,0},{64,32},{96,64},{0,96},{33,1},{65,33},{97,65},{1,97},{34,2}... | collective-permute-start | bytes 1966088 | tf_op jit(solution)/shard_map/ppermute | solution.py:18
  64.3 26.8 %collective-permute-start.18 = (bf16[512,1024]{1,0:T(8,128)(2,1)S(1)}, bf16[512,1024]{1,0:T(8,128)(2,1)S(1)}, u32[]{:S(2)}, u32[]{:S(2)}) collective-permute-start(bf16[512,1024]{1,0:T(8,128)(2,1)S(1)} %collective-permute-done.16), channel_id=1, source_target_pairs={{1,0},{0,1},{3,2},{2,3},{5,4},{4,5},{7,6},{6,7},{9,8},{8,9},{11,10... | collective-permute-start | bytes 3145736 | tf_op jit(solution)/shard_map/ppermute | solution.py:18
  74.8 15.9 %collective-permute-start.26 = (bf16[256,1280]{1,0:T(8,128)(2,1)S(1)}, bf16[256,1280]{1,0:T(8,128)(2,1)S(1)}, u32[]{:S(2)}, u32[]{:S(2)}) collective-permute-start(bf16[256,1280]{1,0:T(8,128)(2,1)S(1)} %collective-permute-done.17.refs_0_), channel_id=1, source_target_pairs={{24,0},{0,8},{8,16},{16,24},{25,1},{1,9},{9,17},{17,25},{26,2},{2,... | collective-permute-start | bytes 1966088 | tf_op jit(solution)/shard_map/ppermute | solution.py:18
  75.1 15.6 %collective-permute-start.24 = (bf16[256,1280]{1,0:T(8,128)(2,1)S(1)}, bf16[256,1280]{1,0:T(8,128)(2,1)S(1)}, u32[]{:S(2)}, u32[]{:S(2)}) collective-permute-start(bf16[256,1280]{1,0:T(8,128)(2,1)S(1)} %collective-permute-done.22.refs_1_), channel_id=1, source_target_pairs={{96,0},{0,32},{32,64},{64,96},{97,1},{1,33},{33,65},{65,97},{98,2}... | collective-permute-start | bytes 1966088 | tf_op jit(solution)/shard_map/ppermute | solution.py:18
  80.6 35.8 %collective-permute-start.23 = (bf16[128,1280]{1,0:T(8,128)(2,1)S(1)}, bf16[128,1280]{1,0:T(8,128)(2,1)S(1)}, u32[]{:S(2)}, u32[]{:S(2)}) collective-permute-start(bf16[128,1280]{1,0:T(8,128)(2,1)S(1)} %slice.33), channel_id=1, source_target_pairs={{24,0},{0,8},{8,16},{16,24},{25,1},{1,9},{9,17},{17,25},{26,2},{2,... | collective-permute-start | bytes 983048 | tf_op jit(solution)/shard_map/ppermute | solution.py:18
  90.7 25.8 %collective-permute-start.27 = (bf16[128,1280]{1,0:T(8,128)(2,1)S(1)}, bf16[128,1280]{1,0:T(8,128)(2,1)S(1)}, u32[]{:S(2)}, u32[]{:S(2)}) collective-permute-start(bf16[128,1280]{1,0:T(8,128)(2,1)S(1)} %slice.35), channel_id=1, source_target_pairs={{96,0},{0,32},{32,64},{64,96},{97,1},{1,33},{33,65},{65,97},{98,2}... | collective-permute-start | bytes 983048 | tf_op jit(solution)/shard_map/ppermute | solution.py:18
  90.8 25.7 %collective-permute-start.25 = (bf16[128,1280]{1,0:T(8,128)(2,1)S(1)}, bf16[128,1280]{1,0:T(8,128)(2,1)S(1)}, u32[]{:S(2)}, u32[]{:S(2)}) collective-permute-start(bf16[128,1280]{1,0:T(8,128)(2,1)S(1)} %slice.34), channel_id=1, source_target_pairs={{8,0},{16,8},{24,16},{0,24},{9,1},{17,9},{25,17},{1,25},{10,2},{18... | collective-permute-start | bytes 983048 | tf_op jit(solution)/shard_map/ppermute | solution.py:18
  97.3 19.2 %collective-permute-start.19 = (bf16[256,1280]{1,0:T(8,128)(2,1)S(1)}, bf16[256,1280]{1,0:T(8,128)(2,1)S(1)}, u32[]{:S(2)}, u32[]{:S(2)}) collective-permute-start(bf16[256,1280]{1,0:T(8,128)(2,1)S(1)} %collective-permute-done.15.refs_3_), channel_id=1, source_target_pairs={{32,0},{64,32},{96,64},{0,96},{33,1},{65,33},{97,65},{1,97},{34,2}... | collective-permute-start | bytes 1966088 | tf_op jit(solution)/shard_map/ppermute | solution.py:18
  105.2 11.2 %collective-permute-start.21 = (bf16[128,1280]{1,0:T(8,128)(2,1)S(1)}, bf16[128,1280]{1,0:T(8,128)(2,1)S(1)}, u32[]{:S(2)}, u32[]{:S(2)}) collective-permute-start(bf16[128,1280]{1,0:T(8,128)(2,1)S(1)} %slice.32), channel_id=1, source_target_pairs={{8,0},{16,8},{24,16},{0,24},{9,1},{17,9},{25,17},{1,25},{10,2},{18... | collective-permute-start | bytes 983048 | tf_op jit(solution)/shard_map/ppermute | solution.py:18
  121.1 12.7 %collective-permute-start.31 = (f32[512,256]{1,0:T(8,128)S(1)}, f32[512,256]{1,0:T(8,128)S(1)}, u32[]{:S(2)}, u32[]{:S(2)}) collective-permute-start(f32[512,256]{1,0:T(8,128)S(1)} %slice.39), channel_id=1, source_target_pairs={{1,0},{0,1},{3,2},{2,3},{5,4},{4,5},{7,6},{6,7},{9,8},{8,9},{11,10... | collective-permute-start | bytes 1572872 | tf_op jit(solution)/shard_map/ppermute | solution.py:18
  133.8 9.0 %collective-permute-start.32 = (bf16[512,256]{1,0:T(8,128)(2,1)S(1)}, bf16[512,256]{1,0:T(8,128)(2,1)S(1)}, u32[]{:S(2)}, u32[]{:S(2)}) collective-permute-start(bf16[512,256]{1,0:T(8,128)(2,1)S(1)} %fusion), channel_id=1, source_target_pairs={{2,0},{0,2},{3,1},{1,3},{6,4},{4,6},{7,5},{5,7},{10,8},{8,10},{11,... | collective-permute-start | bytes 786440 | tf_op jit(solution)/shard_map/ppermute | solution.py:18
  (4 other events, 22.1 us)

commit v3 on v2

--- a/solution.py
+++ b/solution.py
@@ -47,7 +47,7 @@
     )(bases, ids, orb, tgt)
 
 
-def apply_parts(slab, parts, potential, rows, cols, total):
+def apply_parts(slab, parts, potential, rows, cols, total, last=False):
     count = len(cols)
     tile = slab.shape[0] // 2
     norb = slab.shape[1]
@@ -57,7 +57,7 @@
     first = total is None
 
     def body(r, c, slab_ref, *refs):
-        ours, pots, out = refs[: len(parts)], refs[len(parts) : len(parts) + count], refs[-1]
+        ours, pots = refs[: len(parts)], refs[len(parts) : len(parts) + count]
         here = pl.ds(pl.multiple_of(pl.program_id(0) * tile, tile), tile)
         orb = jnp.concatenate([p[:, :norb] for p in ours], axis=0)
         tgt = jnp.concatenate([p[:, norb:] for p in ours], axis=0)
@@ -67,29 +67,41 @@
         pot = jnp.concatenate([p[...] for p in pots], axis=1)
         weighted = (pot.astype(jnp.float32) * products).astype(jnp.bfloat16)
         term = jnp.dot(weighted, tgt, preferred_element_type=jnp.float32)
-        out[here, :] = term if first else refs[len(parts) + count][here, :] + term
+        if not first:
+            term = refs[len(parts) + count][here, :] + term
+        if not last:
+            refs[-1][here, :] = term
+            return
+        for k, out in enumerate(refs[-2:]):
+
+            @pl.when(pl.program_id(0) == k)
+            def _():
+                out[...] = term
 
     def pot_spec(k):
         return pl.BlockSpec((tile, points), lambda i, r, c: (r[i], c[k]))
 
     whole = pl.BlockSpec(memory_space=pltpu.VMEM)
-    specs = [whole] * (1 + len(parts)) + [pot_spec(k) for k in range(count)]
+    fixed = [pl.BlockSpec(p.shape, lambda i, r, c: (0, 0)) for p in parts] if last else [whole] * len(parts)
+    specs = [whole, *fixed] + [pot_spec(k) for k in range(count)]
     args = [slab, *parts] + [potential] * count
     if not first:
         specs.append(whole)
         args.append(total)
     flops = 2 * slab.shape[0] * points * count * width
+    half = jax.ShapeDtypeStruct((tile, nj), jnp.float32)
+    out_spec = pl.BlockSpec((tile, nj), lambda i, r, c: (0, 0))
     return pl.pallas_call(
         body,
-        out_shape=jax.ShapeDtypeStruct((slab.shape[0], nj), jnp.float32),
+        out_shape=(half, half) if last else jax.ShapeDtypeStruct((slab.shape[0], nj), jnp.float32),
         grid_spec=pltpu.PrefetchScalarGridSpec(
-            num_scalar_prefetch=2, grid=(2,), in_specs=specs, out_specs=whole
+            num_scalar_prefetch=2, grid=(2,), in_specs=specs, out_specs=(out_spec,) * 2 if last else whole
         ),
-        input_output_aliases={} if first else {len(args) + 1: 0},
+        input_output_aliases={} if first or last else {len(args) + 1: 0},
         cost_estimate=pl.CostEstimate(
             flops=flops, bytes_accessed=count * slab.shape[0] * points * 2, transcendentals=0
         ),
-        compiler_params=pltpu.CompilerParams(vmem_limit_bytes=24 << 20),
+        compiler_params=pltpu.CompilerParams(vmem_limit_bytes=15 << 20),
         name="apply",
     )(rows, jnp.stack(cols).astype(jnp.int32), *args)
 
@@ -119,59 +131,60 @@
     def column(at):
         return (y + at[0]) % RING * RING + (x + at[1]) % RING
 
-    def near_apply(parts, ats, total):
-        return apply_parts(near_slab, parts, potential, near_rows, [column(at) for at in ats], total)
+    def near_apply(parts, ats, total, last=False):
+        return apply_parts(near_slab, parts, potential, near_rows, [column(at) for at in ats], total, last)
 
-    def far_apply(parts, ats, total):
-        return apply_parts(far_slab, parts, potential, far_rows, [column(at) for at in ats], total)
+    def far_apply(parts, ats, total, last=False):
+        return apply_parts(far_slab, parts, potential, far_rows, [column(at) for at in ats], total, last)
 
     own = {at: take_from(block, axis, side) for at, axis, side in NEXT}
     other = take_from(block, "zl", 1)
+    far_orb = take_from(after(orbitals, other), "zh", 1)
     others = {at: take_from(other, axis, side) for at, axis, side in NEXT}
-    far_orb = take_from(after(orbitals, other, *own.values()), "zh", 1)
     pair = {at: in_order(own[at], others[at]) for at in own}
     pair[0, 0] = in_order(block, other)
     near = near_apply([pair[0, 0]], [(0, 0)], None)
 
-    left, down, up, right = (after(pair[at], near) for at in ((3, 0), (0, 1), (1, 0), (0, 3)))
-    own[0, 1], own[1, 0] = after(own[0, 1], near), after(own[1, 0], near)
-    col = {(0, 2): take_from(own[0, 1], "x", 1), (2, 0): take_from(own[1, 0], "y", 1)}
-    pair[3, 3] = take_from(left, "x", -1)
-    pair[3, 1] = take_from(down, "y", -1)
-    first = tuple(own)
+    def joined(whole, half):
+        return jnp.concatenate([pair[whole], half], axis=0)
+
+    from_right = take_from(joined((1, 0), pair[0, 1][:count]), "x", 1)
+    from_left = take_from(joined((3, 0), pair[0, 3][count:]), "x", -1)
+    from_up = take_from(joined((0, 3), pair[1, 0][:count]), "y", 1)
+    from_down = take_from(joined((0, 1), pair[3, 0][count:]), "y", -1)
+    first = tuple(at for at, _, _ in NEXT)
+    far_sib = take_from(far_orb, "c", 1)
+    far_slab = jnp.concatenate([far_orb, far_sib], axis=0)
     near = near_apply([pair[at] for at in first], first, near)
-    pair[1, 1] = take_from(after(up, near, *col.values()), "x", 1)
-    pair[1, 3] = take_from(after(right, near, *col.values()), "y", 1)
-    for at in col:
-        pair[at] = in_order(col[at], take_from(after(col[at], near), "zl", 1))
-    far_sib = take_from(after(far_orb, pair[3, 3]), "c", 1)
-    far_slab = jnp.concatenate([far_orb, far_sib], axis=0)
-    pair[3, 2] = take_from(pair[3, 3], "x", -1)
-    pair[2, 1] = take_from(pair[3, 1], "y", -1)
     far = far_apply([pair[0, 0]] + [pair[at] for at in first], ((0, 0),) + first, None)
+    both = 2 * count
+    pair[1, 1], pair[3, 3] = from_right[:both], from_left[:both]
+    pair[1, 3], pair[3, 1] = from_up[:both], from_down[:both]
+    pair[0, 2] = jnp.concatenate([from_right[both:], from_left[both:]], axis=0)
+    pair[2, 0] = jnp.concatenate([from_up[both:], from_down[both:]], axis=0)
 
-    pair[2, 3] = take_from(after(pair[1, 3], far), "y", 1)
-    edge = take_from(after(pair[1, 1][:count], far), "x", 1)
-    second = ((3, 3), (3, 1), (1, 1), (1, 3))
-    near = near_apply([pair[at] for at in second], second, near)
+    low, high = after(pair[1, 1], near, far), after(pair[3, 3], near, far)
+    pair[1, 2] = take_from(low, "x", 1)
+    pair[3, 2] = take_from(high, "x", -1)
+    pair[2, 1] = take_from(low, "y", 1)
+    pair[2, 3] = take_from(high, "y", -1)
+    second = ((1, 1), (3, 3), (1, 3), (3, 1), (0, 2), (2, 0))
+    far = far_apply([pair[at] for at in second], second, far)
+    near = near_apply([pair[at] for at in second], second, after(near, far))
 
-    edge = [edge, take_from(after(pair[1, 3][count:], near), "x", -1)]
-    corner = [
-        take_from(after(pair[2, 1][:count], near), "x", 1),
-        take_from(after(pair[3, 2][count:], near), "y", -1),
+    third = ((1, 2), (3, 2), (2, 1), (2, 3))
+    part = both // 4
+    sides = (((2, 1), "x", 1), ((2, 3), "x", -1), ((1, 2), "y", 1), ((3, 2), "y", -1))
+    last = [
+        take_from(after(pair[at][k * part : (k + 1) * part], near, far), axis, side)
+        for k, (at, axis, side) in enumerate(sides)
     ]
-    far = far_apply([pair[at] for at in second], second, far)
-    third = ((0, 2), (2, 0), (3, 2), (2, 1))
-    near = near_apply([pair[at] for at in third], third, after(near, far))
-    far = far_apply([pair[at] for at in third], third, after(far, near))
-    last = [pair[2, 3], *edge, *corner]
-    ats = ((2, 3), (1, 2), (2, 2))
-    far = far_apply(last, ats, far)
-    near = near_apply(last, ats, after(near, far))
-
-    far = far[:own_rows] + take_from(far[own_rows:], "c", 1)
-    away = take_from(far.astype(jnp.bfloat16), "zh", 1)
-    near = near[:own_rows] + take_from(near[own_rows:], "c", 1)
+    far = far_apply([pair[at] for at in third], third, far)
+    kept, sent = far_apply(last, [(2, 2)], far, True)
+    far = (kept + take_from(sent, "c", 1)).astype(jnp.bfloat16)
+    away = take_from(far, "zh", 1)
+    kept, sent = near_apply([pair[at] for at in third] + last, third + ((2, 2),), after(near, far), True)
+    near = kept + take_from(after(sent, away), "c", 1)
     return (-(near + away.astype(jnp.float32))).astype(jnp.bfloat16)
 
 

time: 144 us -> 144 us (level)
  waiting for transfers between devices: 41.6 us -> 33.3 us
  local copies, waits for them, and re-layouts: 1.76 us -> 9.92 us
  Pallas kernels: 46 us -> 44.5 us
    ppermute x33 -> x30, waiting for transfers between devices: 41.6 us -> 33.3 us  [take_from(): return lax.ppermute(value, axis, [((i + side) % n, i) for i in range(n)])]
    unnamed x8 -> x36, local copies, waits for them, and re-layouts: 1.38 us -> 8.36 us
    pallas_call x9 -> x8, Pallas kernels: 44.6 us -> 43 us  [apply_parts(): pl.pallas_call(body, out_shape=(half, half) if last else jax.ShapeDtypeSt...]
    ppermute x33 -> x30, starting transfers between devices: 50.7 us -> 50.3 us  [take_from(): return lax.ppermute(value, axis, [((i + side) % n, i) for i in range(n)])]
  transfers between devices with their start and end apart: 33 -> 30, of which waited for: 11 -> 11; matrix products, arithmetic and copies ran while one was open for 3% -> 3% of each run, Pallas kernels for 28% -> 23%
where the time goes in v3:
time: 144 us; the launch traced here: 143 us
  starting transfers between devices  50.3 us (35%)
  Pallas kernels  44.5 us (31%)
  waiting for transfers between devices  33.3 us (23%)
  local copies, waits for them, and re-layouts  9.92 us (7%)
  other arithmetic  4.39 us (3%)
    ppermute x30, starting transfers between devices, take_from(): return lax.ppermute(value, axis, [((i + side) % n, i) for i in range(n)])  50.3 us
    pallas_call x8, Pallas kernels, apply_parts(): pl.pallas_call(body, out_shape=(half, half) if last else jax.ShapeDtypeSt...  43 us
    ppermute x30, waiting for transfers between devices, take_from(): return lax.ppermute(value, axis, [((i + side) % n, i) for i in range(n)])  33.3 us
    unnamed x36, local copies, waits for them, and re-layouts  8.36 us
  transfers between devices with their start and end apart: 30, of which 11 were waited for; matrix products, arithmetic and copies ran while one was open for 3% of the time, Pallas kernels for 23%

profile of v3, /device:TPU:1, one launch (start us, length us, event | category | flops | bytes accessed | tf_op | source)
XLA Modules:
  0.0 142.9 jit_solution(16006027464441127303)
XLA Ops:
  1.4 3.7 %collective-permute-start.1 = (s32[1,128]{1,0:T(1,128)}, s32[1,128]{1,0:T(1,128)S(1)}, u32[]{:S(2)}, u32[]{:S(2)}) collective-permute-start(s32[1,128]{1,0:T(1,128)} %param.6), channel_id=1, source_target_pairs={{2,0},{0,2},{3,1},{1,3},{6,4},{4,6},{7,5},{5,7},{10,8},{8,10},{11,... | collective-permute-start | bytes 1544 | tf_op jit(solution)/shard_map/ppermute | solution.py:18
  8.1 1.4 %pick.1 = (bf16[128,1280]{1,0:T(8,128)(2,1)S(1)}, bf16[128,1280]{1,0:T(8,128)(2,1)S(1)}) custom-call(s32[2]{0:T(128)S(1)} %get-tuple-element.37.bases, s32[2,128]{1,0:T(2,128)S(1)} %pad_add_fusion.ids, bf16[1024,1024]{1,0:T(8,128)(2,1)S(1)} %constant_dynamic-update-slice_fusion.orb.slab_ref, bf16[1024,256]{1,0:T(8,128)(2,1)S(1)} %pad_maximum_fusion.11.tgt), custom_call_target="tpu_custom_call" | custom-call | tf_op jit(solution)/shard_map/pick/pallas_call | solution.py:40
  9.5 2.3 %collective-permute-start.3 = (bf16[128,1280]{1,0:T(8,128)(2,1)S(1)}, bf16[128,1280]{1,0:T(8,128)(2,1)S(1)}, u32[]{:S(2)}, u32[]{:S(2)}) collective-permute-start(bf16[128,1280]{1,0:T(8,128)(2,1)S(1)} %get-tuple-element.22), channel_id=1, source_target_pairs={{2,0},{0,2},{3,1},{1,3},{6,4},{4,6},{7,5},{5,7},{10,8},{8,10},{11,... | collective-permute-start | bytes 983048 | tf_op jit(solution)/shard_map/ppermute | solution.py:18
  12.0 8.1 %collective-permute-done.3 = bf16[128,1280]{1,0:T(8,128)(2,1)S(1)} collective-permute-done((bf16[128,1280]{1,0:T(8,128)(2,1)S(1)}, bf16[128,1280]{1,0:T(8,128)(2,1)S(1)}, u32[]{:S(2)}, u32[]{:S(2)}) %collective-permute-start.3) | collective-permute-done | bytes 327712 | tf_op jit(solution)/shard_map/ppermute | solution.py:18
  22.1 2.5 %collective-permute-start.7 = (bf16[128,1280]{1,0:T(8,128)(2,1)S(1)}, bf16[128,1280]{1,0:T(8,128)(2,1)S(1)}, u32[]{:S(2)}, u32[]{:S(2)}) collective-permute-start(bf16[128,1280]{1,0:T(8,128)(2,1)S(1)} %add.264), channel_id=1, source_target_pairs={{8,0},{16,8},{24,16},{0,24},{9,1},{17,9},{25,17},{1,25},{10,2},{18... | collective-permute-start | bytes 983048 | tf_op jit(solution)/shard_map/ppermute | solution.py:18
  24.5 1.5 %collective-permute-start.4 = (bf16[128,1280]{1,0:T(8,128)(2,1)S(1)}, bf16[128,1280]{1,0:T(8,128)(2,1)S(1)}, u32[]{:S(2)}, u32[]{:S(2)}) collective-permute-start(bf16[128,1280]{1,0:T(8,128)(2,1)S(1)} %add.264), channel_id=1, source_target_pairs={{32,0},{64,32},{96,64},{0,96},{33,1},{65,33},{97,65},{1,97},{34,2}... | collective-permute-start | bytes 983048 | tf_op jit(solution)/shard_map/ppermute | solution.py:18
  26.1 2.2 %collective-permute-done.5 = bf16[128,1280]{1,0:T(8,128)(2,1)S(1)} collective-permute-done((bf16[128,1280]{1,0:T(8,128)(2,1)S(1)}, bf16[128,1280]{1,0:T(8,128)(2,1)S(1)}, u32[]{:S(2)}, u32[]{:S(2)}) %collective-permute-start.5) | collective-permute-done | bytes 327712 | tf_op jit(solution)/shard_map/ppermute | solution.py:18
  29.7 1.5 %collective-permute-start.14 = (bf16[512,1024]{1,0:T(8,128)(2,1)S(1)}, bf16[512,1024]{1,0:T(8,128)(2,1)S(1)}, u32[]{:S(2)}, u32[]{:S(2)}) collective-permute-start(bf16[512,1024]{1,0:T(8,128)(2,1)S(1)} %copy-done.14), channel_id=1, source_target_pairs={{2,0},{0,2},{3,1},{1,3},{6,4},{4,6},{7,5},{5,7},{10,8},{8,10},{11,... | collective-permute-start | bytes 3145736 | tf_op jit(solution)/shard_map/ppermute | solution.py:18
  31.1 5.4 %collective-permute-done.13 = bf16[128,1280]{1,0:T(8,128)(2,1)S(1)} collective-permute-done((bf16[128,1280]{1,0:T(8,128)(2,1)S(1)}, bf16[128,1280]{1,0:T(8,128)(2,1)S(1)}, u32[]{:S(2)}, u32[]{:S(2)}) %collective-permute-start.13) | collective-permute-done | bytes 327712 | tf_op jit(solution)/shard_map/ppermute | solution.py:18
  36.6 2.5 %collective-permute-start.8 = (bf16[128,1280]{1,0:T(8,128)(2,1)S(1)}, bf16[128,1280]{1,0:T(8,128)(2,1)S(1)}, u32[]{:S(2)}, u32[]{:S(2)}) collective-permute-start(bf16[128,1280]{1,0:T(8,128)(2,1)S(1)} %collective-permute-done.5), channel_id=1, source_target_pairs={{8,0},{16,8},{24,16},{0,24},{9,1},{17,9},{25,17},{1,25},{10,2},{18... | collective-permute-start | bytes 983048 | tf_op jit(solution)/shard_map/ppermute | solution.py:18
  39.2 1.5 %collective-permute-start.6 = (bf16[128,1280]{1,0:T(8,128)(2,1)S(1)}, bf16[128,1280]{1,0:T(8,128)(2,1)S(1)}, u32[]{:S(2)}, u32[]{:S(2)}) collective-permute-start(bf16[128,1280]{1,0:T(8,128)(2,1)S(1)} %collective-permute-done.5), channel_id=1, source_target_pairs={{32,0},{64,32},{96,64},{0,96},{33,1},{65,33},{97,65},{1,97},{34,2}... | collective-permute-start | bytes 983048 | tf_op jit(solution)/shard_map/ppermute | solution.py:18
  40.6 2.5 %collective-permute-done.8 = bf16[128,1280]{1,0:T(8,128)(2,1)S(1)} collective-permute-done((bf16[128,1280]{1,0:T(8,128)(2,1)S(1)}, bf16[128,1280]{1,0:T(8,128)(2,1)S(1)}, u32[]{:S(2)}, u32[]{:S(2)}) %collective-permute-start.8) | collective-permute-done | bytes 327712 | tf_op jit(solution)/shard_map/ppermute | solution.py:18
  45.5 5.7 %collective-permute-done.11 = bf16[128,1280]{1,0:T(8,128)(2,1)S(1)} collective-permute-done((bf16[128,1280]{1,0:T(8,128)(2,1)S(1)}, bf16[128,1280]{1,0:T(8,128)(2,1)S(1)}, u32[]{:S(2)}, u32[]{:S(2)}) %collective-permute-start.11) | collective-permute-done | bytes 327712 | tf_op jit(solution)/shard_map/ppermute | solution.py:18
  51.8 2.7 %collective-permute-start.9 = (bf16[384,1280]{1,0:T(8,128)(2,1)S(1)}, bf16[384,1280]{1,0:T(8,128)(2,1)S(1)}, u32[]{:S(2)}, u32[]{:S(2)}) collective-permute-start(bf16[384,1280]{1,0:T(8,128)(2,1)S(1)} %get-tuple-element.50), channel_id=1, source_target_pairs={{8,0},{16,8},{24,16},{0,24},{9,1},{17,9},{25,17},{1,25},{10,2},{18... | collective-permute-start | bytes 2949128 | tf_op jit(solution)/shard_map/ppermute | solution.py:18
  54.5 1.4 collective-permute-start.21
  55.9 2.9 %apply.8.refs_8_ = f32[1024,256]{1,0:T(8,128)S(1)} custom-call(s32[2]{0:T(128)S(1)} %get-tuple-element.38.r, s32[1]{0:T(128)} %bitcast.11.c, bf16[1024,1024]{1,0:T(8,128)(2,1)S(1)} %constant_dynamic-update-slice_fusion.orb.slab_ref, bf16[256,1280]{1,0:T(8,128)(2,1)S(1)} %pad_maximum_fusion.8.refs_0_, bf16[2048,4096]{1,0:T(8,128)(2,1)} %refs_12_.1), custom_call_target="tpu_custom_call" | custom-call | flops 671088640 | bytes 524288 | tf_op jit(solution)/shard_map/apply/pallas_call | solution.py:94
  58.9 5.9 %collective-permute-start.15 = (bf16[512,1024]{1,0:T(8,128)(2,1)S(1)}, bf16[512,1024]{1,0:T(8,128)(2,1)S(1)}, u32[]{:S(2)}, u32[]{:S(2)}) collective-permute-start(bf16[512,1024]{1,0:T(8,128)(2,1)S(1)} %collective-permute-done.14), channel_id=1, source_target_pairs={{1,0},{0,1},{3,2},{2,3},{5,4},{4,5},{7,6},{6,7},{9,8},{8,9},{11,10... | collective-permute-start | bytes 3145736 | tf_op jit(solution)/shard_map/ppermute | solution.py:18
  64.9 5.3 %apply.9.refs_12_ = f32[1024,256]{1,0:T(8,128)S(1)} custom-call(s32[2]{0:T(128)S(1)} %get-tuple-element.38.r, s32[4]{0:T(128)S(1)} %pad_add_fusion.2.c, bf16[1024,1024]{1,0:T(8,128)(2,1)S(1)} %constant_dynamic-update-slice_fusion.orb.slab_ref, bf16[256,1280]{1,0:T(8,128)(2,1)S(1)} %get-tuple-element.53.refs_0_.refs_1_, ...), custom_call_target="tpu_custom_call", output_to_operand_aliasing={{}: (11, {})} | custom-call | flops 2684354560 | bytes 2097152 | tf_op jit(solution)/shard_map/apply/pallas_call | solution.py:94
  70.2 1.6 %collective-permute-done.17 = bf16[384,1280]{1,0:T(8,128)(2,1)S(1)} collective-permute-done((bf16[384,1280]{1,0:T(8,128)(2,1)S(1)}, bf16[384,1280]{1,0:T(8,128)(2,1)S(1)}, u32[]{:S(2)}, u32[]{:S(2)}) %collective-permute-start.17) | collective-permute-done | bytes 983072 | tf_op jit(solution)/shard_map/ppermute | solution.py:18
  71.9 3.1 %collective-permute-done.22 = bf16[384,1280]{1,0:T(8,128)(2,1)S(1)} collective-permute-done((bf16[384,1280]{1,0:T(8,128)(2,1)S(1)}, bf16[384,1280]{1,0:T(8,128)(2,1)S(1)}, u32[]{:S(2)}, u32[]{:S(2)}) %collective-permute-start.22) | collective-permute-done | bytes 983072 | tf_op jit(solution)/shard_map/ppermute | solution.py:18
  76.3 6.1 %apply.10.refs_12_ = f32[1024,256]{1,0:T(8,128)S(1)} custom-call(s32[2]{0:T(128)S(1)} %pad_add_fusion.3.r, s32[5]{0:T(128)S(1)} %stack.116.c, bf16[1024,1024]{1,0:T(8,128)(2,1)S(1)} %constant_dynamic-update-slice_fusion.2.slab_ref, bf16[256,1280]{1,0:T(8,128)(2,1)S(1)} %pad_maximum_fusion.8.refs_0_, bf16[256,1280]{1,0:T(8,128)(2,1)S(1)} %get-tuple-element.53.refs_0_.refs_1_, ...), custom_call_target="tpu_custom_call" | custom-call | flops 3355443200 | bytes 2621440 | tf_op jit(solution)/shard_map/apply/pallas_call | solution.py:94
  83.9 1.5 %collective-permute-start.18 = (bf16[256,1280]{1,0:T(8,128)(2,1)S(1)}, bf16[256,1280]{1,0:T(8,128)(2,1)S(1)}, u32[]{:S(2)}, u32[]{:S(2)}) collective-permute-start(bf16[256,1280]{1,0:T(8,128)(2,1)S(1)} %slice.49.refs_1_), channel_id=1, source_target_pairs={{24,0},{0,8},{8,16},{16,24},{25,1},{1,9},{9,17},{17,25},{26,2},{2,... | collective-permute-start | bytes 1966088 | tf_op jit(solution)/shard_map/ppermute | solution.py:18
  85.4 6.9 %apply.11.refs_8_ = f32[1024,256]{1,0:T(8,128)S(1)} custom-call(s32[2]{0:T(128)S(1)} %pad_add_fusion.3.r, s32[6]{0:T(128)S(1)} %stack.123.c, bf16[1024,1024]{1,0:T(8,128)(2,1)S(1)} %constant_dynamic-update-slice_fusion.2.slab_ref, bf16[256,1280]{1,0:T(8,128)(2,1)S(1)} %slice.48.refs_0_, ...), custom_call_target="tpu_custom_call", output_to_operand_aliasing={{}: (15, {})} | custom-call | flops 4026531840 | bytes 3145728 | tf_op jit(solution)/shard_map/apply/pallas_call | solution.py:94
  92.2 6.9 %apply.12.refs_13_ = f32[1024,256]{1,0:T(8,128)S(1)} custom-call(s32[2]{0:T(128)S(1)} %get-tuple-element.38.r, s32[6]{0:T(128)S(1)} %stack.123.c, bf16[1024,1024]{1,0:T(8,128)(2,1)S(1)} %constant_dynamic-update-slice_fusion.orb.slab_ref, bf16[256,1280]{1,0:T(8,128)(2,1)S(1)} %slice.48.refs_0_, ...), custom_call_target="tpu_custom_call", output_to_operand_aliasing={{}: (15, {})} | custom-call | flops 4026531840 | bytes 3145728 | tf_op jit(solution)/shard_map/apply/pallas_call | solution.py:94
  100.8 1.7 %collective-permute-start.25 = (bf16[64,1280]{1,0:T(8,128)(2,1)S(1)}, bf16[64,1280]{1,0:T(8,128)(2,1)S(1)}, u32[]{:S(2)}, u32[]{:S(2)}) collective-permute-start(bf16[64,1280]{1,0:T(8,128)(2,1)S(1)} %slice.58), channel_id=1, source_target_pairs={{32,0},{64,32},{96,64},{0,96},{33,1},{65,33},{97,65},{1,97},{34,2}... | collective-permute-start | bytes 491528 | tf_op jit(solution)/shard_map/ppermute | solution.py:18
  102.9 5.3 %apply.13.refs_5_ = f32[1024,256]{1,0:T(8,128)S(1)} custom-call(s32[2]{0:T(128)S(1)} %pad_add_fusion.3.r, s32[4]{0:T(128)S(1)} %pad_add_fusion.4.c, bf16[1024,1024]{1,0:T(8,128)(2,1)S(1)} %constant_dynamic-update-slice_fusion.2.slab_ref, bf16[256,1280]{1,0:T(8,128)(2,1)S(1)} %collective-permute-done.16.refs_0_, ...), custom_call_target="tpu_custom_call", output_to_operand_aliasing={{}: (11, {})} | custom-call | flops 2684354560 | bytes 2097152 | tf_op jit(solution)/shard_map/apply/pallas_call | solution.py:94
  108.2 3.7 %apply.14 = (f32[512,256]{1,0:T(8,128)S(1)}, f32[512,256]{1,0:T(8,128)}) custom-call(s32[2]{0:T(128)S(1)} %pad_add_fusion.3.r, s32[1]{0:T(128)} %bitcast.6.c, bf16[1024,1024]{1,0:T(8,128)(2,1)S(1)} %constant_dynamic-update-slice_fusion.2.slab_ref, bf16[64,1280]{1,0:T(8,128)(2,1)S(1)} %collective-permute-done.23.refs_0_.refs_4_, ...), custom_call_target="tpu_custom_call" | custom-call | flops 671088640 | bytes 524288 | tf_op jit(solution)/shard_map/apply/pallas_call | solution.py:94
  112.7 8.7 %collective-permute-start.27 = (f32[512,256]{1,0:T(8,128)}, f32[512,256]{1,0:T(8,128)}, u32[]{:S(2)}, u32[]{:S(2)}) collective-permute-start(f32[512,256]{1,0:T(8,128)} %get-tuple-element.32), channel_id=1, source_target_pairs={{1,0},{0,1},{3,2},{2,3},{5,4},{4,5},{7,6},{6,7},{9,8},{8,9},{11,10... | collective-permute-start | bytes 1572872 | tf_op jit(solution)/shard_map/ppermute | solution.py:18
  121.5 1.8 %collective-permute-done.27 = f32[512,256]{1,0:T(8,128)} collective-permute-done((f32[512,256]{1,0:T(8,128)}, f32[512,256]{1,0:T(8,128)}, u32[]{:S(2)}, u32[]{:S(2)}) %collective-permute-start.27) | collective-permute-done | bytes 524320 | tf_op jit(solution)/shard_map/ppermute | solution.py:18
  124.6 3.0 %collective-permute-start.28 = (bf16[512,256]{1,0:T(8,128)(2,1)S(1)}, bf16[512,256]{1,0:T(8,128)(2,1)S(1)}, u32[]{:S(2)}, u32[]{:S(2)}) collective-permute-start(bf16[512,256]{1,0:T(8,128)(2,1)S(1)} %add_convert_fusion), channel_id=1, source_target_pairs={{2,0},{0,2},{3,1},{1,3},{6,4},{4,6},{7,5},{5,7},{10,8},{8,10},{11,... | collective-permute-start | bytes 786440 | tf_op jit(solution)/shard_map/ppermute | solution.py:18
  133.7 6.1 %apply.15 = (f32[512,256]{1,0:T(8,128)S(1)}, f32[512,256]{1,0:T(8,128)S(1)}) custom-call(s32[2]{0:T(128)S(1)} %get-tuple-element.38.r, s32[5]{0:T(128)S(1)} %stack.106.c, bf16[1024,1024]{1,0:T(8,128)(2,1)S(1)} %constant_dynamic-update-slice_fusion.orb.slab_ref, bf16[256,1280]{1,0:T(8,128)(2,1)S(1)} %copy-done.3, bf16[256,1280]{1,0:T(8,128)(2,1)S(1)} %copy-done.7, ...), custom_call_target="tpu_custom_call" | custom-call | flops 3355443200 | bytes 2621440 | tf_op jit(solution)/shard_map/apply/pallas_call | solution.py:94
  140.6 1.5 %collective-permute-done.29 = f32[512,256]{1,0:T(8,128)S(1)} collective-permute-done((f32[512,256]{1,0:T(8,128)S(1)}, f32[512,256]{1,0:T(8,128)S(1)}, u32[]{:S(2)}, u32[]{:S(2)}) %collective-permute-start.29) | collective-permute-done | bytes 524320 | tf_op jit(solution)/shard_map/ppermute | solution.py:18
  (111 shorter events, 25.8 us)
Async XLA Ops:
  0.0 8.0 %collective-permute-start = (bf16[512,1024]{1,0:T(8,128)(2,1)}, bf16[512,1024]{1,0:T(8,128)(2,1)S(1)}, u32[]{:S(2)}, u32[]{:S(2)}) collective-permute-start(bf16[512,1024]{1,0:T(8,128)(2,1)} %param.4), channel_id=1, source_target_pairs={{1,0},{0,1},{3,2},{2,3},{5,4},{4,5},{7,6},{6,7},{9,8},{8,9},{11,10... | collective-permute-start | bytes 3145736 | tf_op jit(solution)/shard_map/ppermute | solution.py:18
  1.4 5.4 %collective-permute-start.1 = (s32[1,128]{1,0:T(1,128)}, s32[1,128]{1,0:T(1,128)S(1)}, u32[]{:S(2)}, u32[]{:S(2)}) collective-permute-start(s32[1,128]{1,0:T(1,128)} %param.6), channel_id=1, source_target_pairs={{2,0},{0,2},{3,1},{1,3},{6,4},{4,6},{7,5},{5,7},{10,8},{8,10},{11,... | collective-permute-start | bytes 1544 | tf_op jit(solution)/shard_map/ppermute | solution.py:18
  5.1 1.9 %collective-permute-start.2 = (bf16[512,256]{1,0:T(8,128)(2,1)}, bf16[512,256]{1,0:T(8,128)(2,1)}, u32[]{:S(2)}, u32[]{:S(2)}) collective-permute-start(bf16[512,256]{1,0:T(8,128)(2,1)} %param.5), channel_id=1, source_target_pairs={{1,0},{0,1},{3,2},{2,3},{5,4},{4,5},{7,6},{6,7},{9,8},{8,9},{11,10... | collective-permute-start | bytes 786440 | tf_op jit(solution)/shard_map/ppermute | solution.py:18
  9.5 10.5 %collective-permute-start.3 = (bf16[128,1280]{1,0:T(8,128)(2,1)S(1)}, bf16[128,1280]{1,0:T(8,128)(2,1)S(1)}, u32[]{:S(2)}, u32[]{:S(2)}) collective-permute-start(bf16[128,1280]{1,0:T(8,128)(2,1)S(1)} %get-tuple-element.22), channel_id=1, source_target_pairs={{2,0},{0,2},{3,1},{1,3},{6,4},{4,6},{7,5},{5,7},{10,8},{8,10},{11,... | collective-permute-start | bytes 983048 | tf_op jit(solution)/shard_map/ppermute | solution.py:18
  12.0 17.7 %copy-start.14 = (bf16[512,1024]{1,0:T(8,128)(2,1)S(1)}, bf16[512,1024]{1,0:T(8,128)(2,1)}, u32[]{:S(2)}) copy-start(bf16[512,1024]{1,0:T(8,128)(2,1)} %param.4) | copy-start | bytes 3145732
  20.1 8.1 %collective-permute-start.5 = (bf16[128,1280]{1,0:T(8,128)(2,1)S(1)}, bf16[128,1280]{1,0:T(8,128)(2,1)S(1)}, u32[]{:S(2)}, u32[]{:S(2)}) collective-permute-start(bf16[128,1280]{1,0:T(8,128)(2,1)S(1)} %add.264), channel_id=1, source_target_pairs={{4,0},{0,4},{5,1},{1,5},{6,2},{2,6},{7,3},{3,7},{12,8},{8,12},{13,... | collective-permute-start | bytes 983048 | tf_op jit(solution)/shard_map/ppermute | solution.py:18
  20.8 8.9 %collective-permute-start.12 = (bf16[128,1280]{1,0:T(8,128)(2,1)S(1)}, bf16[128,1280]{1,0:T(8,128)(2,1)S(1)}, u32[]{:S(2)}, u32[]{:S(2)}) collective-permute-start(bf16[128,1280]{1,0:T(8,128)(2,1)S(1)} %add.264), channel_id=1, source_target_pairs={{96,0},{0,32},{32,64},{64,96},{97,1},{1,33},{33,65},{65,97},{98,2}... | collective-permute-start | bytes 983048 | tf_op jit(solution)/shard_map/ppermute | solution.py:18
  22.1 17.1 %collective-permute-start.7 = (bf16[128,1280]{1,0:T(8,128)(2,1)S(1)}, bf16[128,1280]{1,0:T(8,128)(2,1)S(1)}, u32[]{:S(2)}, u32[]{:S(2)}) collective-permute-start(bf16[128,1280]{1,0:T(8,128)(2,1)S(1)} %add.264), channel_id=1, source_target_pairs={{8,0},{16,8},{24,16},{0,24},{9,1},{17,9},{25,17},{1,25},{10,2},{18... | collective-permute-start | bytes 983048 | tf_op jit(solution)/shard_map/ppermute | solution.py:18
  24.5 19.7 %collective-permute-start.4 = (bf16[128,1280]{1,0:T(8,128)(2,1)S(1)}, bf16[128,1280]{1,0:T(8,128)(2,1)S(1)}, u32[]{:S(2)}, u32[]{:S(2)}) collective-permute-start(bf16[128,1280]{1,0:T(8,128)(2,1)S(1)} %add.264), channel_id=1, source_target_pairs={{32,0},{64,32},{96,64},{0,96},{33,1},{65,33},{97,65},{1,97},{34,2}... | collective-permute-start | bytes 983048 | tf_op jit(solution)/shard_map/ppermute | solution.py:18
  26.1 19.5 %collective-permute-start.10 = (bf16[128,1280]{1,0:T(8,128)(2,1)S(1)}, bf16[128,1280]{1,0:T(8,128)(2,1)S(1)}, u32[]{:S(2)}, u32[]{:S(2)}) collective-permute-start(bf16[128,1280]{1,0:T(8,128)(2,1)S(1)} %add.264), channel_id=1, source_target_pairs={{24,0},{0,8},{8,16},{16,24},{25,1},{1,9},{9,17},{17,25},{26,2},{2,... | collective-permute-start | bytes 983048 | tf_op jit(solution)/shard_map/ppermute | solution.py:18
  28.2 8.3 %collective-permute-start.13 = (bf16[128,1280]{1,0:T(8,128)(2,1)S(1)}, bf16[128,1280]{1,0:T(8,128)(2,1)S(1)}, u32[]{:S(2)}, u32[]{:S(2)}) collective-permute-start(bf16[128,1280]{1,0:T(8,128)(2,1)S(1)} %collective-permute-done.5), channel_id=1, source_target_pairs={{96,0},{0,32},{32,64},{64,96},{97,1},{1,33},{33,65},{65,97},{98,2}... | collective-permute-start | bytes 983048 | tf_op jit(solution)/shard_map/ppermute | solution.py:18
  29.7 29.2 %collective-permute-start.14 = (bf16[512,1024]{1,0:T(8,128)(2,1)S(1)}, bf16[512,1024]{1,0:T(8,128)(2,1)S(1)}, u32[]{:S(2)}, u32[]{:S(2)}) collective-permute-start(bf16[512,1024]{1,0:T(8,128)(2,1)S(1)} %copy-done.14), channel_id=1, source_target_pairs={{2,0},{0,2},{3,1},{1,3},{6,4},{4,6},{7,5},{5,7},{10,8},{8,10},{11,... | collective-permute-start | bytes 3145736 | tf_op jit(solution)/shard_map/ppermute | solution.py:18
  36.6 6.5 %collective-permute-start.8 = (bf16[128,1280]{1,0:T(8,128)(2,1)S(1)}, bf16[128,1280]{1,0:T(8,128)(2,1)S(1)}, u32[]{:S(2)}, u32[]{:S(2)}) collective-permute-start(bf16[128,1280]{1,0:T(8,128)(2,1)S(1)} %collective-permute-done.5), channel_id=1, source_target_pairs={{8,0},{16,8},{24,16},{0,24},{9,1},{17,9},{25,17},{1,25},{10,2},{18... | collective-permute-start | bytes 983048 | tf_op jit(solution)/shard_map/ppermute | solution.py:18
  39.2 6.3 %collective-permute-start.6 = (bf16[128,1280]{1,0:T(8,128)(2,1)S(1)}, bf16[128,1280]{1,0:T(8,128)(2,1)S(1)}, u32[]{:S(2)}, u32[]{:S(2)}) collective-permute-start(bf16[128,1280]{1,0:T(8,128)(2,1)S(1)} %collective-permute-done.5), channel_id=1, source_target_pairs={{32,0},{64,32},{96,64},{0,96},{33,1},{65,33},{97,65},{1,97},{34,2}... | collective-permute-start | bytes 983048 | tf_op jit(solution)/shard_map/ppermute | solution.py:18
  43.1 8.2 %collective-permute-start.11 = (bf16[128,1280]{1,0:T(8,128)(2,1)S(1)}, bf16[128,1280]{1,0:T(8,128)(2,1)S(1)}, u32[]{:S(2)}, u32[]{:S(2)}) collective-permute-start(bf16[128,1280]{1,0:T(8,128)(2,1)S(1)} %collective-permute-done.5), channel_id=1, source_target_pairs={{24,0},{0,8},{8,16},{16,24},{25,1},{1,9},{9,17},{17,25},{26,2},{2,... | collective-permute-start | bytes 983048 | tf_op jit(solution)/shard_map/ppermute | solution.py:18
  51.7 20.0 %collective-permute-start.17 = (bf16[384,1280]{1,0:T(8,128)(2,1)S(1)}, bf16[384,1280]{1,0:T(8,128)(2,1)S(1)}, u32[]{:S(2)}, u32[]{:S(2)}) collective-permute-start(bf16[384,1280]{1,0:T(8,128)(2,1)S(1)} %get-tuple-element.52), channel_id=1, source_target_pairs={{24,0},{0,8},{8,16},{16,24},{25,1},{1,9},{9,17},{17,25},{26,2},{2,... | collective-permute-start | bytes 2949128 | tf_op jit(solution)/shard_map/ppermute | solution.py:18
  51.8 20.0 %collective-permute-start.9 = (bf16[384,1280]{1,0:T(8,128)(2,1)S(1)}, bf16[384,1280]{1,0:T(8,128)(2,1)S(1)}, u32[]{:S(2)}, u32[]{:S(2)}) collective-permute-start(bf16[384,1280]{1,0:T(8,128)(2,1)S(1)} %get-tuple-element.50), channel_id=1, source_target_pairs={{8,0},{16,8},{24,16},{0,24},{9,1},{17,9},{25,17},{1,25},{10,2},{18... | collective-permute-start | bytes 2949128 | tf_op jit(solution)/shard_map/ppermute | solution.py:18
  54.5 20.7 %collective-permute-start.21 = (bf16[384,1280]{1,0:T(8,128)(2,1)S(1)}, bf16[384,1280]{1,0:T(8,128)(2,1)S(1)}, u32[]{:S(2)}, u32[]{:S(2)}) collective-permute-start(bf16[384,1280]{1,0:T(8,128)(2,1)S(1)} %get-tuple-element.51), channel_id=1, source_target_pairs={{32,0},{64,32},{96,64},{0,96},{33,1},{65,33},{97,65},{1,97},{34,2}... | collective-permute-start | bytes 2949128 | tf_op jit(solution)/shard_map/ppermute | solution.py:18
  55.9 19.1 %collective-permute-start.22 = (bf16[384,1280]{1,0:T(8,128)(2,1)S(1)}, bf16[384,1280]{1,0:T(8,128)(2,1)S(1)}, u32[]{:S(2)}, u32[]{:S(2)}) collective-permute-start(bf16[384,1280]{1,0:T(8,128)(2,1)S(1)} %get-tuple-element.49), channel_id=1, source_target_pairs={{96,0},{0,32},{32,64},{64,96},{97,1},{1,33},{33,65},{65,97},{98,2}... | collective-permute-start | bytes 2949128 | tf_op jit(solution)/shard_map/ppermute | solution.py:18
  58.9 17.3 %collective-permute-start.15 = (bf16[512,1024]{1,0:T(8,128)(2,1)S(1)}, bf16[512,1024]{1,0:T(8,128)(2,1)S(1)}, u32[]{:S(2)}, u32[]{:S(2)}) collective-permute-start(bf16[512,1024]{1,0:T(8,128)(2,1)S(1)} %collective-permute-done.14), channel_id=1, source_target_pairs={{1,0},{0,1},{3,2},{2,3},{5,4},{4,5},{7,6},{6,7},{9,8},{8,9},{11,10... | collective-permute-start | bytes 3145736 | tf_op jit(solution)/shard_map/ppermute | solution.py:18
  82.4 16.8 %collective-permute-start.19 = (bf16[256,1280]{1,0:T(8,128)(2,1)S(1)}, bf16[256,1280]{1,0:T(8,128)(2,1)S(1)}, u32[]{:S(2)}, u32[]{:S(2)}) collective-permute-start(bf16[256,1280]{1,0:T(8,128)(2,1)S(1)} %slice.48.refs_0_), channel_id=1, source_target_pairs={{32,0},{64,32},{96,64},{0,96},{33,1},{65,33},{97,65},{1,97},{34,2}... | collective-permute-start | bytes 1966088 | tf_op jit(solution)/shard_map/ppermute | solution.py:18
  82.4 18.4 %collective-permute-start.16 = (bf16[256,1280]{1,0:T(8,128)(2,1)S(1)}, bf16[256,1280]{1,0:T(8,128)(2,1)S(1)}, u32[]{:S(2)}, u32[]{:S(2)}) collective-permute-start(bf16[256,1280]{1,0:T(8,128)(2,1)S(1)} %slice.48.refs_0_), channel_id=1, source_target_pairs={{8,0},{16,8},{24,16},{0,24},{9,1},{17,9},{25,17},{1,25},{10,2},{18... | collective-permute-start | bytes 1966088 | tf_op jit(solution)/shard_map/ppermute | solution.py:18
  83.1 17.4 %collective-permute-start.20 = (bf16[256,1280]{1,0:T(8,128)(2,1)S(1)}, bf16[256,1280]{1,0:T(8,128)(2,1)S(1)}, u32[]{:S(2)}, u32[]{:S(2)}) collective-permute-start(bf16[256,1280]{1,0:T(8,128)(2,1)S(1)} %slice.49.refs_1_), channel_id=1, source_target_pairs={{96,0},{0,32},{32,64},{64,96},{97,1},{1,33},{33,65},{65,97},{98,2}... | collective-permute-start | bytes 1966088 | tf_op jit(solution)/shard_map/ppermute | solution.py:18
  83.9 18.6 %collective-permute-start.18 = (bf16[256,1280]{1,0:T(8,128)(2,1)S(1)}, bf16[256,1280]{1,0:T(8,128)(2,1)S(1)}, u32[]{:S(2)}, u32[]{:S(2)}) collective-permute-start(bf16[256,1280]{1,0:T(8,128)(2,1)S(1)} %slice.49.refs_1_), channel_id=1, source_target_pairs={{24,0},{0,8},{8,16},{16,24},{25,1},{1,9},{9,17},{17,25},{26,2},{2,... | collective-permute-start | bytes 1966088 | tf_op jit(solution)/shard_map/ppermute | solution.py:18
  99.2 9.0 %copy-start = (bf16[256,1280]{1,0:T(8,128)(2,1)}, bf16[256,1280]{1,0:T(8,128)(2,1)S(1)}, u32[]{:S(2)}) copy-start(bf16[256,1280]{1,0:T(8,128)(2,1)S(1)} %collective-permute-done.19.refs_2_) | copy-start | bytes 1966084
  99.2 9.0 %collective-permute-start.23 = (bf16[64,1280]{1,0:T(8,128)(2,1)S(1)}, bf16[64,1280]{1,0:T(8,128)(2,1)S(1)}, u32[]{:S(2)}, u32[]{:S(2)}) collective-permute-start(bf16[64,1280]{1,0:T(8,128)(2,1)S(1)} %slice.50), channel_id=1, source_target_pairs={{8,0},{16,8},{24,16},{0,24},{9,1},{17,9},{25,17},{1,25},{10,2},{18... | collective-permute-start | bytes 491528 | tf_op jit(solution)/shard_map/ppermute | solution.py:18
  100.5 7.7 %collective-permute-start.24 = (bf16[64,1280]{1,0:T(8,128)(2,1)S(1)}, bf16[64,1280]{1,0:T(8,128)(2,1)S(1)}, u32[]{:S(2)}, u32[]{:S(2)}) collective-permute-start(bf16[64,1280]{1,0:T(8,128)(2,1)S(1)} %slice.57), channel_id=1, source_target_pairs={{24,0},{0,8},{8,16},{16,24},{25,1},{1,9},{9,17},{17,25},{26,2},{2,... | collective-permute-start | bytes 491528 | tf_op jit(solution)/shard_map/ppermute | solution.py:18
  100.8 7.4 %collective-permute-start.25 = (bf16[64,1280]{1,0:T(8,128)(2,1)S(1)}, bf16[64,1280]{1,0:T(8,128)(2,1)S(1)}, u32[]{:S(2)}, u32[]{:S(2)}) collective-permute-start(bf16[64,1280]{1,0:T(8,128)(2,1)S(1)} %slice.58), channel_id=1, source_target_pairs={{32,0},{64,32},{96,64},{0,96},{33,1},{65,33},{97,65},{1,97},{34,2}... | collective-permute-start | bytes 491528 | tf_op jit(solution)/shard_map/ppermute | solution.py:18
  102.6 5.7 %collective-permute-start.26 = (bf16[64,1280]{1,0:T(8,128)(2,1)S(1)}, bf16[64,1280]{1,0:T(8,128)(2,1)S(1)}, u32[]{:S(2)}, u32[]{:S(2)}) collective-permute-start(bf16[64,1280]{1,0:T(8,128)(2,1)S(1)} %slice.59), channel_id=1, source_target_pairs={{96,0},{0,32},{32,64},{64,96},{97,1},{1,33},{33,65},{65,97},{98,2}... | collective-permute-start | bytes 491528 | tf_op jit(solution)/shard_map/ppermute | solution.py:18
  112.7 10.6 %collective-permute-start.27 = (f32[512,256]{1,0:T(8,128)}, f32[512,256]{1,0:T(8,128)}, u32[]{:S(2)}, u32[]{:S(2)}) collective-permute-start(f32[512,256]{1,0:T(8,128)} %get-tuple-element.32), channel_id=1, source_target_pairs={{1,0},{0,1},{3,2},{2,3},{5,4},{4,5},{7,6},{6,7},{9,8},{8,9},{11,10... | collective-permute-start | bytes 1572872 | tf_op jit(solution)/shard_map/ppermute | solution.py:18
  124.6 15.3 %collective-permute-start.28 = (bf16[512,256]{1,0:T(8,128)(2,1)S(1)}, bf16[512,256]{1,0:T(8,128)(2,1)S(1)}, u32[]{:S(2)}, u32[]{:S(2)}) collective-permute-start(bf16[512,256]{1,0:T(8,128)(2,1)S(1)} %add_convert_fusion), channel_id=1, source_target_pairs={{2,0},{0,2},{3,1},{1,3},{6,4},{4,6},{7,5},{5,7},{10,8},{8,10},{11,... | collective-permute-start | bytes 786440 | tf_op jit(solution)/shard_map/ppermute | solution.py:18
  139.9 2.3 %collective-permute-start.29 = (f32[512,256]{1,0:T(8,128)S(1)}, f32[512,256]{1,0:T(8,128)S(1)}, u32[]{:S(2)}, u32[]{:S(2)}) collective-permute-start(f32[512,256]{1,0:T(8,128)S(1)} %get-tuple-element.36), channel_id=1, source_target_pairs={{1,0},{0,1},{3,2},{2,3},{5,4},{4,5},{7,6},{6,7},{9,8},{8,9},{11,10... | collective-permute-start | bytes 1572872 | tf_op jit(solution)/shard_map/ppermute | solution.py:18
  (16 other events, 53.3 us)

commit v4 on v3

v4 whole, which is shorter than its diff:
```python
import jax
import jax.numpy as jnp
from jax import lax
from jax.experimental import pallas as pl
from jax.experimental.pallas import tpu as pltpu
from jax.sharding import Mesh
from jax.sharding import PartitionSpec as P

AXES = ("y", "x", "zl", "zh", "c")
SLABS = ("y", "x", "zl")
IPTS = ("zh", "c")
RING = 4
ORDER = (
    (0, 0), (0, 1), (0, 3), (1, 0), (3, 0), (1, 1), (3, 3), (1, 3), (3, 1), (0, 2), (2, 0),
    (1, 2), (3, 2), (2, 1), (2, 3), (2, 2),
)
NEAR, FAR, BASE, SIDE = 16, 18, 20, 21
NEXT = (((0, 1), "x", 1), ((0, 3), "x", -1), ((1, 0), "y", 1), ((3, 0), "y", -1))


def take_from(value, axis, side):
    n = lax.axis_size(axis)
    return lax.ppermute(value, axis, [((i + side) % n, i) for i in range(n)])


def after(value, *others):
    return lax.optimization_barrier((value, others))[0]


def pick_kernel(table, ids, orb, tgt, mine, theirs):
    rows, norb = orb.shape
    half = rows // 2
    bases = [table[BASE] + table[NEAR + k] * half for k in range(2)]
    for k, out in ((0, mine), (1, theirs)):
        row = lax.broadcasted_iota(jnp.int32, (rows, out.shape[0]), 0)
        row = row + jnp.where(row < half, bases[0], bases[1] - half)
        hot = (row == ids[k : k + 1, :]).astype(jnp.bfloat16)
        dims = (((0,), (0,)), ((), ()))
        out[:, :norb] = lax.dot_general(hot, orb[...], dims, preferred_element_type=jnp.float32).astype(out.dtype)
        out[:, norb:] = lax.dot_general(hot, tgt[...], dims, preferred_element_type=jnp.float32).astype(out.dtype)


def pick(table, ids, orb, tgt):
    out = jax.ShapeDtypeStruct((ids.shape[1], orb.shape[1] + tgt.shape[1]), orb.dtype)
    whole = pl.BlockSpec(memory_space=pltpu.VMEM)
    return pl.pallas_call(
        pick_kernel,
        out_shape=(out, out),
        in_specs=[pl.BlockSpec(memory_space=pltpu.SMEM)] + [whole] * 3,
        out_specs=(whole, whole),
        compiler_params=pltpu.CompilerParams(vmem_limit_bytes=32 << 20),
        name="pick",
    )(table, ids, orb, tgt)


def apply_parts(slab, parts, potential, table, row_at, col_at, count, total, last=False):
    tile = slab.shape[0] // 2
    norb = slab.shape[1]
    points = sum(p.shape[0] for p in parts) // count
    width = parts[0].shape[1]
    nj = width - norb
    first = total is None

    def body(t, slab_ref, *refs):
        ours, pots = refs[: len(parts)], refs[len(parts) : len(parts) + count]
        here = pl.ds(pl.multiple_of(pl.program_id(0) * tile, tile), tile)
        orb = jnp.concatenate([p[:, :norb] for p in ours], axis=0)
        tgt = jnp.concatenate([p[:, norb:] for p in ours], axis=0)
        products = lax.dot_general(
            slab_ref[here, :], orb, (((1,), (1,)), ((), ())), preferred_element_type=jnp.float32
        )
        pot = jnp.concatenate([p[...] for p in pots], axis=1)
        weighted = (pot.astype(jnp.float32) * products).astype(jnp.bfloat16)
        term = jnp.dot(weighted, tgt, preferred_element_type=jnp.float32)
        if not first:
            term = refs[len(parts) + count][here, :] + term
        if not last:
            refs[-1][here, :] = term
            return
        for k, out in enumerate(refs[-2:]):

            @pl.when(pl.program_id(0) == k)
            def _():
                out[...] = term

    def pot_spec(k):
        return pl.BlockSpec((tile, points), lambda i, t: (t[row_at + i], t[col_at + k]))

    whole = pl.BlockSpec(memory_space=pltpu.VMEM)
    specs = [whole] * (1 + len(parts)) + [pot_spec(k) for k in range(count)]
    args = [slab, *parts] + [potential] * count
    if not first:
        specs.append(whole)
        args.append(total)
    flops = slab.shape[0] * points * count * width // 2
    half = jax.ShapeDtypeStruct((tile, nj), jnp.float32)
    return pl.pallas_call(
        body,
        out_shape=(half, half) if last else jax.ShapeDtypeStruct((slab.shape[0], nj), jnp.float32),
        grid_spec=pltpu.PrefetchScalarGridSpec(
            num_scalar_prefetch=1, grid=(2,), in_specs=specs, out_specs=(whole,) * 2 if last else whole
        ),
        input_output_aliases={} if first or last else {len(args): 0},
        cost_estimate=pl.CostEstimate(
            flops=flops, bytes_accessed=count * slab.shape[0] * points * 2, transcendentals=0
        ),
        compiler_params=pltpu.CompilerParams(vmem_limit_bytes=15 << 20),
        name="apply",
    )(table, *args)


def local(orbitals, targets, points, potential):
    own_rows = orbitals.shape[0]
    potential = pltpu.with_memory_space_constraint(potential, pltpu.HBM)
    count = points.shape[1]
    y, x, zl, zh, c = (lax.axis_index(a) for a in AXES)
    slab_start = ((y * RING + x) * 2 + zl) * own_rows * 4

    n = lax.iota(jnp.int32, SIDE + 1)
    code = jnp.zeros_like(n)
    for k, (dy, dx) in enumerate(ORDER):
        code = jnp.where(n == k, dy * RING + dx, code)
    cols = (y + code // RING) % RING * RING + (x + code % RING) % RING
    half_at = jnp.where(n < FAR, zh, 1 - zh)
    rows = half_at * 2 + jnp.where((n - NEAR) % 2 == 0, c, 1 - c)
    table = jnp.where(n < NEAR, cols, jnp.where(n < BASE, rows, jnp.where(n < SIDE, slab_start, zl)))
    table = table.astype(jnp.int32)

    sib_orb = take_from(orbitals, "c", 1)
    sib_tgt = take_from(targets, "c", 1)
    far_points = take_from(points, "zh", 1)
    near_slab = jnp.concatenate([orbitals, sib_orb], axis=0)
    near_tgt = jnp.concatenate([targets, sib_tgt], axis=0)
    ids = jnp.concatenate([points, far_points], axis=0)
    mine, theirs = pick(table, ids, near_slab, near_tgt)
    block = mine + take_from(theirs, "zh", 1)

    def near_apply(parts, ats, total, last=False):
        return apply_parts(near_slab, parts, potential, table, NEAR, ORDER.index(ats[0]), len(ats), total, last)

    def far_apply(parts, ats, total, last=False):
        return apply_parts(far_slab, parts, potential, table, FAR, ORDER.index(ats[0]), len(ats), total, last)

    other = take_from(block, "zl", 1)
    lower = table[SIDE:].reshape(1, 1) == 0
    low, high = jnp.where(lower, block, other), jnp.where(lower, other, block)
    pair = {(0, 0): jnp.concatenate([low, high], axis=0)}
    far_orb = take_from(after(orbitals, other), "zh", 1)
    for at, axis, side in NEXT:
        pair[at] = take_from(pair[0, 0], axis, side)
    near = near_apply([pair[0, 0]], [(0, 0)], None)

    def joined(whole, half):
        return jnp.concatenate([pair[whole], half], axis=0)

    from_right = take_from(joined((1, 0), pair[0, 1][:count]), "x", 1)
    from_left = take_from(joined((3, 0), pair[0, 3][count:]), "x", -1)
    from_up = take_from(joined((0, 3), pair[1, 0][:count]), "y", 1)
    from_down = take_from(joined((0, 1), pair[3, 0][count:]), "y", -1)
    first = tuple(at for at, _, _ in NEXT)
    near = near_apply([pair[at] for at in first], first, near)
    far_sib = take_from(far_orb, "c", 1)
    far_slab = jnp.concatenate([far_orb, far_sib], axis=0)
    far = far_apply([pair[0, 0]] + [pair[at] for at in first], ((0, 0),) + first, None)
    from_right, from_left, from_up, from_down = lax.optimization_barrier(
        (from_right, from_left, from_up, from_down, near, far)
    )[:4]
    both = 2 * count
    pair[1, 1], pair[3, 3] = from_right[:both], from_left[:both]
    pair[1, 3], pair[3, 1] = from_up[:both], from_down[:both]
    pair[0, 2] = jnp.concatenate([from_right[both:], from_left[both:]], axis=0)
    pair[2, 0] = jnp.concatenate([from_up[both:], from_down[both:]], axis=0)

    pair[1, 2] = take_from(pair[1, 1], "x", 1)
    pair[3, 2] = take_from(pair[3, 3], "x", -1)
    pair[2, 1] = take_from(pair[1, 1], "y", 1)
    pair[2, 3] = take_from(pair[3, 3], "y", -1)
    second = ((1, 1), (3, 3), (1, 3), (3, 1), (0, 2), (2, 0))
    far = far_apply([pair[at] for at in second], second, far)
    near = near_apply([pair[at] for at in second], second, after(near, far))

    third = ((1, 2), (3, 2), (2, 1), (2, 3))
    ready = lax.optimization_barrier((*(pair[at] for at in third), near, far))[:4]
    pair.update(zip(third, ready))
    part = both // 4
    sides = (((2, 1), "x", 1), ((2, 3), "x", -1), ((1, 2), "y", 1), ((3, 2), "y", -1))
    last = [
        take_from(pair[at][k * part : (k + 1) * part], axis, side)
        for k, (at, axis, side) in enumerate(sides)
    ]
    far = far_apply([pair[at] for at in third], third, far)
    kept, sent = far_apply(last, [(2, 2)], far, True)
    far = (kept + take_from(sent, "c", 1)).astype(jnp.bfloat16)
    away = take_from(far, "zh", 1)
    kept, sent = near_apply([pair[at] for at in third] + last, third + ((2, 2),), after(near, far), True)
    near = kept + take_from(after(sent, away), "c", 1)
    return (-(near + away.astype(jnp.float32))).astype(jnp.bfloat16)


def solution(mesh):
    torus = Mesh(mesh.devices.reshape(RING, RING, 2, 2, 2), AXES)
    placed = (P(AXES, None), P(AXES, None), P(IPTS, SLABS), P(SLABS, IPTS))
    return jax.shard_map(local, mesh=torus, in_specs=placed, out_specs=P(AXES, None), check_vma=False)
```

time: 144 us -> 134 us (0.931)
  starting transfers between devices: 50.3 us -> 40.5 us
  waiting for transfers between devices: 33.3 us -> 42.5 us
  local copies, waits for them, and re-layouts: 9.92 us -> 3.51 us
  other arithmetic: 4.39 us -> 2.44 us
    ppermute x30 -> x26, starting transfers between devices: 50.3 us -> 40.5 us  [take_from(): return lax.ppermute(value, axis, [((i + side) % n, i) for i in range(n)])]
    ppermute x30 -> x26, waiting for transfers between devices: 33.3 us -> 42.5 us  [take_from(): return lax.ppermute(value, axis, [((i + side) % n, i) for i in range(n)])]
    unnamed x36 -> x14, local copies, waits for them, and re-layouts: 8.36 us -> 1.39 us
  transfers between devices with their start and end apart: 30 -> 26, of which waited for: 11 -> 12; matrix products, arithmetic and copies ran while one was open for 3% -> 3% of each run, Pallas kernels for 23% -> 29%
where the time goes in v4:
time: 134 us
  Pallas kernels  43.9 us (33%)
  waiting for transfers between devices  42.5 us (32%)
  starting transfers between devices  40.5 us (30%)
  local copies, waits for them, and re-layouts  3.51 us (3%)
  other arithmetic  2.44 us (2%)
    ppermute x26, waiting for transfers between devices, take_from(): return lax.ppermute(value, axis, [((i + side) % n, i) for i in range(n)])  42.5 us
    pallas_call x8, Pallas kernels, apply_parts(): pl.pallas_call(body, out_shape=(half, half) if last else jax.ShapeDtypeSt...  42.4 us
    ppermute x26, starting transfers between devices, take_from(): return lax.ppermute(value, axis, [((i + side) % n, i) for i in range(n)])  40.5 us
  transfers between devices with their start and end apart: 26, of which 12 were waited for; matrix products, arithmetic and copies ran while one was open for 3% of the time, Pallas kernels for 29%

profile of v4, /device:TPU:1, one launch (start us, length us, event | category | flops | bytes accessed | tf_op | source)
XLA Modules:
  0.0 134.0 jit_solution(15170522764664762289)
XLA Ops:
  0.0 1.4 %collective-permute-start = (bf16[512,1024]{1,0:T(8,128)(2,1)}, bf16[512,1024]{1,0:T(8,128)(2,1)S(1)}, u32[]{:S(2)}, u32[]{:S(2)}) collective-permute-start(bf16[512,1024]{1,0:T(8,128)(2,1)} %param.4), channel_id=1, source_target_pairs={{1,0},{0,1},{3,2},{2,3},{5,4},{4,5},{7,6},{6,7},{9,8},{8,9},{11,10... | collective-permute-start | bytes 3145736 | tf_op jit(solution)/shard_map/ppermute | solution.py:23
  1.4 3.8 %collective-permute-start.1 = (s32[1,128]{1,0:T(1,128)}, s32[1,128]{1,0:T(1,128)S(1)}, u32[]{:S(2)}, u32[]{:S(2)}) collective-permute-start(s32[1,128]{1,0:T(1,128)} %param.6), channel_id=1, source_target_pairs={{2,0},{0,2},{3,1},{1,3},{6,4},{4,6},{7,5},{5,7},{10,8},{8,10},{11,... | collective-permute-start | bytes 1544 | tf_op jit(solution)/shard_map/ppermute | solution.py:23
  7.7 1.5 %pick.1 = (bf16[128,1280]{1,0:T(8,128)(2,1)S(1)}, bf16[128,1280]{1,0:T(8,128)(2,1)S(1)}) custom-call(s32[22]{0:T(128)S(1)} %compare_select_fusion.10.table.t, s32[2,128]{1,0:T(2,128)S(1)} %pad_add_fusion.ids, bf16[1024,1024]{1,0:T(8,128)(2,1)S(1)} %constant_dynamic-update-slice_fusion.orb.slab_ref, bf16[1024,256]{1,0:T(8,128)(2,1)S(1)} %pad_maximum_fusion.7.tgt), custom_call_target="tpu_custom_call" | custom-call | tf_op jit(solution)/shard_map/pick/pallas_call | solution.py:46
  9.2 2.7 %collective-permute-start.3 = (bf16[128,1280]{1,0:T(8,128)(2,1)S(1)}, bf16[128,1280]{1,0:T(8,128)(2,1)S(1)}, u32[]{:S(2)}, u32[]{:S(2)}) collective-permute-start(bf16[128,1280]{1,0:T(8,128)(2,1)S(1)} %get-tuple-element.24), channel_id=1, source_target_pairs={{2,0},{0,2},{3,1},{1,3},{6,4},{4,6},{7,5},{5,7},{10,8},{8,10},{11,... | collective-permute-start | bytes 983048 | tf_op jit(solution)/shard_map/ppermute | solution.py:23
  11.9 7.1 %collective-permute-done.3 = bf16[128,1280]{1,0:T(8,128)(2,1)S(1)} collective-permute-done((bf16[128,1280]{1,0:T(8,128)(2,1)S(1)}, bf16[128,1280]{1,0:T(8,128)(2,1)S(1)}, u32[]{:S(2)}, u32[]{:S(2)}) %collective-permute-start.3) | collective-permute-done | bytes 327712 | tf_op jit(solution)/shard_map/ppermute | solution.py:23
  20.6 5.9 %collective-permute-done.4 = bf16[128,1280]{1,0:T(8,128)(2,1)S(1)} collective-permute-done((bf16[128,1280]{1,0:T(8,128)(2,1)S(1)}, bf16[128,1280]{1,0:T(8,128)(2,1)S(1)}, u32[]{:S(2)}, u32[]{:S(2)}) %collective-permute-start.4) | collective-permute-done | bytes 327712 | tf_op jit(solution)/shard_map/ppermute | solution.py:23
  27.9 2.5 %collective-permute-start.6 = (bf16[256,1280]{1,0:T(8,128)(2,1)S(1)}, bf16[256,1280]{1,0:T(8,128)(2,1)S(1)}, u32[]{:S(2)}, u32[]{:S(2)}) collective-permute-start(bf16[256,1280]{1,0:T(8,128)(2,1)S(1)} %pad_maximum_fusion.4.refs_0_), channel_id=1, source_target_pairs={{8,0},{16,8},{24,16},{0,24},{9,1},{17,9},{25,17},{1,25},{10,2},{18... | collective-permute-start | bytes 1966088 | tf_op jit(solution)/shard_map/ppermute | solution.py:23
  30.4 1.5 %collective-permute-start.13 = (bf16[512,1024]{1,0:T(8,128)(2,1)S(1)}, bf16[512,1024]{1,0:T(8,128)(2,1)S(1)}, u32[]{:S(2)}, u32[]{:S(2)}) collective-permute-start(bf16[512,1024]{1,0:T(8,128)(2,1)S(1)} %copy-done.3), channel_id=1, source_target_pairs={{2,0},{0,2},{3,1},{1,3},{6,4},{4,6},{7,5},{5,7},{10,8},{8,10},{11,... | collective-permute-start | bytes 3145736 | tf_op jit(solution)/shard_map/ppermute | solution.py:23
  31.9 1.5 %collective-permute-start.5 = (bf16[256,1280]{1,0:T(8,128)(2,1)S(1)}, bf16[256,1280]{1,0:T(8,128)(2,1)S(1)}, u32[]{:S(2)}, u32[]{:S(2)}) collective-permute-start(bf16[256,1280]{1,0:T(8,128)(2,1)S(1)} %pad_maximum_fusion.4.refs_0_), channel_id=1, source_target_pairs={{32,0},{64,32},{96,64},{0,96},{33,1},{65,33},{97,65},{1,97},{34,2}... | collective-permute-start | bytes 1966088 | tf_op jit(solution)/shard_map/ppermute | solution.py:23
  33.4 7.9 %collective-permute-done.8.refs_3_.refs_4_ = bf16[256,1280]{1,0:T(8,128)(2,1)S(1)} collective-permute-done((bf16[256,1280]{1,0:T(8,128)(2,1)S(1)}, bf16[256,1280]{1,0:T(8,128)(2,1)S(1)}, u32[]{:S(2)}, u32[]{:S(2)}) %collective-permute-start.8) | collective-permute-done | bytes 655392 | tf_op jit(solution)/shard_map/ppermute | solution.py:23
  43.9 2.6 %collective-permute-done.9.refs_1_.refs_2_ = bf16[256,1280]{1,0:T(8,128)(2,1)S(1)} collective-permute-done((bf16[256,1280]{1,0:T(8,128)(2,1)S(1)}, bf16[256,1280]{1,0:T(8,128)(2,1)S(1)}, u32[]{:S(2)}, u32[]{:S(2)}) %collective-permute-start.9) | collective-permute-done | bytes 655392 | tf_op jit(solution)/shard_map/ppermute | solution.py:23
  47.9 5.3 %collective-permute-done.13 = bf16[512,1024]{1,0:T(8,128)(2,1)S(1)} collective-permute-done((bf16[512,1024]{1,0:T(8,128)(2,1)S(1)}, bf16[512,1024]{1,0:T(8,128)(2,1)S(1)}, u32[]{:S(2)}, u32[]{:S(2)}) %collective-permute-start.13) | collective-permute-done | bytes 1048608 | tf_op jit(solution)/shard_map/ppermute | solution.py:23
  53.2 4.3 %collective-permute-start.14 = (bf16[512,1024]{1,0:T(8,128)(2,1)S(1)}, bf16[512,1024]{1,0:T(8,128)(2,1)S(1)}, u32[]{:S(2)}, u32[]{:S(2)}) collective-permute-start(bf16[512,1024]{1,0:T(8,128)(2,1)S(1)} %collective-permute-done.13), channel_id=1, source_target_pairs={{1,0},{0,1},{3,2},{2,3},{5,4},{4,5},{7,6},{6,7},{9,8},{8,9},{11,10... | collective-permute-start | bytes 3145736 | tf_op jit(solution)/shard_map/ppermute | solution.py:23
  57.7 2.7 %collective-permute-start.7 = (bf16[384,1280]{1,0:T(8,128)(2,1)S(1)}, bf16[384,1280]{1,0:T(8,128)(2,1)S(1)}, u32[]{:S(2)}, u32[]{:S(2)}) collective-permute-start(bf16[384,1280]{1,0:T(8,128)(2,1)S(1)} %pad_maximum_fusion), channel_id=1, source_target_pairs={{8,0},{16,8},{24,16},{0,24},{9,1},{17,9},{25,17},{1,25},{10,2},{18... | collective-permute-start | bytes 2949128 | tf_op jit(solution)/shard_map/ppermute | solution.py:23
  60.5 2.9 %apply.8.refs_8_ = f32[1024,256]{1,0:T(8,128)S(1)} custom-call(s32[22]{0:T(128)S(1)} %compare_select_fusion.10.table.t, bf16[1024,1024]{1,0:T(8,128)(2,1)S(1)} %constant_dynamic-update-slice_fusion.orb.slab_ref, bf16[256,1280]{1,0:T(8,128)(2,1)S(1)} %pad_maximum_fusion.4.refs_0_, bf16[2048,4096]{1,0:T(8,128)(2,1)} %refs_12_.1), custom_call_target="tpu_custom_call" | custom-call | flops 167772160 | bytes 524288 | tf_op jit(solution)/shard_map/apply/pallas_call | solution.py:97
  63.3 5.3 %apply.9.refs_12_ = f32[1024,256]{1,0:T(8,128)S(1)} custom-call(s32[22]{0:T(128)S(1)} %compare_select_fusion.10.table.t, bf16[1024,1024]{1,0:T(8,128)(2,1)S(1)} %constant_dynamic-update-slice_fusion.orb.slab_ref, bf16[256,1280]{1,0:T(8,128)(2,1)S(1)} %collective-permute-done.6.refs_0_.refs_1_, ...), custom_call_target="tpu_custom_call", output_to_operand_aliasing={{}: (10, {})} | custom-call | flops 671088640 | bytes 2097152 | tf_op jit(solution)/shard_map/apply/pallas_call | solution.py:97
  68.8 6.1 %apply.10.refs_12_ = f32[1024,256]{1,0:T(8,128)S(1)} custom-call(s32[22]{0:T(128)S(1)} %compare_select_fusion.10.table.t, bf16[1024,1024]{1,0:T(8,128)(2,1)S(1)} %constant_dynamic-update-slice_fusion.2.slab_ref, bf16[256,1280]{1,0:T(8,128)(2,1)S(1)} %pad_maximum_fusion.4.refs_0_, bf16[256,1280]{1,0:T(8,128)(2,1)S(1)} %collective-permute-done.6.refs_0_.refs_1_, ...), custom_call_target="tpu_custom_call" | custom-call | flops 838860800 | bytes 2621440 | tf_op jit(solution)/shard_map/apply/pallas_call | solution.py:97
  74.9 7.3 %collective-permute-done.10 = bf16[384,1280]{1,0:T(8,128)(2,1)S(1)} collective-permute-done((bf16[384,1280]{1,0:T(8,128)(2,1)S(1)}, bf16[384,1280]{1,0:T(8,128)(2,1)S(1)}, u32[]{:S(2)}, u32[]{:S(2)}) %collective-permute-start.10) | collective-permute-done | bytes 983072 | tf_op jit(solution)/shard_map/ppermute | solution.py:23
  82.3 2.6 %collective-permute-start.15 = (bf16[256,1280]{1,0:T(8,128)(2,1)S(1)}, bf16[256,1280]{1,0:T(8,128)(2,1)S(1)}, u32[]{:S(2)}, u32[]{:S(2)}) collective-permute-start(bf16[256,1280]{1,0:T(8,128)(2,1)S(1)} %slice.56.refs_0_), channel_id=1, source_target_pairs={{8,0},{16,8},{24,16},{0,24},{9,1},{17,9},{25,17},{1,25},{10,2},{18... | collective-permute-start | bytes 1966088 | tf_op jit(solution)/shard_map/ppermute | solution.py:23
  84.9 1.5 %collective-permute-start.17 = (bf16[256,1280]{1,0:T(8,128)(2,1)S(1)}, bf16[256,1280]{1,0:T(8,128)(2,1)S(1)}, u32[]{:S(2)}, u32[]{:S(2)}) collective-permute-start(bf16[256,1280]{1,0:T(8,128)(2,1)S(1)} %slice.56.refs_0_), channel_id=1, source_target_pairs={{32,0},{64,32},{96,64},{0,96},{33,1},{65,33},{97,65},{1,97},{34,2}... | collective-permute-start | bytes 1966088 | tf_op jit(solution)/shard_map/ppermute | solution.py:23
  87.8 6.9 %apply.11.refs_8_ = f32[1024,256]{1,0:T(8,128)S(1)} custom-call(s32[22]{0:T(128)S(1)} %compare_select_fusion.10.table.t, bf16[1024,1024]{1,0:T(8,128)(2,1)S(1)} %constant_dynamic-update-slice_fusion.2.slab_ref, bf16[256,1280]{1,0:T(8,128)(2,1)S(1)} %slice.56.refs_0_, bf16[256,1280]{1,0:T(8,128)(2,1)S(1)} %slice.57.refs_1_, ...), custom_call_target="tpu_custom_call", output_to_operand_aliasing={{}: (14, {})} | custom-call | flops 1006632960 | bytes 3145728 | tf_op jit(solution)/shard_map/apply/pallas_call | solution.py:97
  94.7 6.9 %apply.12.refs_13_ = f32[1024,256]{1,0:T(8,128)S(1)} custom-call(s32[22]{0:T(128)S(1)} %compare_select_fusion.10.table.t, bf16[1024,1024]{1,0:T(8,128)(2,1)S(1)} %constant_dynamic-update-slice_fusion.orb.slab_ref, bf16[256,1280]{1,0:T(8,128)(2,1)S(1)} %slice.56.refs_0_, bf16[256,1280]{1,0:T(8,128)(2,1)S(1)} %slice.57.refs_1_, ...), custom_call_target="tpu_custom_call", output_to_operand_aliasing={{}: (14, {})} | custom-call | flops 1006632960 | bytes 3145728 | tf_op jit(solution)/shard_map/apply/pallas_call | solution.py:97
  102.2 2.5 %collective-permute-start.19 = (bf16[64,1280]{1,0:T(8,128)(2,1)S(1)}, bf16[64,1280]{1,0:T(8,128)(2,1)S(1)}, u32[]{:S(2)}, u32[]{:S(2)}) collective-permute-start(bf16[64,1280]{1,0:T(8,128)(2,1)S(1)} %slice.64), channel_id=1, source_target_pairs={{8,0},{16,8},{24,16},{0,24},{9,1},{17,9},{25,17},{1,25},{10,2},{18... | collective-permute-start | bytes 491528 | tf_op jit(solution)/shard_map/ppermute | solution.py:23
  104.8 2.5 %collective-permute-start.21 = (bf16[64,1280]{1,0:T(8,128)(2,1)S(1)}, bf16[64,1280]{1,0:T(8,128)(2,1)S(1)}, u32[]{:S(2)}, u32[]{:S(2)}) collective-permute-start(bf16[64,1280]{1,0:T(8,128)(2,1)S(1)} %slice.66), channel_id=1, source_target_pairs={{32,0},{64,32},{96,64},{0,96},{33,1},{65,33},{97,65},{1,97},{34,2}... | collective-permute-start | bytes 491528 | tf_op jit(solution)/shard_map/ppermute | solution.py:23
  107.4 5.3 %apply.13.refs_5_ = f32[1024,256]{1,0:T(8,128)S(1)} custom-call(s32[22]{0:T(128)S(1)} %compare_select_fusion.10.table.t, bf16[1024,1024]{1,0:T(8,128)(2,1)S(1)} %constant_dynamic-update-slice_fusion.2.slab_ref, bf16[256,1280]{1,0:T(8,128)(2,1)S(1)} %collective-permute-done.15.refs_0_, ...), custom_call_target="tpu_custom_call", output_to_operand_aliasing={{}: (10, {})} | custom-call | flops 671088640 | bytes 2097152 | tf_op jit(solution)/shard_map/apply/pallas_call | solution.py:97
  113.0 2.9 %apply.14 = (f32[512,256]{1,0:T(8,128)S(1)}, f32[512,256]{1,0:T(8,128)S(1)}) custom-call(s32[22]{0:T(128)S(1)} %compare_select_fusion.10.table.t, bf16[1024,1024]{1,0:T(8,128)(2,1)S(1)} %constant_dynamic-update-slice_fusion.2.slab_ref, bf16[64,1280]{1,0:T(8,128)(2,1)S(1)} %collective-permute-done.19.refs_0_.refs_4_, ...), custom_call_target="tpu_custom_call" | custom-call | flops 167772160 | bytes 524288 | tf_op jit(solution)/shard_map/apply/pallas_call | solution.py:97
  116.0 3.7 %collective-permute-start.23 = (f32[512,256]{1,0:T(8,128)S(1)}, f32[512,256]{1,0:T(8,128)S(1)}, u32[]{:S(2)}, u32[]{:S(2)}) collective-permute-start(f32[512,256]{1,0:T(8,128)S(1)} %get-tuple-element.36), channel_id=1, source_target_pairs={{1,0},{0,1},{3,2},{2,3},{5,4},{4,5},{7,6},{6,7},{9,8},{8,9},{11,10... | collective-permute-start | bytes 1572872 | tf_op jit(solution)/shard_map/ppermute | solution.py:23
  119.7 1.5 %collective-permute-done.23 = f32[512,256]{1,0:T(8,128)S(1)} collective-permute-done((f32[512,256]{1,0:T(8,128)S(1)}, f32[512,256]{1,0:T(8,128)S(1)}, u32[]{:S(2)}, u32[]{:S(2)}) %collective-permute-start.23) | collective-permute-done | bytes 524320 | tf_op jit(solution)/shard_map/ppermute | solution.py:23
  121.3 1.6 %collective-permute-start.24 = (bf16[512,256]{1,0:T(8,128)(2,1)S(1)}, bf16[512,256]{1,0:T(8,128)(2,1)S(1)}, u32[]{:S(2)}, u32[]{:S(2)}) collective-permute-start(bf16[512,256]{1,0:T(8,128)(2,1)S(1)} %add_convert_fusion), channel_id=1, source_target_pairs={{2,0},{0,2},{3,1},{1,3},{6,4},{4,6},{7,5},{5,7},{10,8},{8,10},{11,... | collective-permute-start | bytes 786440 | tf_op jit(solution)/shard_map/ppermute | solution.py:23
  122.9 6.1 %apply.15 = (f32[512,256]{1,0:T(8,128)S(1)}, f32[512,256]{1,0:T(8,128)S(1)}) custom-call(s32[22]{0:T(128)S(1)} %compare_select_fusion.10.table.t, bf16[1024,1024]{1,0:T(8,128)(2,1)S(1)} %constant_dynamic-update-slice_fusion.orb.slab_ref, bf16[256,1280]{1,0:T(8,128)(2,1)S(1)} %collective-permute-done.15.refs_0_, ...), custom_call_target="tpu_custom_call" | custom-call | flops 838860800 | bytes 2621440 | tf_op jit(solution)/shard_map/apply/pallas_call | solution.py:97
  129.0 1.4 %collective-permute-done.24 = bf16[512,256]{1,0:T(8,128)(2,1)S(1)} collective-permute-done((bf16[512,256]{1,0:T(8,128)(2,1)S(1)}, bf16[512,256]{1,0:T(8,128)(2,1)S(1)}, u32[]{:S(2)}, u32[]{:S(2)}) %collective-permute-start.24) | collective-permute-done | bytes 262176 | tf_op jit(solution)/shard_map/ppermute | solution.py:23
  131.6 1.5 %collective-permute-done.25 = f32[512,256]{1,0:T(8,128)S(1)} collective-permute-done((f32[512,256]{1,0:T(8,128)S(1)}, f32[512,256]{1,0:T(8,128)S(1)}, u32[]{:S(2)}, u32[]{:S(2)}) %collective-permute-start.25) | collective-permute-done | bytes 524320 | tf_op jit(solution)/shard_map/ppermute | solution.py:23
  (78 shorter events, 13.6 us)
Async XLA Ops:
  0.0 6.6 %copy-start.4 = (bf16[512,256]{1,0:T(8,128)(2,1)S(1)}, bf16[512,256]{1,0:T(8,128)(2,1)}, u32[]{:S(2)}) copy-start(bf16[512,256]{1,0:T(8,128)(2,1)} %param.5) | copy-start | bytes 786436
  0.0 6.6 %copy-start.5 = (s32[1,128]{1,0:T(1,128)S(1)}, s32[1,128]{1,0:T(1,128)}, u32[]{:S(2)}) copy-start(s32[1,128]{1,0:T(1,128)} %param.6) | copy-start | bytes 1540
  0.0 7.6 %collective-permute-start = (bf16[512,1024]{1,0:T(8,128)(2,1)}, bf16[512,1024]{1,0:T(8,128)(2,1)S(1)}, u32[]{:S(2)}, u32[]{:S(2)}) collective-permute-start(bf16[512,1024]{1,0:T(8,128)(2,1)} %param.4), channel_id=1, source_target_pairs={{1,0},{0,1},{3,2},{2,3},{5,4},{4,5},{7,6},{6,7},{9,8},{8,9},{11,10... | collective-permute-start | bytes 3145736 | tf_op jit(solution)/shard_map/ppermute | solution.py:23
  1.4 5.2 %collective-permute-start.2 = (bf16[512,256]{1,0:T(8,128)(2,1)}, bf16[512,256]{1,0:T(8,128)(2,1)}, u32[]{:S(2)}, u32[]{:S(2)}) collective-permute-start(bf16[512,256]{1,0:T(8,128)(2,1)} %param.5), channel_id=1, source_target_pairs={{1,0},{0,1},{3,2},{2,3},{5,4},{4,5},{7,6},{6,7},{9,8},{8,9},{11,10... | collective-permute-start | bytes 786440 | tf_op jit(solution)/shard_map/ppermute | solution.py:23
  1.4 5.1 %collective-permute-start.1 = (s32[1,128]{1,0:T(1,128)}, s32[1,128]{1,0:T(1,128)S(1)}, u32[]{:S(2)}, u32[]{:S(2)}) collective-permute-start(s32[1,128]{1,0:T(1,128)} %param.6), channel_id=1, source_target_pairs={{2,0},{0,2},{3,1},{1,3},{6,4},{4,6},{7,5},{5,7},{10,8},{8,10},{11,... | collective-permute-start | bytes 1544 | tf_op jit(solution)/shard_map/ppermute | solution.py:23
  9.2 21.2 %copy-start.3 = (bf16[512,1024]{1,0:T(8,128)(2,1)S(1)}, bf16[512,1024]{1,0:T(8,128)(2,1)}, u32[]{:S(2)}) copy-start(bf16[512,1024]{1,0:T(8,128)(2,1)} %param.4) | copy-start | bytes 3145732
  9.2 9.8 %collective-permute-start.3 = (bf16[128,1280]{1,0:T(8,128)(2,1)S(1)}, bf16[128,1280]{1,0:T(8,128)(2,1)S(1)}, u32[]{:S(2)}, u32[]{:S(2)}) collective-permute-start(bf16[128,1280]{1,0:T(8,128)(2,1)S(1)} %get-tuple-element.24), channel_id=1, source_target_pairs={{2,0},{0,2},{3,1},{1,3},{6,4},{4,6},{7,5},{5,7},{10,8},{8,10},{11,... | collective-permute-start | bytes 983048 | tf_op jit(solution)/shard_map/ppermute | solution.py:23
  19.1 7.4 %collective-permute-start.4 = (bf16[128,1280]{1,0:T(8,128)(2,1)S(1)}, bf16[128,1280]{1,0:T(8,128)(2,1)S(1)}, u32[]{:S(2)}, u32[]{:S(2)}) collective-permute-start(bf16[128,1280]{1,0:T(8,128)(2,1)S(1)} %add.68), channel_id=1, source_target_pairs={{4,0},{0,4},{5,1},{1,5},{6,2},{2,6},{7,3},{3,7},{12,8},{8,12},{13,... | collective-permute-start | bytes 983048 | tf_op jit(solution)/shard_map/ppermute | solution.py:23
  26.5 14.8 %collective-permute-start.8 = (bf16[256,1280]{1,0:T(8,128)(2,1)S(1)}, bf16[256,1280]{1,0:T(8,128)(2,1)S(1)}, u32[]{:S(2)}, u32[]{:S(2)}) collective-permute-start(bf16[256,1280]{1,0:T(8,128)(2,1)S(1)} %pad_maximum_fusion.4.refs_0_), channel_id=1, source_target_pairs={{96,0},{0,32},{32,64},{64,96},{97,1},{1,33},{33,65},{65,97},{98,2}... | collective-permute-start | bytes 1966088 | tf_op jit(solution)/shard_map/ppermute | solution.py:23
  27.9 13.5 %collective-permute-start.6 = (bf16[256,1280]{1,0:T(8,128)(2,1)S(1)}, bf16[256,1280]{1,0:T(8,128)(2,1)S(1)}, u32[]{:S(2)}, u32[]{:S(2)}) collective-permute-start(bf16[256,1280]{1,0:T(8,128)(2,1)S(1)} %pad_maximum_fusion.4.refs_0_), channel_id=1, source_target_pairs={{8,0},{16,8},{24,16},{0,24},{9,1},{17,9},{25,17},{1,25},{10,2},{18... | collective-permute-start | bytes 1966088 | tf_op jit(solution)/shard_map/ppermute | solution.py:23
  30.4 22.8 %collective-permute-start.13 = (bf16[512,1024]{1,0:T(8,128)(2,1)S(1)}, bf16[512,1024]{1,0:T(8,128)(2,1)S(1)}, u32[]{:S(2)}, u32[]{:S(2)}) collective-permute-start(bf16[512,1024]{1,0:T(8,128)(2,1)S(1)} %copy-done.3), channel_id=1, source_target_pairs={{2,0},{0,2},{3,1},{1,3},{6,4},{4,6},{7,5},{5,7},{10,8},{8,10},{11,... | collective-permute-start | bytes 3145736 | tf_op jit(solution)/shard_map/ppermute | solution.py:23
  31.9 12.0 %collective-permute-start.5 = (bf16[256,1280]{1,0:T(8,128)(2,1)S(1)}, bf16[256,1280]{1,0:T(8,128)(2,1)S(1)}, u32[]{:S(2)}, u32[]{:S(2)}) collective-permute-start(bf16[256,1280]{1,0:T(8,128)(2,1)S(1)} %pad_maximum_fusion.4.refs_0_), channel_id=1, source_target_pairs={{32,0},{64,32},{96,64},{0,96},{33,1},{65,33},{97,65},{1,97},{34,2}... | collective-permute-start | bytes 1966088 | tf_op jit(solution)/shard_map/ppermute | solution.py:23
  33.4 13.1 %collective-permute-start.9 = (bf16[256,1280]{1,0:T(8,128)(2,1)S(1)}, bf16[256,1280]{1,0:T(8,128)(2,1)S(1)}, u32[]{:S(2)}, u32[]{:S(2)}) collective-permute-start(bf16[256,1280]{1,0:T(8,128)(2,1)S(1)} %pad_maximum_fusion.4.refs_0_), channel_id=1, source_target_pairs={{24,0},{0,8},{8,16},{16,24},{25,1},{1,9},{9,17},{17,25},{26,2},{2,... | collective-permute-start | bytes 1966088 | tf_op jit(solution)/shard_map/ppermute | solution.py:23
  41.5 33.4 %collective-permute-start.12 = (bf16[384,1280]{1,0:T(8,128)(2,1)S(1)}, bf16[384,1280]{1,0:T(8,128)(2,1)S(1)}, u32[]{:S(2)}, u32[]{:S(2)}) collective-permute-start(bf16[384,1280]{1,0:T(8,128)(2,1)S(1)} %pad_maximum_fusion.3), channel_id=1, source_target_pairs={{96,0},{0,32},{32,64},{64,96},{97,1},{1,33},{33,65},{65,97},{98,2}... | collective-permute-start | bytes 2949128 | tf_op jit(solution)/shard_map/ppermute | solution.py:23
  46.5 28.3 %collective-permute-start.11 = (bf16[384,1280]{1,0:T(8,128)(2,1)S(1)}, bf16[384,1280]{1,0:T(8,128)(2,1)S(1)}, u32[]{:S(2)}, u32[]{:S(2)}) collective-permute-start(bf16[384,1280]{1,0:T(8,128)(2,1)S(1)} %pad_maximum_fusion.2), channel_id=1, source_target_pairs={{32,0},{64,32},{96,64},{0,96},{33,1},{65,33},{97,65},{1,97},{34,2}... | collective-permute-start | bytes 2949128 | tf_op jit(solution)/shard_map/ppermute | solution.py:23
  53.2 15.5 %collective-permute-start.14 = (bf16[512,1024]{1,0:T(8,128)(2,1)S(1)}, bf16[512,1024]{1,0:T(8,128)(2,1)S(1)}, u32[]{:S(2)}, u32[]{:S(2)}) collective-permute-start(bf16[512,1024]{1,0:T(8,128)(2,1)S(1)} %collective-permute-done.13), channel_id=1, source_target_pairs={{1,0},{0,1},{3,2},{2,3},{5,4},{4,5},{7,6},{6,7},{9,8},{8,9},{11,10... | collective-permute-start | bytes 3145736 | tf_op jit(solution)/shard_map/ppermute | solution.py:23
  57.5 24.7 %collective-permute-start.10 = (bf16[384,1280]{1,0:T(8,128)(2,1)S(1)}, bf16[384,1280]{1,0:T(8,128)(2,1)S(1)}, u32[]{:S(2)}, u32[]{:S(2)}) collective-permute-start(bf16[384,1280]{1,0:T(8,128)(2,1)S(1)} %pad_maximum_fusion.1), channel_id=1, source_target_pairs={{24,0},{0,8},{8,16},{16,24},{25,1},{1,9},{9,17},{17,25},{26,2},{2,... | collective-permute-start | bytes 2949128 | tf_op jit(solution)/shard_map/ppermute | solution.py:23
  57.7 24.5 %collective-permute-start.7 = (bf16[384,1280]{1,0:T(8,128)(2,1)S(1)}, bf16[384,1280]{1,0:T(8,128)(2,1)S(1)}, u32[]{:S(2)}, u32[]{:S(2)}) collective-permute-start(bf16[384,1280]{1,0:T(8,128)(2,1)S(1)} %pad_maximum_fusion), channel_id=1, source_target_pairs={{8,0},{16,8},{24,16},{0,24},{9,1},{17,9},{25,17},{1,25},{10,2},{18... | collective-permute-start | bytes 2949128 | tf_op jit(solution)/shard_map/ppermute | solution.py:23
  74.9 11.5 %copy-start.2 = (bf16[384,1280]{1,0:T(8,128)(2,1)}, bf16[384,1280]{1,0:T(8,128)(2,1)S(1)}, u32[]{:S(2)}) copy-start(bf16[384,1280]{1,0:T(8,128)(2,1)S(1)} %collective-permute-done.11) | copy-start | bytes 2949124
  82.2 4.2 %copy-start.1 = (bf16[384,1280]{1,0:T(8,128)(2,1)}, bf16[384,1280]{1,0:T(8,128)(2,1)S(1)}, u32[]{:S(2)}) copy-start(bf16[384,1280]{1,0:T(8,128)(2,1)S(1)} %collective-permute-done.10) | copy-start | bytes 2949124
  82.2 4.2 %copy-start = (bf16[384,1280]{1,0:T(8,128)(2,1)}, bf16[384,1280]{1,0:T(8,128)(2,1)S(1)}, u32[]{:S(2)}) copy-start(bf16[384,1280]{1,0:T(8,128)(2,1)S(1)} %collective-permute-done.7) | copy-start | bytes 2949124
  82.3 19.3 %collective-permute-start.15 = (bf16[256,1280]{1,0:T(8,128)(2,1)S(1)}, bf16[256,1280]{1,0:T(8,128)(2,1)S(1)}, u32[]{:S(2)}, u32[]{:S(2)}) collective-permute-start(bf16[256,1280]{1,0:T(8,128)(2,1)S(1)} %slice.56.refs_0_), channel_id=1, source_target_pairs={{8,0},{16,8},{24,16},{0,24},{9,1},{17,9},{25,17},{1,25},{10,2},{18... | collective-permute-start | bytes 1966088 | tf_op jit(solution)/shard_map/ppermute | solution.py:23
  84.9 16.7 %collective-permute-start.16 = (bf16[256,1280]{1,0:T(8,128)(2,1)S(1)}, bf16[256,1280]{1,0:T(8,128)(2,1)S(1)}, u32[]{:S(2)}, u32[]{:S(2)}) collective-permute-start(bf16[256,1280]{1,0:T(8,128)(2,1)S(1)} %slice.57.refs_1_), channel_id=1, source_target_pairs={{24,0},{0,8},{8,16},{16,24},{25,1},{1,9},{9,17},{17,25},{26,2},{2,... | collective-permute-start | bytes 1966088 | tf_op jit(solution)/shard_map/ppermute | solution.py:23
  84.9 16.7 %collective-permute-start.17 = (bf16[256,1280]{1,0:T(8,128)(2,1)S(1)}, bf16[256,1280]{1,0:T(8,128)(2,1)S(1)}, u32[]{:S(2)}, u32[]{:S(2)}) collective-permute-start(bf16[256,1280]{1,0:T(8,128)(2,1)S(1)} %slice.56.refs_0_), channel_id=1, source_target_pairs={{32,0},{64,32},{96,64},{0,96},{33,1},{65,33},{97,65},{1,97},{34,2}... | collective-permute-start | bytes 1966088 | tf_op jit(solution)/shard_map/ppermute | solution.py:23
  86.4 15.8 %collective-permute-start.18 = (bf16[256,1280]{1,0:T(8,128)(2,1)S(1)}, bf16[256,1280]{1,0:T(8,128)(2,1)S(1)}, u32[]{:S(2)}, u32[]{:S(2)}) collective-permute-start(bf16[256,1280]{1,0:T(8,128)(2,1)S(1)} %slice.57.refs_1_), channel_id=1, source_target_pairs={{96,0},{0,32},{32,64},{64,96},{97,1},{1,33},{33,65},{65,97},{98,2}... | collective-permute-start | bytes 1966088 | tf_op jit(solution)/shard_map/ppermute | solution.py:23
  102.2 10.4 %collective-permute-start.19 = (bf16[64,1280]{1,0:T(8,128)(2,1)S(1)}, bf16[64,1280]{1,0:T(8,128)(2,1)S(1)}, u32[]{:S(2)}, u32[]{:S(2)}) collective-permute-start(bf16[64,1280]{1,0:T(8,128)(2,1)S(1)} %slice.64), channel_id=1, source_target_pairs={{8,0},{16,8},{24,16},{0,24},{9,1},{17,9},{25,17},{1,25},{10,2},{18... | collective-permute-start | bytes 491528 | tf_op jit(solution)/shard_map/ppermute | solution.py:23
  104.7 8.0 %collective-permute-start.20 = (bf16[64,1280]{1,0:T(8,128)(2,1)S(1)}, bf16[64,1280]{1,0:T(8,128)(2,1)S(1)}, u32[]{:S(2)}, u32[]{:S(2)}) collective-permute-start(bf16[64,1280]{1,0:T(8,128)(2,1)S(1)} %slice.65), channel_id=1, source_target_pairs={{24,0},{0,8},{8,16},{16,24},{25,1},{1,9},{9,17},{17,25},{26,2},{2,... | collective-permute-start | bytes 491528 | tf_op jit(solution)/shard_map/ppermute | solution.py:23
  104.8 7.9 %collective-permute-start.21 = (bf16[64,1280]{1,0:T(8,128)(2,1)S(1)}, bf16[64,1280]{1,0:T(8,128)(2,1)S(1)}, u32[]{:S(2)}, u32[]{:S(2)}) collective-permute-start(bf16[64,1280]{1,0:T(8,128)(2,1)S(1)} %slice.66), channel_id=1, source_target_pairs={{32,0},{64,32},{96,64},{0,96},{33,1},{65,33},{97,65},{1,97},{34,2}... | collective-permute-start | bytes 491528 | tf_op jit(solution)/shard_map/ppermute | solution.py:23
  107.3 5.7 %collective-permute-start.22 = (bf16[64,1280]{1,0:T(8,128)(2,1)S(1)}, bf16[64,1280]{1,0:T(8,128)(2,1)S(1)}, u32[]{:S(2)}, u32[]{:S(2)}) collective-permute-start(bf16[64,1280]{1,0:T(8,128)(2,1)S(1)} %slice.67), channel_id=1, source_target_pairs={{96,0},{0,32},{32,64},{64,96},{97,1},{1,33},{33,65},{65,97},{98,2}... | collective-permute-start | bytes 491528 | tf_op jit(solution)/shard_map/ppermute | solution.py:23
  116.0 5.3 %collective-permute-start.23 = (f32[512,256]{1,0:T(8,128)S(1)}, f32[512,256]{1,0:T(8,128)S(1)}, u32[]{:S(2)}, u32[]{:S(2)}) collective-permute-start(f32[512,256]{1,0:T(8,128)S(1)} %get-tuple-element.36), channel_id=1, source_target_pairs={{1,0},{0,1},{3,2},{2,3},{5,4},{4,5},{7,6},{6,7},{9,8},{8,9},{11,10... | collective-permute-start | bytes 1572872 | tf_op jit(solution)/shard_map/ppermute | solution.py:23
  121.3 9.1 %collective-permute-start.24 = (bf16[512,256]{1,0:T(8,128)(2,1)S(1)}, bf16[512,256]{1,0:T(8,128)(2,1)S(1)}, u32[]{:S(2)}, u32[]{:S(2)}) collective-permute-start(bf16[512,256]{1,0:T(8,128)(2,1)S(1)} %add_convert_fusion), channel_id=1, source_target_pairs={{2,0},{0,2},{3,1},{1,3},{6,4},{4,6},{7,5},{5,7},{10,8},{8,10},{11,... | collective-permute-start | bytes 786440 | tf_op jit(solution)/shard_map/ppermute | solution.py:23
  130.4 2.7 %collective-permute-start.25 = (f32[512,256]{1,0:T(8,128)S(1)}, f32[512,256]{1,0:T(8,128)S(1)}, u32[]{:S(2)}, u32[]{:S(2)}) collective-permute-start(f32[512,256]{1,0:T(8,128)S(1)} %get-tuple-element.40), channel_id=1, source_target_pairs={{1,0},{0,1},{3,2},{2,3},{5,4},{4,5},{7,6},{6,7},{9,8},{8,9},{11,10... | collective-permute-start | bytes 1572872 | tf_op jit(solution)/shard_map/ppermute | solution.py:23
  (3 other events, 3.2 us)

commit v5 on v4

--- a/solution.py
+++ b/solution.py
@@ -133,7 +133,9 @@
     near_tgt = jnp.concatenate([targets, sib_tgt], axis=0)
     ids = jnp.concatenate([points, far_points], axis=0)
     mine, theirs = pick(table, ids, near_slab, near_tgt)
-    block = mine + take_from(theirs, "zh", 1)
+    early = own_rows * 3 // 8
+    far_early = take_from(orbitals[:early], "zh", 1)
+    block = mine + take_from(after(theirs, far_early), "zh", 1)
 
     def near_apply(parts, ats, total, last=False):
         return apply_parts(near_slab, parts, potential, table, NEAR, ORDER.index(ats[0]), len(ats), total, last)
@@ -145,10 +147,10 @@
     lower = table[SIDE:].reshape(1, 1) == 0
     low, high = jnp.where(lower, block, other), jnp.where(lower, other, block)
     pair = {(0, 0): jnp.concatenate([low, high], axis=0)}
-    far_orb = take_from(after(orbitals, other), "zh", 1)
+    far_late = take_from(after(orbitals[early:], other), "zh", 1)
     for at, axis, side in NEXT:
         pair[at] = take_from(pair[0, 0], axis, side)
-    near = near_apply([pair[0, 0]], [(0, 0)], None)
+    far_orb = jnp.concatenate([far_early, far_late], axis=0)
 
     def joined(whole, half):
         return jnp.concatenate([pair[whole], half], axis=0)
@@ -158,7 +160,7 @@
     from_up = take_from(joined((0, 3), pair[1, 0][:count]), "y", 1)
     from_down = take_from(joined((0, 1), pair[3, 0][count:]), "y", -1)
     first = tuple(at for at, _, _ in NEXT)
-    near = near_apply([pair[at] for at in first], first, near)
+    near = near_apply([pair[0, 0]] + [pair[at] for at in first], ((0, 0),) + first, None)
     far_sib = take_from(far_orb, "c", 1)
     far_slab = jnp.concatenate([far_orb, far_sib], axis=0)
     far = far_apply([pair[0, 0]] + [pair[at] for at in first], ((0, 0),) + first, None)
@@ -182,12 +184,7 @@
     third = ((1, 2), (3, 2), (2, 1), (2, 3))
     ready = lax.optimization_barrier((*(pair[at] for at in third), near, far))[:4]
     pair.update(zip(third, ready))
-    part = both // 4
-    sides = (((2, 1), "x", 1), ((2, 3), "x", -1), ((1, 2), "y", 1), ((3, 2), "y", -1))
-    last = [
-        take_from(pair[at][k * part : (k + 1) * part], axis, side)
-        for k, (at, axis, side) in enumerate(sides)
-    ]
+    last = [take_from(pair[2, 1][:count], "x", 1), take_from(pair[1, 2][count:], "y", 1)]
     far = far_apply([pair[at] for at in third], third, far)
     kept, sent = far_apply(last, [(2, 2)], far, True)
     far = (kept + take_from(sent, "c", 1)).astype(jnp.bfloat16)

time: 134 us -> 132 us (0.985)
  waiting for transfers between devices: 42.5 us -> 38.9 us
  Pallas kernels: 43.9 us -> 41.8 us
  local copies, waits for them, and re-layouts: 3.51 us -> 5.32 us
    ppermute x26 -> x25, waiting for transfers between devices: 42.5 us -> 38.9 us  [take_from(): return lax.ppermute(value, axis, [((i + side) % n, i) for i in range(n)])]
    pallas_call x8 -> x7, Pallas kernels: 42.4 us -> 40.3 us  [apply_parts(): pl.pallas_call(body, out_shape=(half, half) if last else jax.ShapeDtypeSt...]
    slice x4, local copies, waits for them, and re-layouts: 0.05 us -> 1.86 us  [the longest x1 1.77 us: local(): far_early = take_from(orbitals[:early], 'zh', 1)]
    ppermute x26 -> x25, starting transfers between devices: 40.5 us -> 41.8 us  [take_from(): return lax.ppermute(value, axis, [((i + side) % n, i) for i in range(n)])]
  transfers between devices with their start and end apart: 26 -> 25, of which waited for: 12 -> 9; matrix products, arithmetic and copies ran while one was open for 3% -> 4% of each run, Pallas kernels for 29% -> 30%
where the time goes in v5:
time: 132 us
  starting transfers between devices  41.8 us (32%)
  Pallas kernels  41.8 us (32%)
  waiting for transfers between devices  38.9 us (29%)
  local copies, waits for them, and re-layouts  5.32 us (4%)
  other arithmetic  2.61 us (2%)
    ppermute x25, starting transfers between devices, take_from(): return lax.ppermute(value, axis, [((i + side) % n, i) for i in range(n)])  41.8 us
    pallas_call x7, Pallas kernels, apply_parts(): pl.pallas_call(body, out_shape=(half, half) if last else jax.ShapeDtypeSt...  40.3 us
    ppermute x25, waiting for transfers between devices, take_from(): return lax.ppermute(value, axis, [((i + side) % n, i) for i in range(n)])  38.9 us
  transfers between devices with their start and end apart: 25, of which 9 were waited for; matrix products, arithmetic and copies ran while one was open for 4% of the time, Pallas kernels for 30%

profile of v5, /device:TPU:1, one launch (start us, length us, event | category | flops | bytes accessed | tf_op | source)
XLA Modules:
  0.0 131.6 jit_solution(12400299344309086386)
XLA Ops:
  0.0 1.4 %collective-permute-start = (bf16[512,1024]{1,0:T(8,128)(2,1)}, bf16[512,1024]{1,0:T(8,128)(2,1)S(1)}, u32[]{:S(2)}, u32[]{:S(2)}) collective-permute-start(bf16[512,1024]{1,0:T(8,128)(2,1)} %param.4), channel_id=1, source_target_pairs={{1,0},{0,1},{3,2},{2,3},{5,4},{4,5},{7,6},{6,7},{9,8},{8,9},{11,10... | collective-permute-start | bytes 3145736 | tf_op jit(solution)/shard_map/ppermute | solution.py:23
  1.4 3.8 %collective-permute-start.1 = (s32[1,128]{1,0:T(1,128)}, s32[1,128]{1,0:T(1,128)S(1)}, u32[]{:S(2)}, u32[]{:S(2)}) collective-permute-start(s32[1,128]{1,0:T(1,128)} %param.6), channel_id=1, source_target_pairs={{2,0},{0,2},{3,1},{1,3},{6,4},{4,6},{7,5},{5,7},{10,8},{8,10},{11,... | collective-permute-start | bytes 1544 | tf_op jit(solution)/shard_map/ppermute | solution.py:23
  5.2 1.8 %slice.52 = bf16[192,1024]{1,0:T(8,128)(2,1)} slice(bf16[512,1024]{1,0:T(8,128)(2,1)} %param.4), slice={[0:192], [0:1024]} | slice | bytes 786432 | tf_op jit(solution)/shard_map/slice | solution.py:137
  9.5 1.5 %pick.1 = (bf16[128,1280]{1,0:T(8,128)(2,1)S(1)}, bf16[128,1280]{1,0:T(8,128)(2,1)S(1)}) custom-call(s32[22]{0:T(128)S(1)} %compare_select_fusion.10.table.t, s32[2,128]{1,0:T(2,128)S(1)} %pad_add_fusion.ids, bf16[1024,1024]{1,0:T(8,128)(2,1)S(1)} %constant_dynamic-update-slice_fusion.orb.slab_ref, bf16[1024,256]{1,0:T(8,128)(2,1)S(1)} %pad_maximum_fusion.8.tgt), custom_call_target="tpu_custom_call" | custom-call | tf_op jit(solution)/shard_map/pick/pallas_call | solution.py:46
  11.0 7.6 %collective-permute-done.3 = bf16[192,1024]{1,0:T(8,128)(2,1)S(1)} collective-permute-done((bf16[192,1024]{1,0:T(8,128)(2,1)}, bf16[192,1024]{1,0:T(8,128)(2,1)S(1)}, u32[]{:S(2)}, u32[]{:S(2)}) %collective-permute-start.3) | collective-permute-done | bytes 393248 | tf_op jit(solution)/shard_map/ppermute | solution.py:23
  18.9 8.8 %collective-permute-done.4 = bf16[128,1280]{1,0:T(8,128)(2,1)S(1)} collective-permute-done((bf16[128,1280]{1,0:T(8,128)(2,1)S(1)}, bf16[128,1280]{1,0:T(8,128)(2,1)S(1)}, u32[]{:S(2)}, u32[]{:S(2)}) %collective-permute-start.4) | collective-permute-done | bytes 327712 | tf_op jit(solution)/shard_map/ppermute | solution.py:23
  29.9 4.7 %collective-permute-done.5 = bf16[128,1280]{1,0:T(8,128)(2,1)S(1)} collective-permute-done((bf16[128,1280]{1,0:T(8,128)(2,1)S(1)}, bf16[128,1280]{1,0:T(8,128)(2,1)S(1)}, u32[]{:S(2)}, u32[]{:S(2)}) %collective-permute-start.5) | collective-permute-done | bytes 327712 | tf_op jit(solution)/shard_map/ppermute | solution.py:23
  35.6 1.4 %collective-permute-start.9 = (bf16[256,1280]{1,0:T(8,128)(2,1)S(1)}, bf16[256,1280]{1,0:T(8,128)(2,1)S(1)}, u32[]{:S(2)}, u32[]{:S(2)}) collective-permute-start(bf16[256,1280]{1,0:T(8,128)(2,1)S(1)} %pad_maximum_fusion.5.refs_0_), channel_id=1, source_target_pairs={{96,0},{0,32},{32,64},{64,96},{97,1},{1,33},{33,65},{65,97},{98,2}... | collective-permute-start | bytes 1966088 | tf_op jit(solution)/shard_map/ppermute | solution.py:23
  37.0 2.5 %collective-permute-start.7 = (bf16[256,1280]{1,0:T(8,128)(2,1)S(1)}, bf16[256,1280]{1,0:T(8,128)(2,1)S(1)}, u32[]{:S(2)}, u32[]{:S(2)}) collective-permute-start(bf16[256,1280]{1,0:T(8,128)(2,1)S(1)} %pad_maximum_fusion.5.refs_0_), channel_id=1, source_target_pairs={{8,0},{16,8},{24,16},{0,24},{9,1},{17,9},{25,17},{1,25},{10,2},{18... | collective-permute-start | bytes 1966088 | tf_op jit(solution)/shard_map/ppermute | solution.py:23
  39.5 1.5 %collective-permute-start.6 = (bf16[256,1280]{1,0:T(8,128)(2,1)S(1)}, bf16[256,1280]{1,0:T(8,128)(2,1)S(1)}, u32[]{:S(2)}, u32[]{:S(2)}) collective-permute-start(bf16[256,1280]{1,0:T(8,128)(2,1)S(1)} %pad_maximum_fusion.5.refs_0_), channel_id=1, source_target_pairs={{32,0},{64,32},{96,64},{0,96},{33,1},{65,33},{97,65},{1,97},{34,2}... | collective-permute-start | bytes 1966088 | tf_op jit(solution)/shard_map/ppermute | solution.py:23
  41.0 7.1 %collective-permute-done.14 = bf16[320,1024]{1,0:T(8,128)(2,1)S(1)} collective-permute-done((bf16[320,1024]{1,0:T(8,128)(2,1)S(1)}, bf16[320,1024]{1,0:T(8,128)(2,1)S(1)}, u32[]{:S(2)}, u32[]{:S(2)}) %collective-permute-start.14) | collective-permute-done | bytes 655392 | tf_op jit(solution)/shard_map/ppermute | solution.py:23
  48.2 5.2 %collective-permute-start.15 = (bf16[512,1024]{1,0:T(8,128)(2,1)S(1)}, bf16[512,1024]{1,0:T(8,128)(2,1)S(1)}, u32[]{:S(2)}, u32[]{:S(2)}) collective-permute-start(bf16[512,1024]{1,0:T(8,128)(2,1)S(1)} %pad_maximum_fusion), channel_id=1, source_target_pairs={{1,0},{0,1},{3,2},{2,3},{5,4},{4,5},{7,6},{6,7},{9,8},{8,9},{11,10... | collective-permute-start | bytes 3145736 | tf_op jit(solution)/shard_map/ppermute | solution.py:23
  53.5 1.4 %collective-permute-start.13 = (bf16[384,1280]{1,0:T(8,128)(2,1)S(1)}, bf16[384,1280]{1,0:T(8,128)(2,1)S(1)}, u32[]{:S(2)}, u32[]{:S(2)}) collective-permute-start(bf16[384,1280]{1,0:T(8,128)(2,1)S(1)} %pad_maximum_fusion.4), channel_id=1, source_target_pairs={{96,0},{0,32},{32,64},{64,96},{97,1},{1,33},{33,65},{65,97},{98,2}... | collective-permute-start | bytes 2949128 | tf_op jit(solution)/shard_map/ppermute | solution.py:23
  55.0 1.5 %collective-permute-start.12 = (bf16[384,1280]{1,0:T(8,128)(2,1)S(1)}, bf16[384,1280]{1,0:T(8,128)(2,1)S(1)}, u32[]{:S(2)}, u32[]{:S(2)}) collective-permute-start(bf16[384,1280]{1,0:T(8,128)(2,1)S(1)} %pad_maximum_fusion.3), channel_id=1, source_target_pairs={{32,0},{64,32},{96,64},{0,96},{33,1},{65,33},{97,65},{1,97},{34,2}... | collective-permute-start | bytes 2949128 | tf_op jit(solution)/shard_map/ppermute | solution.py:23
  58.0 1.5 %collective-permute-start.8 = (bf16[384,1280]{1,0:T(8,128)(2,1)S(1)}, bf16[384,1280]{1,0:T(8,128)(2,1)S(1)}, u32[]{:S(2)}, u32[]{:S(2)}) collective-permute-start(bf16[384,1280]{1,0:T(8,128)(2,1)S(1)} %pad_maximum_fusion.1), channel_id=1, source_target_pairs={{8,0},{16,8},{24,16},{0,24},{9,1},{17,9},{25,17},{1,25},{10,2},{18... | collective-permute-start | bytes 2949128 | tf_op jit(solution)/shard_map/ppermute | solution.py:23
  59.6 6.1 %apply.7.refs_12_ = f32[1024,256]{1,0:T(8,128)S(1)} custom-call(s32[22]{0:T(128)S(1)} %compare_select_fusion.10.table.t, bf16[1024,1024]{1,0:T(8,128)(2,1)S(1)} %constant_dynamic-update-slice_fusion.orb.slab_ref, bf16[256,1280]{1,0:T(8,128)(2,1)S(1)} %pad_maximum_fusion.5.refs_0_, bf16[256,1280]{1,0:T(8,128)(2,1)S(1)} %collective-permute-done.7.refs_1_, ...), custom_call_target="tpu_custom_call" | custom-call | flops 838860800 | bytes 2621440 | tf_op jit(solution)/shard_map/apply/pallas_call | solution.py:97
  65.8 6.1 %apply.8.refs_12_ = f32[1024,256]{1,0:T(8,128)S(1)} custom-call(s32[22]{0:T(128)S(1)} %compare_select_fusion.10.table.t, bf16[1024,1024]{1,0:T(8,128)(2,1)S(1)} %constant_dynamic-update-slice_fusion.2.slab_ref, bf16[256,1280]{1,0:T(8,128)(2,1)S(1)} %pad_maximum_fusion.5.refs_0_, bf16[256,1280]{1,0:T(8,128)(2,1)S(1)} %collective-permute-done.7.refs_1_, ...), custom_call_target="tpu_custom_call" | custom-call | flops 838860800 | bytes 2621440 | tf_op jit(solution)/shard_map/apply/pallas_call | solution.py:97
  71.9 5.3 %collective-permute-done.13 = bf16[384,1280]{1,0:T(8,128)(2,1)S(1)} collective-permute-done((bf16[384,1280]{1,0:T(8,128)(2,1)S(1)}, bf16[384,1280]{1,0:T(8,128)(2,1)S(1)}, u32[]{:S(2)}, u32[]{:S(2)}) %collective-permute-start.13) | collective-permute-done | bytes 983072 | tf_op jit(solution)/shard_map/ppermute | solution.py:23
  77.9 2.2 %collective-permute-start.16 = (bf16[256,1280]{1,0:T(8,128)(2,1)S(1)}, bf16[256,1280]{1,0:T(8,128)(2,1)S(1)}, u32[]{:S(2)}, u32[]{:S(2)}) collective-permute-start(bf16[256,1280]{1,0:T(8,128)(2,1)S(1)} %slice.58.refs_0_), channel_id=1, source_target_pairs={{8,0},{16,8},{24,16},{0,24},{9,1},{17,9},{25,17},{1,25},{10,2},{18... | collective-permute-start | bytes 1966088 | tf_op jit(solution)/shard_map/ppermute | solution.py:23
  80.9 2.5 %collective-permute-start.18 = (bf16[256,1280]{1,0:T(8,128)(2,1)S(1)}, bf16[256,1280]{1,0:T(8,128)(2,1)S(1)}, u32[]{:S(2)}, u32[]{:S(2)}) collective-permute-start(bf16[256,1280]{1,0:T(8,128)(2,1)S(1)} %slice.58.refs_0_), channel_id=1, source_target_pairs={{32,0},{64,32},{96,64},{0,96},{33,1},{65,33},{97,65},{1,97},{34,2}... | collective-permute-start | bytes 1966088 | tf_op jit(solution)/shard_map/ppermute | solution.py:23
  84.7 6.9 %apply.9.refs_8_ = f32[1024,256]{1,0:T(8,128)S(1)} custom-call(s32[22]{0:T(128)S(1)} %compare_select_fusion.10.table.t, bf16[1024,1024]{1,0:T(8,128)(2,1)S(1)} %constant_dynamic-update-slice_fusion.2.slab_ref, bf16[256,1280]{1,0:T(8,128)(2,1)S(1)} %slice.58.refs_0_, bf16[256,1280]{1,0:T(8,128)(2,1)S(1)} %slice.59.refs_1_, ...), custom_call_target="tpu_custom_call", output_to_operand_aliasing={{}: (14, {})} | custom-call | flops 1006632960 | bytes 3145728 | tf_op jit(solution)/shard_map/apply/pallas_call | solution.py:97
  91.6 6.9 %apply.10.refs_11_ = f32[1024,256]{1,0:T(8,128)S(1)} custom-call(s32[22]{0:T(128)S(1)} %compare_select_fusion.10.table.t, bf16[1024,1024]{1,0:T(8,128)(2,1)S(1)} %constant_dynamic-update-slice_fusion.orb.slab_ref, bf16[256,1280]{1,0:T(8,128)(2,1)S(1)} %slice.58.refs_0_, bf16[256,1280]{1,0:T(8,128)(2,1)S(1)} %slice.59.refs_1_, ...), custom_call_target="tpu_custom_call", output_to_operand_aliasing={{}: (14, {})} | custom-call | flops 1006632960 | bytes 3145728 | tf_op jit(solution)/shard_map/apply/pallas_call | solution.py:97
  98.6 2.1 %collective-permute-start.20 = (bf16[128,1280]{1,0:T(8,128)(2,1)S(1)}, bf16[128,1280]{1,0:T(8,128)(2,1)S(1)}, u32[]{:S(2)}, u32[]{:S(2)}) collective-permute-start(bf16[128,1280]{1,0:T(8,128)(2,1)S(1)} %slice.66), channel_id=1, source_target_pairs={{8,0},{16,8},{24,16},{0,24},{9,1},{17,9},{25,17},{1,25},{10,2},{18... | collective-permute-start | bytes 983048 | tf_op jit(solution)/shard_map/ppermute | solution.py:23
  100.8 2.7 %collective-permute-start.21 = (bf16[128,1280]{1,0:T(8,128)(2,1)S(1)}, bf16[128,1280]{1,0:T(8,128)(2,1)S(1)}, u32[]{:S(2)}, u32[]{:S(2)}) collective-permute-start(bf16[128,1280]{1,0:T(8,128)(2,1)S(1)} %slice.67), channel_id=1, source_target_pairs={{32,0},{64,32},{96,64},{0,96},{33,1},{65,33},{97,65},{1,97},{34,2}... | collective-permute-start | bytes 983048 | tf_op jit(solution)/shard_map/ppermute | solution.py:23
  103.5 5.3 %apply.11.refs_3_ = f32[1024,256]{1,0:T(8,128)S(1)} custom-call(s32[22]{0:T(128)S(1)} %compare_select_fusion.10.table.t, bf16[1024,1024]{1,0:T(8,128)(2,1)S(1)} %constant_dynamic-update-slice_fusion.2.slab_ref, bf16[256,1280]{1,0:T(8,128)(2,1)S(1)} %collective-permute-done.16.refs_0_, ...), custom_call_target="tpu_custom_call", output_to_operand_aliasing={{}: (10, {})} | custom-call | flops 671088640 | bytes 2097152 | tf_op jit(solution)/shard_map/apply/pallas_call | solution.py:97
  108.8 2.9 %apply.12 = (f32[512,256]{1,0:T(8,128)S(1)}, f32[512,256]{1,0:T(8,128)S(1)}) custom-call(s32[22]{0:T(128)S(1)} %compare_select_fusion.10.table.t, bf16[1024,1024]{1,0:T(8,128)(2,1)S(1)} %constant_dynamic-update-slice_fusion.2.slab_ref, bf16[128,1280]{1,0:T(8,128)(2,1)S(1)} %collective-permute-done.20.refs_0_.refs_4_, ...), custom_call_target="tpu_custom_call" | custom-call | flops 167772160 | bytes 524288 | tf_op jit(solution)/shard_map/apply/pallas_call | solution.py:97
  111.7 5.5 %collective-permute-start.22 = (f32[512,256]{1,0:T(8,128)S(1)}, f32[512,256]{1,0:T(8,128)S(1)}, u32[]{:S(2)}, u32[]{:S(2)}) collective-permute-start(f32[512,256]{1,0:T(8,128)S(1)} %get-tuple-element.38), channel_id=1, source_target_pairs={{1,0},{0,1},{3,2},{2,3},{5,4},{4,5},{7,6},{6,7},{9,8},{8,9},{11,10... | collective-permute-start | bytes 1572872 | tf_op jit(solution)/shard_map/ppermute | solution.py:23
  117.3 1.5 %collective-permute-done.22 = f32[512,256]{1,0:T(8,128)S(1)} collective-permute-done((f32[512,256]{1,0:T(8,128)S(1)}, f32[512,256]{1,0:T(8,128)S(1)}, u32[]{:S(2)}, u32[]{:S(2)}) %collective-permute-start.22) | collective-permute-done | bytes 524320 | tf_op jit(solution)/shard_map/ppermute | solution.py:23
  118.9 1.3 collective-permute-start.23
  120.2 6.1 %apply.13 = (f32[512,256]{1,0:T(8,128)S(1)}, f32[512,256]{1,0:T(8,128)S(1)}) custom-call(s32[22]{0:T(128)S(1)} %compare_select_fusion.10.table.t, bf16[1024,1024]{1,0:T(8,128)(2,1)S(1)} %constant_dynamic-update-slice_fusion.orb.slab_ref, bf16[256,1280]{1,0:T(8,128)(2,1)S(1)} %collective-permute-done.16.refs_0_, ...), custom_call_target="tpu_custom_call" | custom-call | flops 838860800 | bytes 2621440 | tf_op jit(solution)/shard_map/apply/pallas_call | solution.py:97
  126.4 1.6 %collective-permute-done.23 = bf16[512,256]{1,0:T(8,128)(2,1)S(1)} collective-permute-done((bf16[512,256]{1,0:T(8,128)(2,1)S(1)}, bf16[512,256]{1,0:T(8,128)(2,1)S(1)}, u32[]{:S(2)}, u32[]{:S(2)}) %collective-permute-start.23) | collective-permute-done | bytes 262176 | tf_op jit(solution)/shard_map/ppermute | solution.py:23
  129.2 1.5 %collective-permute-done.24 = f32[512,256]{1,0:T(8,128)S(1)} collective-permute-done((f32[512,256]{1,0:T(8,128)S(1)}, f32[512,256]{1,0:T(8,128)S(1)}, u32[]{:S(2)}, u32[]{:S(2)}) %collective-permute-start.24) | collective-permute-done | bytes 524320 | tf_op jit(solution)/shard_map/ppermute | solution.py:23
  (75 shorter events, 12.2 us)
Async XLA Ops:
  0.0 8.3 %copy-start.4 = (s32[1,128]{1,0:T(1,128)S(1)}, s32[1,128]{1,0:T(1,128)}, u32[]{:S(2)}) copy-start(s32[1,128]{1,0:T(1,128)} %param.6) | copy-start | bytes 1540
  0.0 9.4 %collective-permute-start = (bf16[512,1024]{1,0:T(8,128)(2,1)}, bf16[512,1024]{1,0:T(8,128)(2,1)S(1)}, u32[]{:S(2)}, u32[]{:S(2)}) collective-permute-start(bf16[512,1024]{1,0:T(8,128)(2,1)} %param.4), channel_id=1, source_target_pairs={{1,0},{0,1},{3,2},{2,3},{5,4},{4,5},{7,6},{6,7},{9,8},{8,9},{11,10... | collective-permute-start | bytes 3145736 | tf_op jit(solution)/shard_map/ppermute | solution.py:23
  1.4 6.9 %collective-permute-start.2 = (bf16[512,256]{1,0:T(8,128)(2,1)}, bf16[512,256]{1,0:T(8,128)(2,1)}, u32[]{:S(2)}, u32[]{:S(2)}) collective-permute-start(bf16[512,256]{1,0:T(8,128)(2,1)} %param.5), channel_id=1, source_target_pairs={{1,0},{0,1},{3,2},{2,3},{5,4},{4,5},{7,6},{6,7},{9,8},{8,9},{11,10... | collective-permute-start | bytes 786440 | tf_op jit(solution)/shard_map/ppermute | solution.py:23
  1.4 6.9 %collective-permute-start.1 = (s32[1,128]{1,0:T(1,128)}, s32[1,128]{1,0:T(1,128)S(1)}, u32[]{:S(2)}, u32[]{:S(2)}) collective-permute-start(s32[1,128]{1,0:T(1,128)} %param.6), channel_id=1, source_target_pairs={{2,0},{0,2},{3,1},{1,3},{6,4},{4,6},{7,5},{5,7},{10,8},{8,10},{11,... | collective-permute-start | bytes 1544 | tf_op jit(solution)/shard_map/ppermute | solution.py:23
  7.0 11.7 %collective-permute-start.3 = (bf16[192,1024]{1,0:T(8,128)(2,1)}, bf16[192,1024]{1,0:T(8,128)(2,1)S(1)}, u32[]{:S(2)}, u32[]{:S(2)}) collective-permute-start(bf16[192,1024]{1,0:T(8,128)(2,1)} %slice.52), channel_id=1, source_target_pairs={{2,0},{0,2},{3,1},{1,3},{6,4},{4,6},{7,5},{5,7},{10,8},{8,10},{11,... | collective-permute-start | bytes 1179656 | tf_op jit(solution)/shard_map/ppermute | solution.py:23
  9.5 19.7 %copy-start = (bf16[512,1024]{1,0:T(8,128)(2,1)S(1)}, bf16[512,1024]{1,0:T(8,128)(2,1)}, u32[]{:S(2)}) copy-start(bf16[512,1024]{1,0:T(8,128)(2,1)} %param.4) | copy-start | bytes 3145732
  18.6 9.1 %collective-permute-start.4 = (bf16[128,1280]{1,0:T(8,128)(2,1)S(1)}, bf16[128,1280]{1,0:T(8,128)(2,1)S(1)}, u32[]{:S(2)}, u32[]{:S(2)}) collective-permute-start(bf16[128,1280]{1,0:T(8,128)(2,1)S(1)} %get-tuple-element.26), channel_id=1, source_target_pairs={{2,0},{0,2},{3,1},{1,3},{6,4},{4,6},{7,5},{5,7},{10,8},{8,10},{11,... | collective-permute-start | bytes 983048 | tf_op jit(solution)/shard_map/ppermute | solution.py:23
  27.8 6.8 %collective-permute-start.5 = (bf16[128,1280]{1,0:T(8,128)(2,1)S(1)}, bf16[128,1280]{1,0:T(8,128)(2,1)S(1)}, u32[]{:S(2)}, u32[]{:S(2)}) collective-permute-start(bf16[128,1280]{1,0:T(8,128)(2,1)S(1)} %add.68), channel_id=1, source_target_pairs={{4,0},{0,4},{5,1},{1,5},{6,2},{2,6},{7,3},{3,7},{12,8},{8,12},{13,... | collective-permute-start | bytes 983048 | tf_op jit(solution)/shard_map/ppermute | solution.py:23
  34.6 13.6 %collective-permute-start.14 = (bf16[320,1024]{1,0:T(8,128)(2,1)S(1)}, bf16[320,1024]{1,0:T(8,128)(2,1)S(1)}, u32[]{:S(2)}, u32[]{:S(2)}) collective-permute-start(bf16[320,1024]{1,0:T(8,128)(2,1)S(1)} %slice.57), channel_id=1, source_target_pairs={{2,0},{0,2},{3,1},{1,3},{6,4},{4,6},{7,5},{5,7},{10,8},{8,10},{11,... | collective-permute-start | bytes 1966088 | tf_op jit(solution)/shard_map/ppermute | solution.py:23
  35.6 17.7 %collective-permute-start.9 = (bf16[256,1280]{1,0:T(8,128)(2,1)S(1)}, bf16[256,1280]{1,0:T(8,128)(2,1)S(1)}, u32[]{:S(2)}, u32[]{:S(2)}) collective-permute-start(bf16[256,1280]{1,0:T(8,128)(2,1)S(1)} %pad_maximum_fusion.5.refs_0_), channel_id=1, source_target_pairs={{96,0},{0,32},{32,64},{64,96},{97,1},{1,33},{33,65},{65,97},{98,2}... | collective-permute-start | bytes 1966088 | tf_op jit(solution)/shard_map/ppermute | solution.py:23
  37.0 16.4 %collective-permute-start.7 = (bf16[256,1280]{1,0:T(8,128)(2,1)S(1)}, bf16[256,1280]{1,0:T(8,128)(2,1)S(1)}, u32[]{:S(2)}, u32[]{:S(2)}) collective-permute-start(bf16[256,1280]{1,0:T(8,128)(2,1)S(1)} %pad_maximum_fusion.5.refs_0_), channel_id=1, source_target_pairs={{8,0},{16,8},{24,16},{0,24},{9,1},{17,9},{25,17},{1,25},{10,2},{18... | collective-permute-start | bytes 1966088 | tf_op jit(solution)/shard_map/ppermute | solution.py:23
  39.5 15.4 %collective-permute-start.6 = (bf16[256,1280]{1,0:T(8,128)(2,1)S(1)}, bf16[256,1280]{1,0:T(8,128)(2,1)S(1)}, u32[]{:S(2)}, u32[]{:S(2)}) collective-permute-start(bf16[256,1280]{1,0:T(8,128)(2,1)S(1)} %pad_maximum_fusion.5.refs_0_), channel_id=1, source_target_pairs={{32,0},{64,32},{96,64},{0,96},{33,1},{65,33},{97,65},{1,97},{34,2}... | collective-permute-start | bytes 1966088 | tf_op jit(solution)/shard_map/ppermute | solution.py:23
  41.0 13.9 %collective-permute-start.10 = (bf16[256,1280]{1,0:T(8,128)(2,1)S(1)}, bf16[256,1280]{1,0:T(8,128)(2,1)S(1)}, u32[]{:S(2)}, u32[]{:S(2)}) collective-permute-start(bf16[256,1280]{1,0:T(8,128)(2,1)S(1)} %pad_maximum_fusion.5.refs_0_), channel_id=1, source_target_pairs={{24,0},{0,8},{8,16},{16,24},{25,1},{1,9},{9,17},{17,25},{26,2},{2,... | collective-permute-start | bytes 1966088 | tf_op jit(solution)/shard_map/ppermute | solution.py:23
  48.2 17.5 %collective-permute-start.15 = (bf16[512,1024]{1,0:T(8,128)(2,1)S(1)}, bf16[512,1024]{1,0:T(8,128)(2,1)S(1)}, u32[]{:S(2)}, u32[]{:S(2)}) collective-permute-start(bf16[512,1024]{1,0:T(8,128)(2,1)S(1)} %pad_maximum_fusion), channel_id=1, source_target_pairs={{1,0},{0,1},{3,2},{2,3},{5,4},{4,5},{7,6},{6,7},{9,8},{8,9},{11,10... | collective-permute-start | bytes 3145736 | tf_op jit(solution)/shard_map/ppermute | solution.py:23
  53.5 23.7 %collective-permute-start.13 = (bf16[384,1280]{1,0:T(8,128)(2,1)S(1)}, bf16[384,1280]{1,0:T(8,128)(2,1)S(1)}, u32[]{:S(2)}, u32[]{:S(2)}) collective-permute-start(bf16[384,1280]{1,0:T(8,128)(2,1)S(1)} %pad_maximum_fusion.4), channel_id=1, source_target_pairs={{96,0},{0,32},{32,64},{64,96},{97,1},{1,33},{33,65},{65,97},{98,2}... | collective-permute-start | bytes 2949128 | tf_op jit(solution)/shard_map/ppermute | solution.py:23
  55.0 22.2 %collective-permute-start.12 = (bf16[384,1280]{1,0:T(8,128)(2,1)S(1)}, bf16[384,1280]{1,0:T(8,128)(2,1)S(1)}, u32[]{:S(2)}, u32[]{:S(2)}) collective-permute-start(bf16[384,1280]{1,0:T(8,128)(2,1)S(1)} %pad_maximum_fusion.3), channel_id=1, source_target_pairs={{32,0},{64,32},{96,64},{0,96},{33,1},{65,33},{97,65},{1,97},{34,2}... | collective-permute-start | bytes 2949128 | tf_op jit(solution)/shard_map/ppermute | solution.py:23
  56.6 20.6 %collective-permute-start.11 = (bf16[384,1280]{1,0:T(8,128)(2,1)S(1)}, bf16[384,1280]{1,0:T(8,128)(2,1)S(1)}, u32[]{:S(2)}, u32[]{:S(2)}) collective-permute-start(bf16[384,1280]{1,0:T(8,128)(2,1)S(1)} %pad_maximum_fusion.2), channel_id=1, source_target_pairs={{24,0},{0,8},{8,16},{16,24},{25,1},{1,9},{9,17},{17,25},{26,2},{2,... | collective-permute-start | bytes 2949128 | tf_op jit(solution)/shard_map/ppermute | solution.py:23
  58.0 19.9 %collective-permute-start.8 = (bf16[384,1280]{1,0:T(8,128)(2,1)S(1)}, bf16[384,1280]{1,0:T(8,128)(2,1)S(1)}, u32[]{:S(2)}, u32[]{:S(2)}) collective-permute-start(bf16[384,1280]{1,0:T(8,128)(2,1)S(1)} %pad_maximum_fusion.1), channel_id=1, source_target_pairs={{8,0},{16,8},{24,16},{0,24},{9,1},{17,9},{25,17},{1,25},{10,2},{18... | collective-permute-start | bytes 2949128 | tf_op jit(solution)/shard_map/ppermute | solution.py:23
  77.2 6.2 %copy-start.3 = (bf16[384,1280]{1,0:T(8,128)(2,1)}, bf16[384,1280]{1,0:T(8,128)(2,1)S(1)}, u32[]{:S(2)}) copy-start(bf16[384,1280]{1,0:T(8,128)(2,1)S(1)} %collective-permute-done.12) | copy-start | bytes 2949124
  77.2 6.2 %copy-start.2 = (bf16[384,1280]{1,0:T(8,128)(2,1)}, bf16[384,1280]{1,0:T(8,128)(2,1)S(1)}, u32[]{:S(2)}) copy-start(bf16[384,1280]{1,0:T(8,128)(2,1)S(1)} %collective-permute-done.11) | copy-start | bytes 2949124
  77.8 5.5 %copy-start.1 = (bf16[384,1280]{1,0:T(8,128)(2,1)}, bf16[384,1280]{1,0:T(8,128)(2,1)S(1)}, u32[]{:S(2)}) copy-start(bf16[384,1280]{1,0:T(8,128)(2,1)S(1)} %collective-permute-done.8) | copy-start | bytes 2949124
  77.9 20.6 %collective-permute-start.16 = (bf16[256,1280]{1,0:T(8,128)(2,1)S(1)}, bf16[256,1280]{1,0:T(8,128)(2,1)S(1)}, u32[]{:S(2)}, u32[]{:S(2)}) collective-permute-start(bf16[256,1280]{1,0:T(8,128)(2,1)S(1)} %slice.58.refs_0_), channel_id=1, source_target_pairs={{8,0},{16,8},{24,16},{0,24},{9,1},{17,9},{25,17},{1,25},{10,2},{18... | collective-permute-start | bytes 1966088 | tf_op jit(solution)/shard_map/ppermute | solution.py:23
  80.2 18.4 %collective-permute-start.17 = (bf16[256,1280]{1,0:T(8,128)(2,1)S(1)}, bf16[256,1280]{1,0:T(8,128)(2,1)S(1)}, u32[]{:S(2)}, u32[]{:S(2)}) collective-permute-start(bf16[256,1280]{1,0:T(8,128)(2,1)S(1)} %slice.59.refs_1_), channel_id=1, source_target_pairs={{24,0},{0,8},{8,16},{16,24},{25,1},{1,9},{9,17},{17,25},{26,2},{2,... | collective-permute-start | bytes 1966088 | tf_op jit(solution)/shard_map/ppermute | solution.py:23
  80.9 17.7 %collective-permute-start.18 = (bf16[256,1280]{1,0:T(8,128)(2,1)S(1)}, bf16[256,1280]{1,0:T(8,128)(2,1)S(1)}, u32[]{:S(2)}, u32[]{:S(2)}) collective-permute-start(bf16[256,1280]{1,0:T(8,128)(2,1)S(1)} %slice.58.refs_0_), channel_id=1, source_target_pairs={{32,0},{64,32},{96,64},{0,96},{33,1},{65,33},{97,65},{1,97},{34,2}... | collective-permute-start | bytes 1966088 | tf_op jit(solution)/shard_map/ppermute | solution.py:23
  83.4 15.2 %collective-permute-start.19 = (bf16[256,1280]{1,0:T(8,128)(2,1)S(1)}, bf16[256,1280]{1,0:T(8,128)(2,1)S(1)}, u32[]{:S(2)}, u32[]{:S(2)}) collective-permute-start(bf16[256,1280]{1,0:T(8,128)(2,1)S(1)} %slice.59.refs_1_), channel_id=1, source_target_pairs={{96,0},{0,32},{32,64},{64,96},{97,1},{1,33},{33,65},{65,97},{98,2}... | collective-permute-start | bytes 1966088 | tf_op jit(solution)/shard_map/ppermute | solution.py:23
  83.5 1.1 slice-start.1
  83.5 1.2 slice-start.2
  98.6 10.2 %collective-permute-start.20 = (bf16[128,1280]{1,0:T(8,128)(2,1)S(1)}, bf16[128,1280]{1,0:T(8,128)(2,1)S(1)}, u32[]{:S(2)}, u32[]{:S(2)}) collective-permute-start(bf16[128,1280]{1,0:T(8,128)(2,1)S(1)} %slice.66), channel_id=1, source_target_pairs={{8,0},{16,8},{24,16},{0,24},{9,1},{17,9},{25,17},{1,25},{10,2},{18... | collective-permute-start | bytes 983048 | tf_op jit(solution)/shard_map/ppermute | solution.py:23
  100.8 8.0 %collective-permute-start.21 = (bf16[128,1280]{1,0:T(8,128)(2,1)S(1)}, bf16[128,1280]{1,0:T(8,128)(2,1)S(1)}, u32[]{:S(2)}, u32[]{:S(2)}) collective-permute-start(bf16[128,1280]{1,0:T(8,128)(2,1)S(1)} %slice.67), channel_id=1, source_target_pairs={{32,0},{64,32},{96,64},{0,96},{33,1},{65,33},{97,65},{1,97},{34,2}... | collective-permute-start | bytes 983048 | tf_op jit(solution)/shard_map/ppermute | solution.py:23
  111.7 7.1 %collective-permute-start.22 = (f32[512,256]{1,0:T(8,128)S(1)}, f32[512,256]{1,0:T(8,128)S(1)}, u32[]{:S(2)}, u32[]{:S(2)}) collective-permute-start(f32[512,256]{1,0:T(8,128)S(1)} %get-tuple-element.38), channel_id=1, source_target_pairs={{1,0},{0,1},{3,2},{2,3},{5,4},{4,5},{7,6},{6,7},{9,8},{8,9},{11,10... | collective-permute-start | bytes 1572872 | tf_op jit(solution)/shard_map/ppermute | solution.py:23
  118.9 9.1 %collective-permute-start.23 = (bf16[512,256]{1,0:T(8,128)(2,1)S(1)}, bf16[512,256]{1,0:T(8,128)(2,1)S(1)}, u32[]{:S(2)}, u32[]{:S(2)}) collective-permute-start(bf16[512,256]{1,0:T(8,128)(2,1)S(1)} %add_convert_fusion), channel_id=1, source_target_pairs={{2,0},{0,2},{3,1},{1,3},{6,4},{4,6},{7,5},{5,7},{10,8},{8,10},{11,... | collective-permute-start | bytes 786440 | tf_op jit(solution)/shard_map/ppermute | solution.py:23
  128.0 2.7 %collective-permute-start.24 = (f32[512,256]{1,0:T(8,128)S(1)}, f32[512,256]{1,0:T(8,128)S(1)}, u32[]{:S(2)}, u32[]{:S(2)}) collective-permute-start(f32[512,256]{1,0:T(8,128)S(1)} %get-tuple-element.42), channel_id=1, source_target_pairs={{1,0},{0,1},{3,2},{2,3},{5,4},{4,5},{7,6},{6,7},{9,8},{8,9},{11,10... | collective-permute-start | bytes 1572872 | tf_op jit(solution)/shard_map/ppermute | solution.py:23
  (1 other events, 1.0 us)

commit v6 on v5

--- a/solution.py
+++ b/solution.py
@@ -133,9 +133,11 @@
     near_tgt = jnp.concatenate([targets, sib_tgt], axis=0)
     ids = jnp.concatenate([points, far_points], axis=0)
     mine, theirs = pick(table, ids, near_slab, near_tgt)
-    early = own_rows * 3 // 8
-    far_early = take_from(orbitals[:early], "zh", 1)
-    block = mine + take_from(after(theirs, far_early), "zh", 1)
+    block = mine + take_from(theirs, "zh", 1)
+    lower = table[SIDE:].reshape(1, 1) == 0
+
+    def in_order(own, other):
+        return jnp.concatenate([jnp.where(lower, own, other), jnp.where(lower, other, own)], axis=0)
 
     def near_apply(parts, ats, total, last=False):
         return apply_parts(near_slab, parts, potential, table, NEAR, ORDER.index(ats[0]), len(ats), total, last)
@@ -143,14 +145,11 @@
     def far_apply(parts, ats, total, last=False):
         return apply_parts(far_slab, parts, potential, table, FAR, ORDER.index(ats[0]), len(ats), total, last)
 
+    own = {at: take_from(block, axis, side) for at, axis, side in NEXT}
     other = take_from(block, "zl", 1)
-    lower = table[SIDE:].reshape(1, 1) == 0
-    low, high = jnp.where(lower, block, other), jnp.where(lower, other, block)
-    pair = {(0, 0): jnp.concatenate([low, high], axis=0)}
-    far_late = take_from(after(orbitals[early:], other), "zh", 1)
-    for at, axis, side in NEXT:
-        pair[at] = take_from(pair[0, 0], axis, side)
-    far_orb = jnp.concatenate([far_early, far_late], axis=0)
+    far_slab = take_from(after(near_slab, *own.values()), "zh", 1)
+    pair = {at: in_order(own[at], take_from(other, axis, side)) for at, axis, side in NEXT}
+    pair[0, 0] = in_order(block, other)
 
     def joined(whole, half):
         return jnp.concatenate([pair[whole], half], axis=0)
@@ -159,13 +158,10 @@
     from_left = take_from(joined((3, 0), pair[0, 3][count:]), "x", -1)
     from_up = take_from(joined((0, 3), pair[1, 0][:count]), "y", 1)
     from_down = take_from(joined((0, 1), pair[3, 0][count:]), "y", -1)
-    first = tuple(at for at, _, _ in NEXT)
-    near = near_apply([pair[0, 0]] + [pair[at] for at in first], ((0, 0),) + first, None)
-    far_sib = take_from(far_orb, "c", 1)
-    far_slab = jnp.concatenate([far_orb, far_sib], axis=0)
-    far = far_apply([pair[0, 0]] + [pair[at] for at in first], ((0, 0),) + first, None)
+    first = ((0, 0), *(at for at, _, _ in NEXT))
+    near = near_apply([pair[at] for at in first], first, None)
     from_right, from_left, from_up, from_down = lax.optimization_barrier(
-        (from_right, from_left, from_up, from_down, near, far)
+        (from_right, from_left, from_up, from_down, near)
     )[:4]
     both = 2 * count
     pair[1, 1], pair[3, 3] = from_right[:both], from_left[:both]
@@ -178,18 +174,20 @@
     pair[2, 1] = take_from(pair[1, 1], "y", 1)
     pair[2, 3] = take_from(pair[3, 3], "y", -1)
     second = ((1, 1), (3, 3), (1, 3), (3, 1), (0, 2), (2, 0))
+    far = far_apply([pair[at] for at in first], first, None)
     far = far_apply([pair[at] for at in second], second, far)
-    near = near_apply([pair[at] for at in second], second, after(near, far))
 
     third = ((1, 2), (3, 2), (2, 1), (2, 3))
-    ready = lax.optimization_barrier((*(pair[at] for at in third), near, far))[:4]
+    ready = lax.optimization_barrier((*(pair[at] for at in third), far))[:4]
     pair.update(zip(third, ready))
     last = [take_from(pair[2, 1][:count], "x", 1), take_from(pair[1, 2][count:], "y", 1)]
-    far = far_apply([pair[at] for at in third], third, far)
-    kept, sent = far_apply(last, [(2, 2)], far, True)
+    near = near_apply([pair[at] for at in second], second, after(near, far))
+    third += ((2, 2),)
+    last = [pair[at] for at in third[:4]] + last
+    kept, sent = far_apply(last, third, after(far, near), True)
     far = (kept + take_from(sent, "c", 1)).astype(jnp.bfloat16)
     away = take_from(far, "zh", 1)
-    kept, sent = near_apply([pair[at] for at in third] + last, third + ((2, 2),), after(near, far), True)
+    kept, sent = near_apply(last, third, after(near, far), True)
     near = kept + take_from(after(sent, away), "c", 1)
     return (-(near + away.astype(jnp.float32))).astype(jnp.bfloat16)
 

time: 132 us -> 127 us (0.962)
  local copies, waits for them, and re-layouts: 5.32 us -> 3.05 us
  Pallas kernels: 41.8 us -> 39.7 us
    pallas_call x7 -> x6, Pallas kernels: 40.3 us -> 38.3 us  [apply_parts(): pl.pallas_call(body, out_shape=(half, half) if last else jax.ShapeDtypeSt...]
    slice x6 -> x0, local copies, waits for them, and re-layouts: 1.9 us -> none  [the longest x1 1.77 us: local(): far_early = take_from(orbitals[:early], 'zh', 1)]
    ppermute x25 -> x27, starting transfers between devices: 41.8 us -> 40.7 us  [take_from(): return lax.ppermute(value, axis, [((i + side) % n, i) for i in range(n)])]
    ppermute x25 -> x27, waiting for transfers between devices: 38.9 us -> 39.5 us  [take_from(): return lax.ppermute(value, axis, [((i + side) % n, i) for i in range(n)])]
  transfers between devices with their start and end apart: 25 -> 27, of which waited for: 9 -> 12; matrix products, arithmetic and copies ran while one was open for 4% -> 3% of each run, Pallas kernels for 30% -> 25%
where the time goes in v6:
time: 127 us
  starting transfers between devices  40.7 us (32%)
  Pallas kernels  39.7 us (31%)
  waiting for transfers between devices  39.5 us (31%)
  local copies, waits for them, and re-layouts  3.05 us (2%)
  other arithmetic  2.91 us (2%)
    ppermute x27, starting transfers between devices, take_from(): return lax.ppermute(value, axis, [((i + side) % n, i) for i in range(n)])  40.7 us
    ppermute x27, waiting for transfers between devices, take_from(): return lax.ppermute(value, axis, [((i + side) % n, i) for i in range(n)])  39.5 us
    pallas_call x6, Pallas kernels, apply_parts(): pl.pallas_call(body, out_shape=(half, half) if last else jax.ShapeDtypeSt...  38.3 us
  transfers between devices with their start and end apart: 27, of which 12 were waited for; matrix products, arithmetic and copies ran while one was open for 3% of the time, Pallas kernels for 25%

profile of v6, /device:TPU:1, one launch (start us, length us, event | category | flops | bytes accessed | tf_op | source)
XLA Modules:
  0.0 127.0 jit_solution(8337175502729275722)
XLA Ops:
  0.0 1.4 %collective-permute-start = (bf16[512,1024]{1,0:T(8,128)(2,1)}, bf16[512,1024]{1,0:T(8,128)(2,1)S(1)}, u32[]{:S(2)}, u32[]{:S(2)}) collective-permute-start(bf16[512,1024]{1,0:T(8,128)(2,1)} %param.4), channel_id=1, source_target_pairs={{1,0},{0,1},{3,2},{2,3},{5,4},{4,5},{7,6},{6,7},{9,8},{8,9},{11,10... | collective-permute-start | bytes 3145736 | tf_op jit(solution)/shard_map/ppermute | solution.py:23
  1.4 3.8 %collective-permute-start.1 = (s32[1,128]{1,0:T(1,128)}, s32[1,128]{1,0:T(1,128)S(1)}, u32[]{:S(2)}, u32[]{:S(2)}) collective-permute-start(s32[1,128]{1,0:T(1,128)} %param.6), channel_id=1, source_target_pairs={{2,0},{0,2},{3,1},{1,3},{6,4},{4,6},{7,5},{5,7},{10,8},{8,10},{11,... | collective-permute-start | bytes 1544 | tf_op jit(solution)/shard_map/ppermute | solution.py:23
  7.7 1.5 %pick.1 = (bf16[128,1280]{1,0:T(8,128)(2,1)S(1)}, bf16[128,1280]{1,0:T(8,128)(2,1)S(1)}) custom-call(s32[22]{0:T(128)S(1)} %compare_select_fusion.10.table.t, s32[2,128]{1,0:T(2,128)S(1)} %pad_add_fusion.ids, bf16[1024,1024]{1,0:T(8,128)(2,1)S(1)} %constant_dynamic-update-slice_fusion.orb.slab_ref, bf16[1024,256]{1,0:T(8,128)(2,1)S(1)} %pad_maximum_fusion.11.tgt), custom_call_target="tpu_custom_call" | custom-call | tf_op jit(solution)/shard_map/pick/pallas_call | solution.py:46
  9.2 2.7 %collective-permute-start.3 = (bf16[128,1280]{1,0:T(8,128)(2,1)S(1)}, bf16[128,1280]{1,0:T(8,128)(2,1)S(1)}, u32[]{:S(2)}, u32[]{:S(2)}) collective-permute-start(bf16[128,1280]{1,0:T(8,128)(2,1)S(1)} %get-tuple-element.25), channel_id=1, source_target_pairs={{2,0},{0,2},{3,1},{1,3},{6,4},{4,6},{7,5},{5,7},{10,8},{8,10},{11,... | collective-permute-start | bytes 983048 | tf_op jit(solution)/shard_map/ppermute | solution.py:23
  11.9 7.1 %collective-permute-done.3 = bf16[128,1280]{1,0:T(8,128)(2,1)S(1)} collective-permute-done((bf16[128,1280]{1,0:T(8,128)(2,1)S(1)}, bf16[128,1280]{1,0:T(8,128)(2,1)S(1)}, u32[]{:S(2)}, u32[]{:S(2)}) %collective-permute-start.3) | collective-permute-done | bytes 327712 | tf_op jit(solution)/shard_map/ppermute | solution.py:23
  20.5 2.7 %collective-permute-start.4 = (bf16[128,1280]{1,0:T(8,128)(2,1)S(1)}, bf16[128,1280]{1,0:T(8,128)(2,1)S(1)}, u32[]{:S(2)}, u32[]{:S(2)}) collective-permute-start(bf16[128,1280]{1,0:T(8,128)(2,1)S(1)} %add.68), channel_id=1, source_target_pairs={{32,0},{64,32},{96,64},{0,96},{33,1},{65,33},{97,65},{1,97},{34,2}... | collective-permute-start | bytes 983048 | tf_op jit(solution)/shard_map/ppermute | solution.py:23
  23.3 1.5 %collective-permute-start.7 = (bf16[128,1280]{1,0:T(8,128)(2,1)S(1)}, bf16[128,1280]{1,0:T(8,128)(2,1)S(1)}, u32[]{:S(2)}, u32[]{:S(2)}) collective-permute-start(bf16[128,1280]{1,0:T(8,128)(2,1)S(1)} %add.68), channel_id=1, source_target_pairs={{8,0},{16,8},{24,16},{0,24},{9,1},{17,9},{25,17},{1,25},{10,2},{18... | collective-permute-start | bytes 983048 | tf_op jit(solution)/shard_map/ppermute | solution.py:23
  24.7 1.7 %collective-permute-done.5 = bf16[128,1280]{1,0:T(8,128)(2,1)S(1)} collective-permute-done((bf16[128,1280]{1,0:T(8,128)(2,1)S(1)}, bf16[128,1280]{1,0:T(8,128)(2,1)S(1)}, u32[]{:S(2)}, u32[]{:S(2)}) %collective-permute-start.5) | collective-permute-done | bytes 327712 | tf_op jit(solution)/shard_map/ppermute | solution.py:23
  29.5 2.4 %collective-permute-done.10 = bf16[128,1280]{1,0:T(8,128)(2,1)S(1)} collective-permute-done((bf16[128,1280]{1,0:T(8,128)(2,1)S(1)}, bf16[128,1280]{1,0:T(8,128)(2,1)S(1)}, u32[]{:S(2)}, u32[]{:S(2)}) %collective-permute-start.10) | collective-permute-done | bytes 327712 | tf_op jit(solution)/shard_map/ppermute | solution.py:23
  31.8 3.2 %collective-permute-start.21 = (bf16[1024,1024]{1,0:T(8,128)(2,1)S(1)}, bf16[1024,1024]{1,0:T(8,128)(2,1)S(1)}, u32[]{:S(2)}, u32[]{:S(2)}) collective-permute-start(bf16[1024,1024]{1,0:T(8,128)(2,1)S(1)} %constant_dynamic-update-slice_fusion.orb.slab_ref), channel_id=1, source_target_pairs={{2,0},{0,2},{3,1},{1,3},{6,4},{4,6},{7,5},{5,7},{10,8},{8,10},{11,... | collective-permute-start | bytes 6291464 | tf_op jit(solution)/shard_map/ppermute | solution.py:23
  35.1 1.6 %collective-permute-start.8 = (bf16[128,1280]{1,0:T(8,128)(2,1)S(1)}, bf16[128,1280]{1,0:T(8,128)(2,1)S(1)}, u32[]{:S(2)}, u32[]{:S(2)}) collective-permute-start(bf16[128,1280]{1,0:T(8,128)(2,1)S(1)} %collective-permute-done.5), channel_id=1, source_target_pairs={{8,0},{16,8},{24,16},{0,24},{9,1},{17,9},{25,17},{1,25},{10,2},{18... | collective-permute-start | bytes 983048 | tf_op jit(solution)/shard_map/ppermute | solution.py:23
  36.7 1.5 %collective-permute-start.11 = (bf16[128,1280]{1,0:T(8,128)(2,1)S(1)}, bf16[128,1280]{1,0:T(8,128)(2,1)S(1)}, u32[]{:S(2)}, u32[]{:S(2)}) collective-permute-start(bf16[128,1280]{1,0:T(8,128)(2,1)S(1)} %collective-permute-done.5), channel_id=1, source_target_pairs={{96,0},{0,32},{32,64},{64,96},{97,1},{1,33},{33,65},{65,97},{98,2}... | collective-permute-start | bytes 983048 | tf_op jit(solution)/shard_map/ppermute | solution.py:23
  38.2 2.8 %collective-permute-done.6 = bf16[128,1280]{1,0:T(8,128)(2,1)S(1)} collective-permute-done((bf16[128,1280]{1,0:T(8,128)(2,1)S(1)}, bf16[128,1280]{1,0:T(8,128)(2,1)S(1)}, u32[]{:S(2)}, u32[]{:S(2)}) %collective-permute-start.6) | collective-permute-done | bytes 327712 | tf_op jit(solution)/shard_map/ppermute | solution.py:23
  41.1 3.0 %collective-permute-done.11 = bf16[128,1280]{1,0:T(8,128)(2,1)S(1)} collective-permute-done((bf16[128,1280]{1,0:T(8,128)(2,1)S(1)}, bf16[128,1280]{1,0:T(8,128)(2,1)S(1)}, u32[]{:S(2)}, u32[]{:S(2)}) %collective-permute-start.11) | collective-permute-done | bytes 327712 | tf_op jit(solution)/shard_map/ppermute | solution.py:23
  44.7 1.5 %collective-permute-start.16 = (bf16[384,1280]{1,0:T(8,128)(2,1)S(1)}, bf16[384,1280]{1,0:T(8,128)(2,1)S(1)}, u32[]{:S(2)}, u32[]{:S(2)}) collective-permute-start(bf16[384,1280]{1,0:T(8,128)(2,1)S(1)} %get-tuple-element.53), channel_id=1, source_target_pairs={{96,0},{0,32},{32,64},{64,96},{97,1},{1,33},{33,65},{65,97},{98,2}... | collective-permute-start | bytes 2949128 | tf_op jit(solution)/shard_map/ppermute | solution.py:23
  46.2 2.6 %collective-permute-start.9 = (bf16[384,1280]{1,0:T(8,128)(2,1)S(1)}, bf16[384,1280]{1,0:T(8,128)(2,1)S(1)}, u32[]{:S(2)}, u32[]{:S(2)}) collective-permute-start(bf16[384,1280]{1,0:T(8,128)(2,1)S(1)} %get-tuple-element.54), channel_id=1, source_target_pairs={{8,0},{16,8},{24,16},{0,24},{9,1},{17,9},{25,17},{1,25},{10,2},{18... | collective-permute-start | bytes 2949128 | tf_op jit(solution)/shard_map/ppermute | solution.py:23
  49.0 6.1 %apply.6.refs_12_ = f32[1024,256]{1,0:T(8,128)S(1)} custom-call(s32[22]{0:T(128)S(1)} %compare_select_fusion.10.table.t, bf16[1024,1024]{1,0:T(8,128)(2,1)S(1)} %constant_dynamic-update-slice_fusion.orb.slab_ref, bf16[256,1280]{1,0:T(8,128)(2,1)S(1)} %get-tuple-element.57.refs_0_, bf16[256,1280]{1,0:T(8,128)(2,1)S(1)} %get-tuple-element.58.refs_1_, ...), custom_call_target="tpu_custom_call" | custom-call | flops 838860800 | bytes 2621440 | tf_op jit(solution)/shard_map/apply/pallas_call | solution.py:97
  55.1 7.2 %collective-permute-done.14 = bf16[384,1280]{1,0:T(8,128)(2,1)S(1)} collective-permute-done((bf16[384,1280]{1,0:T(8,128)(2,1)S(1)}, bf16[384,1280]{1,0:T(8,128)(2,1)S(1)}, u32[]{:S(2)}, u32[]{:S(2)}) %collective-permute-start.14) | collective-permute-done | bytes 983072 | tf_op jit(solution)/shard_map/ppermute | solution.py:23
  62.4 1.3 %collective-permute-done.16 = bf16[384,1280]{1,0:T(8,128)(2,1)S(1)} collective-permute-done((bf16[384,1280]{1,0:T(8,128)(2,1)S(1)}, bf16[384,1280]{1,0:T(8,128)(2,1)S(1)}, u32[]{:S(2)}, u32[]{:S(2)}) %collective-permute-start.16) | collective-permute-done | bytes 983072 | tf_op jit(solution)/shard_map/ppermute | solution.py:23
  64.8 2.0 %collective-permute-start.17 = (bf16[256,1280]{1,0:T(8,128)(2,1)S(1)}, bf16[256,1280]{1,0:T(8,128)(2,1)S(1)}, u32[]{:S(2)}, u32[]{:S(2)}) collective-permute-start(bf16[256,1280]{1,0:T(8,128)(2,1)S(1)} %slice.34.refs_0_), channel_id=1, source_target_pairs={{8,0},{16,8},{24,16},{0,24},{9,1},{17,9},{25,17},{1,25},{10,2},{18... | collective-permute-start | bytes 1966088 | tf_op jit(solution)/shard_map/ppermute | solution.py:23
  66.9 1.5 %collective-permute-start.19 = (bf16[256,1280]{1,0:T(8,128)(2,1)S(1)}, bf16[256,1280]{1,0:T(8,128)(2,1)S(1)}, u32[]{:S(2)}, u32[]{:S(2)}) collective-permute-start(bf16[256,1280]{1,0:T(8,128)(2,1)S(1)} %slice.34.refs_0_), channel_id=1, source_target_pairs={{32,0},{64,32},{96,64},{0,96},{33,1},{65,33},{97,65},{1,97},{34,2}... | collective-permute-start | bytes 1966088 | tf_op jit(solution)/shard_map/ppermute | solution.py:23
  68.5 7.8 %collective-permute-done.21.slab_ref = bf16[1024,1024]{1,0:T(8,128)(2,1)S(1)} collective-permute-done((bf16[1024,1024]{1,0:T(8,128)(2,1)S(1)}, bf16[1024,1024]{1,0:T(8,128)(2,1)S(1)}, u32[]{:S(2)}, u32[]{:S(2)}) %collective-permute-start.21) | collective-permute-done | bytes 2097184 | tf_op jit(solution)/shard_map/ppermute | solution.py:23
  76.2 6.1 %apply.7.refs_12_ = f32[1024,256]{1,0:T(8,128)S(1)} custom-call(s32[22]{0:T(128)S(1)} %compare_select_fusion.10.table.t, bf16[1024,1024]{1,0:T(8,128)(2,1)S(1)} %collective-permute-done.21.slab_ref, bf16[256,1280]{1,0:T(8,128)(2,1)S(1)} %get-tuple-element.57.refs_0_, bf16[256,1280]{1,0:T(8,128)(2,1)S(1)} %get-tuple-element.58.refs_1_, ...), custom_call_target="tpu_custom_call" | custom-call | flops 838860800 | bytes 2621440 | tf_op jit(solution)/shard_map/apply/pallas_call | solution.py:97
  82.3 6.9 %apply.8.refs_11_ = f32[1024,256]{1,0:T(8,128)S(1)} custom-call(s32[22]{0:T(128)S(1)} %compare_select_fusion.10.table.t, bf16[1024,1024]{1,0:T(8,128)(2,1)S(1)} %collective-permute-done.21.slab_ref, bf16[256,1280]{1,0:T(8,128)(2,1)S(1)} %slice.34.refs_0_, bf16[256,1280]{1,0:T(8,128)(2,1)S(1)} %slice.35.refs_1_, ...), custom_call_target="tpu_custom_call", output_to_operand_aliasing={{}: (14, {})} | custom-call | flops 1006632960 | bytes 3145728 | tf_op jit(solution)/shard_map/apply/pallas_call | solution.py:97
  89.3 1.9 %collective-permute-start.22 = (bf16[128,1280]{1,0:T(8,128)(2,1)S(1)}, bf16[128,1280]{1,0:T(8,128)(2,1)S(1)}, u32[]{:S(2)}, u32[]{:S(2)}) collective-permute-start(bf16[128,1280]{1,0:T(8,128)(2,1)S(1)} %slice.42), channel_id=1, source_target_pairs={{8,0},{16,8},{24,16},{0,24},{9,1},{17,9},{25,17},{1,25},{10,2},{18... | collective-permute-start | bytes 983048 | tf_op jit(solution)/shard_map/ppermute | solution.py:23
  91.4 6.9 %apply.9.refs_11_ = f32[1024,256]{1,0:T(8,128)S(1)} custom-call(s32[22]{0:T(128)S(1)} %compare_select_fusion.10.table.t, bf16[1024,1024]{1,0:T(8,128)(2,1)S(1)} %constant_dynamic-update-slice_fusion.orb.slab_ref, bf16[256,1280]{1,0:T(8,128)(2,1)S(1)} %slice.34.refs_0_, bf16[256,1280]{1,0:T(8,128)(2,1)S(1)} %slice.35.refs_1_, ...), custom_call_target="tpu_custom_call", output_to_operand_aliasing={{}: (14, {})} | custom-call | flops 1006632960 | bytes 3145728 | tf_op jit(solution)/shard_map/apply/pallas_call | solution.py:97
  98.3 6.2 %apply.10 = (f32[512,256]{1,0:T(8,128)S(1)}, f32[512,256]{1,0:T(8,128)S(1)}) custom-call(s32[22]{0:T(128)S(1)} %compare_select_fusion.10.table.t, bf16[1024,1024]{1,0:T(8,128)(2,1)S(1)} %collective-permute-done.21.slab_ref, bf16[256,1280]{1,0:T(8,128)(2,1)S(1)} %collective-permute-done.17.refs_0_, bf16[256,1280]{1,0:T(8,128)(2,1)S(1)} %collective-permute-done.18.refs_1_, ...), custom_call_target="tpu_custom_call" | custom-call | flops 838860800 | bytes 2621440 | tf_op jit(solution)/shard_map/apply/pallas_call | solution.py:97
  104.5 8.3 %collective-permute-start.24 = (f32[512,256]{1,0:T(8,128)S(1)}, f32[512,256]{1,0:T(8,128)S(1)}, u32[]{:S(2)}, u32[]{:S(2)}) collective-permute-start(f32[512,256]{1,0:T(8,128)S(1)} %get-tuple-element.38), channel_id=1, source_target_pairs={{1,0},{0,1},{3,2},{2,3},{5,4},{4,5},{7,6},{6,7},{9,8},{8,9},{11,10... | collective-permute-start | bytes 1572872 | tf_op jit(solution)/shard_map/ppermute | solution.py:23
  112.7 1.5 %collective-permute-done.24 = f32[512,256]{1,0:T(8,128)S(1)} collective-permute-done((f32[512,256]{1,0:T(8,128)S(1)}, f32[512,256]{1,0:T(8,128)S(1)}, u32[]{:S(2)}, u32[]{:S(2)}) %collective-permute-start.24) | collective-permute-done | bytes 524320 | tf_op jit(solution)/shard_map/ppermute | solution.py:23
  114.7 6.1 %apply.11 = (f32[512,256]{1,0:T(8,128)S(1)}, f32[512,256]{1,0:T(8,128)S(1)}) custom-call(s32[22]{0:T(128)S(1)} %compare_select_fusion.10.table.t, bf16[1024,1024]{1,0:T(8,128)(2,1)S(1)} %constant_dynamic-update-slice_fusion.orb.slab_ref, bf16[256,1280]{1,0:T(8,128)(2,1)S(1)} %collective-permute-done.17.refs_0_, ...), custom_call_target="tpu_custom_call" | custom-call | flops 838860800 | bytes 2621440 | tf_op jit(solution)/shard_map/apply/pallas_call | solution.py:97
  120.8 2.6 %collective-permute-done.25 = bf16[512,256]{1,0:T(8,128)(2,1)S(1)} collective-permute-done((bf16[512,256]{1,0:T(8,128)(2,1)S(1)}, bf16[512,256]{1,0:T(8,128)(2,1)S(1)}, u32[]{:S(2)}, u32[]{:S(2)}) %collective-permute-start.25) | collective-permute-done | bytes 262176 | tf_op jit(solution)/shard_map/ppermute | solution.py:23
  124.6 1.5 %collective-permute-done.26 = f32[512,256]{1,0:T(8,128)S(1)} collective-permute-done((f32[512,256]{1,0:T(8,128)S(1)}, f32[512,256]{1,0:T(8,128)S(1)}, u32[]{:S(2)}, u32[]{:S(2)}) %collective-permute-start.26) | collective-permute-done | bytes 524320 | tf_op jit(solution)/shard_map/ppermute | solution.py:23
  (72 shorter events, 11.1 us)
Async XLA Ops:
  0.0 6.6 %copy-start.3 = (bf16[512,256]{1,0:T(8,128)(2,1)S(1)}, bf16[512,256]{1,0:T(8,128)(2,1)}, u32[]{:S(2)}) copy-start(bf16[512,256]{1,0:T(8,128)(2,1)} %param.5) | copy-start | bytes 786436
  0.0 6.5 %copy-start.4 = (s32[1,128]{1,0:T(1,128)S(1)}, s32[1,128]{1,0:T(1,128)}, u32[]{:S(2)}) copy-start(s32[1,128]{1,0:T(1,128)} %param.6) | copy-start | bytes 1540
  0.0 7.6 %collective-permute-start = (bf16[512,1024]{1,0:T(8,128)(2,1)}, bf16[512,1024]{1,0:T(8,128)(2,1)S(1)}, u32[]{:S(2)}, u32[]{:S(2)}) collective-permute-start(bf16[512,1024]{1,0:T(8,128)(2,1)} %param.4), channel_id=1, source_target_pairs={{1,0},{0,1},{3,2},{2,3},{5,4},{4,5},{7,6},{6,7},{9,8},{8,9},{11,10... | collective-permute-start | bytes 3145736 | tf_op jit(solution)/shard_map/ppermute | solution.py:23
  1.4 5.1 %collective-permute-start.2 = (bf16[512,256]{1,0:T(8,128)(2,1)}, bf16[512,256]{1,0:T(8,128)(2,1)}, u32[]{:S(2)}, u32[]{:S(2)}) collective-permute-start(bf16[512,256]{1,0:T(8,128)(2,1)} %param.5), channel_id=1, source_target_pairs={{1,0},{0,1},{3,2},{2,3},{5,4},{4,5},{7,6},{6,7},{9,8},{8,9},{11,10... | collective-permute-start | bytes 786440 | tf_op jit(solution)/shard_map/ppermute | solution.py:23
  1.4 5.1 %collective-permute-start.1 = (s32[1,128]{1,0:T(1,128)}, s32[1,128]{1,0:T(1,128)S(1)}, u32[]{:S(2)}, u32[]{:S(2)}) collective-permute-start(s32[1,128]{1,0:T(1,128)} %param.6), channel_id=1, source_target_pairs={{2,0},{0,2},{3,1},{1,3},{6,4},{4,6},{7,5},{5,7},{10,8},{8,10},{11,... | collective-permute-start | bytes 1544 | tf_op jit(solution)/shard_map/ppermute | solution.py:23
  9.2 9.8 %collective-permute-start.3 = (bf16[128,1280]{1,0:T(8,128)(2,1)S(1)}, bf16[128,1280]{1,0:T(8,128)(2,1)S(1)}, u32[]{:S(2)}, u32[]{:S(2)}) collective-permute-start(bf16[128,1280]{1,0:T(8,128)(2,1)S(1)} %get-tuple-element.25), channel_id=1, source_target_pairs={{2,0},{0,2},{3,1},{1,3},{6,4},{4,6},{7,5},{5,7},{10,8},{8,10},{11,... | collective-permute-start | bytes 983048 | tf_op jit(solution)/shard_map/ppermute | solution.py:23
  19.0 7.4 %collective-permute-start.5 = (bf16[128,1280]{1,0:T(8,128)(2,1)S(1)}, bf16[128,1280]{1,0:T(8,128)(2,1)S(1)}, u32[]{:S(2)}, u32[]{:S(2)}) collective-permute-start(bf16[128,1280]{1,0:T(8,128)(2,1)S(1)} %add.68), channel_id=1, source_target_pairs={{4,0},{0,4},{5,1},{1,5},{6,2},{2,6},{7,3},{3,7},{12,8},{8,12},{13,... | collective-permute-start | bytes 983048 | tf_op jit(solution)/shard_map/ppermute | solution.py:23
  19.3 9.5 %collective-permute-start.13 = (bf16[128,1280]{1,0:T(8,128)(2,1)S(1)}, bf16[128,1280]{1,0:T(8,128)(2,1)S(1)}, u32[]{:S(2)}, u32[]{:S(2)}) collective-permute-start(bf16[128,1280]{1,0:T(8,128)(2,1)S(1)} %add.68), channel_id=1, source_target_pairs={{24,0},{0,8},{8,16},{16,24},{25,1},{1,9},{9,17},{17,25},{26,2},{2,... | collective-permute-start | bytes 983048 | tf_op jit(solution)/shard_map/ppermute | solution.py:23
  20.5 8.3 %collective-permute-start.4 = (bf16[128,1280]{1,0:T(8,128)(2,1)S(1)}, bf16[128,1280]{1,0:T(8,128)(2,1)S(1)}, u32[]{:S(2)}, u32[]{:S(2)}) collective-permute-start(bf16[128,1280]{1,0:T(8,128)(2,1)S(1)} %add.68), channel_id=1, source_target_pairs={{32,0},{64,32},{96,64},{0,96},{33,1},{65,33},{97,65},{1,97},{34,2}... | collective-permute-start | bytes 983048 | tf_op jit(solution)/shard_map/ppermute | solution.py:23
  23.3 6.2 %collective-permute-start.7 = (bf16[128,1280]{1,0:T(8,128)(2,1)S(1)}, bf16[128,1280]{1,0:T(8,128)(2,1)S(1)}, u32[]{:S(2)}, u32[]{:S(2)}) collective-permute-start(bf16[128,1280]{1,0:T(8,128)(2,1)S(1)} %add.68), channel_id=1, source_target_pairs={{8,0},{16,8},{24,16},{0,24},{9,1},{17,9},{25,17},{1,25},{10,2},{18... | collective-permute-start | bytes 983048 | tf_op jit(solution)/shard_map/ppermute | solution.py:23
  24.7 7.1 %collective-permute-start.10 = (bf16[128,1280]{1,0:T(8,128)(2,1)S(1)}, bf16[128,1280]{1,0:T(8,128)(2,1)S(1)}, u32[]{:S(2)}, u32[]{:S(2)}) collective-permute-start(bf16[128,1280]{1,0:T(8,128)(2,1)S(1)} %add.68), channel_id=1, source_target_pairs={{96,0},{0,32},{32,64},{64,96},{97,1},{1,33},{33,65},{65,97},{98,2}... | collective-permute-start | bytes 983048 | tf_op jit(solution)/shard_map/ppermute | solution.py:23
  26.4 11.7 %collective-permute-start.12 = (bf16[128,1280]{1,0:T(8,128)(2,1)S(1)}, bf16[128,1280]{1,0:T(8,128)(2,1)S(1)}, u32[]{:S(2)}, u32[]{:S(2)}) collective-permute-start(bf16[128,1280]{1,0:T(8,128)(2,1)S(1)} %collective-permute-done.5), channel_id=1, source_target_pairs={{24,0},{0,8},{8,16},{16,24},{25,1},{1,9},{9,17},{17,25},{26,2},{2,... | collective-permute-start | bytes 983048 | tf_op jit(solution)/shard_map/ppermute | solution.py:23
  31.8 44.4 %collective-permute-start.21 = (bf16[1024,1024]{1,0:T(8,128)(2,1)S(1)}, bf16[1024,1024]{1,0:T(8,128)(2,1)S(1)}, u32[]{:S(2)}, u32[]{:S(2)}) collective-permute-start(bf16[1024,1024]{1,0:T(8,128)(2,1)S(1)} %constant_dynamic-update-slice_fusion.orb.slab_ref), channel_id=1, source_target_pairs={{2,0},{0,2},{3,1},{1,3},{6,4},{4,6},{7,5},{5,7},{10,8},{8,10},{11,... | collective-permute-start | bytes 6291464 | tf_op jit(solution)/shard_map/ppermute | solution.py:23
  35.1 5.9 %collective-permute-start.6 = (bf16[128,1280]{1,0:T(8,128)(2,1)S(1)}, bf16[128,1280]{1,0:T(8,128)(2,1)S(1)}, u32[]{:S(2)}, u32[]{:S(2)}) collective-permute-start(bf16[128,1280]{1,0:T(8,128)(2,1)S(1)} %collective-permute-done.5), channel_id=1, source_target_pairs={{32,0},{64,32},{96,64},{0,96},{33,1},{65,33},{97,65},{1,97},{34,2}... | collective-permute-start | bytes 983048 | tf_op jit(solution)/shard_map/ppermute | solution.py:23
  35.1 6.0 %collective-permute-start.8 = (bf16[128,1280]{1,0:T(8,128)(2,1)S(1)}, bf16[128,1280]{1,0:T(8,128)(2,1)S(1)}, u32[]{:S(2)}, u32[]{:S(2)}) collective-permute-start(bf16[128,1280]{1,0:T(8,128)(2,1)S(1)} %collective-permute-done.5), channel_id=1, source_target_pairs={{8,0},{16,8},{24,16},{0,24},{9,1},{17,9},{25,17},{1,25},{10,2},{18... | collective-permute-start | bytes 983048 | tf_op jit(solution)/shard_map/ppermute | solution.py:23
  36.7 7.4 %collective-permute-start.11 = (bf16[128,1280]{1,0:T(8,128)(2,1)S(1)}, bf16[128,1280]{1,0:T(8,128)(2,1)S(1)}, u32[]{:S(2)}, u32[]{:S(2)}) collective-permute-start(bf16[128,1280]{1,0:T(8,128)(2,1)S(1)} %collective-permute-done.5), channel_id=1, source_target_pairs={{96,0},{0,32},{32,64},{64,96},{97,1},{1,33},{33,65},{65,97},{98,2}... | collective-permute-start | bytes 983048 | tf_op jit(solution)/shard_map/ppermute | solution.py:23
  44.5 17.8 %collective-permute-start.14 = (bf16[384,1280]{1,0:T(8,128)(2,1)S(1)}, bf16[384,1280]{1,0:T(8,128)(2,1)S(1)}, u32[]{:S(2)}, u32[]{:S(2)}) collective-permute-start(bf16[384,1280]{1,0:T(8,128)(2,1)S(1)} %get-tuple-element.56), channel_id=1, source_target_pairs={{24,0},{0,8},{8,16},{16,24},{25,1},{1,9},{9,17},{17,25},{26,2},{2,... | collective-permute-start | bytes 2949128 | tf_op jit(solution)/shard_map/ppermute | solution.py:23
  44.6 17.7 %collective-permute-start.15 = (bf16[384,1280]{1,0:T(8,128)(2,1)S(1)}, bf16[384,1280]{1,0:T(8,128)(2,1)S(1)}, u32[]{:S(2)}, u32[]{:S(2)}) collective-permute-start(bf16[384,1280]{1,0:T(8,128)(2,1)S(1)} %get-tuple-element.55), channel_id=1, source_target_pairs={{32,0},{64,32},{96,64},{0,96},{33,1},{65,33},{97,65},{1,97},{34,2}... | collective-permute-start | bytes 2949128 | tf_op jit(solution)/shard_map/ppermute | solution.py:23
  44.7 19.0 %collective-permute-start.16 = (bf16[384,1280]{1,0:T(8,128)(2,1)S(1)}, bf16[384,1280]{1,0:T(8,128)(2,1)S(1)}, u32[]{:S(2)}, u32[]{:S(2)}) collective-permute-start(bf16[384,1280]{1,0:T(8,128)(2,1)S(1)} %get-tuple-element.53), channel_id=1, source_target_pairs={{96,0},{0,32},{32,64},{64,96},{97,1},{1,33},{33,65},{65,97},{98,2}... | collective-permute-start | bytes 2949128 | tf_op jit(solution)/shard_map/ppermute | solution.py:23
  46.2 17.5 %collective-permute-start.9 = (bf16[384,1280]{1,0:T(8,128)(2,1)S(1)}, bf16[384,1280]{1,0:T(8,128)(2,1)S(1)}, u32[]{:S(2)}, u32[]{:S(2)}) collective-permute-start(bf16[384,1280]{1,0:T(8,128)(2,1)S(1)} %get-tuple-element.54), channel_id=1, source_target_pairs={{8,0},{16,8},{24,16},{0,24},{9,1},{17,9},{25,17},{1,25},{10,2},{18... | collective-permute-start | bytes 2949128 | tf_op jit(solution)/shard_map/ppermute | solution.py:23
  64.7 3.7 %slice-start.2 = ((bf16[384,1280]{1,0:T(8,128)(2,1)}), bf16[128,1280]{1,0:T(8,128)(2,1)S(1)}, s32[]{:S(2)}) async-start(bf16[384,1280]{1,0:T(8,128)(2,1)} %copy-done.2), calls=%async_computation.2 | async-start | bytes 655360 | tf_op jit(solution)/shard_map/slice | solution.py:170
  64.7 3.7 %slice-start = ((bf16[384,1280]{1,0:T(8,128)(2,1)}), bf16[128,1280]{1,0:T(8,128)(2,1)S(1)}, s32[]{:S(2)}) async-start(bf16[384,1280]{1,0:T(8,128)(2,1)} %copy-done), calls=%async_computation | async-start | bytes 655360 | tf_op jit(solution)/shard_map/slice | solution.py:169
  64.7 3.7 %slice-start.1 = ((bf16[384,1280]{1,0:T(8,128)(2,1)}), bf16[128,1280]{1,0:T(8,128)(2,1)S(1)}, s32[]{:S(2)}) async-start(bf16[384,1280]{1,0:T(8,128)(2,1)} %copy-done.1), calls=%async_computation.1 | async-start | bytes 655360 | tf_op jit(solution)/shard_map/slice | solution.py:169
  64.8 24.4 %collective-permute-start.17 = (bf16[256,1280]{1,0:T(8,128)(2,1)S(1)}, bf16[256,1280]{1,0:T(8,128)(2,1)S(1)}, u32[]{:S(2)}, u32[]{:S(2)}) collective-permute-start(bf16[256,1280]{1,0:T(8,128)(2,1)S(1)} %slice.34.refs_0_), channel_id=1, source_target_pairs={{8,0},{16,8},{24,16},{0,24},{9,1},{17,9},{25,17},{1,25},{10,2},{18... | collective-permute-start | bytes 1966088 | tf_op jit(solution)/shard_map/ppermute | solution.py:23
  66.9 22.4 %collective-permute-start.19 = (bf16[256,1280]{1,0:T(8,128)(2,1)S(1)}, bf16[256,1280]{1,0:T(8,128)(2,1)S(1)}, u32[]{:S(2)}, u32[]{:S(2)}) collective-permute-start(bf16[256,1280]{1,0:T(8,128)(2,1)S(1)} %slice.34.refs_0_), channel_id=1, source_target_pairs={{32,0},{64,32},{96,64},{0,96},{33,1},{65,33},{97,65},{1,97},{34,2}... | collective-permute-start | bytes 1966088 | tf_op jit(solution)/shard_map/ppermute | solution.py:23
  68.3 20.9 %collective-permute-start.18 = (bf16[256,1280]{1,0:T(8,128)(2,1)S(1)}, bf16[256,1280]{1,0:T(8,128)(2,1)S(1)}, u32[]{:S(2)}, u32[]{:S(2)}) collective-permute-start(bf16[256,1280]{1,0:T(8,128)(2,1)S(1)} %slice.35.refs_1_), channel_id=1, source_target_pairs={{24,0},{0,8},{8,16},{16,24},{25,1},{1,9},{9,17},{17,25},{26,2},{2,... | collective-permute-start | bytes 1966088 | tf_op jit(solution)/shard_map/ppermute | solution.py:23
  68.3 20.9 %collective-permute-start.20 = (bf16[256,1280]{1,0:T(8,128)(2,1)S(1)}, bf16[256,1280]{1,0:T(8,128)(2,1)S(1)}, u32[]{:S(2)}, u32[]{:S(2)}) collective-permute-start(bf16[256,1280]{1,0:T(8,128)(2,1)S(1)} %slice.35.refs_1_), channel_id=1, source_target_pairs={{96,0},{0,32},{32,64},{64,96},{97,1},{1,33},{33,65},{65,97},{98,2}... | collective-permute-start | bytes 1966088 | tf_op jit(solution)/shard_map/ppermute | solution.py:23
  89.3 9.0 %collective-permute-start.22 = (bf16[128,1280]{1,0:T(8,128)(2,1)S(1)}, bf16[128,1280]{1,0:T(8,128)(2,1)S(1)}, u32[]{:S(2)}, u32[]{:S(2)}) collective-permute-start(bf16[128,1280]{1,0:T(8,128)(2,1)S(1)} %slice.42), channel_id=1, source_target_pairs={{8,0},{16,8},{24,16},{0,24},{9,1},{17,9},{25,17},{1,25},{10,2},{18... | collective-permute-start | bytes 983048 | tf_op jit(solution)/shard_map/ppermute | solution.py:23
  91.3 7.0 %collective-permute-start.23 = (bf16[128,1280]{1,0:T(8,128)(2,1)S(1)}, bf16[128,1280]{1,0:T(8,128)(2,1)S(1)}, u32[]{:S(2)}, u32[]{:S(2)}) collective-permute-start(bf16[128,1280]{1,0:T(8,128)(2,1)S(1)} %slice.43), channel_id=1, source_target_pairs={{32,0},{64,32},{96,64},{0,96},{33,1},{65,33},{97,65},{1,97},{34,2}... | collective-permute-start | bytes 983048 | tf_op jit(solution)/shard_map/ppermute | solution.py:23
  104.5 9.8 %collective-permute-start.24 = (f32[512,256]{1,0:T(8,128)S(1)}, f32[512,256]{1,0:T(8,128)S(1)}, u32[]{:S(2)}, u32[]{:S(2)}) collective-permute-start(f32[512,256]{1,0:T(8,128)S(1)} %get-tuple-element.38), channel_id=1, source_target_pairs={{1,0},{0,1},{3,2},{2,3},{5,4},{4,5},{7,6},{6,7},{9,8},{8,9},{11,10... | collective-permute-start | bytes 1572872 | tf_op jit(solution)/shard_map/ppermute | solution.py:23
  114.3 9.1 %collective-permute-start.25 = (bf16[512,256]{1,0:T(8,128)(2,1)S(1)}, bf16[512,256]{1,0:T(8,128)(2,1)S(1)}, u32[]{:S(2)}, u32[]{:S(2)}) collective-permute-start(bf16[512,256]{1,0:T(8,128)(2,1)S(1)} %add_convert_fusion), channel_id=1, source_target_pairs={{2,0},{0,2},{3,1},{1,3},{6,4},{4,6},{7,5},{5,7},{10,8},{8,10},{11,... | collective-permute-start | bytes 786440 | tf_op jit(solution)/shard_map/ppermute | solution.py:23
  123.4 2.7 %collective-permute-start.26 = (f32[512,256]{1,0:T(8,128)S(1)}, f32[512,256]{1,0:T(8,128)S(1)}, u32[]{:S(2)}, u32[]{:S(2)}) collective-permute-start(f32[512,256]{1,0:T(8,128)S(1)} %get-tuple-element.42), channel_id=1, source_target_pairs={{1,0},{0,1},{3,2},{2,3},{5,4},{4,5},{7,6},{6,7},{9,8},{8,9},{11,10... | collective-permute-start | bytes 1572872 | tf_op jit(solution)/shard_map/ppermute | solution.py:23
  (3 other events, 3.8 us)

commit v7 on v6

--- a/solution.py
+++ b/solution.py
@@ -27,7 +27,7 @@
     return lax.optimization_barrier((value, others))[0]
 
 
-def pick_kernel(table, ids, orb, tgt, mine, theirs):
+def pick_kernel(table, ids, orb, own_tgt, sib_tgt, mine, theirs):
     rows, norb = orb.shape
     half = rows // 2
     bases = [table[BASE] + table[NEAR + k] * half for k in range(2)]
@@ -37,20 +37,24 @@
         hot = (row == ids[k : k + 1, :]).astype(jnp.bfloat16)
         dims = (((0,), (0,)), ((), ()))
         out[:, :norb] = lax.dot_general(hot, orb[...], dims, preferred_element_type=jnp.float32).astype(out.dtype)
-        out[:, norb:] = lax.dot_general(hot, tgt[...], dims, preferred_element_type=jnp.float32).astype(out.dtype)
+        picked = [
+            lax.dot_general(hot[k * half : (k + 1) * half], tgt[...], dims, preferred_element_type=jnp.float32)
+            for k, tgt in enumerate((own_tgt, sib_tgt))
+        ]
+        out[:, norb:] = (picked[0] + picked[1]).astype(out.dtype)
 
 
-def pick(table, ids, orb, tgt):
-    out = jax.ShapeDtypeStruct((ids.shape[1], orb.shape[1] + tgt.shape[1]), orb.dtype)
+def pick(table, ids, orb, own_tgt, sib_tgt):
+    out = jax.ShapeDtypeStruct((ids.shape[1], orb.shape[1] + own_tgt.shape[1]), orb.dtype)
     whole = pl.BlockSpec(memory_space=pltpu.VMEM)
     return pl.pallas_call(
         pick_kernel,
         out_shape=(out, out),
-        in_specs=[pl.BlockSpec(memory_space=pltpu.SMEM)] + [whole] * 3,
+        in_specs=[pl.BlockSpec(memory_space=pltpu.SMEM)] + [whole] * 4,
         out_specs=(whole, whole),
         compiler_params=pltpu.CompilerParams(vmem_limit_bytes=32 << 20),
         name="pick",
-    )(table, ids, orb, tgt)
+    )(table, ids, orb, own_tgt, sib_tgt)
 
 
 def apply_parts(slab, parts, potential, table, row_at, col_at, count, total, last=False):
@@ -81,7 +85,7 @@
 
             @pl.when(pl.program_id(0) == k)
             def _():
-                out[...] = term
+                out[...] = term.astype(out.dtype)
 
     def pot_spec(k):
         return pl.BlockSpec((tile, points), lambda i, t: (t[row_at + i], t[col_at + k]))
@@ -93,10 +97,10 @@
         specs.append(whole)
         args.append(total)
     flops = slab.shape[0] * points * count * width // 2
-    half = jax.ShapeDtypeStruct((tile, nj), jnp.float32)
+    halves = tuple(jax.ShapeDtypeStruct((tile, nj), t) for t in (jnp.float32, jnp.bfloat16))
     return pl.pallas_call(
         body,
-        out_shape=(half, half) if last else jax.ShapeDtypeStruct((slab.shape[0], nj), jnp.float32),
+        out_shape=halves if last else jax.ShapeDtypeStruct((slab.shape[0], nj), jnp.float32),
         grid_spec=pltpu.PrefetchScalarGridSpec(
             num_scalar_prefetch=1, grid=(2,), in_specs=specs, out_specs=(whole,) * 2 if last else whole
         ),
@@ -130,9 +134,8 @@
     sib_tgt = take_from(targets, "c", 1)
     far_points = take_from(points, "zh", 1)
     near_slab = jnp.concatenate([orbitals, sib_orb], axis=0)
-    near_tgt = jnp.concatenate([targets, sib_tgt], axis=0)
     ids = jnp.concatenate([points, far_points], axis=0)
-    mine, theirs = pick(table, ids, near_slab, near_tgt)
+    mine, theirs = pick(table, ids, near_slab, targets, sib_tgt)
     block = mine + take_from(theirs, "zh", 1)
     lower = table[SIDE:].reshape(1, 1) == 0
 
@@ -160,9 +163,7 @@
     from_down = take_from(joined((0, 1), pair[3, 0][count:]), "y", -1)
     first = ((0, 0), *(at for at, _, _ in NEXT))
     near = near_apply([pair[at] for at in first], first, None)
-    from_right, from_left, from_up, from_down = lax.optimization_barrier(
-        (from_right, from_left, from_up, from_down, near)
-    )[:4]
+    from_right, from_left = after(from_right, near), after(from_left, near)
     both = 2 * count
     pair[1, 1], pair[3, 3] = from_right[:both], from_left[:both]
     pair[1, 3], pair[3, 1] = from_up[:both], from_down[:both]
@@ -178,8 +179,7 @@
     far = far_apply([pair[at] for at in second], second, far)
 
     third = ((1, 2), (3, 2), (2, 1), (2, 3))
-    ready = lax.optimization_barrier((*(pair[at] for at in third), far))[:4]
-    pair.update(zip(third, ready))
+    pair[2, 1], pair[1, 2] = after(pair[2, 1], far), after(pair[1, 2], far)
     last = [take_from(pair[2, 1][:count], "x", 1), take_from(pair[1, 2][count:], "y", 1)]
     near = near_apply([pair[at] for at in second], second, after(near, far))
     third += ((2, 2),)

time: 127 us -> 125 us (0.984)
  waiting for transfers between devices: 39.5 us -> 33.9 us
  starting transfers between devices: 40.7 us -> 45.3 us
    ppermute x27, waiting for transfers between devices: 39.5 us -> 33.9 us  [take_from(): return lax.ppermute(value, axis, [((i + side) % n, i) for i in range(n)])]
    ppermute x27, starting transfers between devices: 40.7 us -> 45.3 us  [take_from(): return lax.ppermute(value, axis, [((i + side) % n, i) for i in range(n)])]
  transfers between devices with their start and end apart: 27 -> 27, of which waited for: 12 -> 10; matrix products, arithmetic and copies ran while one was open for 3% -> 3% of each run, Pallas kernels for 25% -> 26%
where the time goes in v7:
time: 125 us
  starting transfers between devices  45.3 us (36%)
  Pallas kernels  39.7 us (32%)
  waiting for transfers between devices  33.9 us (27%)
  local copies, waits for them, and re-layouts  2.84 us (2%)
  other arithmetic  1.92 us (2%)
    ppermute x27, starting transfers between devices, take_from(): return lax.ppermute(value, axis, [((i + side) % n, i) for i in range(n)])  45.3 us
    pallas_call x6, Pallas kernels, apply_parts(): pl.pallas_call(body, out_shape=halves if last else jax.ShapeDtypeStruct((...  38.2 us
    ppermute x27, waiting for transfers between devices, take_from(): return lax.ppermute(value, axis, [((i + side) % n, i) for i in range(n)])  33.9 us
  transfers between devices with their start and end apart: 27, of which 10 were waited for; matrix products, arithmetic and copies ran while one was open for 3% of the time, Pallas kernels for 26%

profile of v7, /device:TPU:1, one launch (start us, length us, event | category | flops | bytes accessed | tf_op | source)
XLA Modules:
  0.0 124.7 jit_solution(10361409086889212291)
XLA Ops:
  0.0 1.4 %collective-permute-start = (bf16[512,1024]{1,0:T(8,128)(2,1)}, bf16[512,1024]{1,0:T(8,128)(2,1)S(1)}, u32[]{:S(2)}, u32[]{:S(2)}) collective-permute-start(bf16[512,1024]{1,0:T(8,128)(2,1)} %param.4), channel_id=1, source_target_pairs={{1,0},{0,1},{3,2},{2,3},{5,4},{4,5},{7,6},{6,7},{9,8},{8,9},{11,10... | collective-permute-start | bytes 3145736 | tf_op jit(solution)/shard_map/ppermute | solution.py:23
  1.4 3.8 %collective-permute-start.1 = (s32[1,128]{1,0:T(1,128)}, s32[1,128]{1,0:T(1,128)S(1)}, u32[]{:S(2)}, u32[]{:S(2)}) collective-permute-start(s32[1,128]{1,0:T(1,128)} %param.6), channel_id=1, source_target_pairs={{2,0},{0,2},{3,1},{1,3},{6,4},{4,6},{7,5},{5,7},{10,8},{8,10},{11,... | collective-permute-start | bytes 1544 | tf_op jit(solution)/shard_map/ppermute | solution.py:23
  5.2 1.3 %constant_dynamic-update-slice_fusion.1 = bf16[1024,1024]{1,0:T(8,128)(2,1)S(1)} fusion(bf16[512,1024]{1,0:T(8,128)(2,1)} %param.4), kind=kLoop, calls=%fused_computation.24 | loop fusion | bytes 2097152
  6.7 1.5 %pick.1 = (bf16[128,1280]{1,0:T(8,128)(2,1)S(1)}, bf16[128,1280]{1,0:T(8,128)(2,1)S(1)}) custom-call(s32[22]{0:T(128)S(1)} %compare_select_fusion.10.table.t, s32[2,128]{1,0:T(2,128)S(1)} %pad_add_fusion.ids, bf16[1024,1024]{1,0:T(8,128)(2,1)S(1)} %constant_dynamic-update-slice_fusion.orb.slab_ref, bf16[512,256]{1,0:T(8,128)(2,1)S(1)} %copy-done, ...), custom_call_target="tpu_custom_call" | custom-call | tf_op jit(solution)/shard_map/pick/pallas_call | solution.py:50
  8.2 2.7 %collective-permute-start.3 = (bf16[128,1280]{1,0:T(8,128)(2,1)S(1)}, bf16[128,1280]{1,0:T(8,128)(2,1)S(1)}, u32[]{:S(2)}, u32[]{:S(2)}) collective-permute-start(bf16[128,1280]{1,0:T(8,128)(2,1)S(1)} %get-tuple-element.21), channel_id=1, source_target_pairs={{2,0},{0,2},{3,1},{1,3},{6,4},{4,6},{7,5},{5,7},{10,8},{8,10},{11,... | collective-permute-start | bytes 983048 | tf_op jit(solution)/shard_map/ppermute | solution.py:23
  10.9 7.1 %collective-permute-done.3 = bf16[128,1280]{1,0:T(8,128)(2,1)S(1)} collective-permute-done((bf16[128,1280]{1,0:T(8,128)(2,1)S(1)}, bf16[128,1280]{1,0:T(8,128)(2,1)S(1)}, u32[]{:S(2)}, u32[]{:S(2)}) %collective-permute-start.3) | collective-permute-done | bytes 327712 | tf_op jit(solution)/shard_map/ppermute | solution.py:23
  18.3 1.3 %collective-permute-start.12 = (bf16[128,1280]{1,0:T(8,128)(2,1)S(1)}, bf16[128,1280]{1,0:T(8,128)(2,1)S(1)}, u32[]{:S(2)}, u32[]{:S(2)}) collective-permute-start(bf16[128,1280]{1,0:T(8,128)(2,1)S(1)} %add.68), channel_id=1, source_target_pairs={{96,0},{0,32},{32,64},{64,96},{97,1},{1,33},{33,65},{65,97},{98,2}... | collective-permute-start | bytes 983048 | tf_op jit(solution)/shard_map/ppermute | solution.py:23
  20.9 1.4 %collective-permute-start.4 = (bf16[128,1280]{1,0:T(8,128)(2,1)S(1)}, bf16[128,1280]{1,0:T(8,128)(2,1)S(1)}, u32[]{:S(2)}, u32[]{:S(2)}) collective-permute-start(bf16[128,1280]{1,0:T(8,128)(2,1)S(1)} %add.68), channel_id=1, source_target_pairs={{32,0},{64,32},{96,64},{0,96},{33,1},{65,33},{97,65},{1,97},{34,2}... | collective-permute-start | bytes 983048 | tf_op jit(solution)/shard_map/ppermute | solution.py:23
  22.3 1.5 %collective-permute-start.7 = (bf16[128,1280]{1,0:T(8,128)(2,1)S(1)}, bf16[128,1280]{1,0:T(8,128)(2,1)S(1)}, u32[]{:S(2)}, u32[]{:S(2)}) collective-permute-start(bf16[128,1280]{1,0:T(8,128)(2,1)S(1)} %add.68), channel_id=1, source_target_pairs={{8,0},{16,8},{24,16},{0,24},{9,1},{17,9},{25,17},{1,25},{10,2},{18... | collective-permute-start | bytes 983048 | tf_op jit(solution)/shard_map/ppermute | solution.py:23
  23.8 1.7 %collective-permute-done.5 = bf16[128,1280]{1,0:T(8,128)(2,1)S(1)} collective-permute-done((bf16[128,1280]{1,0:T(8,128)(2,1)S(1)}, bf16[128,1280]{1,0:T(8,128)(2,1)S(1)}, u32[]{:S(2)}, u32[]{:S(2)}) %collective-permute-start.5) | collective-permute-done | bytes 327712 | tf_op jit(solution)/shard_map/ppermute | solution.py:23
  25.5 1.3 %collective-permute-start.13 = (bf16[128,1280]{1,0:T(8,128)(2,1)S(1)}, bf16[128,1280]{1,0:T(8,128)(2,1)S(1)}, u32[]{:S(2)}, u32[]{:S(2)}) collective-permute-start(bf16[128,1280]{1,0:T(8,128)(2,1)S(1)} %collective-permute-done.5), channel_id=1, source_target_pairs={{96,0},{0,32},{32,64},{64,96},{97,1},{1,33},{33,65},{65,97},{98,2}... | collective-permute-start | bytes 983048 | tf_op jit(solution)/shard_map/ppermute | solution.py:23
  28.5 3.2 %collective-permute-start.15 = (bf16[1024,1024]{1,0:T(8,128)(2,1)S(1)}, bf16[1024,1024]{1,0:T(8,128)(2,1)S(1)}, u32[]{:S(2)}, u32[]{:S(2)}) collective-permute-start(bf16[1024,1024]{1,0:T(8,128)(2,1)S(1)} %constant_dynamic-update-slice_fusion.orb.slab_ref), channel_id=1, source_target_pairs={{2,0},{0,2},{3,1},{1,3},{6,4},{4,6},{7,5},{5,7},{10,8},{8,10},{11,... | collective-permute-start | bytes 6291464 | tf_op jit(solution)/shard_map/ppermute | solution.py:23
  32.9 1.5 %collective-permute-start.6 = (bf16[128,1280]{1,0:T(8,128)(2,1)S(1)}, bf16[128,1280]{1,0:T(8,128)(2,1)S(1)}, u32[]{:S(2)}, u32[]{:S(2)}) collective-permute-start(bf16[128,1280]{1,0:T(8,128)(2,1)S(1)} %collective-permute-done.5), channel_id=1, source_target_pairs={{32,0},{64,32},{96,64},{0,96},{33,1},{65,33},{97,65},{1,97},{34,2}... | collective-permute-start | bytes 983048 | tf_op jit(solution)/shard_map/ppermute | solution.py:23
  34.4 1.5 %collective-permute-start.8 = (bf16[128,1280]{1,0:T(8,128)(2,1)S(1)}, bf16[128,1280]{1,0:T(8,128)(2,1)S(1)}, u32[]{:S(2)}, u32[]{:S(2)}) collective-permute-start(bf16[128,1280]{1,0:T(8,128)(2,1)S(1)} %collective-permute-done.5), channel_id=1, source_target_pairs={{8,0},{16,8},{24,16},{0,24},{9,1},{17,9},{25,17},{1,25},{10,2},{18... | collective-permute-start | bytes 983048 | tf_op jit(solution)/shard_map/ppermute | solution.py:23
  35.9 3.2 %collective-permute-done.11 = bf16[128,1280]{1,0:T(8,128)(2,1)S(1)} collective-permute-done((bf16[128,1280]{1,0:T(8,128)(2,1)S(1)}, bf16[128,1280]{1,0:T(8,128)(2,1)S(1)}, u32[]{:S(2)}, u32[]{:S(2)}) %collective-permute-start.11) | collective-permute-done | bytes 327712 | tf_op jit(solution)/shard_map/ppermute | solution.py:23
  39.2 1.3 %collective-permute-done.8 = bf16[128,1280]{1,0:T(8,128)(2,1)S(1)} collective-permute-done((bf16[128,1280]{1,0:T(8,128)(2,1)S(1)}, bf16[128,1280]{1,0:T(8,128)(2,1)S(1)}, u32[]{:S(2)}, u32[]{:S(2)}) %collective-permute-start.8) | collective-permute-done | bytes 327712 | tf_op jit(solution)/shard_map/ppermute | solution.py:23
  41.0 1.3 %collective-permute-start.17 = (bf16[384,1280]{1,0:T(8,128)(2,1)S(1)}, bf16[384,1280]{1,0:T(8,128)(2,1)S(1)}, u32[]{:S(2)}, u32[]{:S(2)}) collective-permute-start(bf16[384,1280]{1,0:T(8,128)(2,1)S(1)} %get-tuple-element.47), channel_id=1, source_target_pairs={{32,0},{64,32},{96,64},{0,96},{33,1},{65,33},{97,65},{1,97},{34,2}... | collective-permute-start | bytes 2949128 | tf_op jit(solution)/shard_map/ppermute | solution.py:23
  43.5 1.8 %collective-permute-start.9 = (bf16[384,1280]{1,0:T(8,128)(2,1)S(1)}, bf16[384,1280]{1,0:T(8,128)(2,1)S(1)}, u32[]{:S(2)}, u32[]{:S(2)}) collective-permute-start(bf16[384,1280]{1,0:T(8,128)(2,1)S(1)} %get-tuple-element.46), channel_id=1, source_target_pairs={{8,0},{16,8},{24,16},{0,24},{9,1},{17,9},{25,17},{1,25},{10,2},{18... | collective-permute-start | bytes 2949128 | tf_op jit(solution)/shard_map/ppermute | solution.py:23
  45.5 6.1 %apply.6.refs_12_ = f32[1024,256]{1,0:T(8,128)S(1)} custom-call(s32[22]{0:T(128)S(1)} %compare_select_fusion.10.table.t, bf16[1024,1024]{1,0:T(8,128)(2,1)S(1)} %constant_dynamic-update-slice_fusion.orb.slab_ref, bf16[256,1280]{1,0:T(8,128)(2,1)S(1)} %get-tuple-element.49.refs_0_, bf16[256,1280]{1,0:T(8,128)(2,1)S(1)} %get-tuple-element.50.refs_1_, ...), custom_call_target="tpu_custom_call" | custom-call | flops 838860800 | bytes 2621440 | tf_op jit(solution)/shard_map/apply/pallas_call | solution.py:101
  51.6 8.5 %collective-permute-done.16 = bf16[384,1280]{1,0:T(8,128)(2,1)S(1)} collective-permute-done((bf16[384,1280]{1,0:T(8,128)(2,1)S(1)}, bf16[384,1280]{1,0:T(8,128)(2,1)S(1)}, u32[]{:S(2)}, u32[]{:S(2)}) %collective-permute-start.16) | collective-permute-done | bytes 983072 | tf_op jit(solution)/shard_map/ppermute | solution.py:23
  60.3 2.1 %collective-permute-start.20 = (bf16[256,1280]{1,0:T(8,128)(2,1)S(1)}, bf16[256,1280]{1,0:T(8,128)(2,1)S(1)}, u32[]{:S(2)}, u32[]{:S(2)}) collective-permute-start(bf16[256,1280]{1,0:T(8,128)(2,1)S(1)} %slice.34.refs_0_), channel_id=1, source_target_pairs={{32,0},{64,32},{96,64},{0,96},{33,1},{65,33},{97,65},{1,97},{34,2}... | collective-permute-start | bytes 1966088 | tf_op jit(solution)/shard_map/ppermute | solution.py:23
  62.3 2.3 %collective-permute-start.14 = (bf16[256,1280]{1,0:T(8,128)(2,1)S(1)}, bf16[256,1280]{1,0:T(8,128)(2,1)S(1)}, u32[]{:S(2)}, u32[]{:S(2)}) collective-permute-start(bf16[256,1280]{1,0:T(8,128)(2,1)S(1)} %slice.34.refs_0_), channel_id=1, source_target_pairs={{8,0},{16,8},{24,16},{0,24},{9,1},{17,9},{25,17},{1,25},{10,2},{18... | collective-permute-start | bytes 1966088 | tf_op jit(solution)/shard_map/ppermute | solution.py:23
  65.8 7.4 %collective-permute-done.15.slab_ref = bf16[1024,1024]{1,0:T(8,128)(2,1)S(1)} collective-permute-done((bf16[1024,1024]{1,0:T(8,128)(2,1)S(1)}, bf16[1024,1024]{1,0:T(8,128)(2,1)S(1)}, u32[]{:S(2)}, u32[]{:S(2)}) %collective-permute-start.15) | collective-permute-done | bytes 2097184 | tf_op jit(solution)/shard_map/ppermute | solution.py:23
  73.2 6.1 %apply.7.refs_12_ = f32[1024,256]{1,0:T(8,128)S(1)} custom-call(s32[22]{0:T(128)S(1)} %compare_select_fusion.10.table.t, bf16[1024,1024]{1,0:T(8,128)(2,1)S(1)} %collective-permute-done.15.slab_ref, bf16[256,1280]{1,0:T(8,128)(2,1)S(1)} %get-tuple-element.49.refs_0_, bf16[256,1280]{1,0:T(8,128)(2,1)S(1)} %get-tuple-element.50.refs_1_, ...), custom_call_target="tpu_custom_call" | custom-call | flops 838860800 | bytes 2621440 | tf_op jit(solution)/shard_map/apply/pallas_call | solution.py:101
  79.3 6.9 %apply.8.refs_11_ = f32[1024,256]{1,0:T(8,128)S(1)} custom-call(s32[22]{0:T(128)S(1)} %compare_select_fusion.10.table.t, bf16[1024,1024]{1,0:T(8,128)(2,1)S(1)} %collective-permute-done.15.slab_ref, bf16[256,1280]{1,0:T(8,128)(2,1)S(1)} %slice.34.refs_0_, bf16[256,1280]{1,0:T(8,128)(2,1)S(1)} %slice.35.refs_1_, ...), custom_call_target="tpu_custom_call", output_to_operand_aliasing={{}: (14, {})} | custom-call | flops 1006632960 | bytes 3145728 | tf_op jit(solution)/shard_map/apply/pallas_call | solution.py:101
  86.2 2.7 %collective-permute-start.22 = (bf16[128,1280]{1,0:T(8,128)(2,1)S(1)}, bf16[128,1280]{1,0:T(8,128)(2,1)S(1)}, u32[]{:S(2)}, u32[]{:S(2)}) collective-permute-start(bf16[128,1280]{1,0:T(8,128)(2,1)S(1)} %slice.42), channel_id=1, source_target_pairs={{8,0},{16,8},{24,16},{0,24},{9,1},{17,9},{25,17},{1,25},{10,2},{18... | collective-permute-start | bytes 983048 | tf_op jit(solution)/shard_map/ppermute | solution.py:23
  89.0 1.5 %collective-permute-start.23 = (bf16[128,1280]{1,0:T(8,128)(2,1)S(1)}, bf16[128,1280]{1,0:T(8,128)(2,1)S(1)}, u32[]{:S(2)}, u32[]{:S(2)}) collective-permute-start(bf16[128,1280]{1,0:T(8,128)(2,1)S(1)} %slice.43), channel_id=1, source_target_pairs={{32,0},{64,32},{96,64},{0,96},{33,1},{65,33},{97,65},{1,97},{34,2}... | collective-permute-start | bytes 983048 | tf_op jit(solution)/shard_map/ppermute | solution.py:23
  90.4 6.9 %apply.9.refs_11_ = f32[1024,256]{1,0:T(8,128)S(1)} custom-call(s32[22]{0:T(128)S(1)} %compare_select_fusion.10.table.t, bf16[1024,1024]{1,0:T(8,128)(2,1)S(1)} %constant_dynamic-update-slice_fusion.orb.slab_ref, bf16[256,1280]{1,0:T(8,128)(2,1)S(1)} %slice.34.refs_0_, bf16[256,1280]{1,0:T(8,128)(2,1)S(1)} %slice.35.refs_1_, ...), custom_call_target="tpu_custom_call", output_to_operand_aliasing={{}: (14, {})} | custom-call | flops 1006632960 | bytes 3145728 | tf_op jit(solution)/shard_map/apply/pallas_call | solution.py:101
  97.4 6.1 %apply.10 = (f32[512,256]{1,0:T(8,128)S(1)}, bf16[512,256]{1,0:T(8,128)(2,1)S(1)}) custom-call(s32[22]{0:T(128)S(1)} %compare_select_fusion.10.table.t, bf16[1024,1024]{1,0:T(8,128)(2,1)S(1)} %collective-permute-done.15.slab_ref, bf16[256,1280]{1,0:T(8,128)(2,1)S(1)} %collective-permute-done.14.refs_0_, ...), custom_call_target="tpu_custom_call" | custom-call | flops 838860800 | bytes 2621440 | tf_op jit(solution)/shard_map/apply/pallas_call | solution.py:101
  103.5 7.7 %collective-permute-start.24 = (bf16[512,256]{1,0:T(8,128)(2,1)S(1)}, bf16[512,256]{1,0:T(8,128)(2,1)S(1)}, u32[]{:S(2)}, u32[]{:S(2)}) collective-permute-start(bf16[512,256]{1,0:T(8,128)(2,1)S(1)} %get-tuple-element.30), channel_id=1, source_target_pairs={{1,0},{0,1},{3,2},{2,3},{5,4},{4,5},{7,6},{6,7},{9,8},{8,9},{11,10... | collective-permute-start | bytes 786440 | tf_op jit(solution)/shard_map/ppermute | solution.py:23
  113.6 6.1 %apply.11 = (f32[512,256]{1,0:T(8,128)S(1)}, bf16[512,256]{1,0:T(8,128)(2,1)S(1)}) custom-call(s32[22]{0:T(128)S(1)} %compare_select_fusion.10.table.t, bf16[1024,1024]{1,0:T(8,128)(2,1)S(1)} %constant_dynamic-update-slice_fusion.orb.slab_ref, bf16[256,1280]{1,0:T(8,128)(2,1)S(1)} %collective-permute-done.14.refs_0_, ...), custom_call_target="tpu_custom_call" | custom-call | flops 838860800 | bytes 2621440 | tf_op jit(solution)/shard_map/apply/pallas_call | solution.py:101
  119.7 1.8 %collective-permute-done.25 = bf16[512,256]{1,0:T(8,128)(2,1)S(1)} collective-permute-done((bf16[512,256]{1,0:T(8,128)(2,1)S(1)}, bf16[512,256]{1,0:T(8,128)(2,1)S(1)}, u32[]{:S(2)}, u32[]{:S(2)}) %collective-permute-start.25) | collective-permute-done | bytes 262176 | tf_op jit(solution)/shard_map/ppermute | solution.py:23
  (65 shorter events, 12.7 us)
Async XLA Ops:
  0.0 6.6 %copy-start.2 = (s32[1,128]{1,0:T(1,128)S(1)}, s32[1,128]{1,0:T(1,128)}, u32[]{:S(2)}) copy-start(s32[1,128]{1,0:T(1,128)} %param.6) | copy-start | bytes 1540
  0.0 6.6 %collective-permute-start = (bf16[512,1024]{1,0:T(8,128)(2,1)}, bf16[512,1024]{1,0:T(8,128)(2,1)S(1)}, u32[]{:S(2)}, u32[]{:S(2)}) collective-permute-start(bf16[512,1024]{1,0:T(8,128)(2,1)} %param.4), channel_id=1, source_target_pairs={{1,0},{0,1},{3,2},{2,3},{5,4},{4,5},{7,6},{6,7},{9,8},{8,9},{11,10... | collective-permute-start | bytes 3145736 | tf_op jit(solution)/shard_map/ppermute | solution.py:23
  1.4 5.3 %collective-permute-start.2 = (bf16[512,256]{1,0:T(8,128)(2,1)}, bf16[512,256]{1,0:T(8,128)(2,1)S(1)}, u32[]{:S(2)}, u32[]{:S(2)}) collective-permute-start(bf16[512,256]{1,0:T(8,128)(2,1)} %own_tgt.1), channel_id=1, source_target_pairs={{1,0},{0,1},{3,2},{2,3},{5,4},{4,5},{7,6},{6,7},{9,8},{8,9},{11,10... | collective-permute-start | bytes 786440 | tf_op jit(solution)/shard_map/ppermute | solution.py:23
  1.4 5.1 %collective-permute-start.1 = (s32[1,128]{1,0:T(1,128)}, s32[1,128]{1,0:T(1,128)S(1)}, u32[]{:S(2)}, u32[]{:S(2)}) collective-permute-start(s32[1,128]{1,0:T(1,128)} %param.6), channel_id=1, source_target_pairs={{2,0},{0,2},{3,1},{1,3},{6,4},{4,6},{7,5},{5,7},{10,8},{8,10},{11,... | collective-permute-start | bytes 1544 | tf_op jit(solution)/shard_map/ppermute | solution.py:23
  5.2 1.5 %copy-start = (bf16[512,256]{1,0:T(8,128)(2,1)S(1)}, bf16[512,256]{1,0:T(8,128)(2,1)}, u32[]{:S(2)}) copy-start(bf16[512,256]{1,0:T(8,128)(2,1)} %own_tgt.1) | copy-start | bytes 786436
  8.2 9.8 %collective-permute-start.3 = (bf16[128,1280]{1,0:T(8,128)(2,1)S(1)}, bf16[128,1280]{1,0:T(8,128)(2,1)S(1)}, u32[]{:S(2)}, u32[]{:S(2)}) collective-permute-start(bf16[128,1280]{1,0:T(8,128)(2,1)S(1)} %get-tuple-element.21), channel_id=1, source_target_pairs={{2,0},{0,2},{3,1},{1,3},{6,4},{4,6},{7,5},{5,7},{10,8},{8,10},{11,... | collective-permute-start | bytes 983048 | tf_op jit(solution)/shard_map/ppermute | solution.py:23
  18.1 7.4 %collective-permute-start.5 = (bf16[128,1280]{1,0:T(8,128)(2,1)S(1)}, bf16[128,1280]{1,0:T(8,128)(2,1)S(1)}, u32[]{:S(2)}, u32[]{:S(2)}) collective-permute-start(bf16[128,1280]{1,0:T(8,128)(2,1)S(1)} %add.68), channel_id=1, source_target_pairs={{4,0},{0,4},{5,1},{1,5},{6,2},{2,6},{7,3},{3,7},{12,8},{8,12},{13,... | collective-permute-start | bytes 983048 | tf_op jit(solution)/shard_map/ppermute | solution.py:23
  18.3 9.7 %collective-permute-start.12 = (bf16[128,1280]{1,0:T(8,128)(2,1)S(1)}, bf16[128,1280]{1,0:T(8,128)(2,1)S(1)}, u32[]{:S(2)}, u32[]{:S(2)}) collective-permute-start(bf16[128,1280]{1,0:T(8,128)(2,1)S(1)} %add.68), channel_id=1, source_target_pairs={{96,0},{0,32},{32,64},{64,96},{97,1},{1,33},{33,65},{65,97},{98,2}... | collective-permute-start | bytes 983048 | tf_op jit(solution)/shard_map/ppermute | solution.py:23
  19.7 8.4 %collective-permute-start.10 = (bf16[128,1280]{1,0:T(8,128)(2,1)S(1)}, bf16[128,1280]{1,0:T(8,128)(2,1)S(1)}, u32[]{:S(2)}, u32[]{:S(2)}) collective-permute-start(bf16[128,1280]{1,0:T(8,128)(2,1)S(1)} %add.68), channel_id=1, source_target_pairs={{24,0},{0,8},{8,16},{16,24},{25,1},{1,9},{9,17},{17,25},{26,2},{2,... | collective-permute-start | bytes 983048 | tf_op jit(solution)/shard_map/ppermute | solution.py:23
  20.9 7.2 %collective-permute-start.4 = (bf16[128,1280]{1,0:T(8,128)(2,1)S(1)}, bf16[128,1280]{1,0:T(8,128)(2,1)S(1)}, u32[]{:S(2)}, u32[]{:S(2)}) collective-permute-start(bf16[128,1280]{1,0:T(8,128)(2,1)S(1)} %add.68), channel_id=1, source_target_pairs={{32,0},{64,32},{96,64},{0,96},{33,1},{65,33},{97,65},{1,97},{34,2}... | collective-permute-start | bytes 983048 | tf_op jit(solution)/shard_map/ppermute | solution.py:23
  22.3 6.2 %collective-permute-start.7 = (bf16[128,1280]{1,0:T(8,128)(2,1)S(1)}, bf16[128,1280]{1,0:T(8,128)(2,1)S(1)}, u32[]{:S(2)}, u32[]{:S(2)}) collective-permute-start(bf16[128,1280]{1,0:T(8,128)(2,1)S(1)} %add.68), channel_id=1, source_target_pairs={{8,0},{16,8},{24,16},{0,24},{9,1},{17,9},{25,17},{1,25},{10,2},{18... | collective-permute-start | bytes 983048 | tf_op jit(solution)/shard_map/ppermute | solution.py:23
  25.5 10.4 %collective-permute-start.13 = (bf16[128,1280]{1,0:T(8,128)(2,1)S(1)}, bf16[128,1280]{1,0:T(8,128)(2,1)S(1)}, u32[]{:S(2)}, u32[]{:S(2)}) collective-permute-start(bf16[128,1280]{1,0:T(8,128)(2,1)S(1)} %collective-permute-done.5), channel_id=1, source_target_pairs={{96,0},{0,32},{32,64},{64,96},{97,1},{1,33},{33,65},{65,97},{98,2}... | collective-permute-start | bytes 983048 | tf_op jit(solution)/shard_map/ppermute | solution.py:23
  28.5 44.7 %collective-permute-start.15 = (bf16[1024,1024]{1,0:T(8,128)(2,1)S(1)}, bf16[1024,1024]{1,0:T(8,128)(2,1)S(1)}, u32[]{:S(2)}, u32[]{:S(2)}) collective-permute-start(bf16[1024,1024]{1,0:T(8,128)(2,1)S(1)} %constant_dynamic-update-slice_fusion.orb.slab_ref), channel_id=1, source_target_pairs={{2,0},{0,2},{3,1},{1,3},{6,4},{4,6},{7,5},{5,7},{10,8},{8,10},{11,... | collective-permute-start | bytes 6291464 | tf_op jit(solution)/shard_map/ppermute | solution.py:23
  31.7 7.4 %collective-permute-start.11 = (bf16[128,1280]{1,0:T(8,128)(2,1)S(1)}, bf16[128,1280]{1,0:T(8,128)(2,1)S(1)}, u32[]{:S(2)}, u32[]{:S(2)}) collective-permute-start(bf16[128,1280]{1,0:T(8,128)(2,1)S(1)} %collective-permute-done.5), channel_id=1, source_target_pairs={{24,0},{0,8},{8,16},{16,24},{25,1},{1,9},{9,17},{17,25},{26,2},{2,... | collective-permute-start | bytes 983048 | tf_op jit(solution)/shard_map/ppermute | solution.py:23
  32.9 6.3 %collective-permute-start.6 = (bf16[128,1280]{1,0:T(8,128)(2,1)S(1)}, bf16[128,1280]{1,0:T(8,128)(2,1)S(1)}, u32[]{:S(2)}, u32[]{:S(2)}) collective-permute-start(bf16[128,1280]{1,0:T(8,128)(2,1)S(1)} %collective-permute-done.5), channel_id=1, source_target_pairs={{32,0},{64,32},{96,64},{0,96},{33,1},{65,33},{97,65},{1,97},{34,2}... | collective-permute-start | bytes 983048 | tf_op jit(solution)/shard_map/ppermute | solution.py:23
  34.4 6.2 %collective-permute-start.8 = (bf16[128,1280]{1,0:T(8,128)(2,1)S(1)}, bf16[128,1280]{1,0:T(8,128)(2,1)S(1)}, u32[]{:S(2)}, u32[]{:S(2)}) collective-permute-start(bf16[128,1280]{1,0:T(8,128)(2,1)S(1)} %collective-permute-done.5), channel_id=1, source_target_pairs={{8,0},{16,8},{24,16},{0,24},{9,1},{17,9},{25,17},{1,25},{10,2},{18... | collective-permute-start | bytes 983048 | tf_op jit(solution)/shard_map/ppermute | solution.py:23
  41.0 23.7 %collective-permute-start.17 = (bf16[384,1280]{1,0:T(8,128)(2,1)S(1)}, bf16[384,1280]{1,0:T(8,128)(2,1)S(1)}, u32[]{:S(2)}, u32[]{:S(2)}) collective-permute-start(bf16[384,1280]{1,0:T(8,128)(2,1)S(1)} %get-tuple-element.47), channel_id=1, source_target_pairs={{32,0},{64,32},{96,64},{0,96},{33,1},{65,33},{97,65},{1,97},{34,2}... | collective-permute-start | bytes 2949128 | tf_op jit(solution)/shard_map/ppermute | solution.py:23
  42.4 22.4 %collective-permute-start.18 = (bf16[384,1280]{1,0:T(8,128)(2,1)S(1)}, bf16[384,1280]{1,0:T(8,128)(2,1)S(1)}, u32[]{:S(2)}, u32[]{:S(2)}) collective-permute-start(bf16[384,1280]{1,0:T(8,128)(2,1)S(1)} %get-tuple-element.45), channel_id=1, source_target_pairs={{96,0},{0,32},{32,64},{64,96},{97,1},{1,33},{33,65},{65,97},{98,2}... | collective-permute-start | bytes 2949128 | tf_op jit(solution)/shard_map/ppermute | solution.py:23
  42.6 17.6 %collective-permute-start.16 = (bf16[384,1280]{1,0:T(8,128)(2,1)S(1)}, bf16[384,1280]{1,0:T(8,128)(2,1)S(1)}, u32[]{:S(2)}, u32[]{:S(2)}) collective-permute-start(bf16[384,1280]{1,0:T(8,128)(2,1)S(1)} %get-tuple-element.48), channel_id=1, source_target_pairs={{24,0},{0,8},{8,16},{16,24},{25,1},{1,9},{9,17},{17,25},{26,2},{2,... | collective-permute-start | bytes 2949128 | tf_op jit(solution)/shard_map/ppermute | solution.py:23
  43.5 16.7 %collective-permute-start.9 = (bf16[384,1280]{1,0:T(8,128)(2,1)S(1)}, bf16[384,1280]{1,0:T(8,128)(2,1)S(1)}, u32[]{:S(2)}, u32[]{:S(2)}) collective-permute-start(bf16[384,1280]{1,0:T(8,128)(2,1)S(1)} %get-tuple-element.46), channel_id=1, source_target_pairs={{8,0},{16,8},{24,16},{0,24},{9,1},{17,9},{25,17},{1,25},{10,2},{18... | collective-permute-start | bytes 2949128 | tf_op jit(solution)/shard_map/ppermute | solution.py:23
  60.1 4.6 %copy-start.1 = (bf16[384,1280]{1,0:T(8,128)(2,1)}, bf16[384,1280]{1,0:T(8,128)(2,1)S(1)}, u32[]{:S(2)}) copy-start(bf16[384,1280]{1,0:T(8,128)(2,1)S(1)} %collective-permute-done.16) | copy-start | bytes 2949124
  60.3 25.9 %collective-permute-start.20 = (bf16[256,1280]{1,0:T(8,128)(2,1)S(1)}, bf16[256,1280]{1,0:T(8,128)(2,1)S(1)}, u32[]{:S(2)}, u32[]{:S(2)}) collective-permute-start(bf16[256,1280]{1,0:T(8,128)(2,1)S(1)} %slice.34.refs_0_), channel_id=1, source_target_pairs={{32,0},{64,32},{96,64},{0,96},{33,1},{65,33},{97,65},{1,97},{34,2}... | collective-permute-start | bytes 1966088 | tf_op jit(solution)/shard_map/ppermute | solution.py:23
  62.3 26.6 %collective-permute-start.14 = (bf16[256,1280]{1,0:T(8,128)(2,1)S(1)}, bf16[256,1280]{1,0:T(8,128)(2,1)S(1)}, u32[]{:S(2)}, u32[]{:S(2)}) collective-permute-start(bf16[256,1280]{1,0:T(8,128)(2,1)S(1)} %slice.34.refs_0_), channel_id=1, source_target_pairs={{8,0},{16,8},{24,16},{0,24},{9,1},{17,9},{25,17},{1,25},{10,2},{18... | collective-permute-start | bytes 1966088 | tf_op jit(solution)/shard_map/ppermute | solution.py:23
  64.7 32.7 %collective-permute-start.19 = (bf16[256,1280]{1,0:T(8,128)(2,1)S(1)}, bf16[256,1280]{1,0:T(8,128)(2,1)S(1)}, u32[]{:S(2)}, u32[]{:S(2)}) collective-permute-start(bf16[256,1280]{1,0:T(8,128)(2,1)S(1)} %slice.35.refs_1_), channel_id=1, source_target_pairs={{24,0},{0,8},{8,16},{16,24},{25,1},{1,9},{9,17},{17,25},{26,2},{2,... | collective-permute-start | bytes 1966088 | tf_op jit(solution)/shard_map/ppermute | solution.py:23
  64.8 1.0 slice-start
  64.8 32.6 %collective-permute-start.21 = (bf16[256,1280]{1,0:T(8,128)(2,1)S(1)}, bf16[256,1280]{1,0:T(8,128)(2,1)S(1)}, u32[]{:S(2)}, u32[]{:S(2)}) collective-permute-start(bf16[256,1280]{1,0:T(8,128)(2,1)S(1)} %slice.35.refs_1_), channel_id=1, source_target_pairs={{96,0},{0,32},{32,64},{64,96},{97,1},{1,33},{33,65},{65,97},{98,2}... | collective-permute-start | bytes 1966088 | tf_op jit(solution)/shard_map/ppermute | solution.py:23
  86.2 11.1 %collective-permute-start.22 = (bf16[128,1280]{1,0:T(8,128)(2,1)S(1)}, bf16[128,1280]{1,0:T(8,128)(2,1)S(1)}, u32[]{:S(2)}, u32[]{:S(2)}) collective-permute-start(bf16[128,1280]{1,0:T(8,128)(2,1)S(1)} %slice.42), channel_id=1, source_target_pairs={{8,0},{16,8},{24,16},{0,24},{9,1},{17,9},{25,17},{1,25},{10,2},{18... | collective-permute-start | bytes 983048 | tf_op jit(solution)/shard_map/ppermute | solution.py:23
  89.0 8.4 %collective-permute-start.23 = (bf16[128,1280]{1,0:T(8,128)(2,1)S(1)}, bf16[128,1280]{1,0:T(8,128)(2,1)S(1)}, u32[]{:S(2)}, u32[]{:S(2)}) collective-permute-start(bf16[128,1280]{1,0:T(8,128)(2,1)S(1)} %slice.43), channel_id=1, source_target_pairs={{32,0},{64,32},{96,64},{0,96},{33,1},{65,33},{97,65},{1,97},{34,2}... | collective-permute-start | bytes 983048 | tf_op jit(solution)/shard_map/ppermute | solution.py:23
  103.5 8.8 %collective-permute-start.24 = (bf16[512,256]{1,0:T(8,128)(2,1)S(1)}, bf16[512,256]{1,0:T(8,128)(2,1)S(1)}, u32[]{:S(2)}, u32[]{:S(2)}) collective-permute-start(bf16[512,256]{1,0:T(8,128)(2,1)S(1)} %get-tuple-element.30), channel_id=1, source_target_pairs={{1,0},{0,1},{3,2},{2,3},{5,4},{4,5},{7,6},{6,7},{9,8},{8,9},{11,10... | collective-permute-start | bytes 786440 | tf_op jit(solution)/shard_map/ppermute | solution.py:23
  112.4 9.1 %collective-permute-start.25 = (bf16[512,256]{1,0:T(8,128)(2,1)S(1)}, bf16[512,256]{1,0:T(8,128)(2,1)S(1)}, u32[]{:S(2)}, u32[]{:S(2)}) collective-permute-start(bf16[512,256]{1,0:T(8,128)(2,1)S(1)} %add_convert_fusion), channel_id=1, source_target_pairs={{2,0},{0,2},{3,1},{1,3},{6,4},{4,6},{7,5},{5,7},{10,8},{8,10},{11,... | collective-permute-start | bytes 786440 | tf_op jit(solution)/shard_map/ppermute | solution.py:23
  121.5 2.4 %collective-permute-start.26 = (bf16[512,256]{1,0:T(8,128)(2,1)S(1)}, bf16[512,256]{1,0:T(8,128)(2,1)S(1)}, u32[]{:S(2)}, u32[]{:S(2)}) collective-permute-start(bf16[512,256]{1,0:T(8,128)(2,1)S(1)} %get-tuple-element.34), channel_id=1, source_target_pairs={{1,0},{0,1},{3,2},{2,3},{5,4},{4,5},{7,6},{6,7},{9,8},{8,9},{11,10... | collective-permute-start | bytes 786440 | tf_op jit(solution)/shard_map/ppermute | solution.py:23

commit v8 on v7

--- a/solution.py
+++ b/solution.py
@@ -12,7 +12,7 @@
 RING = 4
 ORDER = (
     (0, 0), (0, 1), (0, 3), (1, 0), (3, 0), (1, 1), (3, 3), (1, 3), (3, 1), (0, 2), (2, 0),
-    (1, 2), (3, 2), (2, 1), (2, 3), (2, 2),
+    (2, 1), (2, 3), (3, 2), (1, 2), (2, 2),
 )
 NEAR, FAR, BASE, SIDE = 16, 18, 20, 21
 NEXT = (((0, 1), "x", 1), ((0, 3), "x", -1), ((1, 0), "y", 1), ((3, 0), "y", -1))
@@ -163,28 +163,27 @@
     from_down = take_from(joined((0, 1), pair[3, 0][count:]), "y", -1)
     first = ((0, 0), *(at for at, _, _ in NEXT))
     near = near_apply([pair[at] for at in first], first, None)
-    from_right, from_left = after(from_right, near), after(from_left, near)
     both = 2 * count
+    from_right, from_left, from_up, from_down = (after(v, near) for v in (from_right, from_left, from_up, from_down))
     pair[1, 1], pair[3, 3] = from_right[:both], from_left[:both]
     pair[1, 3], pair[3, 1] = from_up[:both], from_down[:both]
     pair[0, 2] = jnp.concatenate([from_right[both:], from_left[both:]], axis=0)
     pair[2, 0] = jnp.concatenate([from_up[both:], from_down[both:]], axis=0)
 
-    pair[1, 2] = take_from(pair[1, 1], "x", 1)
-    pair[3, 2] = take_from(pair[3, 3], "x", -1)
-    pair[2, 1] = take_from(pair[1, 1], "y", 1)
-    pair[2, 3] = take_from(pair[3, 3], "y", -1)
     second = ((1, 1), (3, 3), (1, 3), (3, 1), (0, 2), (2, 0))
+    third = ((2, 1), (2, 3), (3, 2), (1, 2), (2, 2))
+    last = [
+        take_from(jnp.concatenate([pair[1, 1], pair[1, 3][:count]], axis=0), "y", 1),
+        take_from(jnp.concatenate([pair[3, 3][count:], pair[0, 2]], axis=0), "y", -1),
+        take_from(pair[1, 1][:count], "x", 1),
+        take_from(pair[1, 3][count:], "x", -1),
+        take_from(pair[2, 0], "x", 2),
+    ]
     far = far_apply([pair[at] for at in first], first, None)
     far = far_apply([pair[at] for at in second], second, far)
-
-    third = ((1, 2), (3, 2), (2, 1), (2, 3))
-    pair[2, 1], pair[1, 2] = after(pair[2, 1], far), after(pair[1, 2], far)
-    last = [take_from(pair[2, 1][:count], "x", 1), take_from(pair[1, 2][count:], "y", 1)]
     near = near_apply([pair[at] for at in second], second, after(near, far))
-    third += ((2, 2),)
-    last = [pair[at] for at in third[:4]] + last
-    kept, sent = far_apply(last, third, after(far, near), True)
+    last, far, near = lax.optimization_barrier((last, far, near))
+    kept, sent = far_apply(last, third, far, True)
     far = (kept + take_from(sent, "c", 1)).astype(jnp.bfloat16)
     away = take_from(far, "zh", 1)
     kept, sent = near_apply(last, third, after(near, far), True)

time: 125 us -> 122 us (0.976)
  waiting for transfers between devices: 33.9 us -> 32.1 us
    ppermute x27 -> x26, waiting for transfers between devices: 33.9 us -> 32.1 us  [take_from(): return lax.ppermute(value, axis, [((i + side) % n, i) for i in range(n)])]
    ppermute x27 -> x26, starting transfers between devices: 45.3 us -> 44.8 us  [take_from(): return lax.ppermute(value, axis, [((i + side) % n, i) for i in range(n)])]
  transfers between devices with their start and end apart: 27 -> 26, of which waited for: 10 -> 10; matrix products, arithmetic and copies ran while one was open for 3% -> 3% of each run, Pallas kernels for 26% -> 26%
where the time goes in v8:
time: 122 us
  starting transfers between devices  44.8 us (37%)
  Pallas kernels  39.7 us (33%)
  waiting for transfers between devices  32.1 us (26%)
  local copies, waits for them, and re-layouts  2.35 us (2%)
  other arithmetic  2.05 us (2%)
    ppermute x26, starting transfers between devices, take_from(): return lax.ppermute(value, axis, [((i + side) % n, i) for i in range(n)])  44.8 us
    pallas_call x6, Pallas kernels, apply_parts(): pl.pallas_call(body, out_shape=halves if last else jax.ShapeDtypeStruct((...  38.2 us
    ppermute x26, waiting for transfers between devices, take_from(): return lax.ppermute(value, axis, [((i + side) % n, i) for i in range(n)])  32.1 us
  transfers between devices with their start and end apart: 26, of which 10 were waited for; matrix products, arithmetic and copies ran while one was open for 3% of the time, Pallas kernels for 26%

profile of v8, /device:TPU:1, one launch (start us, length us, event | category | flops | bytes accessed | tf_op | source)
XLA Modules:
  0.0 122.1 jit_solution(16586092208370779961)
XLA Ops:
  0.0 1.4 %collective-permute-start = (bf16[512,1024]{1,0:T(8,128)(2,1)}, bf16[512,1024]{1,0:T(8,128)(2,1)S(1)}, u32[]{:S(2)}, u32[]{:S(2)}) collective-permute-start(bf16[512,1024]{1,0:T(8,128)(2,1)} %param.4), channel_id=1, source_target_pairs={{1,0},{0,1},{3,2},{2,3},{5,4},{4,5},{7,6},{6,7},{9,8},{8,9},{11,10... | collective-permute-start | bytes 3145736 | tf_op jit(solution)/shard_map/ppermute | solution.py:23
  1.4 3.8 %collective-permute-start.1 = (s32[1,128]{1,0:T(1,128)}, s32[1,128]{1,0:T(1,128)S(1)}, u32[]{:S(2)}, u32[]{:S(2)}) collective-permute-start(s32[1,128]{1,0:T(1,128)} %param.6), channel_id=1, source_target_pairs={{2,0},{0,2},{3,1},{1,3},{6,4},{4,6},{7,5},{5,7},{10,8},{8,10},{11,... | collective-permute-start | bytes 1544 | tf_op jit(solution)/shard_map/ppermute | solution.py:23
  5.2 1.3 %constant_dynamic-update-slice_fusion.1 = bf16[1024,1024]{1,0:T(8,128)(2,1)S(1)} fusion(bf16[512,1024]{1,0:T(8,128)(2,1)} %param.4), kind=kLoop, calls=%fused_computation.26 | loop fusion | bytes 2097152
  6.7 1.5 %pick.1 = (bf16[128,1280]{1,0:T(8,128)(2,1)S(1)}, bf16[128,1280]{1,0:T(8,128)(2,1)S(1)}) custom-call(s32[22]{0:T(128)S(1)} %compare_select_fusion.10.table.t, s32[2,128]{1,0:T(2,128)S(1)} %pad_add_fusion.ids, bf16[1024,1024]{1,0:T(8,128)(2,1)S(1)} %constant_dynamic-update-slice_fusion.orb.slab_ref, bf16[512,256]{1,0:T(8,128)(2,1)S(1)} %copy-done, ...), custom_call_target="tpu_custom_call" | custom-call | tf_op jit(solution)/shard_map/pick/pallas_call | solution.py:50
  8.2 2.7 %collective-permute-start.3 = (bf16[128,1280]{1,0:T(8,128)(2,1)S(1)}, bf16[128,1280]{1,0:T(8,128)(2,1)S(1)}, u32[]{:S(2)}, u32[]{:S(2)}) collective-permute-start(bf16[128,1280]{1,0:T(8,128)(2,1)S(1)} %get-tuple-element.27), channel_id=1, source_target_pairs={{2,0},{0,2},{3,1},{1,3},{6,4},{4,6},{7,5},{5,7},{10,8},{8,10},{11,... | collective-permute-start | bytes 983048 | tf_op jit(solution)/shard_map/ppermute | solution.py:23
  10.9 7.1 %collective-permute-done.3 = bf16[128,1280]{1,0:T(8,128)(2,1)S(1)} collective-permute-done((bf16[128,1280]{1,0:T(8,128)(2,1)S(1)}, bf16[128,1280]{1,0:T(8,128)(2,1)S(1)}, u32[]{:S(2)}, u32[]{:S(2)}) %collective-permute-start.3) | collective-permute-done | bytes 327712 | tf_op jit(solution)/shard_map/ppermute | solution.py:23
  18.3 1.3 %collective-permute-start.12 = (bf16[128,1280]{1,0:T(8,128)(2,1)S(1)}, bf16[128,1280]{1,0:T(8,128)(2,1)S(1)}, u32[]{:S(2)}, u32[]{:S(2)}) collective-permute-start(bf16[128,1280]{1,0:T(8,128)(2,1)S(1)} %add.68), channel_id=1, source_target_pairs={{96,0},{0,32},{32,64},{64,96},{97,1},{1,33},{33,65},{65,97},{98,2}... | collective-permute-start | bytes 983048 | tf_op jit(solution)/shard_map/ppermute | solution.py:23
  20.9 1.4 %collective-permute-start.4 = (bf16[128,1280]{1,0:T(8,128)(2,1)S(1)}, bf16[128,1280]{1,0:T(8,128)(2,1)S(1)}, u32[]{:S(2)}, u32[]{:S(2)}) collective-permute-start(bf16[128,1280]{1,0:T(8,128)(2,1)S(1)} %add.68), channel_id=1, source_target_pairs={{32,0},{64,32},{96,64},{0,96},{33,1},{65,33},{97,65},{1,97},{34,2}... | collective-permute-start | bytes 983048 | tf_op jit(solution)/shard_map/ppermute | solution.py:23
  22.3 1.5 %collective-permute-start.7 = (bf16[128,1280]{1,0:T(8,128)(2,1)S(1)}, bf16[128,1280]{1,0:T(8,128)(2,1)S(1)}, u32[]{:S(2)}, u32[]{:S(2)}) collective-permute-start(bf16[128,1280]{1,0:T(8,128)(2,1)S(1)} %add.68), channel_id=1, source_target_pairs={{8,0},{16,8},{24,16},{0,24},{9,1},{17,9},{25,17},{1,25},{10,2},{18... | collective-permute-start | bytes 983048 | tf_op jit(solution)/shard_map/ppermute | solution.py:23
  23.8 1.7 %collective-permute-done.5 = bf16[128,1280]{1,0:T(8,128)(2,1)S(1)} collective-permute-done((bf16[128,1280]{1,0:T(8,128)(2,1)S(1)}, bf16[128,1280]{1,0:T(8,128)(2,1)S(1)}, u32[]{:S(2)}, u32[]{:S(2)}) %collective-permute-start.5) | collective-permute-done | bytes 327712 | tf_op jit(solution)/shard_map/ppermute | solution.py:23
  25.5 1.3 %collective-permute-start.13 = (bf16[128,1280]{1,0:T(8,128)(2,1)S(1)}, bf16[128,1280]{1,0:T(8,128)(2,1)S(1)}, u32[]{:S(2)}, u32[]{:S(2)}) collective-permute-start(bf16[128,1280]{1,0:T(8,128)(2,1)S(1)} %collective-permute-done.5), channel_id=1, source_target_pairs={{96,0},{0,32},{32,64},{64,96},{97,1},{1,33},{33,65},{65,97},{98,2}... | collective-permute-start | bytes 983048 | tf_op jit(solution)/shard_map/ppermute | solution.py:23
  28.5 3.2 %collective-permute-start.22 = (bf16[1024,1024]{1,0:T(8,128)(2,1)S(1)}, bf16[1024,1024]{1,0:T(8,128)(2,1)S(1)}, u32[]{:S(2)}, u32[]{:S(2)}) collective-permute-start(bf16[1024,1024]{1,0:T(8,128)(2,1)S(1)} %constant_dynamic-update-slice_fusion.orb.slab_ref), channel_id=1, source_target_pairs={{2,0},{0,2},{3,1},{1,3},{6,4},{4,6},{7,5},{5,7},{10,8},{8,10},{11,... | collective-permute-start | bytes 6291464 | tf_op jit(solution)/shard_map/ppermute | solution.py:23
  31.7 1.2 collective-permute-start.11
  32.9 1.5 %collective-permute-start.6 = (bf16[128,1280]{1,0:T(8,128)(2,1)S(1)}, bf16[128,1280]{1,0:T(8,128)(2,1)S(1)}, u32[]{:S(2)}, u32[]{:S(2)}) collective-permute-start(bf16[128,1280]{1,0:T(8,128)(2,1)S(1)} %collective-permute-done.5), channel_id=1, source_target_pairs={{32,0},{64,32},{96,64},{0,96},{33,1},{65,33},{97,65},{1,97},{34,2}... | collective-permute-start | bytes 983048 | tf_op jit(solution)/shard_map/ppermute | solution.py:23
  34.4 1.5 %collective-permute-start.8 = (bf16[128,1280]{1,0:T(8,128)(2,1)S(1)}, bf16[128,1280]{1,0:T(8,128)(2,1)S(1)}, u32[]{:S(2)}, u32[]{:S(2)}) collective-permute-start(bf16[128,1280]{1,0:T(8,128)(2,1)S(1)} %collective-permute-done.5), channel_id=1, source_target_pairs={{8,0},{16,8},{24,16},{0,24},{9,1},{17,9},{25,17},{1,25},{10,2},{18... | collective-permute-start | bytes 983048 | tf_op jit(solution)/shard_map/ppermute | solution.py:23
  35.9 3.2 %collective-permute-done.11 = bf16[128,1280]{1,0:T(8,128)(2,1)S(1)} collective-permute-done((bf16[128,1280]{1,0:T(8,128)(2,1)S(1)}, bf16[128,1280]{1,0:T(8,128)(2,1)S(1)}, u32[]{:S(2)}, u32[]{:S(2)}) %collective-permute-start.11) | collective-permute-done | bytes 327712 | tf_op jit(solution)/shard_map/ppermute | solution.py:23
  39.2 1.3 %collective-permute-done.8 = bf16[128,1280]{1,0:T(8,128)(2,1)S(1)} collective-permute-done((bf16[128,1280]{1,0:T(8,128)(2,1)S(1)}, bf16[128,1280]{1,0:T(8,128)(2,1)S(1)}, u32[]{:S(2)}, u32[]{:S(2)}) %collective-permute-start.8) | collective-permute-done | bytes 327712 | tf_op jit(solution)/shard_map/ppermute | solution.py:23
  41.0 2.8 %collective-permute-start.9 = (bf16[384,1280]{1,0:T(8,128)(2,1)S(1)}, bf16[384,1280]{1,0:T(8,128)(2,1)S(1)}, u32[]{:S(2)}, u32[]{:S(2)}) collective-permute-start(bf16[384,1280]{1,0:T(8,128)(2,1)S(1)} %get-tuple-element.65), channel_id=1, source_target_pairs={{8,0},{16,8},{24,16},{0,24},{9,1},{17,9},{25,17},{1,25},{10,2},{18... | collective-permute-start | bytes 2949128 | tf_op jit(solution)/shard_map/ppermute | solution.py:23
  44.0 2.7 %collective-permute-start.14 = (bf16[384,1280]{1,0:T(8,128)(2,1)S(1)}, bf16[384,1280]{1,0:T(8,128)(2,1)S(1)}, u32[]{:S(2)}, u32[]{:S(2)}) collective-permute-start(bf16[384,1280]{1,0:T(8,128)(2,1)S(1)} %get-tuple-element.66), channel_id=1, source_target_pairs={{32,0},{64,32},{96,64},{0,96},{33,1},{65,33},{97,65},{1,97},{34,2}... | collective-permute-start | bytes 2949128 | tf_op jit(solution)/shard_map/ppermute | solution.py:23
  46.9 6.1 %apply.6.refs_12_ = f32[1024,256]{1,0:T(8,128)S(1)} custom-call(s32[22]{0:T(128)S(1)} %compare_select_fusion.10.table.t, bf16[1024,1024]{1,0:T(8,128)(2,1)S(1)} %constant_dynamic-update-slice_fusion.orb.slab_ref, bf16[256,1280]{1,0:T(8,128)(2,1)S(1)} %get-tuple-element.68.refs_0_, bf16[256,1280]{1,0:T(8,128)(2,1)S(1)} %get-tuple-element.69.refs_1_, ...), custom_call_target="tpu_custom_call" | custom-call | flops 838860800 | bytes 2621440 | tf_op jit(solution)/shard_map/apply/pallas_call | solution.py:101
  53.0 7.7 %collective-permute-done.9 = bf16[384,1280]{1,0:T(8,128)(2,1)S(1)} collective-permute-done((bf16[384,1280]{1,0:T(8,128)(2,1)S(1)}, bf16[384,1280]{1,0:T(8,128)(2,1)S(1)}, u32[]{:S(2)}, u32[]{:S(2)}) %collective-permute-start.9) | collective-permute-done | bytes 983072 | tf_op jit(solution)/shard_map/ppermute | solution.py:23
  61.2 2.7 %collective-permute-start.15 = (bf16[384,1280]{1,0:T(8,128)(2,1)S(1)}, bf16[384,1280]{1,0:T(8,128)(2,1)S(1)}, u32[]{:S(2)}, u32[]{:S(2)}) collective-permute-start(bf16[384,1280]{1,0:T(8,128)(2,1)S(1)} %pad_maximum_fusion.2), channel_id=1, source_target_pairs={{32,0},{64,32},{96,64},{0,96},{33,1},{65,33},{97,65},{1,97},{34,2}... | collective-permute-start | bytes 2949128 | tf_op jit(solution)/shard_map/ppermute | solution.py:23
  64.0 2.7 %collective-permute-start.21 = (bf16[256,1280]{1,0:T(8,128)(2,1)S(1)}, bf16[256,1280]{1,0:T(8,128)(2,1)S(1)}, u32[]{:S(2)}, u32[]{:S(2)}) collective-permute-start(bf16[256,1280]{1,0:T(8,128)(2,1)S(1)} %pad_maximum_fusion.11.refs_5_), channel_id=1, source_target_pairs={{16,0},{24,8},{0,16},{8,24},{17,1},{25,9},{1,17},{9,25},{18,2},{26... | collective-permute-start | bytes 1966088 | tf_op jit(solution)/shard_map/ppermute | solution.py:23
  67.4 5.8 %collective-permute-done.22.slab_ref = bf16[1024,1024]{1,0:T(8,128)(2,1)S(1)} collective-permute-done((bf16[1024,1024]{1,0:T(8,128)(2,1)S(1)}, bf16[1024,1024]{1,0:T(8,128)(2,1)S(1)}, u32[]{:S(2)}, u32[]{:S(2)}) %collective-permute-start.22) | collective-permute-done | bytes 2097184 | tf_op jit(solution)/shard_map/ppermute | solution.py:23
  74.6 6.1 %apply.7.refs_12_ = f32[1024,256]{1,0:T(8,128)S(1)} custom-call(s32[22]{0:T(128)S(1)} %compare_select_fusion.10.table.t, bf16[1024,1024]{1,0:T(8,128)(2,1)S(1)} %collective-permute-done.22.slab_ref, bf16[256,1280]{1,0:T(8,128)(2,1)S(1)} %get-tuple-element.68.refs_0_, bf16[256,1280]{1,0:T(8,128)(2,1)S(1)} %get-tuple-element.69.refs_1_, ...), custom_call_target="tpu_custom_call" | custom-call | flops 838860800 | bytes 2621440 | tf_op jit(solution)/shard_map/apply/pallas_call | solution.py:101
  80.7 6.9 %apply.8.refs_10_ = f32[1024,256]{1,0:T(8,128)S(1)} custom-call(s32[22]{0:T(128)S(1)} %compare_select_fusion.10.table.t, bf16[1024,1024]{1,0:T(8,128)(2,1)S(1)} %collective-permute-done.22.slab_ref, bf16[256,1280]{1,0:T(8,128)(2,1)S(1)} %slice.44.refs_0_, bf16[256,1280]{1,0:T(8,128)(2,1)S(1)} %slice.53.refs_1_, ...), custom_call_target="tpu_custom_call", output_to_operand_aliasing={{}: (14, {})} | custom-call | flops 1006632960 | bytes 3145728 | tf_op jit(solution)/shard_map/apply/pallas_call | solution.py:101
  87.6 6.9 %apply.9.refs_10_ = f32[1024,256]{1,0:T(8,128)S(1)} custom-call(s32[22]{0:T(128)S(1)} %compare_select_fusion.10.table.t, bf16[1024,1024]{1,0:T(8,128)(2,1)S(1)} %constant_dynamic-update-slice_fusion.orb.slab_ref, bf16[256,1280]{1,0:T(8,128)(2,1)S(1)} %slice.44.refs_0_, bf16[256,1280]{1,0:T(8,128)(2,1)S(1)} %slice.53.refs_1_, ...), custom_call_target="tpu_custom_call", output_to_operand_aliasing={{}: (14, {})} | custom-call | flops 1006632960 | bytes 3145728 | tf_op jit(solution)/shard_map/apply/pallas_call | solution.py:101
  94.6 6.1 %apply.10 = (f32[512,256]{1,0:T(8,128)S(1)}, bf16[512,256]{1,0:T(8,128)(2,1)S(1)}) custom-call(s32[22]{0:T(128)S(1)} %compare_select_fusion.10.table.t, bf16[1024,1024]{1,0:T(8,128)(2,1)S(1)} %collective-permute-done.22.slab_ref, bf16[384,1280]{1,0:T(8,128)(2,1)S(1)} %collective-permute-done.15.refs_0_, ...), custom_call_target="tpu_custom_call" | custom-call | flops 838860800 | bytes 2621440 | tf_op jit(solution)/shard_map/apply/pallas_call | solution.py:101
  100.7 7.9 %collective-permute-start.23 = (bf16[512,256]{1,0:T(8,128)(2,1)S(1)}, bf16[512,256]{1,0:T(8,128)(2,1)S(1)}, u32[]{:S(2)}, u32[]{:S(2)}) collective-permute-start(bf16[512,256]{1,0:T(8,128)(2,1)S(1)} %get-tuple-element.42), channel_id=1, source_target_pairs={{1,0},{0,1},{3,2},{2,3},{5,4},{4,5},{7,6},{6,7},{9,8},{8,9},{11,10... | collective-permute-start | bytes 786440 | tf_op jit(solution)/shard_map/ppermute | solution.py:23
  110.4 6.1 %apply.11 = (f32[512,256]{1,0:T(8,128)S(1)}, bf16[512,256]{1,0:T(8,128)(2,1)S(1)}) custom-call(s32[22]{0:T(128)S(1)} %compare_select_fusion.10.table.t, bf16[1024,1024]{1,0:T(8,128)(2,1)S(1)} %constant_dynamic-update-slice_fusion.orb.slab_ref, bf16[384,1280]{1,0:T(8,128)(2,1)S(1)} %collective-permute-done.15.refs_0_, ...), custom_call_target="tpu_custom_call" | custom-call | flops 838860800 | bytes 2621440 | tf_op jit(solution)/shard_map/apply/pallas_call | solution.py:101
  116.6 2.4 %collective-permute-done.24 = bf16[512,256]{1,0:T(8,128)(2,1)S(1)} collective-permute-done((bf16[512,256]{1,0:T(8,128)(2,1)S(1)}, bf16[512,256]{1,0:T(8,128)(2,1)S(1)}, u32[]{:S(2)}, u32[]{:S(2)}) %collective-permute-start.24) | collective-permute-done | bytes 262176 | tf_op jit(solution)/shard_map/ppermute | solution.py:23
  118.9 1.2 collective-permute-start.25
  (60 shorter events, 10.0 us)
Async XLA Ops:
  0.0 6.6 %copy-start.1 = (s32[1,128]{1,0:T(1,128)S(1)}, s32[1,128]{1,0:T(1,128)}, u32[]{:S(2)}) copy-start(s32[1,128]{1,0:T(1,128)} %param.6) | copy-start | bytes 1540
  0.0 6.6 %collective-permute-start = (bf16[512,1024]{1,0:T(8,128)(2,1)}, bf16[512,1024]{1,0:T(8,128)(2,1)S(1)}, u32[]{:S(2)}, u32[]{:S(2)}) collective-permute-start(bf16[512,1024]{1,0:T(8,128)(2,1)} %param.4), channel_id=1, source_target_pairs={{1,0},{0,1},{3,2},{2,3},{5,4},{4,5},{7,6},{6,7},{9,8},{8,9},{11,10... | collective-permute-start | bytes 3145736 | tf_op jit(solution)/shard_map/ppermute | solution.py:23
  1.4 5.3 %collective-permute-start.2 = (bf16[512,256]{1,0:T(8,128)(2,1)}, bf16[512,256]{1,0:T(8,128)(2,1)S(1)}, u32[]{:S(2)}, u32[]{:S(2)}) collective-permute-start(bf16[512,256]{1,0:T(8,128)(2,1)} %own_tgt.1), channel_id=1, source_target_pairs={{1,0},{0,1},{3,2},{2,3},{5,4},{4,5},{7,6},{6,7},{9,8},{8,9},{11,10... | collective-permute-start | bytes 786440 | tf_op jit(solution)/shard_map/ppermute | solution.py:23
  1.4 5.1 %collective-permute-start.1 = (s32[1,128]{1,0:T(1,128)}, s32[1,128]{1,0:T(1,128)S(1)}, u32[]{:S(2)}, u32[]{:S(2)}) collective-permute-start(s32[1,128]{1,0:T(1,128)} %param.6), channel_id=1, source_target_pairs={{2,0},{0,2},{3,1},{1,3},{6,4},{4,6},{7,5},{5,7},{10,8},{8,10},{11,... | collective-permute-start | bytes 1544 | tf_op jit(solution)/shard_map/ppermute | solution.py:23
  5.2 1.5 %copy-start = (bf16[512,256]{1,0:T(8,128)(2,1)S(1)}, bf16[512,256]{1,0:T(8,128)(2,1)}, u32[]{:S(2)}) copy-start(bf16[512,256]{1,0:T(8,128)(2,1)} %own_tgt.1) | copy-start | bytes 786436
  8.2 9.8 %collective-permute-start.3 = (bf16[128,1280]{1,0:T(8,128)(2,1)S(1)}, bf16[128,1280]{1,0:T(8,128)(2,1)S(1)}, u32[]{:S(2)}, u32[]{:S(2)}) collective-permute-start(bf16[128,1280]{1,0:T(8,128)(2,1)S(1)} %get-tuple-element.27), channel_id=1, source_target_pairs={{2,0},{0,2},{3,1},{1,3},{6,4},{4,6},{7,5},{5,7},{10,8},{8,10},{11,... | collective-permute-start | bytes 983048 | tf_op jit(solution)/shard_map/ppermute | solution.py:23
  18.1 7.4 %collective-permute-start.5 = (bf16[128,1280]{1,0:T(8,128)(2,1)S(1)}, bf16[128,1280]{1,0:T(8,128)(2,1)S(1)}, u32[]{:S(2)}, u32[]{:S(2)}) collective-permute-start(bf16[128,1280]{1,0:T(8,128)(2,1)S(1)} %add.68), channel_id=1, source_target_pairs={{4,0},{0,4},{5,1},{1,5},{6,2},{2,6},{7,3},{3,7},{12,8},{8,12},{13,... | collective-permute-start | bytes 983048 | tf_op jit(solution)/shard_map/ppermute | solution.py:23
  18.3 9.7 %collective-permute-start.12 = (bf16[128,1280]{1,0:T(8,128)(2,1)S(1)}, bf16[128,1280]{1,0:T(8,128)(2,1)S(1)}, u32[]{:S(2)}, u32[]{:S(2)}) collective-permute-start(bf16[128,1280]{1,0:T(8,128)(2,1)S(1)} %add.68), channel_id=1, source_target_pairs={{96,0},{0,32},{32,64},{64,96},{97,1},{1,33},{33,65},{65,97},{98,2}... | collective-permute-start | bytes 983048 | tf_op jit(solution)/shard_map/ppermute | solution.py:23
  19.7 8.4 %collective-permute-start.10 = (bf16[128,1280]{1,0:T(8,128)(2,1)S(1)}, bf16[128,1280]{1,0:T(8,128)(2,1)S(1)}, u32[]{:S(2)}, u32[]{:S(2)}) collective-permute-start(bf16[128,1280]{1,0:T(8,128)(2,1)S(1)} %add.68), channel_id=1, source_target_pairs={{24,0},{0,8},{8,16},{16,24},{25,1},{1,9},{9,17},{17,25},{26,2},{2,... | collective-permute-start | bytes 983048 | tf_op jit(solution)/shard_map/ppermute | solution.py:23
  20.9 7.2 %collective-permute-start.4 = (bf16[128,1280]{1,0:T(8,128)(2,1)S(1)}, bf16[128,1280]{1,0:T(8,128)(2,1)S(1)}, u32[]{:S(2)}, u32[]{:S(2)}) collective-permute-start(bf16[128,1280]{1,0:T(8,128)(2,1)S(1)} %add.68), channel_id=1, source_target_pairs={{32,0},{64,32},{96,64},{0,96},{33,1},{65,33},{97,65},{1,97},{34,2}... | collective-permute-start | bytes 983048 | tf_op jit(solution)/shard_map/ppermute | solution.py:23
  22.3 6.2 %collective-permute-start.7 = (bf16[128,1280]{1,0:T(8,128)(2,1)S(1)}, bf16[128,1280]{1,0:T(8,128)(2,1)S(1)}, u32[]{:S(2)}, u32[]{:S(2)}) collective-permute-start(bf16[128,1280]{1,0:T(8,128)(2,1)S(1)} %add.68), channel_id=1, source_target_pairs={{8,0},{16,8},{24,16},{0,24},{9,1},{17,9},{25,17},{1,25},{10,2},{18... | collective-permute-start | bytes 983048 | tf_op jit(solution)/shard_map/ppermute | solution.py:23
  25.5 10.4 %collective-permute-start.13 = (bf16[128,1280]{1,0:T(8,128)(2,1)S(1)}, bf16[128,1280]{1,0:T(8,128)(2,1)S(1)}, u32[]{:S(2)}, u32[]{:S(2)}) collective-permute-start(bf16[128,1280]{1,0:T(8,128)(2,1)S(1)} %collective-permute-done.5), channel_id=1, source_target_pairs={{96,0},{0,32},{32,64},{64,96},{97,1},{1,33},{33,65},{65,97},{98,2}... | collective-permute-start | bytes 983048 | tf_op jit(solution)/shard_map/ppermute | solution.py:23
  28.5 44.7 %collective-permute-start.22 = (bf16[1024,1024]{1,0:T(8,128)(2,1)S(1)}, bf16[1024,1024]{1,0:T(8,128)(2,1)S(1)}, u32[]{:S(2)}, u32[]{:S(2)}) collective-permute-start(bf16[1024,1024]{1,0:T(8,128)(2,1)S(1)} %constant_dynamic-update-slice_fusion.orb.slab_ref), channel_id=1, source_target_pairs={{2,0},{0,2},{3,1},{1,3},{6,4},{4,6},{7,5},{5,7},{10,8},{8,10},{11,... | collective-permute-start | bytes 6291464 | tf_op jit(solution)/shard_map/ppermute | solution.py:23
  31.7 7.4 %collective-permute-start.11 = (bf16[128,1280]{1,0:T(8,128)(2,1)S(1)}, bf16[128,1280]{1,0:T(8,128)(2,1)S(1)}, u32[]{:S(2)}, u32[]{:S(2)}) collective-permute-start(bf16[128,1280]{1,0:T(8,128)(2,1)S(1)} %collective-permute-done.5), channel_id=1, source_target_pairs={{24,0},{0,8},{8,16},{16,24},{25,1},{1,9},{9,17},{17,25},{26,2},{2,... | collective-permute-start | bytes 983048 | tf_op jit(solution)/shard_map/ppermute | solution.py:23
  32.9 6.3 %collective-permute-start.6 = (bf16[128,1280]{1,0:T(8,128)(2,1)S(1)}, bf16[128,1280]{1,0:T(8,128)(2,1)S(1)}, u32[]{:S(2)}, u32[]{:S(2)}) collective-permute-start(bf16[128,1280]{1,0:T(8,128)(2,1)S(1)} %collective-permute-done.5), channel_id=1, source_target_pairs={{32,0},{64,32},{96,64},{0,96},{33,1},{65,33},{97,65},{1,97},{34,2}... | collective-permute-start | bytes 983048 | tf_op jit(solution)/shard_map/ppermute | solution.py:23
  34.4 6.2 %collective-permute-start.8 = (bf16[128,1280]{1,0:T(8,128)(2,1)S(1)}, bf16[128,1280]{1,0:T(8,128)(2,1)S(1)}, u32[]{:S(2)}, u32[]{:S(2)}) collective-permute-start(bf16[128,1280]{1,0:T(8,128)(2,1)S(1)} %collective-permute-done.5), channel_id=1, source_target_pairs={{8,0},{16,8},{24,16},{0,24},{9,1},{17,9},{25,17},{1,25},{10,2},{18... | collective-permute-start | bytes 983048 | tf_op jit(solution)/shard_map/ppermute | solution.py:23
  41.0 19.7 %collective-permute-start.9 = (bf16[384,1280]{1,0:T(8,128)(2,1)S(1)}, bf16[384,1280]{1,0:T(8,128)(2,1)S(1)}, u32[]{:S(2)}, u32[]{:S(2)}) collective-permute-start(bf16[384,1280]{1,0:T(8,128)(2,1)S(1)} %get-tuple-element.65), channel_id=1, source_target_pairs={{8,0},{16,8},{24,16},{0,24},{9,1},{17,9},{25,17},{1,25},{10,2},{18... | collective-permute-start | bytes 2949128 | tf_op jit(solution)/shard_map/ppermute | solution.py:23
  43.8 17.0 %collective-permute-start.16 = (bf16[384,1280]{1,0:T(8,128)(2,1)S(1)}, bf16[384,1280]{1,0:T(8,128)(2,1)S(1)}, u32[]{:S(2)}, u32[]{:S(2)}) collective-permute-start(bf16[384,1280]{1,0:T(8,128)(2,1)S(1)} %get-tuple-element.67), channel_id=1, source_target_pairs={{24,0},{0,8},{8,16},{16,24},{25,1},{1,9},{9,17},{17,25},{26,2},{2,... | collective-permute-start | bytes 2949128 | tf_op jit(solution)/shard_map/ppermute | solution.py:23
  43.9 20.0 %collective-permute-start.20 = (bf16[384,1280]{1,0:T(8,128)(2,1)S(1)}, bf16[384,1280]{1,0:T(8,128)(2,1)S(1)}, u32[]{:S(2)}, u32[]{:S(2)}) collective-permute-start(bf16[384,1280]{1,0:T(8,128)(2,1)S(1)} %get-tuple-element.64), channel_id=1, source_target_pairs={{96,0},{0,32},{32,64},{64,96},{97,1},{1,33},{33,65},{65,97},{98,2}... | collective-permute-start | bytes 2949128 | tf_op jit(solution)/shard_map/ppermute | solution.py:23
  44.0 16.8 %collective-permute-start.14 = (bf16[384,1280]{1,0:T(8,128)(2,1)S(1)}, bf16[384,1280]{1,0:T(8,128)(2,1)S(1)}, u32[]{:S(2)}, u32[]{:S(2)}) collective-permute-start(bf16[384,1280]{1,0:T(8,128)(2,1)S(1)} %get-tuple-element.66), channel_id=1, source_target_pairs={{32,0},{64,32},{96,64},{0,96},{33,1},{65,33},{97,65},{1,97},{34,2}... | collective-permute-start | bytes 2949128 | tf_op jit(solution)/shard_map/ppermute | solution.py:23
  61.0 33.6 %collective-permute-start.17 = (bf16[384,1280]{1,0:T(8,128)(2,1)S(1)}, bf16[384,1280]{1,0:T(8,128)(2,1)S(1)}, u32[]{:S(2)}, u32[]{:S(2)}) collective-permute-start(bf16[384,1280]{1,0:T(8,128)(2,1)S(1)} %pad_maximum_fusion.4), channel_id=1, source_target_pairs={{96,0},{0,32},{32,64},{64,96},{97,1},{1,33},{33,65},{65,97},{98,2}... | collective-permute-start | bytes 2949128 | tf_op jit(solution)/shard_map/ppermute | solution.py:23
  61.2 33.4 %collective-permute-start.15 = (bf16[384,1280]{1,0:T(8,128)(2,1)S(1)}, bf16[384,1280]{1,0:T(8,128)(2,1)S(1)}, u32[]{:S(2)}, u32[]{:S(2)}) collective-permute-start(bf16[384,1280]{1,0:T(8,128)(2,1)S(1)} %pad_maximum_fusion.2), channel_id=1, source_target_pairs={{32,0},{64,32},{96,64},{0,96},{33,1},{65,33},{97,65},{1,97},{34,2}... | collective-permute-start | bytes 2949128 | tf_op jit(solution)/shard_map/ppermute | solution.py:23
  64.0 30.5 %collective-permute-start.21 = (bf16[256,1280]{1,0:T(8,128)(2,1)S(1)}, bf16[256,1280]{1,0:T(8,128)(2,1)S(1)}, u32[]{:S(2)}, u32[]{:S(2)}) collective-permute-start(bf16[256,1280]{1,0:T(8,128)(2,1)S(1)} %pad_maximum_fusion.11.refs_5_), channel_id=1, source_target_pairs={{16,0},{24,8},{0,16},{8,24},{17,1},{25,9},{1,17},{9,25},{18,2},{26... | collective-permute-start | bytes 1966088 | tf_op jit(solution)/shard_map/ppermute | solution.py:23
  66.7 27.8 %collective-permute-start.18 = (bf16[128,1280]{1,0:T(8,128)(2,1)S(1)}, bf16[128,1280]{1,0:T(8,128)(2,1)S(1)}, u32[]{:S(2)}, u32[]{:S(2)}) collective-permute-start(bf16[128,1280]{1,0:T(8,128)(2,1)S(1)} %get-tuple-element.50), channel_id=1, source_target_pairs={{8,0},{16,8},{24,16},{0,24},{9,1},{17,9},{25,17},{1,25},{10,2},{18... | collective-permute-start | bytes 983048 | tf_op jit(solution)/shard_map/ppermute | solution.py:23
  73.2 21.3 %collective-permute-start.19 = (bf16[128,1280]{1,0:T(8,128)(2,1)S(1)}, bf16[128,1280]{1,0:T(8,128)(2,1)S(1)}, u32[]{:S(2)}, u32[]{:S(2)}) collective-permute-start(bf16[128,1280]{1,0:T(8,128)(2,1)S(1)} %get-tuple-element.48), channel_id=1, source_target_pairs={{24,0},{0,8},{8,16},{16,24},{25,1},{1,9},{9,17},{17,25},{26,2},{2,... | collective-permute-start | bytes 983048 | tf_op jit(solution)/shard_map/ppermute | solution.py:23
  100.7 9.1 %collective-permute-start.23 = (bf16[512,256]{1,0:T(8,128)(2,1)S(1)}, bf16[512,256]{1,0:T(8,128)(2,1)S(1)}, u32[]{:S(2)}, u32[]{:S(2)}) collective-permute-start(bf16[512,256]{1,0:T(8,128)(2,1)S(1)} %get-tuple-element.42), channel_id=1, source_target_pairs={{1,0},{0,1},{3,2},{2,3},{5,4},{4,5},{7,6},{6,7},{9,8},{8,9},{11,10... | collective-permute-start | bytes 786440 | tf_op jit(solution)/shard_map/ppermute | solution.py:23
  109.8 9.1 %collective-permute-start.24 = (bf16[512,256]{1,0:T(8,128)(2,1)S(1)}, bf16[512,256]{1,0:T(8,128)(2,1)S(1)}, u32[]{:S(2)}, u32[]{:S(2)}) collective-permute-start(bf16[512,256]{1,0:T(8,128)(2,1)S(1)} %add_convert_fusion), channel_id=1, source_target_pairs={{2,0},{0,2},{3,1},{1,3},{6,4},{4,6},{7,5},{5,7},{10,8},{8,10},{11,... | collective-permute-start | bytes 786440 | tf_op jit(solution)/shard_map/ppermute | solution.py:23
  118.9 2.4 %collective-permute-start.25 = (bf16[512,256]{1,0:T(8,128)(2,1)S(1)}, bf16[512,256]{1,0:T(8,128)(2,1)S(1)}, u32[]{:S(2)}, u32[]{:S(2)}) collective-permute-start(bf16[512,256]{1,0:T(8,128)(2,1)S(1)} %get-tuple-element.46), channel_id=1, source_target_pairs={{1,0},{0,1},{3,2},{2,3},{5,4},{4,5},{7,6},{6,7},{9,8},{8,9},{11,10... | collective-permute-start | bytes 786440 | tf_op jit(solution)/shard_map/ppermute | solution.py:23

commit v9 on v8

--- a/solution.py
+++ b/solution.py
@@ -151,8 +151,10 @@
     own = {at: take_from(block, axis, side) for at, axis, side in NEXT}
     other = take_from(block, "zl", 1)
     far_slab = take_from(after(near_slab, *own.values()), "zh", 1)
-    pair = {at: in_order(own[at], take_from(other, axis, side)) for at, axis, side in NEXT}
-    pair[0, 0] = in_order(block, other)
+    pair = {(0, 0): in_order(block, other)}
+    other = after(other, *own.values())
+    for at, axis, side in NEXT:
+        pair[at] = in_order(own[at], take_from(other, axis, side))
 
     def joined(whole, half):
         return jnp.concatenate([pair[whole], half], axis=0)
@@ -179,8 +181,7 @@
         take_from(pair[1, 3][count:], "x", -1),
         take_from(pair[2, 0], "x", 2),
     ]
-    far = far_apply([pair[at] for at in first], first, None)
-    far = far_apply([pair[at] for at in second], second, far)
+    far = far_apply([pair[at] for at in first + second], first + second, None)
     near = near_apply([pair[at] for at in second], second, after(near, far))
     last, far, near = lax.optimization_barrier((last, far, near))
     kept, sent = far_apply(last, third, far, True)

time: 122 us -> 126 us (1.033)
  waiting for transfers between devices: 32.1 us -> 42.5 us
  starting transfers between devices: 44.8 us -> 39.8 us
  Pallas kernels: 39.7 us -> 37.6 us
    ppermute x26, waiting for transfers between devices: 32.1 us -> 42.5 us  [take_from(): return lax.ppermute(value, axis, [((i + side) % n, i) for i in range(n)])]
    ppermute x26, starting transfers between devices: 44.8 us -> 39.8 us  [take_from(): return lax.ppermute(value, axis, [((i + side) % n, i) for i in range(n)])]
    pallas_call x6 -> x5, Pallas kernels: 38.2 us -> 36.2 us  [apply_parts(): pl.pallas_call(body, out_shape=halves if last else jax.ShapeDtypeStruct((...]
  transfers between devices with their start and end apart: 26 -> 26, of which waited for: 10 -> 12; matrix products, arithmetic and copies ran while one was open for 3% -> 3% of each run, Pallas kernels for 26% -> 24%
where the time goes in v9:
time: 126 us; the launch traced here: 125 us
  waiting for transfers between devices  42.5 us (34%)
  starting transfers between devices  39.8 us (32%)
  Pallas kernels  37.6 us (30%)
  local copies, waits for them, and re-layouts  2.35 us (2%)
  other arithmetic  2.08 us (2%)
    ppermute x26, waiting for transfers between devices, take_from(): return lax.ppermute(value, axis, [((i + side) % n, i) for i in range(n)])  42.5 us
    ppermute x26, starting transfers between devices, take_from(): return lax.ppermute(value, axis, [((i + side) % n, i) for i in range(n)])  39.8 us
    pallas_call x5, Pallas kernels, apply_parts(): pl.pallas_call(body, out_shape=halves if last else jax.ShapeDtypeStruct((...  36.2 us
  transfers between devices with their start and end apart: 26, of which 12 were waited for; matrix products, arithmetic and copies ran while one was open for 3% of the time, Pallas kernels for 24%

profile of v9, /device:TPU:1, one launch (start us, length us, event | category | flops | bytes accessed | tf_op | source)
XLA Modules:
  0.0 125.4 jit_solution(9673421711648164628)
XLA Ops:
  0.0 1.4 %collective-permute-start = (bf16[512,1024]{1,0:T(8,128)(2,1)}, bf16[512,1024]{1,0:T(8,128)(2,1)S(1)}, u32[]{:S(2)}, u32[]{:S(2)}) collective-permute-start(bf16[512,1024]{1,0:T(8,128)(2,1)} %param.4), channel_id=1, source_target_pairs={{1,0},{0,1},{3,2},{2,3},{5,4},{4,5},{7,6},{6,7},{9,8},{8,9},{11,10... | collective-permute-start | bytes 3145736 | tf_op jit(solution)/shard_map/ppermute | solution.py:23
  1.4 3.8 %collective-permute-start.1 = (s32[1,128]{1,0:T(1,128)}, s32[1,128]{1,0:T(1,128)S(1)}, u32[]{:S(2)}, u32[]{:S(2)}) collective-permute-start(s32[1,128]{1,0:T(1,128)} %param.6), channel_id=1, source_target_pairs={{2,0},{0,2},{3,1},{1,3},{6,4},{4,6},{7,5},{5,7},{10,8},{8,10},{11,... | collective-permute-start | bytes 1544 | tf_op jit(solution)/shard_map/ppermute | solution.py:23
  5.2 1.3 %constant_dynamic-update-slice_fusion.1 = bf16[1024,1024]{1,0:T(8,128)(2,1)S(1)} fusion(bf16[512,1024]{1,0:T(8,128)(2,1)} %param.4), kind=kLoop, calls=%fused_computation.26 | loop fusion | bytes 2097152
  6.7 1.5 %pick.1 = (bf16[128,1280]{1,0:T(8,128)(2,1)S(1)}, bf16[128,1280]{1,0:T(8,128)(2,1)S(1)}) custom-call(s32[22]{0:T(128)S(1)} %compare_select_fusion.10.table.t, s32[2,128]{1,0:T(2,128)S(1)} %pad_add_fusion.ids, bf16[1024,1024]{1,0:T(8,128)(2,1)S(1)} %constant_dynamic-update-slice_fusion.orb.slab_ref, bf16[512,256]{1,0:T(8,128)(2,1)S(1)} %copy-done, ...), custom_call_target="tpu_custom_call" | custom-call | tf_op jit(solution)/shard_map/pick/pallas_call | solution.py:50
  8.2 2.7 %collective-permute-start.3 = (bf16[128,1280]{1,0:T(8,128)(2,1)S(1)}, bf16[128,1280]{1,0:T(8,128)(2,1)S(1)}, u32[]{:S(2)}, u32[]{:S(2)}) collective-permute-start(bf16[128,1280]{1,0:T(8,128)(2,1)S(1)} %get-tuple-element.28), channel_id=1, source_target_pairs={{2,0},{0,2},{3,1},{1,3},{6,4},{4,6},{7,5},{5,7},{10,8},{8,10},{11,... | collective-permute-start | bytes 983048 | tf_op jit(solution)/shard_map/ppermute | solution.py:23
  10.9 7.1 %collective-permute-done.3 = bf16[128,1280]{1,0:T(8,128)(2,1)S(1)} collective-permute-done((bf16[128,1280]{1,0:T(8,128)(2,1)S(1)}, bf16[128,1280]{1,0:T(8,128)(2,1)S(1)}, u32[]{:S(2)}, u32[]{:S(2)}) %collective-permute-start.3) | collective-permute-done | bytes 327712 | tf_op jit(solution)/shard_map/ppermute | solution.py:23
  18.1 2.8 %collective-permute-start.4 = (bf16[128,1280]{1,0:T(8,128)(2,1)S(1)}, bf16[128,1280]{1,0:T(8,128)(2,1)S(1)}, u32[]{:S(2)}, u32[]{:S(2)}) collective-permute-start(bf16[128,1280]{1,0:T(8,128)(2,1)S(1)} %add.68), channel_id=1, source_target_pairs={{32,0},{64,32},{96,64},{0,96},{33,1},{65,33},{97,65},{1,97},{34,2}... | collective-permute-start | bytes 983048 | tf_op jit(solution)/shard_map/ppermute | solution.py:23
  20.9 2.5 %collective-permute-start.6 = (bf16[128,1280]{1,0:T(8,128)(2,1)S(1)}, bf16[128,1280]{1,0:T(8,128)(2,1)S(1)}, u32[]{:S(2)}, u32[]{:S(2)}) collective-permute-start(bf16[128,1280]{1,0:T(8,128)(2,1)S(1)} %add.68), channel_id=1, source_target_pairs={{8,0},{16,8},{24,16},{0,24},{9,1},{17,9},{25,17},{1,25},{10,2},{18... | collective-permute-start | bytes 983048 | tf_op jit(solution)/shard_map/ppermute | solution.py:23
  23.6 2.5 %collective-permute-done.4 = bf16[128,1280]{1,0:T(8,128)(2,1)S(1)} collective-permute-done((bf16[128,1280]{1,0:T(8,128)(2,1)S(1)}, bf16[128,1280]{1,0:T(8,128)(2,1)S(1)}, u32[]{:S(2)}, u32[]{:S(2)}) %collective-permute-start.4) | collective-permute-done | bytes 327712 | tf_op jit(solution)/shard_map/ppermute | solution.py:23
  26.0 2.2 %collective-permute-done.6 = bf16[128,1280]{1,0:T(8,128)(2,1)S(1)} collective-permute-done((bf16[128,1280]{1,0:T(8,128)(2,1)S(1)}, bf16[128,1280]{1,0:T(8,128)(2,1)S(1)}, u32[]{:S(2)}, u32[]{:S(2)}) %collective-permute-start.6) | collective-permute-done | bytes 327712 | tf_op jit(solution)/shard_map/ppermute | solution.py:23
  28.2 3.1 %collective-permute-done.7 = bf16[128,1280]{1,0:T(8,128)(2,1)S(1)} collective-permute-done((bf16[128,1280]{1,0:T(8,128)(2,1)S(1)}, bf16[128,1280]{1,0:T(8,128)(2,1)S(1)}, u32[]{:S(2)}, u32[]{:S(2)}) %collective-permute-start.7) | collective-permute-done | bytes 327712 | tf_op jit(solution)/shard_map/ppermute | solution.py:23
  32.7 2.7 %collective-permute-start.9 = (bf16[128,1280]{1,0:T(8,128)(2,1)S(1)}, bf16[128,1280]{1,0:T(8,128)(2,1)S(1)}, u32[]{:S(2)}, u32[]{:S(2)}) collective-permute-start(bf16[128,1280]{1,0:T(8,128)(2,1)S(1)} %collective-permute-done.5), channel_id=1, source_target_pairs={{32,0},{64,32},{96,64},{0,96},{33,1},{65,33},{97,65},{1,97},{34,2}... | collective-permute-start | bytes 983048 | tf_op jit(solution)/shard_map/ppermute | solution.py:23
  35.4 2.6 %collective-permute-start.10 = (bf16[128,1280]{1,0:T(8,128)(2,1)S(1)}, bf16[128,1280]{1,0:T(8,128)(2,1)S(1)}, u32[]{:S(2)}, u32[]{:S(2)}) collective-permute-start(bf16[128,1280]{1,0:T(8,128)(2,1)S(1)} %collective-permute-done.5), channel_id=1, source_target_pairs={{8,0},{16,8},{24,16},{0,24},{9,1},{17,9},{25,17},{1,25},{10,2},{18... | collective-permute-start | bytes 983048 | tf_op jit(solution)/shard_map/ppermute | solution.py:23
  38.0 1.5 %collective-permute-start.22 = (bf16[1024,1024]{1,0:T(8,128)(2,1)S(1)}, bf16[1024,1024]{1,0:T(8,128)(2,1)S(1)}, u32[]{:S(2)}, u32[]{:S(2)}) collective-permute-start(bf16[1024,1024]{1,0:T(8,128)(2,1)S(1)} %constant_dynamic-update-slice_fusion.orb.slab_ref), channel_id=1, source_target_pairs={{2,0},{0,2},{3,1},{1,3},{6,4},{4,6},{7,5},{5,7},{10,8},{8,10},{11,... | collective-permute-start | bytes 6291464 | tf_op jit(solution)/shard_map/ppermute | solution.py:23
  40.2 1.8 %collective-permute-done.10 = bf16[128,1280]{1,0:T(8,128)(2,1)S(1)} collective-permute-done((bf16[128,1280]{1,0:T(8,128)(2,1)S(1)}, bf16[128,1280]{1,0:T(8,128)(2,1)S(1)}, u32[]{:S(2)}, u32[]{:S(2)}) %collective-permute-start.10) | collective-permute-done | bytes 327712 | tf_op jit(solution)/shard_map/ppermute | solution.py:23
  42.5 3.3 %collective-permute-start.11 = (bf16[384,1280]{1,0:T(8,128)(2,1)S(1)}, bf16[384,1280]{1,0:T(8,128)(2,1)S(1)}, u32[]{:S(2)}, u32[]{:S(2)}) collective-permute-start(bf16[384,1280]{1,0:T(8,128)(2,1)S(1)} %get-tuple-element.67), channel_id=1, source_target_pairs={{8,0},{16,8},{24,16},{0,24},{9,1},{17,9},{25,17},{1,25},{10,2},{18... | collective-permute-start | bytes 2949128 | tf_op jit(solution)/shard_map/ppermute | solution.py:23
  46.0 2.7 %collective-permute-start.14 = (bf16[384,1280]{1,0:T(8,128)(2,1)S(1)}, bf16[384,1280]{1,0:T(8,128)(2,1)S(1)}, u32[]{:S(2)}, u32[]{:S(2)}) collective-permute-start(bf16[384,1280]{1,0:T(8,128)(2,1)S(1)} %get-tuple-element.68), channel_id=1, source_target_pairs={{32,0},{64,32},{96,64},{0,96},{33,1},{65,33},{97,65},{1,97},{34,2}... | collective-permute-start | bytes 2949128 | tf_op jit(solution)/shard_map/ppermute | solution.py:23
  48.9 6.1 %apply.5.refs_12_ = f32[1024,256]{1,0:T(8,128)S(1)} custom-call(s32[22]{0:T(128)S(1)} %compare_select_fusion.10.table.t, bf16[1024,1024]{1,0:T(8,128)(2,1)S(1)} %constant_dynamic-update-slice_fusion.orb.slab_ref, bf16[256,1280]{1,0:T(8,128)(2,1)S(1)} %get-tuple-element.70.refs_0_, bf16[256,1280]{1,0:T(8,128)(2,1)S(1)} %get-tuple-element.71.refs_1_, ...), custom_call_target="tpu_custom_call" | custom-call | flops 838860800 | bytes 2621440 | tf_op jit(solution)/shard_map/apply/pallas_call | solution.py:101
  55.0 7.1 %collective-permute-done.11 = bf16[384,1280]{1,0:T(8,128)(2,1)S(1)} collective-permute-done((bf16[384,1280]{1,0:T(8,128)(2,1)S(1)}, bf16[384,1280]{1,0:T(8,128)(2,1)S(1)}, u32[]{:S(2)}, u32[]{:S(2)}) %collective-permute-start.11) | collective-permute-done | bytes 983072 | tf_op jit(solution)/shard_map/ppermute | solution.py:23
  62.2 2.4 %collective-permute-done.16 = bf16[384,1280]{1,0:T(8,128)(2,1)S(1)} collective-permute-done((bf16[384,1280]{1,0:T(8,128)(2,1)S(1)}, bf16[384,1280]{1,0:T(8,128)(2,1)S(1)}, u32[]{:S(2)}, u32[]{:S(2)}) %collective-permute-start.16) | collective-permute-done | bytes 983072 | tf_op jit(solution)/shard_map/ppermute | solution.py:23
  64.9 2.7 %collective-permute-start.15 = (bf16[384,1280]{1,0:T(8,128)(2,1)S(1)}, bf16[384,1280]{1,0:T(8,128)(2,1)S(1)}, u32[]{:S(2)}, u32[]{:S(2)}) collective-permute-start(bf16[384,1280]{1,0:T(8,128)(2,1)S(1)} %pad_maximum_fusion.2), channel_id=1, source_target_pairs={{32,0},{64,32},{96,64},{0,96},{33,1},{65,33},{97,65},{1,97},{34,2}... | collective-permute-start | bytes 2949128 | tf_op jit(solution)/shard_map/ppermute | solution.py:23
  68.7 1.3 %collective-permute-start.18 = (bf16[128,1280]{1,0:T(8,128)(2,1)S(1)}, bf16[128,1280]{1,0:T(8,128)(2,1)S(1)}, u32[]{:S(2)}, u32[]{:S(2)}) collective-permute-start(bf16[128,1280]{1,0:T(8,128)(2,1)S(1)} %get-tuple-element.52), channel_id=1, source_target_pairs={{8,0},{16,8},{24,16},{0,24},{9,1},{17,9},{25,17},{1,25},{10,2},{18... | collective-permute-start | bytes 983048 | tf_op jit(solution)/shard_map/ppermute | solution.py:23
  70.0 12.1 %collective-permute-done.22.slab_ref = bf16[1024,1024]{1,0:T(8,128)(2,1)S(1)} collective-permute-done((bf16[1024,1024]{1,0:T(8,128)(2,1)S(1)}, bf16[1024,1024]{1,0:T(8,128)(2,1)S(1)}, u32[]{:S(2)}, u32[]{:S(2)}) %collective-permute-start.22) | collective-permute-done | bytes 2097184 | tf_op jit(solution)/shard_map/ppermute | solution.py:23
  82.4 10.9 %apply.6.refs_10_ = f32[1024,256]{1,0:T(8,128)S(1)} custom-call(s32[22]{0:T(128)S(1)} %compare_select_fusion.10.table.t, bf16[1024,1024]{1,0:T(8,128)(2,1)S(1)} %collective-permute-done.22.slab_ref, bf16[256,1280]{1,0:T(8,128)(2,1)S(1)} %get-tuple-element.70.refs_0_, bf16[256,1280]{1,0:T(8,128)(2,1)S(1)} %get-tuple-element.71.refs_1_, ...), custom_call_target="tpu_custom_call" | custom-call | flops 1845493760 | bytes 5767168 | tf_op jit(solution)/shard_map/apply/pallas_call | solution.py:101
  93.3 6.9 %apply.7.refs_10_ = f32[1024,256]{1,0:T(8,128)S(1)} custom-call(s32[22]{0:T(128)S(1)} %compare_select_fusion.10.table.t, bf16[1024,1024]{1,0:T(8,128)(2,1)S(1)} %constant_dynamic-update-slice_fusion.orb.slab_ref, bf16[256,1280]{1,0:T(8,128)(2,1)S(1)} %slice.44.refs_5_.refs_0_, ...), custom_call_target="tpu_custom_call", output_to_operand_aliasing={{}: (14, {})} | custom-call | flops 1006632960 | bytes 3145728 | tf_op jit(solution)/shard_map/apply/pallas_call | solution.py:101
  100.3 6.1 %apply.8 = (f32[512,256]{1,0:T(8,128)S(1)}, bf16[512,256]{1,0:T(8,128)(2,1)S(1)}) custom-call(s32[22]{0:T(128)S(1)} %compare_select_fusion.10.table.t, bf16[1024,1024]{1,0:T(8,128)(2,1)S(1)} %collective-permute-done.22.slab_ref, bf16[384,1280]{1,0:T(8,128)(2,1)S(1)} %collective-permute-done.15.refs_0_, ...), custom_call_target="tpu_custom_call" | custom-call | flops 838860800 | bytes 2621440 | tf_op jit(solution)/shard_map/apply/pallas_call | solution.py:101
  106.4 5.5 %collective-permute-start.23 = (bf16[512,256]{1,0:T(8,128)(2,1)S(1)}, bf16[512,256]{1,0:T(8,128)(2,1)S(1)}, u32[]{:S(2)}, u32[]{:S(2)}) collective-permute-start(bf16[512,256]{1,0:T(8,128)(2,1)S(1)} %get-tuple-element.44), channel_id=1, source_target_pairs={{1,0},{0,1},{3,2},{2,3},{5,4},{4,5},{7,6},{6,7},{9,8},{8,9},{11,10... | collective-permute-start | bytes 786440 | tf_op jit(solution)/shard_map/ppermute | solution.py:23
  111.9 1.2 collective-permute-done.23
  113.1 1.6 %collective-permute-start.24 = (bf16[512,256]{1,0:T(8,128)(2,1)S(1)}, bf16[512,256]{1,0:T(8,128)(2,1)S(1)}, u32[]{:S(2)}, u32[]{:S(2)}) collective-permute-start(bf16[512,256]{1,0:T(8,128)(2,1)S(1)} %add_convert_fusion), channel_id=1, source_target_pairs={{2,0},{0,2},{3,1},{1,3},{6,4},{4,6},{7,5},{5,7},{10,8},{8,10},{11,... | collective-permute-start | bytes 786440 | tf_op jit(solution)/shard_map/ppermute | solution.py:23
  114.7 6.1 %apply.9 = (f32[512,256]{1,0:T(8,128)S(1)}, bf16[512,256]{1,0:T(8,128)(2,1)S(1)}) custom-call(s32[22]{0:T(128)S(1)} %compare_select_fusion.10.table.t, bf16[1024,1024]{1,0:T(8,128)(2,1)S(1)} %constant_dynamic-update-slice_fusion.orb.slab_ref, bf16[384,1280]{1,0:T(8,128)(2,1)S(1)} %collective-permute-done.15.refs_0_, ...), custom_call_target="tpu_custom_call" | custom-call | flops 838860800 | bytes 2621440 | tf_op jit(solution)/shard_map/apply/pallas_call | solution.py:101
  120.9 1.4 %collective-permute-done.24 = bf16[512,256]{1,0:T(8,128)(2,1)S(1)} collective-permute-done((bf16[512,256]{1,0:T(8,128)(2,1)S(1)}, bf16[512,256]{1,0:T(8,128)(2,1)S(1)}, u32[]{:S(2)}, u32[]{:S(2)}) %collective-permute-start.24) | collective-permute-done | bytes 262176 | tf_op jit(solution)/shard_map/ppermute | solution.py:23
  122.2 1.2 collective-permute-start.25
  (59 shorter events, 6.3 us)
Async XLA Ops:
  0.0 6.6 %copy-start.1 = (s32[1,128]{1,0:T(1,128)S(1)}, s32[1,128]{1,0:T(1,128)}, u32[]{:S(2)}) copy-start(s32[1,128]{1,0:T(1,128)} %param.6) | copy-start | bytes 1540
  0.0 6.6 %collective-permute-start = (bf16[512,1024]{1,0:T(8,128)(2,1)}, bf16[512,1024]{1,0:T(8,128)(2,1)S(1)}, u32[]{:S(2)}, u32[]{:S(2)}) collective-permute-start(bf16[512,1024]{1,0:T(8,128)(2,1)} %param.4), channel_id=1, source_target_pairs={{1,0},{0,1},{3,2},{2,3},{5,4},{4,5},{7,6},{6,7},{9,8},{8,9},{11,10... | collective-permute-start | bytes 3145736 | tf_op jit(solution)/shard_map/ppermute | solution.py:23
  1.4 5.3 %collective-permute-start.2 = (bf16[512,256]{1,0:T(8,128)(2,1)}, bf16[512,256]{1,0:T(8,128)(2,1)S(1)}, u32[]{:S(2)}, u32[]{:S(2)}) collective-permute-start(bf16[512,256]{1,0:T(8,128)(2,1)} %own_tgt.1), channel_id=1, source_target_pairs={{1,0},{0,1},{3,2},{2,3},{5,4},{4,5},{7,6},{6,7},{9,8},{8,9},{11,10... | collective-permute-start | bytes 786440 | tf_op jit(solution)/shard_map/ppermute | solution.py:23
  1.4 5.1 %collective-permute-start.1 = (s32[1,128]{1,0:T(1,128)}, s32[1,128]{1,0:T(1,128)S(1)}, u32[]{:S(2)}, u32[]{:S(2)}) collective-permute-start(s32[1,128]{1,0:T(1,128)} %param.6), channel_id=1, source_target_pairs={{2,0},{0,2},{3,1},{1,3},{6,4},{4,6},{7,5},{5,7},{10,8},{8,10},{11,... | collective-permute-start | bytes 1544 | tf_op jit(solution)/shard_map/ppermute | solution.py:23
  5.2 1.5 %copy-start = (bf16[512,256]{1,0:T(8,128)(2,1)S(1)}, bf16[512,256]{1,0:T(8,128)(2,1)}, u32[]{:S(2)}) copy-start(bf16[512,256]{1,0:T(8,128)(2,1)} %own_tgt.1) | copy-start | bytes 786436
  8.2 9.8 %collective-permute-start.3 = (bf16[128,1280]{1,0:T(8,128)(2,1)S(1)}, bf16[128,1280]{1,0:T(8,128)(2,1)S(1)}, u32[]{:S(2)}, u32[]{:S(2)}) collective-permute-start(bf16[128,1280]{1,0:T(8,128)(2,1)S(1)} %get-tuple-element.28), channel_id=1, source_target_pairs={{2,0},{0,2},{3,1},{1,3},{6,4},{4,6},{7,5},{5,7},{10,8},{8,10},{11,... | collective-permute-start | bytes 983048 | tf_op jit(solution)/shard_map/ppermute | solution.py:23
  18.1 7.9 %collective-permute-start.4 = (bf16[128,1280]{1,0:T(8,128)(2,1)S(1)}, bf16[128,1280]{1,0:T(8,128)(2,1)S(1)}, u32[]{:S(2)}, u32[]{:S(2)}) collective-permute-start(bf16[128,1280]{1,0:T(8,128)(2,1)S(1)} %add.68), channel_id=1, source_target_pairs={{32,0},{64,32},{96,64},{0,96},{33,1},{65,33},{97,65},{1,97},{34,2}... | collective-permute-start | bytes 983048 | tf_op jit(solution)/shard_map/ppermute | solution.py:23
  20.9 7.3 %collective-permute-start.6 = (bf16[128,1280]{1,0:T(8,128)(2,1)S(1)}, bf16[128,1280]{1,0:T(8,128)(2,1)S(1)}, u32[]{:S(2)}, u32[]{:S(2)}) collective-permute-start(bf16[128,1280]{1,0:T(8,128)(2,1)S(1)} %add.68), channel_id=1, source_target_pairs={{8,0},{16,8},{24,16},{0,24},{9,1},{17,9},{25,17},{1,25},{10,2},{18... | collective-permute-start | bytes 983048 | tf_op jit(solution)/shard_map/ppermute | solution.py:23
  23.4 8.0 %collective-permute-start.7 = (bf16[128,1280]{1,0:T(8,128)(2,1)S(1)}, bf16[128,1280]{1,0:T(8,128)(2,1)S(1)}, u32[]{:S(2)}, u32[]{:S(2)}) collective-permute-start(bf16[128,1280]{1,0:T(8,128)(2,1)S(1)} %add.68), channel_id=1, source_target_pairs={{24,0},{0,8},{8,16},{16,24},{25,1},{1,9},{9,17},{17,25},{26,2},{2,... | collective-permute-start | bytes 983048 | tf_op jit(solution)/shard_map/ppermute | solution.py:23
  23.4 8.0 %collective-permute-start.8 = (bf16[128,1280]{1,0:T(8,128)(2,1)S(1)}, bf16[128,1280]{1,0:T(8,128)(2,1)S(1)}, u32[]{:S(2)}, u32[]{:S(2)}) collective-permute-start(bf16[128,1280]{1,0:T(8,128)(2,1)S(1)} %add.68), channel_id=1, source_target_pairs={{96,0},{0,32},{32,64},{64,96},{97,1},{1,33},{33,65},{65,97},{98,2}... | collective-permute-start | bytes 983048 | tf_op jit(solution)/shard_map/ppermute | solution.py:23
  23.4 8.0 %collective-permute-start.5 = (bf16[128,1280]{1,0:T(8,128)(2,1)S(1)}, bf16[128,1280]{1,0:T(8,128)(2,1)S(1)}, u32[]{:S(2)}, u32[]{:S(2)}) collective-permute-start(bf16[128,1280]{1,0:T(8,128)(2,1)S(1)} %add.68), channel_id=1, source_target_pairs={{4,0},{0,4},{5,1},{1,5},{6,2},{2,6},{7,3},{3,7},{12,8},{8,12},{13,... | collective-permute-start | bytes 983048 | tf_op jit(solution)/shard_map/ppermute | solution.py:23
  31.4 8.2 %collective-permute-start.13 = (bf16[128,1280]{1,0:T(8,128)(2,1)S(1)}, bf16[128,1280]{1,0:T(8,128)(2,1)S(1)}, u32[]{:S(2)}, u32[]{:S(2)}) collective-permute-start(bf16[128,1280]{1,0:T(8,128)(2,1)S(1)} %collective-permute-done.5), channel_id=1, source_target_pairs={{96,0},{0,32},{32,64},{64,96},{97,1},{1,33},{33,65},{65,97},{98,2}... | collective-permute-start | bytes 983048 | tf_op jit(solution)/shard_map/ppermute | solution.py:23
  32.6 7.5 %collective-permute-start.12 = (bf16[128,1280]{1,0:T(8,128)(2,1)S(1)}, bf16[128,1280]{1,0:T(8,128)(2,1)S(1)}, u32[]{:S(2)}, u32[]{:S(2)}) collective-permute-start(bf16[128,1280]{1,0:T(8,128)(2,1)S(1)} %collective-permute-done.5), channel_id=1, source_target_pairs={{24,0},{0,8},{8,16},{16,24},{25,1},{1,9},{9,17},{17,25},{26,2},{2,... | collective-permute-start | bytes 983048 | tf_op jit(solution)/shard_map/ppermute | solution.py:23
  32.7 7.5 %collective-permute-start.9 = (bf16[128,1280]{1,0:T(8,128)(2,1)S(1)}, bf16[128,1280]{1,0:T(8,128)(2,1)S(1)}, u32[]{:S(2)}, u32[]{:S(2)}) collective-permute-start(bf16[128,1280]{1,0:T(8,128)(2,1)S(1)} %collective-permute-done.5), channel_id=1, source_target_pairs={{32,0},{64,32},{96,64},{0,96},{33,1},{65,33},{97,65},{1,97},{34,2}... | collective-permute-start | bytes 983048 | tf_op jit(solution)/shard_map/ppermute | solution.py:23
  35.4 6.6 %collective-permute-start.10 = (bf16[128,1280]{1,0:T(8,128)(2,1)S(1)}, bf16[128,1280]{1,0:T(8,128)(2,1)S(1)}, u32[]{:S(2)}, u32[]{:S(2)}) collective-permute-start(bf16[128,1280]{1,0:T(8,128)(2,1)S(1)} %collective-permute-done.5), channel_id=1, source_target_pairs={{8,0},{16,8},{24,16},{0,24},{9,1},{17,9},{25,17},{1,25},{10,2},{18... | collective-permute-start | bytes 983048 | tf_op jit(solution)/shard_map/ppermute | solution.py:23
  38.0 44.2 %collective-permute-start.22 = (bf16[1024,1024]{1,0:T(8,128)(2,1)S(1)}, bf16[1024,1024]{1,0:T(8,128)(2,1)S(1)}, u32[]{:S(2)}, u32[]{:S(2)}) collective-permute-start(bf16[1024,1024]{1,0:T(8,128)(2,1)S(1)} %constant_dynamic-update-slice_fusion.orb.slab_ref), channel_id=1, source_target_pairs={{2,0},{0,2},{3,1},{1,3},{6,4},{4,6},{7,5},{5,7},{10,8},{8,10},{11,... | collective-permute-start | bytes 6291464 | tf_op jit(solution)/shard_map/ppermute | solution.py:23
  42.5 19.6 %collective-permute-start.11 = (bf16[384,1280]{1,0:T(8,128)(2,1)S(1)}, bf16[384,1280]{1,0:T(8,128)(2,1)S(1)}, u32[]{:S(2)}, u32[]{:S(2)}) collective-permute-start(bf16[384,1280]{1,0:T(8,128)(2,1)S(1)} %get-tuple-element.67), channel_id=1, source_target_pairs={{8,0},{16,8},{24,16},{0,24},{9,1},{17,9},{25,17},{1,25},{10,2},{18... | collective-permute-start | bytes 2949128 | tf_op jit(solution)/shard_map/ppermute | solution.py:23
  45.9 18.7 %collective-permute-start.16 = (bf16[384,1280]{1,0:T(8,128)(2,1)S(1)}, bf16[384,1280]{1,0:T(8,128)(2,1)S(1)}, u32[]{:S(2)}, u32[]{:S(2)}) collective-permute-start(bf16[384,1280]{1,0:T(8,128)(2,1)S(1)} %get-tuple-element.69), channel_id=1, source_target_pairs={{24,0},{0,8},{8,16},{16,24},{25,1},{1,9},{9,17},{17,25},{26,2},{2,... | collective-permute-start | bytes 2949128 | tf_op jit(solution)/shard_map/ppermute | solution.py:23
  45.9 21.7 %collective-permute-start.20 = (bf16[384,1280]{1,0:T(8,128)(2,1)S(1)}, bf16[384,1280]{1,0:T(8,128)(2,1)S(1)}, u32[]{:S(2)}, u32[]{:S(2)}) collective-permute-start(bf16[384,1280]{1,0:T(8,128)(2,1)S(1)} %get-tuple-element.66), channel_id=1, source_target_pairs={{96,0},{0,32},{32,64},{64,96},{97,1},{1,33},{33,65},{65,97},{98,2}... | collective-permute-start | bytes 2949128 | tf_op jit(solution)/shard_map/ppermute | solution.py:23
  46.0 18.6 %collective-permute-start.14 = (bf16[384,1280]{1,0:T(8,128)(2,1)S(1)}, bf16[384,1280]{1,0:T(8,128)(2,1)S(1)}, u32[]{:S(2)}, u32[]{:S(2)}) collective-permute-start(bf16[384,1280]{1,0:T(8,128)(2,1)S(1)} %get-tuple-element.68), channel_id=1, source_target_pairs={{32,0},{64,32},{96,64},{0,96},{33,1},{65,33},{97,65},{1,97},{34,2}... | collective-permute-start | bytes 2949128 | tf_op jit(solution)/shard_map/ppermute | solution.py:23
  64.7 35.6 %collective-permute-start.17 = (bf16[384,1280]{1,0:T(8,128)(2,1)S(1)}, bf16[384,1280]{1,0:T(8,128)(2,1)S(1)}, u32[]{:S(2)}, u32[]{:S(2)}) collective-permute-start(bf16[384,1280]{1,0:T(8,128)(2,1)S(1)} %pad_maximum_fusion.4), channel_id=1, source_target_pairs={{96,0},{0,32},{32,64},{64,96},{97,1},{1,33},{33,65},{65,97},{98,2}... | collective-permute-start | bytes 2949128 | tf_op jit(solution)/shard_map/ppermute | solution.py:23
  64.9 35.3 %collective-permute-start.15 = (bf16[384,1280]{1,0:T(8,128)(2,1)S(1)}, bf16[384,1280]{1,0:T(8,128)(2,1)S(1)}, u32[]{:S(2)}, u32[]{:S(2)}) collective-permute-start(bf16[384,1280]{1,0:T(8,128)(2,1)S(1)} %pad_maximum_fusion.2), channel_id=1, source_target_pairs={{32,0},{64,32},{96,64},{0,96},{33,1},{65,33},{97,65},{1,97},{34,2}... | collective-permute-start | bytes 2949128 | tf_op jit(solution)/shard_map/ppermute | solution.py:23
  67.7 32.5 %collective-permute-start.21 = (bf16[256,1280]{1,0:T(8,128)(2,1)S(1)}, bf16[256,1280]{1,0:T(8,128)(2,1)S(1)}, u32[]{:S(2)}, u32[]{:S(2)}) collective-permute-start(bf16[256,1280]{1,0:T(8,128)(2,1)S(1)} %pad_maximum_fusion.11.refs_10_.refs_5_), channel_id=1, source_target_pairs={{16,0},{24,8},{0,16},{8,24},{17,1},{25,9},{1,17},{9,25},{18,2},{26... | collective-permute-start | bytes 1966088 | tf_op jit(solution)/shard_map/ppermute | solution.py:23
  68.7 31.5 %collective-permute-start.18 = (bf16[128,1280]{1,0:T(8,128)(2,1)S(1)}, bf16[128,1280]{1,0:T(8,128)(2,1)S(1)}, u32[]{:S(2)}, u32[]{:S(2)}) collective-permute-start(bf16[128,1280]{1,0:T(8,128)(2,1)S(1)} %get-tuple-element.52), channel_id=1, source_target_pairs={{8,0},{16,8},{24,16},{0,24},{9,1},{17,9},{25,17},{1,25},{10,2},{18... | collective-permute-start | bytes 983048 | tf_op jit(solution)/shard_map/ppermute | solution.py:23
  82.2 18.1 %collective-permute-start.19 = (bf16[128,1280]{1,0:T(8,128)(2,1)S(1)}, bf16[128,1280]{1,0:T(8,128)(2,1)S(1)}, u32[]{:S(2)}, u32[]{:S(2)}) collective-permute-start(bf16[128,1280]{1,0:T(8,128)(2,1)S(1)} %get-tuple-element.50), channel_id=1, source_target_pairs={{24,0},{0,8},{8,16},{16,24},{25,1},{1,9},{9,17},{17,25},{26,2},{2,... | collective-permute-start | bytes 983048 | tf_op jit(solution)/shard_map/ppermute | solution.py:23
  106.4 6.6 %collective-permute-start.23 = (bf16[512,256]{1,0:T(8,128)(2,1)S(1)}, bf16[512,256]{1,0:T(8,128)(2,1)S(1)}, u32[]{:S(2)}, u32[]{:S(2)}) collective-permute-start(bf16[512,256]{1,0:T(8,128)(2,1)S(1)} %get-tuple-element.44), channel_id=1, source_target_pairs={{1,0},{0,1},{3,2},{2,3},{5,4},{4,5},{7,6},{6,7},{9,8},{8,9},{11,10... | collective-permute-start | bytes 786440 | tf_op jit(solution)/shard_map/ppermute | solution.py:23
  113.1 9.1 %collective-permute-start.24 = (bf16[512,256]{1,0:T(8,128)(2,1)S(1)}, bf16[512,256]{1,0:T(8,128)(2,1)S(1)}, u32[]{:S(2)}, u32[]{:S(2)}) collective-permute-start(bf16[512,256]{1,0:T(8,128)(2,1)S(1)} %add_convert_fusion), channel_id=1, source_target_pairs={{2,0},{0,2},{3,1},{1,3},{6,4},{4,6},{7,5},{5,7},{10,8},{8,10},{11,... | collective-permute-start | bytes 786440 | tf_op jit(solution)/shard_map/ppermute | solution.py:23
  122.2 2.4 %collective-permute-start.25 = (bf16[512,256]{1,0:T(8,128)(2,1)S(1)}, bf16[512,256]{1,0:T(8,128)(2,1)S(1)}, u32[]{:S(2)}, u32[]{:S(2)}) collective-permute-start(bf16[512,256]{1,0:T(8,128)(2,1)S(1)} %get-tuple-element.48), channel_id=1, source_target_pairs={{1,0},{0,1},{3,2},{2,3},{5,4},{4,5},{7,6},{6,7},{9,8},{8,9},{11,10... | collective-permute-start | bytes 786440 | tf_op jit(solution)/shard_map/ppermute | solution.py:23

commit v10 on v9

--- a/solution.py
+++ b/solution.py
@@ -178,11 +178,13 @@
         take_from(jnp.concatenate([pair[1, 1], pair[1, 3][:count]], axis=0), "y", 1),
         take_from(jnp.concatenate([pair[3, 3][count:], pair[0, 2]], axis=0), "y", -1),
         take_from(pair[1, 1][:count], "x", 1),
-        take_from(pair[1, 3][count:], "x", -1),
+        pair[1, 3][count:],
         take_from(pair[2, 0], "x", 2),
     ]
+    near = near_apply([pair[at] for at in second], second, near)
+    last[3] = take_from(after(last[3], near), "x", -1)
+    far_slab = after(far_slab, near)
     far = far_apply([pair[at] for at in first + second], first + second, None)
-    near = near_apply([pair[at] for at in second], second, after(near, far))
     last, far, near = lax.optimization_barrier((last, far, near))
     kept, sent = far_apply(last, third, far, True)
     far = (kept + take_from(sent, "c", 1)).astype(jnp.bfloat16)

time: 126 us -> 124 us (0.984)
  waiting for transfers between devices: 42.5 us -> 38.4 us
  starting transfers between devices: 39.8 us -> 42 us
    ppermute x26, waiting for transfers between devices: 42.5 us -> 38.4 us  [take_from(): return lax.ppermute(value, axis, [((i + side) % n, i) for i in range(n)])]
    ppermute x26, starting transfers between devices: 39.8 us -> 42 us  [take_from(): return lax.ppermute(value, axis, [((i + side) % n, i) for i in range(n)])]
  transfers between devices with their start and end apart: 26 -> 26, of which waited for: 12 -> 13; matrix products, arithmetic and copies ran while one was open for 3% -> 3% of each run, Pallas kernels for 24% -> 24%
where the time goes in v10:
time: 124 us; the launch traced here: 123 us
  starting transfers between devices  42 us (34%)
  waiting for transfers between devices  38.4 us (31%)
  Pallas kernels  37.6 us (30%)
  local copies, waits for them, and re-layouts  2.35 us (2%)
  other arithmetic  2.05 us (2%)
    ppermute x26, starting transfers between devices, take_from(): return lax.ppermute(value, axis, [((i + side) % n, i) for i in range(n)])  42 us
    ppermute x26, waiting for transfers between devices, take_from(): return lax.ppermute(value, axis, [((i + side) % n, i) for i in range(n)])  38.4 us
    pallas_call x5, Pallas kernels, apply_parts(): pl.pallas_call(body, out_shape=halves if last else jax.ShapeDtypeStruct((...  36.1 us
  transfers between devices with their start and end apart: 26, of which 13 were waited for; matrix products, arithmetic and copies ran while one was open for 3% of the time, Pallas kernels for 24%

profile of v10, /device:TPU:1, one launch (start us, length us, event | category | flops | bytes accessed | tf_op | source)
XLA Modules:
  0.0 123.4 jit_solution(16343667130107115911)
XLA Ops:
  0.0 1.4 %collective-permute-start = (bf16[512,1024]{1,0:T(8,128)(2,1)}, bf16[512,1024]{1,0:T(8,128)(2,1)S(1)}, u32[]{:S(2)}, u32[]{:S(2)}) collective-permute-start(bf16[512,1024]{1,0:T(8,128)(2,1)} %param.4), channel_id=1, source_target_pairs={{1,0},{0,1},{3,2},{2,3},{5,4},{4,5},{7,6},{6,7},{9,8},{8,9},{11,10... | collective-permute-start | bytes 3145736 | tf_op jit(solution)/shard_map/ppermute | solution.py:23
  1.4 3.8 %collective-permute-start.1 = (s32[1,128]{1,0:T(1,128)}, s32[1,128]{1,0:T(1,128)S(1)}, u32[]{:S(2)}, u32[]{:S(2)}) collective-permute-start(s32[1,128]{1,0:T(1,128)} %param.6), channel_id=1, source_target_pairs={{2,0},{0,2},{3,1},{1,3},{6,4},{4,6},{7,5},{5,7},{10,8},{8,10},{11,... | collective-permute-start | bytes 1544 | tf_op jit(solution)/shard_map/ppermute | solution.py:23
  5.2 1.3 %constant_dynamic-update-slice_fusion.1 = bf16[1024,1024]{1,0:T(8,128)(2,1)S(1)} fusion(bf16[512,1024]{1,0:T(8,128)(2,1)} %param.4), kind=kLoop, calls=%fused_computation.26 | loop fusion | bytes 2097152
  6.7 1.5 %pick.1 = (bf16[128,1280]{1,0:T(8,128)(2,1)S(1)}, bf16[128,1280]{1,0:T(8,128)(2,1)S(1)}) custom-call(s32[22]{0:T(128)S(1)} %compare_select_fusion.10.table.t, s32[2,128]{1,0:T(2,128)S(1)} %pad_add_fusion.ids, bf16[1024,1024]{1,0:T(8,128)(2,1)S(1)} %constant_dynamic-update-slice_fusion.orb.slab_ref, bf16[512,256]{1,0:T(8,128)(2,1)S(1)} %copy-done, ...), custom_call_target="tpu_custom_call" | custom-call | tf_op jit(solution)/shard_map/pick/pallas_call | solution.py:50
  8.2 2.7 %collective-permute-start.3 = (bf16[128,1280]{1,0:T(8,128)(2,1)S(1)}, bf16[128,1280]{1,0:T(8,128)(2,1)S(1)}, u32[]{:S(2)}, u32[]{:S(2)}) collective-permute-start(bf16[128,1280]{1,0:T(8,128)(2,1)S(1)} %get-tuple-element.29), channel_id=1, source_target_pairs={{2,0},{0,2},{3,1},{1,3},{6,4},{4,6},{7,5},{5,7},{10,8},{8,10},{11,... | collective-permute-start | bytes 983048 | tf_op jit(solution)/shard_map/ppermute | solution.py:23
  10.9 7.1 %collective-permute-done.3 = bf16[128,1280]{1,0:T(8,128)(2,1)S(1)} collective-permute-done((bf16[128,1280]{1,0:T(8,128)(2,1)S(1)}, bf16[128,1280]{1,0:T(8,128)(2,1)S(1)}, u32[]{:S(2)}, u32[]{:S(2)}) %collective-permute-start.3) | collective-permute-done | bytes 327712 | tf_op jit(solution)/shard_map/ppermute | solution.py:23
  18.1 2.8 %collective-permute-start.4 = (bf16[128,1280]{1,0:T(8,128)(2,1)S(1)}, bf16[128,1280]{1,0:T(8,128)(2,1)S(1)}, u32[]{:S(2)}, u32[]{:S(2)}) collective-permute-start(bf16[128,1280]{1,0:T(8,128)(2,1)S(1)} %add.68), channel_id=1, source_target_pairs={{32,0},{64,32},{96,64},{0,96},{33,1},{65,33},{97,65},{1,97},{34,2}... | collective-permute-start | bytes 983048 | tf_op jit(solution)/shard_map/ppermute | solution.py:23
  20.9 2.5 %collective-permute-start.6 = (bf16[128,1280]{1,0:T(8,128)(2,1)S(1)}, bf16[128,1280]{1,0:T(8,128)(2,1)S(1)}, u32[]{:S(2)}, u32[]{:S(2)}) collective-permute-start(bf16[128,1280]{1,0:T(8,128)(2,1)S(1)} %add.68), channel_id=1, source_target_pairs={{8,0},{16,8},{24,16},{0,24},{9,1},{17,9},{25,17},{1,25},{10,2},{18... | collective-permute-start | bytes 983048 | tf_op jit(solution)/shard_map/ppermute | solution.py:23
  23.6 2.5 %collective-permute-done.4 = bf16[128,1280]{1,0:T(8,128)(2,1)S(1)} collective-permute-done((bf16[128,1280]{1,0:T(8,128)(2,1)S(1)}, bf16[128,1280]{1,0:T(8,128)(2,1)S(1)}, u32[]{:S(2)}, u32[]{:S(2)}) %collective-permute-start.4) | collective-permute-done | bytes 327712 | tf_op jit(solution)/shard_map/ppermute | solution.py:23
  26.0 2.2 %collective-permute-done.6 = bf16[128,1280]{1,0:T(8,128)(2,1)S(1)} collective-permute-done((bf16[128,1280]{1,0:T(8,128)(2,1)S(1)}, bf16[128,1280]{1,0:T(8,128)(2,1)S(1)}, u32[]{:S(2)}, u32[]{:S(2)}) %collective-permute-start.6) | collective-permute-done | bytes 327712 | tf_op jit(solution)/shard_map/ppermute | solution.py:23
  28.2 3.1 %collective-permute-done.7 = bf16[128,1280]{1,0:T(8,128)(2,1)S(1)} collective-permute-done((bf16[128,1280]{1,0:T(8,128)(2,1)S(1)}, bf16[128,1280]{1,0:T(8,128)(2,1)S(1)}, u32[]{:S(2)}, u32[]{:S(2)}) %collective-permute-start.7) | collective-permute-done | bytes 327712 | tf_op jit(solution)/shard_map/ppermute | solution.py:23
  32.7 2.7 %collective-permute-start.9 = (bf16[128,1280]{1,0:T(8,128)(2,1)S(1)}, bf16[128,1280]{1,0:T(8,128)(2,1)S(1)}, u32[]{:S(2)}, u32[]{:S(2)}) collective-permute-start(bf16[128,1280]{1,0:T(8,128)(2,1)S(1)} %collective-permute-done.5), channel_id=1, source_target_pairs={{32,0},{64,32},{96,64},{0,96},{33,1},{65,33},{97,65},{1,97},{34,2}... | collective-permute-start | bytes 983048 | tf_op jit(solution)/shard_map/ppermute | solution.py:23
  35.4 2.6 %collective-permute-start.10 = (bf16[128,1280]{1,0:T(8,128)(2,1)S(1)}, bf16[128,1280]{1,0:T(8,128)(2,1)S(1)}, u32[]{:S(2)}, u32[]{:S(2)}) collective-permute-start(bf16[128,1280]{1,0:T(8,128)(2,1)S(1)} %collective-permute-done.5), channel_id=1, source_target_pairs={{8,0},{16,8},{24,16},{0,24},{9,1},{17,9},{25,17},{1,25},{10,2},{18... | collective-permute-start | bytes 983048 | tf_op jit(solution)/shard_map/ppermute | solution.py:23
  38.0 1.5 %collective-permute-start.22 = (bf16[1024,1024]{1,0:T(8,128)(2,1)S(1)}, bf16[1024,1024]{1,0:T(8,128)(2,1)S(1)}, u32[]{:S(2)}, u32[]{:S(2)}) collective-permute-start(bf16[1024,1024]{1,0:T(8,128)(2,1)S(1)} %constant_dynamic-update-slice_fusion.orb.slab_ref), channel_id=1, source_target_pairs={{2,0},{0,2},{3,1},{1,3},{6,4},{4,6},{7,5},{5,7},{10,8},{8,10},{11,... | collective-permute-start | bytes 6291464 | tf_op jit(solution)/shard_map/ppermute | solution.py:23
  40.2 1.8 %collective-permute-done.10 = bf16[128,1280]{1,0:T(8,128)(2,1)S(1)} collective-permute-done((bf16[128,1280]{1,0:T(8,128)(2,1)S(1)}, bf16[128,1280]{1,0:T(8,128)(2,1)S(1)}, u32[]{:S(2)}, u32[]{:S(2)}) %collective-permute-start.10) | collective-permute-done | bytes 327712 | tf_op jit(solution)/shard_map/ppermute | solution.py:23
  43.1 2.7 %collective-permute-start.11 = (bf16[384,1280]{1,0:T(8,128)(2,1)S(1)}, bf16[384,1280]{1,0:T(8,128)(2,1)S(1)}, u32[]{:S(2)}, u32[]{:S(2)}) collective-permute-start(bf16[384,1280]{1,0:T(8,128)(2,1)S(1)} %get-tuple-element.69), channel_id=1, source_target_pairs={{8,0},{16,8},{24,16},{0,24},{9,1},{17,9},{25,17},{1,25},{10,2},{18... | collective-permute-start | bytes 2949128 | tf_op jit(solution)/shard_map/ppermute | solution.py:23
  45.9 1.5 %collective-permute-start.19 = (bf16[384,1280]{1,0:T(8,128)(2,1)S(1)}, bf16[384,1280]{1,0:T(8,128)(2,1)S(1)}, u32[]{:S(2)}, u32[]{:S(2)}) collective-permute-start(bf16[384,1280]{1,0:T(8,128)(2,1)S(1)} %get-tuple-element.68), channel_id=1, source_target_pairs={{96,0},{0,32},{32,64},{64,96},{97,1},{1,33},{33,65},{65,97},{98,2}... | collective-permute-start | bytes 2949128 | tf_op jit(solution)/shard_map/ppermute | solution.py:23
  47.6 6.1 %apply.5.refs_12_ = f32[1024,256]{1,0:T(8,128)S(1)} custom-call(s32[22]{0:T(128)S(1)} %compare_select_fusion.10.table.t, bf16[1024,1024]{1,0:T(8,128)(2,1)S(1)} %constant_dynamic-update-slice_fusion.orb.slab_ref, bf16[256,1280]{1,0:T(8,128)(2,1)S(1)} %get-tuple-element.72.refs_0_, bf16[256,1280]{1,0:T(8,128)(2,1)S(1)} %get-tuple-element.73.refs_1_, ...), custom_call_target="tpu_custom_call" | custom-call | flops 838860800 | bytes 2621440 | tf_op jit(solution)/shard_map/apply/pallas_call | solution.py:101
  53.7 6.8 %collective-permute-done.14 = bf16[384,1280]{1,0:T(8,128)(2,1)S(1)} collective-permute-done((bf16[384,1280]{1,0:T(8,128)(2,1)S(1)}, bf16[384,1280]{1,0:T(8,128)(2,1)S(1)}, u32[]{:S(2)}, u32[]{:S(2)}) %collective-permute-start.14) | collective-permute-done | bytes 983072 | tf_op jit(solution)/shard_map/ppermute | solution.py:23
  60.5 1.3 %collective-permute-done.11 = bf16[384,1280]{1,0:T(8,128)(2,1)S(1)} collective-permute-done((bf16[384,1280]{1,0:T(8,128)(2,1)S(1)}, bf16[384,1280]{1,0:T(8,128)(2,1)S(1)}, u32[]{:S(2)}, u32[]{:S(2)}) %collective-permute-start.11) | collective-permute-done | bytes 983072 | tf_op jit(solution)/shard_map/ppermute | solution.py:23
  61.9 3.6 %collective-permute-done.16 = bf16[384,1280]{1,0:T(8,128)(2,1)S(1)} collective-permute-done((bf16[384,1280]{1,0:T(8,128)(2,1)S(1)}, bf16[384,1280]{1,0:T(8,128)(2,1)S(1)}, u32[]{:S(2)}, u32[]{:S(2)}) %collective-permute-start.16) | collective-permute-done | bytes 983072 | tf_op jit(solution)/shard_map/ppermute | solution.py:23
  66.2 2.4 %collective-permute-start.15 = (bf16[384,1280]{1,0:T(8,128)(2,1)S(1)}, bf16[384,1280]{1,0:T(8,128)(2,1)S(1)}, u32[]{:S(2)}, u32[]{:S(2)}) collective-permute-start(bf16[384,1280]{1,0:T(8,128)(2,1)S(1)} %pad_maximum_fusion.2), channel_id=1, source_target_pairs={{32,0},{64,32},{96,64},{0,96},{33,1},{65,33},{97,65},{1,97},{34,2}... | collective-permute-start | bytes 2949128 | tf_op jit(solution)/shard_map/ppermute | solution.py:23
  69.2 6.9 %apply.6.refs_10_ = f32[1024,256]{1,0:T(8,128)S(1)} custom-call(s32[22]{0:T(128)S(1)} %compare_select_fusion.10.table.t, bf16[1024,1024]{1,0:T(8,128)(2,1)S(1)} %constant_dynamic-update-slice_fusion.orb.slab_ref, bf16[256,1280]{1,0:T(8,128)(2,1)S(1)} %slice.44.refs_0_.refs_5_, ...), custom_call_target="tpu_custom_call", output_to_operand_aliasing={{}: (14, {})} | custom-call | flops 1006632960 | bytes 3145728 | tf_op jit(solution)/shard_map/apply/pallas_call | solution.py:101
  76.2 6.0 %collective-permute-done.22.slab_ref = bf16[1024,1024]{1,0:T(8,128)(2,1)S(1)} collective-permute-done((bf16[1024,1024]{1,0:T(8,128)(2,1)S(1)}, bf16[1024,1024]{1,0:T(8,128)(2,1)S(1)}, u32[]{:S(2)}, u32[]{:S(2)}) %collective-permute-start.22) | collective-permute-done | bytes 2097184 | tf_op jit(solution)/shard_map/ppermute | solution.py:23
  83.1 10.9 %apply.7.refs_10_ = f32[1024,256]{1,0:T(8,128)S(1)} custom-call(s32[22]{0:T(128)S(1)} %compare_select_fusion.10.table.t, bf16[1024,1024]{1,0:T(8,128)(2,1)S(1)} %collective-permute-done.22.slab_ref, bf16[256,1280]{1,0:T(8,128)(2,1)S(1)} %get-tuple-element.72.refs_0_, bf16[256,1280]{1,0:T(8,128)(2,1)S(1)} %get-tuple-element.73.refs_1_, ...), custom_call_target="tpu_custom_call" | custom-call | flops 1845493760 | bytes 5767168 | tf_op jit(solution)/shard_map/apply/pallas_call | solution.py:101
  94.0 6.1 %apply.8 = (f32[512,256]{1,0:T(8,128)S(1)}, bf16[512,256]{1,0:T(8,128)(2,1)S(1)}) custom-call(s32[22]{0:T(128)S(1)} %compare_select_fusion.10.table.t, bf16[1024,1024]{1,0:T(8,128)(2,1)S(1)} %collective-permute-done.22.slab_ref, bf16[384,1280]{1,0:T(8,128)(2,1)S(1)} %collective-permute-done.15.refs_0_, ...), custom_call_target="tpu_custom_call" | custom-call | flops 838860800 | bytes 2621440 | tf_op jit(solution)/shard_map/apply/pallas_call | solution.py:101
  100.1 9.7 %collective-permute-start.23 = (bf16[512,256]{1,0:T(8,128)(2,1)S(1)}, bf16[512,256]{1,0:T(8,128)(2,1)S(1)}, u32[]{:S(2)}, u32[]{:S(2)}) collective-permute-start(bf16[512,256]{1,0:T(8,128)(2,1)S(1)} %get-tuple-element.46), channel_id=1, source_target_pairs={{1,0},{0,1},{3,2},{2,3},{5,4},{4,5},{7,6},{6,7},{9,8},{8,9},{11,10... | collective-permute-start | bytes 786440 | tf_op jit(solution)/shard_map/ppermute | solution.py:23
  109.9 1.2 collective-permute-done.23
  111.1 1.9 %collective-permute-start.24 = (bf16[512,256]{1,0:T(8,128)(2,1)S(1)}, bf16[512,256]{1,0:T(8,128)(2,1)S(1)}, u32[]{:S(2)}, u32[]{:S(2)}) collective-permute-start(bf16[512,256]{1,0:T(8,128)(2,1)S(1)} %add_convert_fusion), channel_id=1, source_target_pairs={{2,0},{0,2},{3,1},{1,3},{6,4},{4,6},{7,5},{5,7},{10,8},{8,10},{11,... | collective-permute-start | bytes 786440 | tf_op jit(solution)/shard_map/ppermute | solution.py:23
  113.0 6.1 %apply.9 = (f32[512,256]{1,0:T(8,128)S(1)}, bf16[512,256]{1,0:T(8,128)(2,1)S(1)}) custom-call(s32[22]{0:T(128)S(1)} %compare_select_fusion.10.table.t, bf16[1024,1024]{1,0:T(8,128)(2,1)S(1)} %constant_dynamic-update-slice_fusion.orb.slab_ref, bf16[384,1280]{1,0:T(8,128)(2,1)S(1)} %collective-permute-done.15.refs_0_, ...), custom_call_target="tpu_custom_call" | custom-call | flops 838860800 | bytes 2621440 | tf_op jit(solution)/shard_map/apply/pallas_call | solution.py:101
  120.2 1.2 collective-permute-start.25
  121.4 1.2 collective-permute-done.25
  (59 shorter events, 7.3 us)
Async XLA Ops:
  0.0 6.6 %copy-start.1 = (s32[1,128]{1,0:T(1,128)S(1)}, s32[1,128]{1,0:T(1,128)}, u32[]{:S(2)}) copy-start(s32[1,128]{1,0:T(1,128)} %param.6) | copy-start | bytes 1540
  0.0 6.6 %collective-permute-start = (bf16[512,1024]{1,0:T(8,128)(2,1)}, bf16[512,1024]{1,0:T(8,128)(2,1)S(1)}, u32[]{:S(2)}, u32[]{:S(2)}) collective-permute-start(bf16[512,1024]{1,0:T(8,128)(2,1)} %param.4), channel_id=1, source_target_pairs={{1,0},{0,1},{3,2},{2,3},{5,4},{4,5},{7,6},{6,7},{9,8},{8,9},{11,10... | collective-permute-start | bytes 3145736 | tf_op jit(solution)/shard_map/ppermute | solution.py:23
  1.4 5.3 %collective-permute-start.2 = (bf16[512,256]{1,0:T(8,128)(2,1)}, bf16[512,256]{1,0:T(8,128)(2,1)S(1)}, u32[]{:S(2)}, u32[]{:S(2)}) collective-permute-start(bf16[512,256]{1,0:T(8,128)(2,1)} %own_tgt.1), channel_id=1, source_target_pairs={{1,0},{0,1},{3,2},{2,3},{5,4},{4,5},{7,6},{6,7},{9,8},{8,9},{11,10... | collective-permute-start | bytes 786440 | tf_op jit(solution)/shard_map/ppermute | solution.py:23
  1.4 5.1 %collective-permute-start.1 = (s32[1,128]{1,0:T(1,128)}, s32[1,128]{1,0:T(1,128)S(1)}, u32[]{:S(2)}, u32[]{:S(2)}) collective-permute-start(s32[1,128]{1,0:T(1,128)} %param.6), channel_id=1, source_target_pairs={{2,0},{0,2},{3,1},{1,3},{6,4},{4,6},{7,5},{5,7},{10,8},{8,10},{11,... | collective-permute-start | bytes 1544 | tf_op jit(solution)/shard_map/ppermute | solution.py:23
  5.2 1.5 %copy-start = (bf16[512,256]{1,0:T(8,128)(2,1)S(1)}, bf16[512,256]{1,0:T(8,128)(2,1)}, u32[]{:S(2)}) copy-start(bf16[512,256]{1,0:T(8,128)(2,1)} %own_tgt.1) | copy-start | bytes 786436
  8.2 9.8 %collective-permute-start.3 = (bf16[128,1280]{1,0:T(8,128)(2,1)S(1)}, bf16[128,1280]{1,0:T(8,128)(2,1)S(1)}, u32[]{:S(2)}, u32[]{:S(2)}) collective-permute-start(bf16[128,1280]{1,0:T(8,128)(2,1)S(1)} %get-tuple-element.29), channel_id=1, source_target_pairs={{2,0},{0,2},{3,1},{1,3},{6,4},{4,6},{7,5},{5,7},{10,8},{8,10},{11,... | collective-permute-start | bytes 983048 | tf_op jit(solution)/shard_map/ppermute | solution.py:23
  18.1 7.9 %collective-permute-start.4 = (bf16[128,1280]{1,0:T(8,128)(2,1)S(1)}, bf16[128,1280]{1,0:T(8,128)(2,1)S(1)}, u32[]{:S(2)}, u32[]{:S(2)}) collective-permute-start(bf16[128,1280]{1,0:T(8,128)(2,1)S(1)} %add.68), channel_id=1, source_target_pairs={{32,0},{64,32},{96,64},{0,96},{33,1},{65,33},{97,65},{1,97},{34,2}... | collective-permute-start | bytes 983048 | tf_op jit(solution)/shard_map/ppermute | solution.py:23
  20.9 7.3 %collective-permute-start.6 = (bf16[128,1280]{1,0:T(8,128)(2,1)S(1)}, bf16[128,1280]{1,0:T(8,128)(2,1)S(1)}, u32[]{:S(2)}, u32[]{:S(2)}) collective-permute-start(bf16[128,1280]{1,0:T(8,128)(2,1)S(1)} %add.68), channel_id=1, source_target_pairs={{8,0},{16,8},{24,16},{0,24},{9,1},{17,9},{25,17},{1,25},{10,2},{18... | collective-permute-start | bytes 983048 | tf_op jit(solution)/shard_map/ppermute | solution.py:23
  23.4 8.0 %collective-permute-start.7 = (bf16[128,1280]{1,0:T(8,128)(2,1)S(1)}, bf16[128,1280]{1,0:T(8,128)(2,1)S(1)}, u32[]{:S(2)}, u32[]{:S(2)}) collective-permute-start(bf16[128,1280]{1,0:T(8,128)(2,1)S(1)} %add.68), channel_id=1, source_target_pairs={{24,0},{0,8},{8,16},{16,24},{25,1},{1,9},{9,17},{17,25},{26,2},{2,... | collective-permute-start | bytes 983048 | tf_op jit(solution)/shard_map/ppermute | solution.py:23
  23.4 8.0 %collective-permute-start.8 = (bf16[128,1280]{1,0:T(8,128)(2,1)S(1)}, bf16[128,1280]{1,0:T(8,128)(2,1)S(1)}, u32[]{:S(2)}, u32[]{:S(2)}) collective-permute-start(bf16[128,1280]{1,0:T(8,128)(2,1)S(1)} %add.68), channel_id=1, source_target_pairs={{96,0},{0,32},{32,64},{64,96},{97,1},{1,33},{33,65},{65,97},{98,2}... | collective-permute-start | bytes 983048 | tf_op jit(solution)/shard_map/ppermute | solution.py:23
  23.4 8.0 %collective-permute-start.5 = (bf16[128,1280]{1,0:T(8,128)(2,1)S(1)}, bf16[128,1280]{1,0:T(8,128)(2,1)S(1)}, u32[]{:S(2)}, u32[]{:S(2)}) collective-permute-start(bf16[128,1280]{1,0:T(8,128)(2,1)S(1)} %add.68), channel_id=1, source_target_pairs={{4,0},{0,4},{5,1},{1,5},{6,2},{2,6},{7,3},{3,7},{12,8},{8,12},{13,... | collective-permute-start | bytes 983048 | tf_op jit(solution)/shard_map/ppermute | solution.py:23
  31.4 8.2 %collective-permute-start.13 = (bf16[128,1280]{1,0:T(8,128)(2,1)S(1)}, bf16[128,1280]{1,0:T(8,128)(2,1)S(1)}, u32[]{:S(2)}, u32[]{:S(2)}) collective-permute-start(bf16[128,1280]{1,0:T(8,128)(2,1)S(1)} %collective-permute-done.5), channel_id=1, source_target_pairs={{96,0},{0,32},{32,64},{64,96},{97,1},{1,33},{33,65},{65,97},{98,2}... | collective-permute-start | bytes 983048 | tf_op jit(solution)/shard_map/ppermute | solution.py:23
  32.6 7.5 %collective-permute-start.12 = (bf16[128,1280]{1,0:T(8,128)(2,1)S(1)}, bf16[128,1280]{1,0:T(8,128)(2,1)S(1)}, u32[]{:S(2)}, u32[]{:S(2)}) collective-permute-start(bf16[128,1280]{1,0:T(8,128)(2,1)S(1)} %collective-permute-done.5), channel_id=1, source_target_pairs={{24,0},{0,8},{8,16},{16,24},{25,1},{1,9},{9,17},{17,25},{26,2},{2,... | collective-permute-start | bytes 983048 | tf_op jit(solution)/shard_map/ppermute | solution.py:23
  32.7 7.5 %collective-permute-start.9 = (bf16[128,1280]{1,0:T(8,128)(2,1)S(1)}, bf16[128,1280]{1,0:T(8,128)(2,1)S(1)}, u32[]{:S(2)}, u32[]{:S(2)}) collective-permute-start(bf16[128,1280]{1,0:T(8,128)(2,1)S(1)} %collective-permute-done.5), channel_id=1, source_target_pairs={{32,0},{64,32},{96,64},{0,96},{33,1},{65,33},{97,65},{1,97},{34,2}... | collective-permute-start | bytes 983048 | tf_op jit(solution)/shard_map/ppermute | solution.py:23
  35.4 6.6 %collective-permute-start.10 = (bf16[128,1280]{1,0:T(8,128)(2,1)S(1)}, bf16[128,1280]{1,0:T(8,128)(2,1)S(1)}, u32[]{:S(2)}, u32[]{:S(2)}) collective-permute-start(bf16[128,1280]{1,0:T(8,128)(2,1)S(1)} %collective-permute-done.5), channel_id=1, source_target_pairs={{8,0},{16,8},{24,16},{0,24},{9,1},{17,9},{25,17},{1,25},{10,2},{18... | collective-permute-start | bytes 983048 | tf_op jit(solution)/shard_map/ppermute | solution.py:23
  38.0 44.2 %collective-permute-start.22 = (bf16[1024,1024]{1,0:T(8,128)(2,1)S(1)}, bf16[1024,1024]{1,0:T(8,128)(2,1)S(1)}, u32[]{:S(2)}, u32[]{:S(2)}) collective-permute-start(bf16[1024,1024]{1,0:T(8,128)(2,1)S(1)} %constant_dynamic-update-slice_fusion.orb.slab_ref), channel_id=1, source_target_pairs={{2,0},{0,2},{3,1},{1,3},{6,4},{4,6},{7,5},{5,7},{10,8},{8,10},{11,... | collective-permute-start | bytes 6291464 | tf_op jit(solution)/shard_map/ppermute | solution.py:23
  42.5 18.0 %collective-permute-start.14 = (bf16[384,1280]{1,0:T(8,128)(2,1)S(1)}, bf16[384,1280]{1,0:T(8,128)(2,1)S(1)}, u32[]{:S(2)}, u32[]{:S(2)}) collective-permute-start(bf16[384,1280]{1,0:T(8,128)(2,1)S(1)} %get-tuple-element.70), channel_id=1, source_target_pairs={{32,0},{64,32},{96,64},{0,96},{33,1},{65,33},{97,65},{1,97},{34,2}... | collective-permute-start | bytes 2949128 | tf_op jit(solution)/shard_map/ppermute | solution.py:23
  43.1 18.7 %collective-permute-start.11 = (bf16[384,1280]{1,0:T(8,128)(2,1)S(1)}, bf16[384,1280]{1,0:T(8,128)(2,1)S(1)}, u32[]{:S(2)}, u32[]{:S(2)}) collective-permute-start(bf16[384,1280]{1,0:T(8,128)(2,1)S(1)} %get-tuple-element.69), channel_id=1, source_target_pairs={{8,0},{16,8},{24,16},{0,24},{9,1},{17,9},{25,17},{1,25},{10,2},{18... | collective-permute-start | bytes 2949128 | tf_op jit(solution)/shard_map/ppermute | solution.py:23
  45.9 22.7 %collective-permute-start.19 = (bf16[384,1280]{1,0:T(8,128)(2,1)S(1)}, bf16[384,1280]{1,0:T(8,128)(2,1)S(1)}, u32[]{:S(2)}, u32[]{:S(2)}) collective-permute-start(bf16[384,1280]{1,0:T(8,128)(2,1)S(1)} %get-tuple-element.68), channel_id=1, source_target_pairs={{96,0},{0,32},{32,64},{64,96},{97,1},{1,33},{33,65},{65,97},{98,2}... | collective-permute-start | bytes 2949128 | tf_op jit(solution)/shard_map/ppermute | solution.py:23
  47.4 18.2 %collective-permute-start.16 = (bf16[384,1280]{1,0:T(8,128)(2,1)S(1)}, bf16[384,1280]{1,0:T(8,128)(2,1)S(1)}, u32[]{:S(2)}, u32[]{:S(2)}) collective-permute-start(bf16[384,1280]{1,0:T(8,128)(2,1)S(1)} %get-tuple-element.71), channel_id=1, source_target_pairs={{24,0},{0,8},{8,16},{16,24},{25,1},{1,9},{9,17},{17,25},{26,2},{2,... | collective-permute-start | bytes 2949128 | tf_op jit(solution)/shard_map/ppermute | solution.py:23
  65.7 28.3 %collective-permute-start.17 = (bf16[384,1280]{1,0:T(8,128)(2,1)S(1)}, bf16[384,1280]{1,0:T(8,128)(2,1)S(1)}, u32[]{:S(2)}, u32[]{:S(2)}) collective-permute-start(bf16[384,1280]{1,0:T(8,128)(2,1)S(1)} %pad_maximum_fusion.4), channel_id=1, source_target_pairs={{96,0},{0,32},{32,64},{64,96},{97,1},{1,33},{33,65},{65,97},{98,2}... | collective-permute-start | bytes 2949128 | tf_op jit(solution)/shard_map/ppermute | solution.py:23
  66.2 27.7 %collective-permute-start.15 = (bf16[384,1280]{1,0:T(8,128)(2,1)S(1)}, bf16[384,1280]{1,0:T(8,128)(2,1)S(1)}, u32[]{:S(2)}, u32[]{:S(2)}) collective-permute-start(bf16[384,1280]{1,0:T(8,128)(2,1)S(1)} %pad_maximum_fusion.2), channel_id=1, source_target_pairs={{32,0},{64,32},{96,64},{0,96},{33,1},{65,33},{97,65},{1,97},{34,2}... | collective-permute-start | bytes 2949128 | tf_op jit(solution)/shard_map/ppermute | solution.py:23
  68.9 25.1 %collective-permute-start.21 = (bf16[256,1280]{1,0:T(8,128)(2,1)S(1)}, bf16[256,1280]{1,0:T(8,128)(2,1)S(1)}, u32[]{:S(2)}, u32[]{:S(2)}) collective-permute-start(bf16[256,1280]{1,0:T(8,128)(2,1)S(1)} %pad_maximum_fusion.12.refs_5_.refs_10_), channel_id=1, source_target_pairs={{16,0},{24,8},{0,16},{8,24},{17,1},{25,9},{1,17},{9,25},{18,2},{26... | collective-permute-start | bytes 1966088 | tf_op jit(solution)/shard_map/ppermute | solution.py:23
  76.1 17.8 %collective-permute-start.20 = (bf16[128,1280]{1,0:T(8,128)(2,1)S(1)}, bf16[128,1280]{1,0:T(8,128)(2,1)S(1)}, u32[]{:S(2)}, u32[]{:S(2)}) collective-permute-start(bf16[128,1280]{1,0:T(8,128)(2,1)S(1)} %get-tuple-element.35), channel_id=1, source_target_pairs={{24,0},{0,8},{8,16},{16,24},{25,1},{1,9},{9,17},{17,25},{26,2},{2,... | collective-permute-start | bytes 983048 | tf_op jit(solution)/shard_map/ppermute | solution.py:23
  82.2 11.8 %collective-permute-start.18 = (bf16[128,1280]{1,0:T(8,128)(2,1)S(1)}, bf16[128,1280]{1,0:T(8,128)(2,1)S(1)}, u32[]{:S(2)}, u32[]{:S(2)}) collective-permute-start(bf16[128,1280]{1,0:T(8,128)(2,1)S(1)} %get-tuple-element.54), channel_id=1, source_target_pairs={{8,0},{16,8},{24,16},{0,24},{9,1},{17,9},{25,17},{1,25},{10,2},{18... | collective-permute-start | bytes 983048 | tf_op jit(solution)/shard_map/ppermute | solution.py:23
  100.1 10.9 %collective-permute-start.23 = (bf16[512,256]{1,0:T(8,128)(2,1)S(1)}, bf16[512,256]{1,0:T(8,128)(2,1)S(1)}, u32[]{:S(2)}, u32[]{:S(2)}) collective-permute-start(bf16[512,256]{1,0:T(8,128)(2,1)S(1)} %get-tuple-element.46), channel_id=1, source_target_pairs={{1,0},{0,1},{3,2},{2,3},{5,4},{4,5},{7,6},{6,7},{9,8},{8,9},{11,10... | collective-permute-start | bytes 786440 | tf_op jit(solution)/shard_map/ppermute | solution.py:23
  111.1 9.1 %collective-permute-start.24 = (bf16[512,256]{1,0:T(8,128)(2,1)S(1)}, bf16[512,256]{1,0:T(8,128)(2,1)S(1)}, u32[]{:S(2)}, u32[]{:S(2)}) collective-permute-start(bf16[512,256]{1,0:T(8,128)(2,1)S(1)} %add_convert_fusion), channel_id=1, source_target_pairs={{2,0},{0,2},{3,1},{1,3},{6,4},{4,6},{7,5},{5,7},{10,8},{8,10},{11,... | collective-permute-start | bytes 786440 | tf_op jit(solution)/shard_map/ppermute | solution.py:23
  120.2 2.4 %collective-permute-start.25 = (bf16[512,256]{1,0:T(8,128)(2,1)S(1)}, bf16[512,256]{1,0:T(8,128)(2,1)S(1)}, u32[]{:S(2)}, u32[]{:S(2)}) collective-permute-start(bf16[512,256]{1,0:T(8,128)(2,1)S(1)} %get-tuple-element.50), channel_id=1, source_target_pairs={{1,0},{0,1},{3,2},{2,3},{5,4},{4,5},{7,6},{6,7},{9,8},{8,9},{11,10... | collective-permute-start | bytes 786440 | tf_op jit(solution)/shard_map/ppermute | solution.py:23

commit v11 on v8

--- a/solution.py
+++ b/solution.py
@@ -179,8 +179,7 @@
         take_from(pair[1, 3][count:], "x", -1),
         take_from(pair[2, 0], "x", 2),
     ]
-    far = far_apply([pair[at] for at in first], first, None)
-    far = far_apply([pair[at] for at in second], second, far)
+    far = far_apply([pair[at] for at in first + second], first + second, None)
     near = near_apply([pair[at] for at in second], second, after(near, far))
     last, far, near = lax.optimization_barrier((last, far, near))
     kept, sent = far_apply(last, third, far, True)

time: 122 us -> 120 us (0.984)
  Pallas kernels: 39.7 us -> 37.6 us
    pallas_call x6 -> x5, Pallas kernels: 38.2 us -> 36.2 us  [apply_parts(): pl.pallas_call(body, out_shape=halves if last else jax.ShapeDtypeStruct((...]
  transfers between devices with their start and end apart: 26 -> 26, of which waited for: 10 -> 10; matrix products, arithmetic and copies ran while one was open for 3% -> 3% of each run, Pallas kernels for 26% -> 25%
where the time goes in v11:
time: 120 us
  starting transfers between devices  44.9 us (37%)
  Pallas kernels  37.6 us (31%)
  waiting for transfers between devices  32.1 us (27%)
  local copies, waits for them, and re-layouts  2.35 us (2%)
  other arithmetic  2.08 us (2%)
    ppermute x26, starting transfers between devices, take_from(): return lax.ppermute(value, axis, [((i + side) % n, i) for i in range(n)])  44.9 us
    pallas_call x5, Pallas kernels, apply_parts(): pl.pallas_call(body, out_shape=halves if last else jax.ShapeDtypeStruct((...  36.2 us
    ppermute x26, waiting for transfers between devices, take_from(): return lax.ppermute(value, axis, [((i + side) % n, i) for i in range(n)])  32.1 us
  transfers between devices with their start and end apart: 26, of which 10 were waited for; matrix products, arithmetic and copies ran while one was open for 3% of the time, Pallas kernels for 25%

profile of v11, /device:TPU:1, one launch (start us, length us, event | category | flops | bytes accessed | tf_op | source)
XLA Modules:
  0.0 120.1 jit_solution(6837071884177443876)
XLA Ops:
  0.0 1.4 %collective-permute-start = (bf16[512,1024]{1,0:T(8,128)(2,1)}, bf16[512,1024]{1,0:T(8,128)(2,1)S(1)}, u32[]{:S(2)}, u32[]{:S(2)}) collective-permute-start(bf16[512,1024]{1,0:T(8,128)(2,1)} %param.4), channel_id=1, source_target_pairs={{1,0},{0,1},{3,2},{2,3},{5,4},{4,5},{7,6},{6,7},{9,8},{8,9},{11,10... | collective-permute-start | bytes 3145736 | tf_op jit(solution)/shard_map/ppermute | solution.py:23
  1.4 3.8 %collective-permute-start.1 = (s32[1,128]{1,0:T(1,128)}, s32[1,128]{1,0:T(1,128)S(1)}, u32[]{:S(2)}, u32[]{:S(2)}) collective-permute-start(s32[1,128]{1,0:T(1,128)} %param.6), channel_id=1, source_target_pairs={{2,0},{0,2},{3,1},{1,3},{6,4},{4,6},{7,5},{5,7},{10,8},{8,10},{11,... | collective-permute-start | bytes 1544 | tf_op jit(solution)/shard_map/ppermute | solution.py:23
  5.2 1.3 %constant_dynamic-update-slice_fusion.1 = bf16[1024,1024]{1,0:T(8,128)(2,1)S(1)} fusion(bf16[512,1024]{1,0:T(8,128)(2,1)} %param.4), kind=kLoop, calls=%fused_computation.26 | loop fusion | bytes 2097152
  6.7 1.5 %pick.1 = (bf16[128,1280]{1,0:T(8,128)(2,1)S(1)}, bf16[128,1280]{1,0:T(8,128)(2,1)S(1)}) custom-call(s32[22]{0:T(128)S(1)} %compare_select_fusion.10.table.t, s32[2,128]{1,0:T(2,128)S(1)} %pad_add_fusion.ids, bf16[1024,1024]{1,0:T(8,128)(2,1)S(1)} %constant_dynamic-update-slice_fusion.orb.slab_ref, bf16[512,256]{1,0:T(8,128)(2,1)S(1)} %copy-done, ...), custom_call_target="tpu_custom_call" | custom-call | tf_op jit(solution)/shard_map/pick/pallas_call | solution.py:50
  8.2 2.7 %collective-permute-start.3 = (bf16[128,1280]{1,0:T(8,128)(2,1)S(1)}, bf16[128,1280]{1,0:T(8,128)(2,1)S(1)}, u32[]{:S(2)}, u32[]{:S(2)}) collective-permute-start(bf16[128,1280]{1,0:T(8,128)(2,1)S(1)} %get-tuple-element.27), channel_id=1, source_target_pairs={{2,0},{0,2},{3,1},{1,3},{6,4},{4,6},{7,5},{5,7},{10,8},{8,10},{11,... | collective-permute-start | bytes 983048 | tf_op jit(solution)/shard_map/ppermute | solution.py:23
  10.9 7.1 %collective-permute-done.3 = bf16[128,1280]{1,0:T(8,128)(2,1)S(1)} collective-permute-done((bf16[128,1280]{1,0:T(8,128)(2,1)S(1)}, bf16[128,1280]{1,0:T(8,128)(2,1)S(1)}, u32[]{:S(2)}, u32[]{:S(2)}) %collective-permute-start.3) | collective-permute-done | bytes 327712 | tf_op jit(solution)/shard_map/ppermute | solution.py:23
  18.3 1.3 %collective-permute-start.12 = (bf16[128,1280]{1,0:T(8,128)(2,1)S(1)}, bf16[128,1280]{1,0:T(8,128)(2,1)S(1)}, u32[]{:S(2)}, u32[]{:S(2)}) collective-permute-start(bf16[128,1280]{1,0:T(8,128)(2,1)S(1)} %add.68), channel_id=1, source_target_pairs={{96,0},{0,32},{32,64},{64,96},{97,1},{1,33},{33,65},{65,97},{98,2}... | collective-permute-start | bytes 983048 | tf_op jit(solution)/shard_map/ppermute | solution.py:23
  19.7 1.2 collective-permute-start.10
  20.9 1.4 %collective-permute-start.4 = (bf16[128,1280]{1,0:T(8,128)(2,1)S(1)}, bf16[128,1280]{1,0:T(8,128)(2,1)S(1)}, u32[]{:S(2)}, u32[]{:S(2)}) collective-permute-start(bf16[128,1280]{1,0:T(8,128)(2,1)S(1)} %add.68), channel_id=1, source_target_pairs={{32,0},{64,32},{96,64},{0,96},{33,1},{65,33},{97,65},{1,97},{34,2}... | collective-permute-start | bytes 983048 | tf_op jit(solution)/shard_map/ppermute | solution.py:23
  22.3 1.5 %collective-permute-start.7 = (bf16[128,1280]{1,0:T(8,128)(2,1)S(1)}, bf16[128,1280]{1,0:T(8,128)(2,1)S(1)}, u32[]{:S(2)}, u32[]{:S(2)}) collective-permute-start(bf16[128,1280]{1,0:T(8,128)(2,1)S(1)} %add.68), channel_id=1, source_target_pairs={{8,0},{16,8},{24,16},{0,24},{9,1},{17,9},{25,17},{1,25},{10,2},{18... | collective-permute-start | bytes 983048 | tf_op jit(solution)/shard_map/ppermute | solution.py:23
  23.8 1.7 %collective-permute-done.5 = bf16[128,1280]{1,0:T(8,128)(2,1)S(1)} collective-permute-done((bf16[128,1280]{1,0:T(8,128)(2,1)S(1)}, bf16[128,1280]{1,0:T(8,128)(2,1)S(1)}, u32[]{:S(2)}, u32[]{:S(2)}) %collective-permute-start.5) | collective-permute-done | bytes 327712 | tf_op jit(solution)/shard_map/ppermute | solution.py:23
  25.5 1.3 %collective-permute-start.13 = (bf16[128,1280]{1,0:T(8,128)(2,1)S(1)}, bf16[128,1280]{1,0:T(8,128)(2,1)S(1)}, u32[]{:S(2)}, u32[]{:S(2)}) collective-permute-start(bf16[128,1280]{1,0:T(8,128)(2,1)S(1)} %collective-permute-done.5), channel_id=1, source_target_pairs={{96,0},{0,32},{32,64},{64,96},{97,1},{1,33},{33,65},{65,97},{98,2}... | collective-permute-start | bytes 983048 | tf_op jit(solution)/shard_map/ppermute | solution.py:23
  28.5 3.2 %collective-permute-start.22 = (bf16[1024,1024]{1,0:T(8,128)(2,1)S(1)}, bf16[1024,1024]{1,0:T(8,128)(2,1)S(1)}, u32[]{:S(2)}, u32[]{:S(2)}) collective-permute-start(bf16[1024,1024]{1,0:T(8,128)(2,1)S(1)} %constant_dynamic-update-slice_fusion.orb.slab_ref), channel_id=1, source_target_pairs={{2,0},{0,2},{3,1},{1,3},{6,4},{4,6},{7,5},{5,7},{10,8},{8,10},{11,... | collective-permute-start | bytes 6291464 | tf_op jit(solution)/shard_map/ppermute | solution.py:23
  31.7 1.2 %collective-permute-start.11 = (bf16[128,1280]{1,0:T(8,128)(2,1)S(1)}, bf16[128,1280]{1,0:T(8,128)(2,1)S(1)}, u32[]{:S(2)}, u32[]{:S(2)}) collective-permute-start(bf16[128,1280]{1,0:T(8,128)(2,1)S(1)} %collective-permute-done.5), channel_id=1, source_target_pairs={{24,0},{0,8},{8,16},{16,24},{25,1},{1,9},{9,17},{17,25},{26,2},{2,... | collective-permute-start | bytes 983048 | tf_op jit(solution)/shard_map/ppermute | solution.py:23
  32.9 1.5 %collective-permute-start.6 = (bf16[128,1280]{1,0:T(8,128)(2,1)S(1)}, bf16[128,1280]{1,0:T(8,128)(2,1)S(1)}, u32[]{:S(2)}, u32[]{:S(2)}) collective-permute-start(bf16[128,1280]{1,0:T(8,128)(2,1)S(1)} %collective-permute-done.5), channel_id=1, source_target_pairs={{32,0},{64,32},{96,64},{0,96},{33,1},{65,33},{97,65},{1,97},{34,2}... | collective-permute-start | bytes 983048 | tf_op jit(solution)/shard_map/ppermute | solution.py:23
  34.4 1.5 %collective-permute-start.8 = (bf16[128,1280]{1,0:T(8,128)(2,1)S(1)}, bf16[128,1280]{1,0:T(8,128)(2,1)S(1)}, u32[]{:S(2)}, u32[]{:S(2)}) collective-permute-start(bf16[128,1280]{1,0:T(8,128)(2,1)S(1)} %collective-permute-done.5), channel_id=1, source_target_pairs={{8,0},{16,8},{24,16},{0,24},{9,1},{17,9},{25,17},{1,25},{10,2},{18... | collective-permute-start | bytes 983048 | tf_op jit(solution)/shard_map/ppermute | solution.py:23
  35.9 3.2 %collective-permute-done.11 = bf16[128,1280]{1,0:T(8,128)(2,1)S(1)} collective-permute-done((bf16[128,1280]{1,0:T(8,128)(2,1)S(1)}, bf16[128,1280]{1,0:T(8,128)(2,1)S(1)}, u32[]{:S(2)}, u32[]{:S(2)}) %collective-permute-start.11) | collective-permute-done | bytes 327712 | tf_op jit(solution)/shard_map/ppermute | solution.py:23
  39.2 1.3 %collective-permute-done.8 = bf16[128,1280]{1,0:T(8,128)(2,1)S(1)} collective-permute-done((bf16[128,1280]{1,0:T(8,128)(2,1)S(1)}, bf16[128,1280]{1,0:T(8,128)(2,1)S(1)}, u32[]{:S(2)}, u32[]{:S(2)}) %collective-permute-start.8) | collective-permute-done | bytes 327712 | tf_op jit(solution)/shard_map/ppermute | solution.py:23
  41.0 2.8 %collective-permute-start.9 = (bf16[384,1280]{1,0:T(8,128)(2,1)S(1)}, bf16[384,1280]{1,0:T(8,128)(2,1)S(1)}, u32[]{:S(2)}, u32[]{:S(2)}) collective-permute-start(bf16[384,1280]{1,0:T(8,128)(2,1)S(1)} %get-tuple-element.65), channel_id=1, source_target_pairs={{8,0},{16,8},{24,16},{0,24},{9,1},{17,9},{25,17},{1,25},{10,2},{18... | collective-permute-start | bytes 2949128 | tf_op jit(solution)/shard_map/ppermute | solution.py:23
  44.0 2.7 %collective-permute-start.14 = (bf16[384,1280]{1,0:T(8,128)(2,1)S(1)}, bf16[384,1280]{1,0:T(8,128)(2,1)S(1)}, u32[]{:S(2)}, u32[]{:S(2)}) collective-permute-start(bf16[384,1280]{1,0:T(8,128)(2,1)S(1)} %get-tuple-element.66), channel_id=1, source_target_pairs={{32,0},{64,32},{96,64},{0,96},{33,1},{65,33},{97,65},{1,97},{34,2}... | collective-permute-start | bytes 2949128 | tf_op jit(solution)/shard_map/ppermute | solution.py:23
  46.9 6.1 %apply.5.refs_12_ = f32[1024,256]{1,0:T(8,128)S(1)} custom-call(s32[22]{0:T(128)S(1)} %compare_select_fusion.10.table.t, bf16[1024,1024]{1,0:T(8,128)(2,1)S(1)} %constant_dynamic-update-slice_fusion.orb.slab_ref, bf16[256,1280]{1,0:T(8,128)(2,1)S(1)} %get-tuple-element.68.refs_0_, bf16[256,1280]{1,0:T(8,128)(2,1)S(1)} %get-tuple-element.69.refs_1_, ...), custom_call_target="tpu_custom_call" | custom-call | flops 838860800 | bytes 2621440 | tf_op jit(solution)/shard_map/apply/pallas_call | solution.py:101
  53.0 7.7 %collective-permute-done.9 = bf16[384,1280]{1,0:T(8,128)(2,1)S(1)} collective-permute-done((bf16[384,1280]{1,0:T(8,128)(2,1)S(1)}, bf16[384,1280]{1,0:T(8,128)(2,1)S(1)}, u32[]{:S(2)}, u32[]{:S(2)}) %collective-permute-start.9) | collective-permute-done | bytes 983072 | tf_op jit(solution)/shard_map/ppermute | solution.py:23
  61.2 2.7 %collective-permute-start.15 = (bf16[384,1280]{1,0:T(8,128)(2,1)S(1)}, bf16[384,1280]{1,0:T(8,128)(2,1)S(1)}, u32[]{:S(2)}, u32[]{:S(2)}) collective-permute-start(bf16[384,1280]{1,0:T(8,128)(2,1)S(1)} %pad_maximum_fusion.2), channel_id=1, source_target_pairs={{32,0},{64,32},{96,64},{0,96},{33,1},{65,33},{97,65},{1,97},{34,2}... | collective-permute-start | bytes 2949128 | tf_op jit(solution)/shard_map/ppermute | solution.py:23
  64.0 2.7 %collective-permute-start.21 = (bf16[256,1280]{1,0:T(8,128)(2,1)S(1)}, bf16[256,1280]{1,0:T(8,128)(2,1)S(1)}, u32[]{:S(2)}, u32[]{:S(2)}) collective-permute-start(bf16[256,1280]{1,0:T(8,128)(2,1)S(1)} %pad_maximum_fusion.11.refs_10_.refs_5_), channel_id=1, source_target_pairs={{16,0},{24,8},{0,16},{8,24},{17,1},{25,9},{1,17},{9,25},{18,2},{26... | collective-permute-start | bytes 1966088 | tf_op jit(solution)/shard_map/ppermute | solution.py:23
  67.4 5.8 %collective-permute-done.22.slab_ref = bf16[1024,1024]{1,0:T(8,128)(2,1)S(1)} collective-permute-done((bf16[1024,1024]{1,0:T(8,128)(2,1)S(1)}, bf16[1024,1024]{1,0:T(8,128)(2,1)S(1)}, u32[]{:S(2)}, u32[]{:S(2)}) %collective-permute-start.22) | collective-permute-done | bytes 2097184 | tf_op jit(solution)/shard_map/ppermute | solution.py:23
  74.6 10.9 %apply.6.refs_10_ = f32[1024,256]{1,0:T(8,128)S(1)} custom-call(s32[22]{0:T(128)S(1)} %compare_select_fusion.10.table.t, bf16[1024,1024]{1,0:T(8,128)(2,1)S(1)} %collective-permute-done.22.slab_ref, bf16[256,1280]{1,0:T(8,128)(2,1)S(1)} %get-tuple-element.68.refs_0_, bf16[256,1280]{1,0:T(8,128)(2,1)S(1)} %get-tuple-element.69.refs_1_, ...), custom_call_target="tpu_custom_call" | custom-call | flops 1845493760 | bytes 5767168 | tf_op jit(solution)/shard_map/apply/pallas_call | solution.py:101
  85.5 6.9 %apply.7.refs_10_ = f32[1024,256]{1,0:T(8,128)S(1)} custom-call(s32[22]{0:T(128)S(1)} %compare_select_fusion.10.table.t, bf16[1024,1024]{1,0:T(8,128)(2,1)S(1)} %constant_dynamic-update-slice_fusion.orb.slab_ref, bf16[256,1280]{1,0:T(8,128)(2,1)S(1)} %slice.44.refs_5_.refs_0_, ...), custom_call_target="tpu_custom_call", output_to_operand_aliasing={{}: (14, {})} | custom-call | flops 1006632960 | bytes 3145728 | tf_op jit(solution)/shard_map/apply/pallas_call | solution.py:101
  92.5 6.1 %apply.8 = (f32[512,256]{1,0:T(8,128)S(1)}, bf16[512,256]{1,0:T(8,128)(2,1)S(1)}) custom-call(s32[22]{0:T(128)S(1)} %compare_select_fusion.10.table.t, bf16[1024,1024]{1,0:T(8,128)(2,1)S(1)} %collective-permute-done.22.slab_ref, bf16[384,1280]{1,0:T(8,128)(2,1)S(1)} %collective-permute-done.15.refs_0_, ...), custom_call_target="tpu_custom_call" | custom-call | flops 838860800 | bytes 2621440 | tf_op jit(solution)/shard_map/apply/pallas_call | solution.py:101
  98.6 7.9 %collective-permute-start.23 = (bf16[512,256]{1,0:T(8,128)(2,1)S(1)}, bf16[512,256]{1,0:T(8,128)(2,1)S(1)}, u32[]{:S(2)}, u32[]{:S(2)}) collective-permute-start(bf16[512,256]{1,0:T(8,128)(2,1)S(1)} %get-tuple-element.42), channel_id=1, source_target_pairs={{1,0},{0,1},{3,2},{2,3},{5,4},{4,5},{7,6},{6,7},{9,8},{8,9},{11,10... | collective-permute-start | bytes 786440 | tf_op jit(solution)/shard_map/ppermute | solution.py:23
  108.3 6.1 %apply.9 = (f32[512,256]{1,0:T(8,128)S(1)}, bf16[512,256]{1,0:T(8,128)(2,1)S(1)}) custom-call(s32[22]{0:T(128)S(1)} %compare_select_fusion.10.table.t, bf16[1024,1024]{1,0:T(8,128)(2,1)S(1)} %constant_dynamic-update-slice_fusion.orb.slab_ref, bf16[384,1280]{1,0:T(8,128)(2,1)S(1)} %collective-permute-done.15.refs_0_, ...), custom_call_target="tpu_custom_call" | custom-call | flops 838860800 | bytes 2621440 | tf_op jit(solution)/shard_map/apply/pallas_call | solution.py:101
  114.5 2.4 %collective-permute-done.24 = bf16[512,256]{1,0:T(8,128)(2,1)S(1)} collective-permute-done((bf16[512,256]{1,0:T(8,128)(2,1)S(1)}, bf16[512,256]{1,0:T(8,128)(2,1)S(1)}, u32[]{:S(2)}, u32[]{:S(2)}) %collective-permute-start.24) | collective-permute-done | bytes 262176 | tf_op jit(solution)/shard_map/ppermute | solution.py:23
  116.9 1.2 %collective-permute-start.25 = (bf16[512,256]{1,0:T(8,128)(2,1)S(1)}, bf16[512,256]{1,0:T(8,128)(2,1)S(1)}, u32[]{:S(2)}, u32[]{:S(2)}) collective-permute-start(bf16[512,256]{1,0:T(8,128)(2,1)S(1)} %get-tuple-element.46), channel_id=1, source_target_pairs={{1,0},{0,1},{3,2},{2,3},{5,4},{4,5},{7,6},{6,7},{9,8},{8,9},{11,10... | collective-permute-start | bytes 786440 | tf_op jit(solution)/shard_map/ppermute | solution.py:23
  (59 shorter events, 8.9 us)
Async XLA Ops:
  0.0 6.6 %copy-start.1 = (s32[1,128]{1,0:T(1,128)S(1)}, s32[1,128]{1,0:T(1,128)}, u32[]{:S(2)}) copy-start(s32[1,128]{1,0:T(1,128)} %param.6) | copy-start | bytes 1540
  0.0 6.6 %collective-permute-start = (bf16[512,1024]{1,0:T(8,128)(2,1)}, bf16[512,1024]{1,0:T(8,128)(2,1)S(1)}, u32[]{:S(2)}, u32[]{:S(2)}) collective-permute-start(bf16[512,1024]{1,0:T(8,128)(2,1)} %param.4), channel_id=1, source_target_pairs={{1,0},{0,1},{3,2},{2,3},{5,4},{4,5},{7,6},{6,7},{9,8},{8,9},{11,10... | collective-permute-start | bytes 3145736 | tf_op jit(solution)/shard_map/ppermute | solution.py:23
  1.4 5.3 %collective-permute-start.2 = (bf16[512,256]{1,0:T(8,128)(2,1)}, bf16[512,256]{1,0:T(8,128)(2,1)S(1)}, u32[]{:S(2)}, u32[]{:S(2)}) collective-permute-start(bf16[512,256]{1,0:T(8,128)(2,1)} %own_tgt.1), channel_id=1, source_target_pairs={{1,0},{0,1},{3,2},{2,3},{5,4},{4,5},{7,6},{6,7},{9,8},{8,9},{11,10... | collective-permute-start | bytes 786440 | tf_op jit(solution)/shard_map/ppermute | solution.py:23
  1.4 5.1 %collective-permute-start.1 = (s32[1,128]{1,0:T(1,128)}, s32[1,128]{1,0:T(1,128)S(1)}, u32[]{:S(2)}, u32[]{:S(2)}) collective-permute-start(s32[1,128]{1,0:T(1,128)} %param.6), channel_id=1, source_target_pairs={{2,0},{0,2},{3,1},{1,3},{6,4},{4,6},{7,5},{5,7},{10,8},{8,10},{11,... | collective-permute-start | bytes 1544 | tf_op jit(solution)/shard_map/ppermute | solution.py:23
  5.2 1.5 %copy-start = (bf16[512,256]{1,0:T(8,128)(2,1)S(1)}, bf16[512,256]{1,0:T(8,128)(2,1)}, u32[]{:S(2)}) copy-start(bf16[512,256]{1,0:T(8,128)(2,1)} %own_tgt.1) | copy-start | bytes 786436
  8.2 9.8 %collective-permute-start.3 = (bf16[128,1280]{1,0:T(8,128)(2,1)S(1)}, bf16[128,1280]{1,0:T(8,128)(2,1)S(1)}, u32[]{:S(2)}, u32[]{:S(2)}) collective-permute-start(bf16[128,1280]{1,0:T(8,128)(2,1)S(1)} %get-tuple-element.27), channel_id=1, source_target_pairs={{2,0},{0,2},{3,1},{1,3},{6,4},{4,6},{7,5},{5,7},{10,8},{8,10},{11,... | collective-permute-start | bytes 983048 | tf_op jit(solution)/shard_map/ppermute | solution.py:23
  18.1 7.4 %collective-permute-start.5 = (bf16[128,1280]{1,0:T(8,128)(2,1)S(1)}, bf16[128,1280]{1,0:T(8,128)(2,1)S(1)}, u32[]{:S(2)}, u32[]{:S(2)}) collective-permute-start(bf16[128,1280]{1,0:T(8,128)(2,1)S(1)} %add.68), channel_id=1, source_target_pairs={{4,0},{0,4},{5,1},{1,5},{6,2},{2,6},{7,3},{3,7},{12,8},{8,12},{13,... | collective-permute-start | bytes 983048 | tf_op jit(solution)/shard_map/ppermute | solution.py:23
  18.3 9.7 %collective-permute-start.12 = (bf16[128,1280]{1,0:T(8,128)(2,1)S(1)}, bf16[128,1280]{1,0:T(8,128)(2,1)S(1)}, u32[]{:S(2)}, u32[]{:S(2)}) collective-permute-start(bf16[128,1280]{1,0:T(8,128)(2,1)S(1)} %add.68), channel_id=1, source_target_pairs={{96,0},{0,32},{32,64},{64,96},{97,1},{1,33},{33,65},{65,97},{98,2}... | collective-permute-start | bytes 983048 | tf_op jit(solution)/shard_map/ppermute | solution.py:23
  19.7 8.4 %collective-permute-start.10 = (bf16[128,1280]{1,0:T(8,128)(2,1)S(1)}, bf16[128,1280]{1,0:T(8,128)(2,1)S(1)}, u32[]{:S(2)}, u32[]{:S(2)}) collective-permute-start(bf16[128,1280]{1,0:T(8,128)(2,1)S(1)} %add.68), channel_id=1, source_target_pairs={{24,0},{0,8},{8,16},{16,24},{25,1},{1,9},{9,17},{17,25},{26,2},{2,... | collective-permute-start | bytes 983048 | tf_op jit(solution)/shard_map/ppermute | solution.py:23
  20.9 7.2 %collective-permute-start.4 = (bf16[128,1280]{1,0:T(8,128)(2,1)S(1)}, bf16[128,1280]{1,0:T(8,128)(2,1)S(1)}, u32[]{:S(2)}, u32[]{:S(2)}) collective-permute-start(bf16[128,1280]{1,0:T(8,128)(2,1)S(1)} %add.68), channel_id=1, source_target_pairs={{32,0},{64,32},{96,64},{0,96},{33,1},{65,33},{97,65},{1,97},{34,2}... | collective-permute-start | bytes 983048 | tf_op jit(solution)/shard_map/ppermute | solution.py:23
  22.3 6.2 %collective-permute-start.7 = (bf16[128,1280]{1,0:T(8,128)(2,1)S(1)}, bf16[128,1280]{1,0:T(8,128)(2,1)S(1)}, u32[]{:S(2)}, u32[]{:S(2)}) collective-permute-start(bf16[128,1280]{1,0:T(8,128)(2,1)S(1)} %add.68), channel_id=1, source_target_pairs={{8,0},{16,8},{24,16},{0,24},{9,1},{17,9},{25,17},{1,25},{10,2},{18... | collective-permute-start | bytes 983048 | tf_op jit(solution)/shard_map/ppermute | solution.py:23
  25.5 10.4 %collective-permute-start.13 = (bf16[128,1280]{1,0:T(8,128)(2,1)S(1)}, bf16[128,1280]{1,0:T(8,128)(2,1)S(1)}, u32[]{:S(2)}, u32[]{:S(2)}) collective-permute-start(bf16[128,1280]{1,0:T(8,128)(2,1)S(1)} %collective-permute-done.5), channel_id=1, source_target_pairs={{96,0},{0,32},{32,64},{64,96},{97,1},{1,33},{33,65},{65,97},{98,2}... | collective-permute-start | bytes 983048 | tf_op jit(solution)/shard_map/ppermute | solution.py:23
  28.5 44.7 %collective-permute-start.22 = (bf16[1024,1024]{1,0:T(8,128)(2,1)S(1)}, bf16[1024,1024]{1,0:T(8,128)(2,1)S(1)}, u32[]{:S(2)}, u32[]{:S(2)}) collective-permute-start(bf16[1024,1024]{1,0:T(8,128)(2,1)S(1)} %constant_dynamic-update-slice_fusion.orb.slab_ref), channel_id=1, source_target_pairs={{2,0},{0,2},{3,1},{1,3},{6,4},{4,6},{7,5},{5,7},{10,8},{8,10},{11,... | collective-permute-start | bytes 6291464 | tf_op jit(solution)/shard_map/ppermute | solution.py:23
  31.7 7.4 %collective-permute-start.11 = (bf16[128,1280]{1,0:T(8,128)(2,1)S(1)}, bf16[128,1280]{1,0:T(8,128)(2,1)S(1)}, u32[]{:S(2)}, u32[]{:S(2)}) collective-permute-start(bf16[128,1280]{1,0:T(8,128)(2,1)S(1)} %collective-permute-done.5), channel_id=1, source_target_pairs={{24,0},{0,8},{8,16},{16,24},{25,1},{1,9},{9,17},{17,25},{26,2},{2,... | collective-permute-start | bytes 983048 | tf_op jit(solution)/shard_map/ppermute | solution.py:23
  32.9 6.3 %collective-permute-start.6 = (bf16[128,1280]{1,0:T(8,128)(2,1)S(1)}, bf16[128,1280]{1,0:T(8,128)(2,1)S(1)}, u32[]{:S(2)}, u32[]{:S(2)}) collective-permute-start(bf16[128,1280]{1,0:T(8,128)(2,1)S(1)} %collective-permute-done.5), channel_id=1, source_target_pairs={{32,0},{64,32},{96,64},{0,96},{33,1},{65,33},{97,65},{1,97},{34,2}... | collective-permute-start | bytes 983048 | tf_op jit(solution)/shard_map/ppermute | solution.py:23
  34.4 6.2 %collective-permute-start.8 = (bf16[128,1280]{1,0:T(8,128)(2,1)S(1)}, bf16[128,1280]{1,0:T(8,128)(2,1)S(1)}, u32[]{:S(2)}, u32[]{:S(2)}) collective-permute-start(bf16[128,1280]{1,0:T(8,128)(2,1)S(1)} %collective-permute-done.5), channel_id=1, source_target_pairs={{8,0},{16,8},{24,16},{0,24},{9,1},{17,9},{25,17},{1,25},{10,2},{18... | collective-permute-start | bytes 983048 | tf_op jit(solution)/shard_map/ppermute | solution.py:23
  41.0 19.7 %collective-permute-start.9 = (bf16[384,1280]{1,0:T(8,128)(2,1)S(1)}, bf16[384,1280]{1,0:T(8,128)(2,1)S(1)}, u32[]{:S(2)}, u32[]{:S(2)}) collective-permute-start(bf16[384,1280]{1,0:T(8,128)(2,1)S(1)} %get-tuple-element.65), channel_id=1, source_target_pairs={{8,0},{16,8},{24,16},{0,24},{9,1},{17,9},{25,17},{1,25},{10,2},{18... | collective-permute-start | bytes 2949128 | tf_op jit(solution)/shard_map/ppermute | solution.py:23
  43.8 17.0 %collective-permute-start.16 = (bf16[384,1280]{1,0:T(8,128)(2,1)S(1)}, bf16[384,1280]{1,0:T(8,128)(2,1)S(1)}, u32[]{:S(2)}, u32[]{:S(2)}) collective-permute-start(bf16[384,1280]{1,0:T(8,128)(2,1)S(1)} %get-tuple-element.67), channel_id=1, source_target_pairs={{24,0},{0,8},{8,16},{16,24},{25,1},{1,9},{9,17},{17,25},{26,2},{2,... | collective-permute-start | bytes 2949128 | tf_op jit(solution)/shard_map/ppermute | solution.py:23
  43.9 20.0 %collective-permute-start.20 = (bf16[384,1280]{1,0:T(8,128)(2,1)S(1)}, bf16[384,1280]{1,0:T(8,128)(2,1)S(1)}, u32[]{:S(2)}, u32[]{:S(2)}) collective-permute-start(bf16[384,1280]{1,0:T(8,128)(2,1)S(1)} %get-tuple-element.64), channel_id=1, source_target_pairs={{96,0},{0,32},{32,64},{64,96},{97,1},{1,33},{33,65},{65,97},{98,2}... | collective-permute-start | bytes 2949128 | tf_op jit(solution)/shard_map/ppermute | solution.py:23
  44.0 16.8 %collective-permute-start.14 = (bf16[384,1280]{1,0:T(8,128)(2,1)S(1)}, bf16[384,1280]{1,0:T(8,128)(2,1)S(1)}, u32[]{:S(2)}, u32[]{:S(2)}) collective-permute-start(bf16[384,1280]{1,0:T(8,128)(2,1)S(1)} %get-tuple-element.66), channel_id=1, source_target_pairs={{32,0},{64,32},{96,64},{0,96},{33,1},{65,33},{97,65},{1,97},{34,2}... | collective-permute-start | bytes 2949128 | tf_op jit(solution)/shard_map/ppermute | solution.py:23
  61.0 31.5 %collective-permute-start.17 = (bf16[384,1280]{1,0:T(8,128)(2,1)S(1)}, bf16[384,1280]{1,0:T(8,128)(2,1)S(1)}, u32[]{:S(2)}, u32[]{:S(2)}) collective-permute-start(bf16[384,1280]{1,0:T(8,128)(2,1)S(1)} %pad_maximum_fusion.4), channel_id=1, source_target_pairs={{96,0},{0,32},{32,64},{64,96},{97,1},{1,33},{33,65},{65,97},{98,2}... | collective-permute-start | bytes 2949128 | tf_op jit(solution)/shard_map/ppermute | solution.py:23
  61.2 31.3 %collective-permute-start.15 = (bf16[384,1280]{1,0:T(8,128)(2,1)S(1)}, bf16[384,1280]{1,0:T(8,128)(2,1)S(1)}, u32[]{:S(2)}, u32[]{:S(2)}) collective-permute-start(bf16[384,1280]{1,0:T(8,128)(2,1)S(1)} %pad_maximum_fusion.2), channel_id=1, source_target_pairs={{32,0},{64,32},{96,64},{0,96},{33,1},{65,33},{97,65},{1,97},{34,2}... | collective-permute-start | bytes 2949128 | tf_op jit(solution)/shard_map/ppermute | solution.py:23
  64.0 28.4 %collective-permute-start.21 = (bf16[256,1280]{1,0:T(8,128)(2,1)S(1)}, bf16[256,1280]{1,0:T(8,128)(2,1)S(1)}, u32[]{:S(2)}, u32[]{:S(2)}) collective-permute-start(bf16[256,1280]{1,0:T(8,128)(2,1)S(1)} %pad_maximum_fusion.11.refs_10_.refs_5_), channel_id=1, source_target_pairs={{16,0},{24,8},{0,16},{8,24},{17,1},{25,9},{1,17},{9,25},{18,2},{26... | collective-permute-start | bytes 1966088 | tf_op jit(solution)/shard_map/ppermute | solution.py:23
  66.7 25.7 %collective-permute-start.18 = (bf16[128,1280]{1,0:T(8,128)(2,1)S(1)}, bf16[128,1280]{1,0:T(8,128)(2,1)S(1)}, u32[]{:S(2)}, u32[]{:S(2)}) collective-permute-start(bf16[128,1280]{1,0:T(8,128)(2,1)S(1)} %get-tuple-element.50), channel_id=1, source_target_pairs={{8,0},{16,8},{24,16},{0,24},{9,1},{17,9},{25,17},{1,25},{10,2},{18... | collective-permute-start | bytes 983048 | tf_op jit(solution)/shard_map/ppermute | solution.py:23
  73.2 19.2 %collective-permute-start.19 = (bf16[128,1280]{1,0:T(8,128)(2,1)S(1)}, bf16[128,1280]{1,0:T(8,128)(2,1)S(1)}, u32[]{:S(2)}, u32[]{:S(2)}) collective-permute-start(bf16[128,1280]{1,0:T(8,128)(2,1)S(1)} %get-tuple-element.48), channel_id=1, source_target_pairs={{24,0},{0,8},{8,16},{16,24},{25,1},{1,9},{9,17},{17,25},{26,2},{2,... | collective-permute-start | bytes 983048 | tf_op jit(solution)/shard_map/ppermute | solution.py:23
  98.6 9.1 %collective-permute-start.23 = (bf16[512,256]{1,0:T(8,128)(2,1)S(1)}, bf16[512,256]{1,0:T(8,128)(2,1)S(1)}, u32[]{:S(2)}, u32[]{:S(2)}) collective-permute-start(bf16[512,256]{1,0:T(8,128)(2,1)S(1)} %get-tuple-element.42), channel_id=1, source_target_pairs={{1,0},{0,1},{3,2},{2,3},{5,4},{4,5},{7,6},{6,7},{9,8},{8,9},{11,10... | collective-permute-start | bytes 786440 | tf_op jit(solution)/shard_map/ppermute | solution.py:23
  107.8 9.1 %collective-permute-start.24 = (bf16[512,256]{1,0:T(8,128)(2,1)S(1)}, bf16[512,256]{1,0:T(8,128)(2,1)S(1)}, u32[]{:S(2)}, u32[]{:S(2)}) collective-permute-start(bf16[512,256]{1,0:T(8,128)(2,1)S(1)} %add_convert_fusion), channel_id=1, source_target_pairs={{2,0},{0,2},{3,1},{1,3},{6,4},{4,6},{7,5},{5,7},{10,8},{8,10},{11,... | collective-permute-start | bytes 786440 | tf_op jit(solution)/shard_map/ppermute | solution.py:23
  116.9 2.4 %collective-permute-start.25 = (bf16[512,256]{1,0:T(8,128)(2,1)S(1)}, bf16[512,256]{1,0:T(8,128)(2,1)S(1)}, u32[]{:S(2)}, u32[]{:S(2)}) collective-permute-start(bf16[512,256]{1,0:T(8,128)(2,1)S(1)} %get-tuple-element.46), channel_id=1, source_target_pairs={{1,0},{0,1},{3,2},{2,3},{5,4},{4,5},{7,6},{6,7},{9,8},{8,9},{11,10... | collective-permute-start | bytes 786440 | tf_op jit(solution)/shard_map/ppermute | solution.py:23

commit v12 on v11

--- a/solution.py
+++ b/solution.py
@@ -184,9 +184,9 @@
     last, far, near = lax.optimization_barrier((last, far, near))
     kept, sent = far_apply(last, third, far, True)
     far = (kept + take_from(sent, "c", 1)).astype(jnp.bfloat16)
-    away = take_from(far, "zh", 1)
+    away = take_from(jnp.concatenate([far, far[:16]], axis=0), "zh", 1)[:own_rows]
     kept, sent = near_apply(last, third, after(near, far), True)
-    near = kept + take_from(after(sent, away), "c", 1)
+    near = kept + take_from(sent, "c", 1)
     return (-(near + away.astype(jnp.float32))).astype(jnp.bfloat16)
 
 

time: 120 us -> 119 us (level)
  starting transfers between devices: 44.9 us -> 40.9 us
  waiting for transfers between devices: 32.1 us -> 34.5 us
    ppermute x26, starting transfers between devices: 44.9 us -> 40.9 us  [take_from(): return lax.ppermute(value, axis, [((i + side) % n, i) for i in range(n)])]
    ppermute x26, waiting for transfers between devices: 32.1 us -> 34.5 us  [take_from(): return lax.ppermute(value, axis, [((i + side) % n, i) for i in range(n)])]
  transfers between devices with their start and end apart: 26 -> 26, of which waited for: 10 -> 12; matrix products, arithmetic and copies ran while one was open for 3% -> 3% of each run, Pallas kernels for 25% -> 25%
where the time goes in v12:
time: 119 us; the launch traced here: 118 us
  starting transfers between devices  40.9 us (34%)
  Pallas kernels  37.6 us (32%)
  waiting for transfers between devices  34.5 us (29%)
  local copies, waits for them, and re-layouts  2.35 us (2%)
  other arithmetic  2.09 us (2%)
    ppermute x26, starting transfers between devices, take_from(): return lax.ppermute(value, axis, [((i + side) % n, i) for i in range(n)])  40.9 us
    pallas_call x5, Pallas kernels, apply_parts(): pl.pallas_call(body, out_shape=halves if last else jax.ShapeDtypeStruct((...  36.2 us
    ppermute x26, waiting for transfers between devices, take_from(): return lax.ppermute(value, axis, [((i + side) % n, i) for i in range(n)])  34.5 us
  transfers between devices with their start and end apart: 26, of which 12 were waited for; matrix products, arithmetic and copies ran while one was open for 3% of the time, Pallas kernels for 25%

profile of v12, /device:TPU:1, one launch (start us, length us, event | category | flops | bytes accessed | tf_op | source)
XLA Modules:
  0.0 118.4 jit_solution(14715137355027415596)
XLA Ops:
  0.0 1.4 %collective-permute-start = (bf16[512,1024]{1,0:T(8,128)(2,1)}, bf16[512,1024]{1,0:T(8,128)(2,1)S(1)}, u32[]{:S(2)}, u32[]{:S(2)}) collective-permute-start(bf16[512,1024]{1,0:T(8,128)(2,1)} %param.4), channel_id=1, source_target_pairs={{1,0},{0,1},{3,2},{2,3},{5,4},{4,5},{7,6},{6,7},{9,8},{8,9},{11,10... | collective-permute-start | bytes 3145736 | tf_op jit(solution)/shard_map/ppermute | solution.py:23
  1.4 3.8 %collective-permute-start.1 = (s32[1,128]{1,0:T(1,128)}, s32[1,128]{1,0:T(1,128)S(1)}, u32[]{:S(2)}, u32[]{:S(2)}) collective-permute-start(s32[1,128]{1,0:T(1,128)} %param.6), channel_id=1, source_target_pairs={{2,0},{0,2},{3,1},{1,3},{6,4},{4,6},{7,5},{5,7},{10,8},{8,10},{11,... | collective-permute-start | bytes 1544 | tf_op jit(solution)/shard_map/ppermute | solution.py:23
  5.2 1.3 %constant_dynamic-update-slice_fusion.1 = bf16[1024,1024]{1,0:T(8,128)(2,1)S(1)} fusion(bf16[512,1024]{1,0:T(8,128)(2,1)} %param.4), kind=kLoop, calls=%fused_computation.27 | loop fusion | bytes 2097152
  6.7 1.5 %pick.1 = (bf16[128,1280]{1,0:T(8,128)(2,1)S(1)}, bf16[128,1280]{1,0:T(8,128)(2,1)S(1)}) custom-call(s32[22]{0:T(128)S(1)} %compare_select_fusion.10.table.t, s32[2,128]{1,0:T(2,128)S(1)} %pad_add_fusion.ids, bf16[1024,1024]{1,0:T(8,128)(2,1)S(1)} %constant_dynamic-update-slice_fusion.orb.slab_ref, bf16[512,256]{1,0:T(8,128)(2,1)S(1)} %copy-done, ...), custom_call_target="tpu_custom_call" | custom-call | tf_op jit(solution)/shard_map/pick/pallas_call | solution.py:50
  8.2 2.7 %collective-permute-start.3 = (bf16[128,1280]{1,0:T(8,128)(2,1)S(1)}, bf16[128,1280]{1,0:T(8,128)(2,1)S(1)}, u32[]{:S(2)}, u32[]{:S(2)}) collective-permute-start(bf16[128,1280]{1,0:T(8,128)(2,1)S(1)} %get-tuple-element.26), channel_id=1, source_target_pairs={{2,0},{0,2},{3,1},{1,3},{6,4},{4,6},{7,5},{5,7},{10,8},{8,10},{11,... | collective-permute-start | bytes 983048 | tf_op jit(solution)/shard_map/ppermute | solution.py:23
  10.9 7.1 %collective-permute-done.3 = bf16[128,1280]{1,0:T(8,128)(2,1)S(1)} collective-permute-done((bf16[128,1280]{1,0:T(8,128)(2,1)S(1)}, bf16[128,1280]{1,0:T(8,128)(2,1)S(1)}, u32[]{:S(2)}, u32[]{:S(2)}) %collective-permute-start.3) | collective-permute-done | bytes 327712 | tf_op jit(solution)/shard_map/ppermute | solution.py:23
  18.3 1.2 %collective-permute-start.10 = (bf16[128,1280]{1,0:T(8,128)(2,1)S(1)}, bf16[128,1280]{1,0:T(8,128)(2,1)S(1)}, u32[]{:S(2)}, u32[]{:S(2)}) collective-permute-start(bf16[128,1280]{1,0:T(8,128)(2,1)S(1)} %add.68), channel_id=1, source_target_pairs={{24,0},{0,8},{8,16},{16,24},{25,1},{1,9},{9,17},{17,25},{26,2},{2,... | collective-permute-start | bytes 983048 | tf_op jit(solution)/shard_map/ppermute | solution.py:23
  19.6 2.7 %collective-permute-start.4 = (bf16[128,1280]{1,0:T(8,128)(2,1)S(1)}, bf16[128,1280]{1,0:T(8,128)(2,1)S(1)}, u32[]{:S(2)}, u32[]{:S(2)}) collective-permute-start(bf16[128,1280]{1,0:T(8,128)(2,1)S(1)} %add.68), channel_id=1, source_target_pairs={{32,0},{64,32},{96,64},{0,96},{33,1},{65,33},{97,65},{1,97},{34,2}... | collective-permute-start | bytes 983048 | tf_op jit(solution)/shard_map/ppermute | solution.py:23
  22.3 1.5 %collective-permute-start.7 = (bf16[128,1280]{1,0:T(8,128)(2,1)S(1)}, bf16[128,1280]{1,0:T(8,128)(2,1)S(1)}, u32[]{:S(2)}, u32[]{:S(2)}) collective-permute-start(bf16[128,1280]{1,0:T(8,128)(2,1)S(1)} %add.68), channel_id=1, source_target_pairs={{8,0},{16,8},{24,16},{0,24},{9,1},{17,9},{25,17},{1,25},{10,2},{18... | collective-permute-start | bytes 983048 | tf_op jit(solution)/shard_map/ppermute | solution.py:23
  23.8 1.7 %collective-permute-done.5 = bf16[128,1280]{1,0:T(8,128)(2,1)S(1)} collective-permute-done((bf16[128,1280]{1,0:T(8,128)(2,1)S(1)}, bf16[128,1280]{1,0:T(8,128)(2,1)S(1)}, u32[]{:S(2)}, u32[]{:S(2)}) %collective-permute-start.5) | collective-permute-done | bytes 327712 | tf_op jit(solution)/shard_map/ppermute | solution.py:23
  25.5 1.2 %collective-permute-start.11 = (bf16[128,1280]{1,0:T(8,128)(2,1)S(1)}, bf16[128,1280]{1,0:T(8,128)(2,1)S(1)}, u32[]{:S(2)}, u32[]{:S(2)}) collective-permute-start(bf16[128,1280]{1,0:T(8,128)(2,1)S(1)} %collective-permute-done.5), channel_id=1, source_target_pairs={{24,0},{0,8},{8,16},{16,24},{25,1},{1,9},{9,17},{17,25},{26,2},{2,... | collective-permute-start | bytes 983048 | tf_op jit(solution)/shard_map/ppermute | solution.py:23
  28.5 2.4 %collective-permute-done.12 = bf16[128,1280]{1,0:T(8,128)(2,1)S(1)} collective-permute-done((bf16[128,1280]{1,0:T(8,128)(2,1)S(1)}, bf16[128,1280]{1,0:T(8,128)(2,1)S(1)}, u32[]{:S(2)}, u32[]{:S(2)}) %collective-permute-start.12) | collective-permute-done | bytes 327712 | tf_op jit(solution)/shard_map/ppermute | solution.py:23
  30.9 3.2 %collective-permute-start.22 = (bf16[1024,1024]{1,0:T(8,128)(2,1)S(1)}, bf16[1024,1024]{1,0:T(8,128)(2,1)S(1)}, u32[]{:S(2)}, u32[]{:S(2)}) collective-permute-start(bf16[1024,1024]{1,0:T(8,128)(2,1)S(1)} %constant_dynamic-update-slice_fusion.orb.slab_ref), channel_id=1, source_target_pairs={{2,0},{0,2},{3,1},{1,3},{6,4},{4,6},{7,5},{5,7},{10,8},{8,10},{11,... | collective-permute-start | bytes 6291464 | tf_op jit(solution)/shard_map/ppermute | solution.py:23
  34.1 1.6 %collective-permute-start.8 = (bf16[128,1280]{1,0:T(8,128)(2,1)S(1)}, bf16[128,1280]{1,0:T(8,128)(2,1)S(1)}, u32[]{:S(2)}, u32[]{:S(2)}) collective-permute-start(bf16[128,1280]{1,0:T(8,128)(2,1)S(1)} %collective-permute-done.5), channel_id=1, source_target_pairs={{8,0},{16,8},{24,16},{0,24},{9,1},{17,9},{25,17},{1,25},{10,2},{18... | collective-permute-start | bytes 983048 | tf_op jit(solution)/shard_map/ppermute | solution.py:23
  35.6 1.5 %collective-permute-start.13 = (bf16[128,1280]{1,0:T(8,128)(2,1)S(1)}, bf16[128,1280]{1,0:T(8,128)(2,1)S(1)}, u32[]{:S(2)}, u32[]{:S(2)}) collective-permute-start(bf16[128,1280]{1,0:T(8,128)(2,1)S(1)} %collective-permute-done.5), channel_id=1, source_target_pairs={{96,0},{0,32},{32,64},{64,96},{97,1},{1,33},{33,65},{65,97},{98,2}... | collective-permute-start | bytes 983048 | tf_op jit(solution)/shard_map/ppermute | solution.py:23
  37.1 2.8 %collective-permute-done.6 = bf16[128,1280]{1,0:T(8,128)(2,1)S(1)} collective-permute-done((bf16[128,1280]{1,0:T(8,128)(2,1)S(1)}, bf16[128,1280]{1,0:T(8,128)(2,1)S(1)}, u32[]{:S(2)}, u32[]{:S(2)}) %collective-permute-start.6) | collective-permute-done | bytes 327712 | tf_op jit(solution)/shard_map/ppermute | solution.py:23
  40.1 3.0 %collective-permute-done.13 = bf16[128,1280]{1,0:T(8,128)(2,1)S(1)} collective-permute-done((bf16[128,1280]{1,0:T(8,128)(2,1)S(1)}, bf16[128,1280]{1,0:T(8,128)(2,1)S(1)}, u32[]{:S(2)}, u32[]{:S(2)}) %collective-permute-start.13) | collective-permute-done | bytes 327712 | tf_op jit(solution)/shard_map/ppermute | solution.py:23
  43.9 1.3 %collective-permute-start.16 = (bf16[384,1280]{1,0:T(8,128)(2,1)S(1)}, bf16[384,1280]{1,0:T(8,128)(2,1)S(1)}, u32[]{:S(2)}, u32[]{:S(2)}) collective-permute-start(bf16[384,1280]{1,0:T(8,128)(2,1)S(1)} %get-tuple-element.65), channel_id=1, source_target_pairs={{24,0},{0,8},{8,16},{16,24},{25,1},{1,9},{9,17},{17,25},{26,2},{2,... | collective-permute-start | bytes 2949128 | tf_op jit(solution)/shard_map/ppermute | solution.py:23
  45.4 2.4 %collective-permute-start.14 = (bf16[384,1280]{1,0:T(8,128)(2,1)S(1)}, bf16[384,1280]{1,0:T(8,128)(2,1)S(1)}, u32[]{:S(2)}, u32[]{:S(2)}) collective-permute-start(bf16[384,1280]{1,0:T(8,128)(2,1)S(1)} %get-tuple-element.64), channel_id=1, source_target_pairs={{32,0},{64,32},{96,64},{0,96},{33,1},{65,33},{97,65},{1,97},{34,2}... | collective-permute-start | bytes 2949128 | tf_op jit(solution)/shard_map/ppermute | solution.py:23
  48.1 6.1 %apply.5.refs_12_ = f32[1024,256]{1,0:T(8,128)S(1)} custom-call(s32[22]{0:T(128)S(1)} %compare_select_fusion.10.table.t, bf16[1024,1024]{1,0:T(8,128)(2,1)S(1)} %constant_dynamic-update-slice_fusion.orb.slab_ref, bf16[256,1280]{1,0:T(8,128)(2,1)S(1)} %get-tuple-element.66.refs_0_, bf16[256,1280]{1,0:T(8,128)(2,1)S(1)} %get-tuple-element.67.refs_1_, ...), custom_call_target="tpu_custom_call" | custom-call | flops 838860800 | bytes 2621440 | tf_op jit(solution)/shard_map/apply/pallas_call | solution.py:101
  54.2 6.8 %collective-permute-done.9 = bf16[384,1280]{1,0:T(8,128)(2,1)S(1)} collective-permute-done((bf16[384,1280]{1,0:T(8,128)(2,1)S(1)}, bf16[384,1280]{1,0:T(8,128)(2,1)S(1)}, u32[]{:S(2)}, u32[]{:S(2)}) %collective-permute-start.9) | collective-permute-done | bytes 983072 | tf_op jit(solution)/shard_map/ppermute | solution.py:23
  62.9 3.1 %collective-permute-start.15 = (bf16[384,1280]{1,0:T(8,128)(2,1)S(1)}, bf16[384,1280]{1,0:T(8,128)(2,1)S(1)}, u32[]{:S(2)}, u32[]{:S(2)}) collective-permute-start(bf16[384,1280]{1,0:T(8,128)(2,1)S(1)} %pad_maximum_fusion.2), channel_id=1, source_target_pairs={{32,0},{64,32},{96,64},{0,96},{33,1},{65,33},{97,65},{1,97},{34,2}... | collective-permute-start | bytes 2949128 | tf_op jit(solution)/shard_map/ppermute | solution.py:23
  66.2 2.3 %collective-permute-start.18 = (bf16[128,1280]{1,0:T(8,128)(2,1)S(1)}, bf16[128,1280]{1,0:T(8,128)(2,1)S(1)}, u32[]{:S(2)}, u32[]{:S(2)}) collective-permute-start(bf16[128,1280]{1,0:T(8,128)(2,1)S(1)} %get-tuple-element.48), channel_id=1, source_target_pairs={{8,0},{16,8},{24,16},{0,24},{9,1},{17,9},{25,17},{1,25},{10,2},{18... | collective-permute-start | bytes 983048 | tf_op jit(solution)/shard_map/ppermute | solution.py:23
  68.5 6.7 %collective-permute-done.22.slab_ref = bf16[1024,1024]{1,0:T(8,128)(2,1)S(1)} collective-permute-done((bf16[1024,1024]{1,0:T(8,128)(2,1)S(1)}, bf16[1024,1024]{1,0:T(8,128)(2,1)S(1)}, u32[]{:S(2)}, u32[]{:S(2)}) %collective-permute-start.22) | collective-permute-done | bytes 2097184 | tf_op jit(solution)/shard_map/ppermute | solution.py:23
  75.4 10.9 %apply.6.refs_10_ = f32[1024,256]{1,0:T(8,128)S(1)} custom-call(s32[22]{0:T(128)S(1)} %compare_select_fusion.10.table.t, bf16[1024,1024]{1,0:T(8,128)(2,1)S(1)} %collective-permute-done.22.slab_ref, bf16[256,1280]{1,0:T(8,128)(2,1)S(1)} %get-tuple-element.66.refs_0_, bf16[256,1280]{1,0:T(8,128)(2,1)S(1)} %get-tuple-element.67.refs_1_, ...), custom_call_target="tpu_custom_call" | custom-call | flops 1845493760 | bytes 5767168 | tf_op jit(solution)/shard_map/apply/pallas_call | solution.py:101
  86.3 6.9 %apply.7.refs_10_ = f32[1024,256]{1,0:T(8,128)S(1)} custom-call(s32[22]{0:T(128)S(1)} %compare_select_fusion.10.table.t, bf16[1024,1024]{1,0:T(8,128)(2,1)S(1)} %constant_dynamic-update-slice_fusion.orb.slab_ref, bf16[256,1280]{1,0:T(8,128)(2,1)S(1)} %slice.50.refs_5_.refs_0_, ...), custom_call_target="tpu_custom_call", output_to_operand_aliasing={{}: (14, {})} | custom-call | flops 1006632960 | bytes 3145728 | tf_op jit(solution)/shard_map/apply/pallas_call | solution.py:101
  93.3 6.1 %apply.8 = (f32[512,256]{1,0:T(8,128)S(1)}, bf16[512,256]{1,0:T(8,128)(2,1)S(1)}) custom-call(s32[22]{0:T(128)S(1)} %compare_select_fusion.10.table.t, bf16[1024,1024]{1,0:T(8,128)(2,1)S(1)} %collective-permute-done.22.slab_ref, bf16[384,1280]{1,0:T(8,128)(2,1)S(1)} %collective-permute-done.15.refs_0_, ...), custom_call_target="tpu_custom_call" | custom-call | flops 838860800 | bytes 2621440 | tf_op jit(solution)/shard_map/apply/pallas_call | solution.py:101
  99.5 5.8 %collective-permute-start.23 = (bf16[512,256]{1,0:T(8,128)(2,1)S(1)}, bf16[512,256]{1,0:T(8,128)(2,1)S(1)}, u32[]{:S(2)}, u32[]{:S(2)}) collective-permute-start(bf16[512,256]{1,0:T(8,128)(2,1)S(1)} %get-tuple-element.41), channel_id=1, source_target_pairs={{1,0},{0,1},{3,2},{2,3},{5,4},{4,5},{7,6},{6,7},{9,8},{8,9},{11,10... | collective-permute-start | bytes 786440 | tf_op jit(solution)/shard_map/ppermute | solution.py:23
  105.2 1.2 collective-permute-done.23
  106.5 3.0 %collective-permute-start.25 = (bf16[528,256]{1,0:T(8,128)(2,1)S(1)}, bf16[528,256]{1,0:T(8,128)(2,1)S(1)}, u32[]{:S(2)}, u32[]{:S(2)}) collective-permute-start(bf16[528,256]{1,0:T(8,128)(2,1)S(1)} %pad_maximum_fusion.13), channel_id=1, source_target_pairs={{2,0},{0,2},{3,1},{1,3},{6,4},{4,6},{7,5},{5,7},{10,8},{8,10},{11,... | collective-permute-start | bytes 811016 | tf_op jit(solution)/shard_map/ppermute | solution.py:23
  109.6 6.1 %apply.9 = (f32[512,256]{1,0:T(8,128)S(1)}, bf16[512,256]{1,0:T(8,128)(2,1)S(1)}) custom-call(s32[22]{0:T(128)S(1)} %compare_select_fusion.10.table.t, bf16[1024,1024]{1,0:T(8,128)(2,1)S(1)} %constant_dynamic-update-slice_fusion.orb.slab_ref, bf16[384,1280]{1,0:T(8,128)(2,1)S(1)} %collective-permute-done.15.refs_0_, ...), custom_call_target="tpu_custom_call" | custom-call | flops 838860800 | bytes 2621440 | tf_op jit(solution)/shard_map/apply/pallas_call | solution.py:101
  116.4 1.2 collective-permute-done.24
  (61 shorter events, 7.1 us)
Async XLA Ops:
  0.0 6.6 %copy-start.1 = (s32[1,128]{1,0:T(1,128)S(1)}, s32[1,128]{1,0:T(1,128)}, u32[]{:S(2)}) copy-start(s32[1,128]{1,0:T(1,128)} %param.6) | copy-start | bytes 1540
  0.0 6.6 %collective-permute-start = (bf16[512,1024]{1,0:T(8,128)(2,1)}, bf16[512,1024]{1,0:T(8,128)(2,1)S(1)}, u32[]{:S(2)}, u32[]{:S(2)}) collective-permute-start(bf16[512,1024]{1,0:T(8,128)(2,1)} %param.4), channel_id=1, source_target_pairs={{1,0},{0,1},{3,2},{2,3},{5,4},{4,5},{7,6},{6,7},{9,8},{8,9},{11,10... | collective-permute-start | bytes 3145736 | tf_op jit(solution)/shard_map/ppermute | solution.py:23
  1.4 5.3 %collective-permute-start.2 = (bf16[512,256]{1,0:T(8,128)(2,1)}, bf16[512,256]{1,0:T(8,128)(2,1)S(1)}, u32[]{:S(2)}, u32[]{:S(2)}) collective-permute-start(bf16[512,256]{1,0:T(8,128)(2,1)} %own_tgt.1), channel_id=1, source_target_pairs={{1,0},{0,1},{3,2},{2,3},{5,4},{4,5},{7,6},{6,7},{9,8},{8,9},{11,10... | collective-permute-start | bytes 786440 | tf_op jit(solution)/shard_map/ppermute | solution.py:23
  1.4 5.1 %collective-permute-start.1 = (s32[1,128]{1,0:T(1,128)}, s32[1,128]{1,0:T(1,128)S(1)}, u32[]{:S(2)}, u32[]{:S(2)}) collective-permute-start(s32[1,128]{1,0:T(1,128)} %param.6), channel_id=1, source_target_pairs={{2,0},{0,2},{3,1},{1,3},{6,4},{4,6},{7,5},{5,7},{10,8},{8,10},{11,... | collective-permute-start | bytes 1544 | tf_op jit(solution)/shard_map/ppermute | solution.py:23
  5.2 1.5 %copy-start = (bf16[512,256]{1,0:T(8,128)(2,1)S(1)}, bf16[512,256]{1,0:T(8,128)(2,1)}, u32[]{:S(2)}) copy-start(bf16[512,256]{1,0:T(8,128)(2,1)} %own_tgt.1) | copy-start | bytes 786436
  8.2 9.8 %collective-permute-start.3 = (bf16[128,1280]{1,0:T(8,128)(2,1)S(1)}, bf16[128,1280]{1,0:T(8,128)(2,1)S(1)}, u32[]{:S(2)}, u32[]{:S(2)}) collective-permute-start(bf16[128,1280]{1,0:T(8,128)(2,1)S(1)} %get-tuple-element.26), channel_id=1, source_target_pairs={{2,0},{0,2},{3,1},{1,3},{6,4},{4,6},{7,5},{5,7},{10,8},{8,10},{11,... | collective-permute-start | bytes 983048 | tf_op jit(solution)/shard_map/ppermute | solution.py:23
  18.1 7.4 %collective-permute-start.5 = (bf16[128,1280]{1,0:T(8,128)(2,1)S(1)}, bf16[128,1280]{1,0:T(8,128)(2,1)S(1)}, u32[]{:S(2)}, u32[]{:S(2)}) collective-permute-start(bf16[128,1280]{1,0:T(8,128)(2,1)S(1)} %add.68), channel_id=1, source_target_pairs={{4,0},{0,4},{5,1},{1,5},{6,2},{2,6},{7,3},{3,7},{12,8},{8,12},{13,... | collective-permute-start | bytes 983048 | tf_op jit(solution)/shard_map/ppermute | solution.py:23
  18.3 9.6 %collective-permute-start.10 = (bf16[128,1280]{1,0:T(8,128)(2,1)S(1)}, bf16[128,1280]{1,0:T(8,128)(2,1)S(1)}, u32[]{:S(2)}, u32[]{:S(2)}) collective-permute-start(bf16[128,1280]{1,0:T(8,128)(2,1)S(1)} %add.68), channel_id=1, source_target_pairs={{24,0},{0,8},{8,16},{16,24},{25,1},{1,9},{9,17},{17,25},{26,2},{2,... | collective-permute-start | bytes 983048 | tf_op jit(solution)/shard_map/ppermute | solution.py:23
  19.6 8.4 %collective-permute-start.4 = (bf16[128,1280]{1,0:T(8,128)(2,1)S(1)}, bf16[128,1280]{1,0:T(8,128)(2,1)S(1)}, u32[]{:S(2)}, u32[]{:S(2)}) collective-permute-start(bf16[128,1280]{1,0:T(8,128)(2,1)S(1)} %add.68), channel_id=1, source_target_pairs={{32,0},{64,32},{96,64},{0,96},{33,1},{65,33},{97,65},{1,97},{34,2}... | collective-permute-start | bytes 983048 | tf_op jit(solution)/shard_map/ppermute | solution.py:23
  22.3 6.2 %collective-permute-start.7 = (bf16[128,1280]{1,0:T(8,128)(2,1)S(1)}, bf16[128,1280]{1,0:T(8,128)(2,1)S(1)}, u32[]{:S(2)}, u32[]{:S(2)}) collective-permute-start(bf16[128,1280]{1,0:T(8,128)(2,1)S(1)} %add.68), channel_id=1, source_target_pairs={{8,0},{16,8},{24,16},{0,24},{9,1},{17,9},{25,17},{1,25},{10,2},{18... | collective-permute-start | bytes 983048 | tf_op jit(solution)/shard_map/ppermute | solution.py:23
  23.8 7.1 %collective-permute-start.12 = (bf16[128,1280]{1,0:T(8,128)(2,1)S(1)}, bf16[128,1280]{1,0:T(8,128)(2,1)S(1)}, u32[]{:S(2)}, u32[]{:S(2)}) collective-permute-start(bf16[128,1280]{1,0:T(8,128)(2,1)S(1)} %add.68), channel_id=1, source_target_pairs={{96,0},{0,32},{32,64},{64,96},{97,1},{1,33},{33,65},{65,97},{98,2}... | collective-permute-start | bytes 983048 | tf_op jit(solution)/shard_map/ppermute | solution.py:23
  25.5 11.6 %collective-permute-start.11 = (bf16[128,1280]{1,0:T(8,128)(2,1)S(1)}, bf16[128,1280]{1,0:T(8,128)(2,1)S(1)}, u32[]{:S(2)}, u32[]{:S(2)}) collective-permute-start(bf16[128,1280]{1,0:T(8,128)(2,1)S(1)} %collective-permute-done.5), channel_id=1, source_target_pairs={{24,0},{0,8},{8,16},{16,24},{25,1},{1,9},{9,17},{17,25},{26,2},{2,... | collective-permute-start | bytes 983048 | tf_op jit(solution)/shard_map/ppermute | solution.py:23
  30.9 44.3 %collective-permute-start.22 = (bf16[1024,1024]{1,0:T(8,128)(2,1)S(1)}, bf16[1024,1024]{1,0:T(8,128)(2,1)S(1)}, u32[]{:S(2)}, u32[]{:S(2)}) collective-permute-start(bf16[1024,1024]{1,0:T(8,128)(2,1)S(1)} %constant_dynamic-update-slice_fusion.orb.slab_ref), channel_id=1, source_target_pairs={{2,0},{0,2},{3,1},{1,3},{6,4},{4,6},{7,5},{5,7},{10,8},{8,10},{11,... | collective-permute-start | bytes 6291464 | tf_op jit(solution)/shard_map/ppermute | solution.py:23
  34.0 5.9 %collective-permute-start.6 = (bf16[128,1280]{1,0:T(8,128)(2,1)S(1)}, bf16[128,1280]{1,0:T(8,128)(2,1)S(1)}, u32[]{:S(2)}, u32[]{:S(2)}) collective-permute-start(bf16[128,1280]{1,0:T(8,128)(2,1)S(1)} %collective-permute-done.5), channel_id=1, source_target_pairs={{32,0},{64,32},{96,64},{0,96},{33,1},{65,33},{97,65},{1,97},{34,2}... | collective-permute-start | bytes 983048 | tf_op jit(solution)/shard_map/ppermute | solution.py:23
  34.1 6.0 %collective-permute-start.8 = (bf16[128,1280]{1,0:T(8,128)(2,1)S(1)}, bf16[128,1280]{1,0:T(8,128)(2,1)S(1)}, u32[]{:S(2)}, u32[]{:S(2)}) collective-permute-start(bf16[128,1280]{1,0:T(8,128)(2,1)S(1)} %collective-permute-done.5), channel_id=1, source_target_pairs={{8,0},{16,8},{24,16},{0,24},{9,1},{17,9},{25,17},{1,25},{10,2},{18... | collective-permute-start | bytes 983048 | tf_op jit(solution)/shard_map/ppermute | solution.py:23
  35.6 7.4 %collective-permute-start.13 = (bf16[128,1280]{1,0:T(8,128)(2,1)S(1)}, bf16[128,1280]{1,0:T(8,128)(2,1)S(1)}, u32[]{:S(2)}, u32[]{:S(2)}) collective-permute-start(bf16[128,1280]{1,0:T(8,128)(2,1)S(1)} %collective-permute-done.5), channel_id=1, source_target_pairs={{96,0},{0,32},{32,64},{64,96},{97,1},{1,33},{33,65},{65,97},{98,2}... | collective-permute-start | bytes 983048 | tf_op jit(solution)/shard_map/ppermute | solution.py:23
  43.5 17.4 %collective-permute-start.9 = (bf16[384,1280]{1,0:T(8,128)(2,1)S(1)}, bf16[384,1280]{1,0:T(8,128)(2,1)S(1)}, u32[]{:S(2)}, u32[]{:S(2)}) collective-permute-start(bf16[384,1280]{1,0:T(8,128)(2,1)S(1)} %get-tuple-element.63), channel_id=1, source_target_pairs={{8,0},{16,8},{24,16},{0,24},{9,1},{17,9},{25,17},{1,25},{10,2},{18... | collective-permute-start | bytes 2949128 | tf_op jit(solution)/shard_map/ppermute | solution.py:23
  43.9 18.1 %collective-permute-start.16 = (bf16[384,1280]{1,0:T(8,128)(2,1)S(1)}, bf16[384,1280]{1,0:T(8,128)(2,1)S(1)}, u32[]{:S(2)}, u32[]{:S(2)}) collective-permute-start(bf16[384,1280]{1,0:T(8,128)(2,1)S(1)} %get-tuple-element.65), channel_id=1, source_target_pairs={{24,0},{0,8},{8,16},{16,24},{25,1},{1,9},{9,17},{17,25},{26,2},{2,... | collective-permute-start | bytes 2949128 | tf_op jit(solution)/shard_map/ppermute | solution.py:23
  45.2 20.8 %collective-permute-start.20 = (bf16[384,1280]{1,0:T(8,128)(2,1)S(1)}, bf16[384,1280]{1,0:T(8,128)(2,1)S(1)}, u32[]{:S(2)}, u32[]{:S(2)}) collective-permute-start(bf16[384,1280]{1,0:T(8,128)(2,1)S(1)} %get-tuple-element.62), channel_id=1, source_target_pairs={{96,0},{0,32},{32,64},{64,96},{97,1},{1,33},{33,65},{65,97},{98,2}... | collective-permute-start | bytes 2949128 | tf_op jit(solution)/shard_map/ppermute | solution.py:23
  45.4 16.7 %collective-permute-start.14 = (bf16[384,1280]{1,0:T(8,128)(2,1)S(1)}, bf16[384,1280]{1,0:T(8,128)(2,1)S(1)}, u32[]{:S(2)}, u32[]{:S(2)}) collective-permute-start(bf16[384,1280]{1,0:T(8,128)(2,1)S(1)} %get-tuple-element.64), channel_id=1, source_target_pairs={{32,0},{64,32},{96,64},{0,96},{33,1},{65,33},{97,65},{1,97},{34,2}... | collective-permute-start | bytes 2949128 | tf_op jit(solution)/shard_map/ppermute | solution.py:23
  62.3 31.0 %collective-permute-start.17 = (bf16[384,1280]{1,0:T(8,128)(2,1)S(1)}, bf16[384,1280]{1,0:T(8,128)(2,1)S(1)}, u32[]{:S(2)}, u32[]{:S(2)}) collective-permute-start(bf16[384,1280]{1,0:T(8,128)(2,1)S(1)} %pad_maximum_fusion.4), channel_id=1, source_target_pairs={{96,0},{0,32},{32,64},{64,96},{97,1},{1,33},{33,65},{65,97},{98,2}... | collective-permute-start | bytes 2949128 | tf_op jit(solution)/shard_map/ppermute | solution.py:23
  62.9 30.4 %collective-permute-start.15 = (bf16[384,1280]{1,0:T(8,128)(2,1)S(1)}, bf16[384,1280]{1,0:T(8,128)(2,1)S(1)}, u32[]{:S(2)}, u32[]{:S(2)}) collective-permute-start(bf16[384,1280]{1,0:T(8,128)(2,1)S(1)} %pad_maximum_fusion.2), channel_id=1, source_target_pairs={{32,0},{64,32},{96,64},{0,96},{33,1},{65,33},{97,65},{1,97},{34,2}... | collective-permute-start | bytes 2949128 | tf_op jit(solution)/shard_map/ppermute | solution.py:23
  66.1 27.2 %collective-permute-start.21 = (bf16[256,1280]{1,0:T(8,128)(2,1)S(1)}, bf16[256,1280]{1,0:T(8,128)(2,1)S(1)}, u32[]{:S(2)}, u32[]{:S(2)}) collective-permute-start(bf16[256,1280]{1,0:T(8,128)(2,1)S(1)} %pad_maximum_fusion.11.refs_10_.refs_5_), channel_id=1, source_target_pairs={{16,0},{24,8},{0,16},{8,24},{17,1},{25,9},{1,17},{9,25},{18,2},{26... | collective-permute-start | bytes 1966088 | tf_op jit(solution)/shard_map/ppermute | solution.py:23
  66.2 27.0 %collective-permute-start.18 = (bf16[128,1280]{1,0:T(8,128)(2,1)S(1)}, bf16[128,1280]{1,0:T(8,128)(2,1)S(1)}, u32[]{:S(2)}, u32[]{:S(2)}) collective-permute-start(bf16[128,1280]{1,0:T(8,128)(2,1)S(1)} %get-tuple-element.48), channel_id=1, source_target_pairs={{8,0},{16,8},{24,16},{0,24},{9,1},{17,9},{25,17},{1,25},{10,2},{18... | collective-permute-start | bytes 983048 | tf_op jit(solution)/shard_map/ppermute | solution.py:23
  75.2 18.1 %collective-permute-start.19 = (bf16[128,1280]{1,0:T(8,128)(2,1)S(1)}, bf16[128,1280]{1,0:T(8,128)(2,1)S(1)}, u32[]{:S(2)}, u32[]{:S(2)}) collective-permute-start(bf16[128,1280]{1,0:T(8,128)(2,1)S(1)} %get-tuple-element.46), channel_id=1, source_target_pairs={{24,0},{0,8},{8,16},{16,24},{25,1},{1,9},{9,17},{17,25},{26,2},{2,... | collective-permute-start | bytes 983048 | tf_op jit(solution)/shard_map/ppermute | solution.py:23
  99.5 7.0 %collective-permute-start.23 = (bf16[512,256]{1,0:T(8,128)(2,1)S(1)}, bf16[512,256]{1,0:T(8,128)(2,1)S(1)}, u32[]{:S(2)}, u32[]{:S(2)}) collective-permute-start(bf16[512,256]{1,0:T(8,128)(2,1)S(1)} %get-tuple-element.41), channel_id=1, source_target_pairs={{1,0},{0,1},{3,2},{2,3},{5,4},{4,5},{7,6},{6,7},{9,8},{8,9},{11,10... | collective-permute-start | bytes 786440 | tf_op jit(solution)/shard_map/ppermute | solution.py:23
  106.5 11.1 %collective-permute-start.25 = (bf16[528,256]{1,0:T(8,128)(2,1)S(1)}, bf16[528,256]{1,0:T(8,128)(2,1)S(1)}, u32[]{:S(2)}, u32[]{:S(2)}) collective-permute-start(bf16[528,256]{1,0:T(8,128)(2,1)S(1)} %pad_maximum_fusion.13), channel_id=1, source_target_pairs={{2,0},{0,2},{3,1},{1,3},{6,4},{4,6},{7,5},{5,7},{10,8},{8,10},{11,... | collective-permute-start | bytes 811016 | tf_op jit(solution)/shard_map/ppermute | solution.py:23
  115.7 1.9 %collective-permute-start.24 = (bf16[512,256]{1,0:T(8,128)(2,1)S(1)}, bf16[512,256]{1,0:T(8,128)(2,1)S(1)}, u32[]{:S(2)}, u32[]{:S(2)}) collective-permute-start(bf16[512,256]{1,0:T(8,128)(2,1)S(1)} %get-tuple-element.44), channel_id=1, source_target_pairs={{1,0},{0,1},{3,2},{2,3},{5,4},{4,5},{7,6},{6,7},{9,8},{8,9},{11,10... | collective-permute-start | bytes 786440 | tf_op jit(solution)/shard_map/ppermute | solution.py:23

commit v13 on v12

--- a/solution.py
+++ b/solution.py
@@ -164,7 +164,7 @@
     first = ((0, 0), *(at for at, _, _ in NEXT))
     near = near_apply([pair[at] for at in first], first, None)
     both = 2 * count
-    from_right, from_left, from_up, from_down = (after(v, near) for v in (from_right, from_left, from_up, from_down))
+    from_right, from_left = after(from_right, near), after(from_left, near)
     pair[1, 1], pair[3, 3] = from_right[:both], from_left[:both]
     pair[1, 3], pair[3, 1] = from_up[:both], from_down[:both]
     pair[0, 2] = jnp.concatenate([from_right[both:], from_left[both:]], axis=0)

time: 119 us -> 119 us (level)
  starting transfers between devices: 40.9 us -> 39.3 us
  waiting for transfers between devices: 34.5 us -> 36.1 us
    ppermute x26, starting transfers between devices: 40.9 us -> 39.3 us  [take_from(): return lax.ppermute(value, axis, [((i + side) % n, i) for i in range(n)])]
    ppermute x26, waiting for transfers between devices: 34.5 us -> 36.1 us  [take_from(): return lax.ppermute(value, axis, [((i + side) % n, i) for i in range(n)])]
  transfers between devices with their start and end apart: 26 -> 26, of which waited for: 12 -> 11; matrix products, arithmetic and copies ran while one was open for 3% -> 3% of each run, Pallas kernels for 25% -> 25%
where the time goes in v13:
time: 119 us; the launch traced here: 118 us
  starting transfers between devices  39.3 us (33%)
  Pallas kernels  37.6 us (32%)
  waiting for transfers between devices  36.1 us (30%)
  local copies, waits for them, and re-layouts  2.35 us (2%)
  other arithmetic  2.07 us (2%)
    ppermute x26, starting transfers between devices, take_from(): return lax.ppermute(value, axis, [((i + side) % n, i) for i in range(n)])  39.3 us
    pallas_call x5, Pallas kernels, apply_parts(): pl.pallas_call(body, out_shape=halves if last else jax.ShapeDtypeStruct((...  36.2 us
    ppermute x26, waiting for transfers between devices, take_from(): return lax.ppermute(value, axis, [((i + side) % n, i) for i in range(n)])  36.1 us
  transfers between devices with their start and end apart: 26, of which 11 were waited for; matrix products, arithmetic and copies ran while one was open for 3% of the time, Pallas kernels for 25%

profile of v13, /device:TPU:1, one launch (start us, length us, event | category | flops | bytes accessed | tf_op | source)
XLA Modules:
  0.0 118.4 jit_solution(16515356418472575616)
XLA Ops:
  0.0 1.4 %collective-permute-start = (bf16[512,1024]{1,0:T(8,128)(2,1)}, bf16[512,1024]{1,0:T(8,128)(2,1)S(1)}, u32[]{:S(2)}, u32[]{:S(2)}) collective-permute-start(bf16[512,1024]{1,0:T(8,128)(2,1)} %param.4), channel_id=1, source_target_pairs={{1,0},{0,1},{3,2},{2,3},{5,4},{4,5},{7,6},{6,7},{9,8},{8,9},{11,10... | collective-permute-start | bytes 3145736 | tf_op jit(solution)/shard_map/ppermute | solution.py:23
  1.4 3.8 %collective-permute-start.1 = (s32[1,128]{1,0:T(1,128)}, s32[1,128]{1,0:T(1,128)S(1)}, u32[]{:S(2)}, u32[]{:S(2)}) collective-permute-start(s32[1,128]{1,0:T(1,128)} %param.6), channel_id=1, source_target_pairs={{2,0},{0,2},{3,1},{1,3},{6,4},{4,6},{7,5},{5,7},{10,8},{8,10},{11,... | collective-permute-start | bytes 1544 | tf_op jit(solution)/shard_map/ppermute | solution.py:23
  5.2 1.3 %constant_dynamic-update-slice_fusion.1 = bf16[1024,1024]{1,0:T(8,128)(2,1)S(1)} fusion(bf16[512,1024]{1,0:T(8,128)(2,1)} %param.4), kind=kLoop, calls=%fused_computation.27 | loop fusion | bytes 2097152
  6.7 1.5 %pick.1 = (bf16[128,1280]{1,0:T(8,128)(2,1)S(1)}, bf16[128,1280]{1,0:T(8,128)(2,1)S(1)}) custom-call(s32[22]{0:T(128)S(1)} %compare_select_fusion.10.table.t, s32[2,128]{1,0:T(2,128)S(1)} %pad_add_fusion.ids, bf16[1024,1024]{1,0:T(8,128)(2,1)S(1)} %constant_dynamic-update-slice_fusion.orb.slab_ref, bf16[512,256]{1,0:T(8,128)(2,1)S(1)} %copy-done, ...), custom_call_target="tpu_custom_call" | custom-call | tf_op jit(solution)/shard_map/pick/pallas_call | solution.py:50
  8.2 2.7 %collective-permute-start.3 = (bf16[128,1280]{1,0:T(8,128)(2,1)S(1)}, bf16[128,1280]{1,0:T(8,128)(2,1)S(1)}, u32[]{:S(2)}, u32[]{:S(2)}) collective-permute-start(bf16[128,1280]{1,0:T(8,128)(2,1)S(1)} %get-tuple-element.24), channel_id=1, source_target_pairs={{2,0},{0,2},{3,1},{1,3},{6,4},{4,6},{7,5},{5,7},{10,8},{8,10},{11,... | collective-permute-start | bytes 983048 | tf_op jit(solution)/shard_map/ppermute | solution.py:23
  10.9 7.1 %collective-permute-done.3 = bf16[128,1280]{1,0:T(8,128)(2,1)S(1)} collective-permute-done((bf16[128,1280]{1,0:T(8,128)(2,1)S(1)}, bf16[128,1280]{1,0:T(8,128)(2,1)S(1)}, u32[]{:S(2)}, u32[]{:S(2)}) %collective-permute-start.3) | collective-permute-done | bytes 327712 | tf_op jit(solution)/shard_map/ppermute | solution.py:23
  18.3 1.2 %collective-permute-start.10 = (bf16[128,1280]{1,0:T(8,128)(2,1)S(1)}, bf16[128,1280]{1,0:T(8,128)(2,1)S(1)}, u32[]{:S(2)}, u32[]{:S(2)}) collective-permute-start(bf16[128,1280]{1,0:T(8,128)(2,1)S(1)} %add.68), channel_id=1, source_target_pairs={{24,0},{0,8},{8,16},{16,24},{25,1},{1,9},{9,17},{17,25},{26,2},{2,... | collective-permute-start | bytes 983048 | tf_op jit(solution)/shard_map/ppermute | solution.py:23
  19.6 2.7 %collective-permute-start.4 = (bf16[128,1280]{1,0:T(8,128)(2,1)S(1)}, bf16[128,1280]{1,0:T(8,128)(2,1)S(1)}, u32[]{:S(2)}, u32[]{:S(2)}) collective-permute-start(bf16[128,1280]{1,0:T(8,128)(2,1)S(1)} %add.68), channel_id=1, source_target_pairs={{32,0},{64,32},{96,64},{0,96},{33,1},{65,33},{97,65},{1,97},{34,2}... | collective-permute-start | bytes 983048 | tf_op jit(solution)/shard_map/ppermute | solution.py:23
  22.3 1.5 %collective-permute-start.7 = (bf16[128,1280]{1,0:T(8,128)(2,1)S(1)}, bf16[128,1280]{1,0:T(8,128)(2,1)S(1)}, u32[]{:S(2)}, u32[]{:S(2)}) collective-permute-start(bf16[128,1280]{1,0:T(8,128)(2,1)S(1)} %add.68), channel_id=1, source_target_pairs={{8,0},{16,8},{24,16},{0,24},{9,1},{17,9},{25,17},{1,25},{10,2},{18... | collective-permute-start | bytes 983048 | tf_op jit(solution)/shard_map/ppermute | solution.py:23
  23.8 1.7 %collective-permute-done.5 = bf16[128,1280]{1,0:T(8,128)(2,1)S(1)} collective-permute-done((bf16[128,1280]{1,0:T(8,128)(2,1)S(1)}, bf16[128,1280]{1,0:T(8,128)(2,1)S(1)}, u32[]{:S(2)}, u32[]{:S(2)}) %collective-permute-start.5) | collective-permute-done | bytes 327712 | tf_op jit(solution)/shard_map/ppermute | solution.py:23
  25.5 1.2 %collective-permute-start.11 = (bf16[128,1280]{1,0:T(8,128)(2,1)S(1)}, bf16[128,1280]{1,0:T(8,128)(2,1)S(1)}, u32[]{:S(2)}, u32[]{:S(2)}) collective-permute-start(bf16[128,1280]{1,0:T(8,128)(2,1)S(1)} %collective-permute-done.5), channel_id=1, source_target_pairs={{24,0},{0,8},{8,16},{16,24},{25,1},{1,9},{9,17},{17,25},{26,2},{2,... | collective-permute-start | bytes 983048 | tf_op jit(solution)/shard_map/ppermute | solution.py:23
  28.5 2.4 %collective-permute-done.12 = bf16[128,1280]{1,0:T(8,128)(2,1)S(1)} collective-permute-done((bf16[128,1280]{1,0:T(8,128)(2,1)S(1)}, bf16[128,1280]{1,0:T(8,128)(2,1)S(1)}, u32[]{:S(2)}, u32[]{:S(2)}) %collective-permute-start.12) | collective-permute-done | bytes 327712 | tf_op jit(solution)/shard_map/ppermute | solution.py:23
  30.9 3.2 %collective-permute-start.22 = (bf16[1024,1024]{1,0:T(8,128)(2,1)S(1)}, bf16[1024,1024]{1,0:T(8,128)(2,1)S(1)}, u32[]{:S(2)}, u32[]{:S(2)}) collective-permute-start(bf16[1024,1024]{1,0:T(8,128)(2,1)S(1)} %constant_dynamic-update-slice_fusion.orb.slab_ref), channel_id=1, source_target_pairs={{2,0},{0,2},{3,1},{1,3},{6,4},{4,6},{7,5},{5,7},{10,8},{8,10},{11,... | collective-permute-start | bytes 6291464 | tf_op jit(solution)/shard_map/ppermute | solution.py:23
  34.1 1.6 %collective-permute-start.8 = (bf16[128,1280]{1,0:T(8,128)(2,1)S(1)}, bf16[128,1280]{1,0:T(8,128)(2,1)S(1)}, u32[]{:S(2)}, u32[]{:S(2)}) collective-permute-start(bf16[128,1280]{1,0:T(8,128)(2,1)S(1)} %collective-permute-done.5), channel_id=1, source_target_pairs={{8,0},{16,8},{24,16},{0,24},{9,1},{17,9},{25,17},{1,25},{10,2},{18... | collective-permute-start | bytes 983048 | tf_op jit(solution)/shard_map/ppermute | solution.py:23
  35.6 1.5 %collective-permute-start.13 = (bf16[128,1280]{1,0:T(8,128)(2,1)S(1)}, bf16[128,1280]{1,0:T(8,128)(2,1)S(1)}, u32[]{:S(2)}, u32[]{:S(2)}) collective-permute-start(bf16[128,1280]{1,0:T(8,128)(2,1)S(1)} %collective-permute-done.5), channel_id=1, source_target_pairs={{96,0},{0,32},{32,64},{64,96},{97,1},{1,33},{33,65},{65,97},{98,2}... | collective-permute-start | bytes 983048 | tf_op jit(solution)/shard_map/ppermute | solution.py:23
  37.1 2.8 %collective-permute-done.6 = bf16[128,1280]{1,0:T(8,128)(2,1)S(1)} collective-permute-done((bf16[128,1280]{1,0:T(8,128)(2,1)S(1)}, bf16[128,1280]{1,0:T(8,128)(2,1)S(1)}, u32[]{:S(2)}, u32[]{:S(2)}) %collective-permute-start.6) | collective-permute-done | bytes 327712 | tf_op jit(solution)/shard_map/ppermute | solution.py:23
  40.1 3.0 %collective-permute-done.13 = bf16[128,1280]{1,0:T(8,128)(2,1)S(1)} collective-permute-done((bf16[128,1280]{1,0:T(8,128)(2,1)S(1)}, bf16[128,1280]{1,0:T(8,128)(2,1)S(1)}, u32[]{:S(2)}, u32[]{:S(2)}) %collective-permute-start.13) | collective-permute-done | bytes 327712 | tf_op jit(solution)/shard_map/ppermute | solution.py:23
  43.9 1.3 %collective-permute-start.16 = (bf16[384,1280]{1,0:T(8,128)(2,1)S(1)}, bf16[384,1280]{1,0:T(8,128)(2,1)S(1)}, u32[]{:S(2)}, u32[]{:S(2)}) collective-permute-start(bf16[384,1280]{1,0:T(8,128)(2,1)S(1)} %get-tuple-element.61), channel_id=1, source_target_pairs={{24,0},{0,8},{8,16},{16,24},{25,1},{1,9},{9,17},{17,25},{26,2},{2,... | collective-permute-start | bytes 2949128 | tf_op jit(solution)/shard_map/ppermute | solution.py:23
  45.2 1.5 %collective-permute-start.20 = (bf16[384,1280]{1,0:T(8,128)(2,1)S(1)}, bf16[384,1280]{1,0:T(8,128)(2,1)S(1)}, u32[]{:S(2)}, u32[]{:S(2)}) collective-permute-start(bf16[384,1280]{1,0:T(8,128)(2,1)S(1)} %get-tuple-element.58), channel_id=1, source_target_pairs={{96,0},{0,32},{32,64},{64,96},{97,1},{1,33},{33,65},{65,97},{98,2}... | collective-permute-start | bytes 2949128 | tf_op jit(solution)/shard_map/ppermute | solution.py:23
  46.9 6.1 %apply.5.refs_12_ = f32[1024,256]{1,0:T(8,128)S(1)} custom-call(s32[22]{0:T(128)S(1)} %compare_select_fusion.10.table.t, bf16[1024,1024]{1,0:T(8,128)(2,1)S(1)} %constant_dynamic-update-slice_fusion.orb.slab_ref, bf16[256,1280]{1,0:T(8,128)(2,1)S(1)} %get-tuple-element.62.refs_0_, bf16[256,1280]{1,0:T(8,128)(2,1)S(1)} %get-tuple-element.63.refs_1_, ...), custom_call_target="tpu_custom_call" | custom-call | flops 838860800 | bytes 2621440 | tf_op jit(solution)/shard_map/apply/pallas_call | solution.py:101
  53.0 8.0 %collective-permute-done.9 = bf16[384,1280]{1,0:T(8,128)(2,1)S(1)} collective-permute-done((bf16[384,1280]{1,0:T(8,128)(2,1)S(1)}, bf16[384,1280]{1,0:T(8,128)(2,1)S(1)}, u32[]{:S(2)}, u32[]{:S(2)}) %collective-permute-start.9) | collective-permute-done | bytes 983072 | tf_op jit(solution)/shard_map/ppermute | solution.py:23
  63.3 1.7 %collective-permute-start.15 = (bf16[384,1280]{1,0:T(8,128)(2,1)S(1)}, bf16[384,1280]{1,0:T(8,128)(2,1)S(1)}, u32[]{:S(2)}, u32[]{:S(2)}) collective-permute-start(bf16[384,1280]{1,0:T(8,128)(2,1)S(1)} %pad_maximum_fusion.2), channel_id=1, source_target_pairs={{32,0},{64,32},{96,64},{0,96},{33,1},{65,33},{97,65},{1,97},{34,2}... | collective-permute-start | bytes 2949128 | tf_op jit(solution)/shard_map/ppermute | solution.py:23
  65.8 2.0 %collective-permute-start.18 = (bf16[128,1280]{1,0:T(8,128)(2,1)S(1)}, bf16[128,1280]{1,0:T(8,128)(2,1)S(1)}, u32[]{:S(2)}, u32[]{:S(2)}) collective-permute-start(bf16[128,1280]{1,0:T(8,128)(2,1)S(1)} %get-tuple-element.44), channel_id=1, source_target_pairs={{8,0},{16,8},{24,16},{0,24},{9,1},{17,9},{25,17},{1,25},{10,2},{18... | collective-permute-start | bytes 983048 | tf_op jit(solution)/shard_map/ppermute | solution.py:23
  67.9 7.3 %collective-permute-done.22.slab_ref = bf16[1024,1024]{1,0:T(8,128)(2,1)S(1)} collective-permute-done((bf16[1024,1024]{1,0:T(8,128)(2,1)S(1)}, bf16[1024,1024]{1,0:T(8,128)(2,1)S(1)}, u32[]{:S(2)}, u32[]{:S(2)}) %collective-permute-start.22) | collective-permute-done | bytes 2097184 | tf_op jit(solution)/shard_map/ppermute | solution.py:23
  75.4 10.9 %apply.6.refs_10_ = f32[1024,256]{1,0:T(8,128)S(1)} custom-call(s32[22]{0:T(128)S(1)} %compare_select_fusion.10.table.t, bf16[1024,1024]{1,0:T(8,128)(2,1)S(1)} %collective-permute-done.22.slab_ref, bf16[256,1280]{1,0:T(8,128)(2,1)S(1)} %get-tuple-element.62.refs_0_, bf16[256,1280]{1,0:T(8,128)(2,1)S(1)} %get-tuple-element.63.refs_1_, ...), custom_call_target="tpu_custom_call" | custom-call | flops 1845493760 | bytes 5767168 | tf_op jit(solution)/shard_map/apply/pallas_call | solution.py:101
  86.3 6.9 %apply.7.refs_10_ = f32[1024,256]{1,0:T(8,128)S(1)} custom-call(s32[22]{0:T(128)S(1)} %compare_select_fusion.10.table.t, bf16[1024,1024]{1,0:T(8,128)(2,1)S(1)} %constant_dynamic-update-slice_fusion.orb.slab_ref, bf16[256,1280]{1,0:T(8,128)(2,1)S(1)} %slice.50.refs_5_.refs_0_, ...), custom_call_target="tpu_custom_call", output_to_operand_aliasing={{}: (14, {})} | custom-call | flops 1006632960 | bytes 3145728 | tf_op jit(solution)/shard_map/apply/pallas_call | solution.py:101
  93.3 6.1 %apply.8 = (f32[512,256]{1,0:T(8,128)S(1)}, bf16[512,256]{1,0:T(8,128)(2,1)S(1)}) custom-call(s32[22]{0:T(128)S(1)} %compare_select_fusion.10.table.t, bf16[1024,1024]{1,0:T(8,128)(2,1)S(1)} %collective-permute-done.22.slab_ref, bf16[384,1280]{1,0:T(8,128)(2,1)S(1)} %collective-permute-done.15.refs_0_, ...), custom_call_target="tpu_custom_call" | custom-call | flops 838860800 | bytes 2621440 | tf_op jit(solution)/shard_map/apply/pallas_call | solution.py:101
  99.5 5.8 %collective-permute-start.23 = (bf16[512,256]{1,0:T(8,128)(2,1)S(1)}, bf16[512,256]{1,0:T(8,128)(2,1)S(1)}, u32[]{:S(2)}, u32[]{:S(2)}) collective-permute-start(bf16[512,256]{1,0:T(8,128)(2,1)S(1)} %get-tuple-element.37), channel_id=1, source_target_pairs={{1,0},{0,1},{3,2},{2,3},{5,4},{4,5},{7,6},{6,7},{9,8},{8,9},{11,10... | collective-permute-start | bytes 786440 | tf_op jit(solution)/shard_map/ppermute | solution.py:23
  105.2 1.2 collective-permute-done.23
  106.5 3.0 %collective-permute-start.25 = (bf16[528,256]{1,0:T(8,128)(2,1)S(1)}, bf16[528,256]{1,0:T(8,128)(2,1)S(1)}, u32[]{:S(2)}, u32[]{:S(2)}) collective-permute-start(bf16[528,256]{1,0:T(8,128)(2,1)S(1)} %pad_maximum_fusion.13), channel_id=1, source_target_pairs={{2,0},{0,2},{3,1},{1,3},{6,4},{4,6},{7,5},{5,7},{10,8},{8,10},{11,... | collective-permute-start | bytes 811016 | tf_op jit(solution)/shard_map/ppermute | solution.py:23
  109.6 6.1 %apply.9 = (f32[512,256]{1,0:T(8,128)S(1)}, bf16[512,256]{1,0:T(8,128)(2,1)S(1)}) custom-call(s32[22]{0:T(128)S(1)} %compare_select_fusion.10.table.t, bf16[1024,1024]{1,0:T(8,128)(2,1)S(1)} %constant_dynamic-update-slice_fusion.orb.slab_ref, bf16[384,1280]{1,0:T(8,128)(2,1)S(1)} %collective-permute-done.15.refs_0_, ...), custom_call_target="tpu_custom_call" | custom-call | flops 838860800 | bytes 2621440 | tf_op jit(solution)/shard_map/apply/pallas_call | solution.py:101
  116.4 1.2 collective-permute-done.24
  (61 shorter events, 7.8 us)
Async XLA Ops:
  0.0 6.6 %copy-start.1 = (s32[1,128]{1,0:T(1,128)S(1)}, s32[1,128]{1,0:T(1,128)}, u32[]{:S(2)}) copy-start(s32[1,128]{1,0:T(1,128)} %param.6) | copy-start | bytes 1540
  0.0 6.6 %collective-permute-start = (bf16[512,1024]{1,0:T(8,128)(2,1)}, bf16[512,1024]{1,0:T(8,128)(2,1)S(1)}, u32[]{:S(2)}, u32[]{:S(2)}) collective-permute-start(bf16[512,1024]{1,0:T(8,128)(2,1)} %param.4), channel_id=1, source_target_pairs={{1,0},{0,1},{3,2},{2,3},{5,4},{4,5},{7,6},{6,7},{9,8},{8,9},{11,10... | collective-permute-start | bytes 3145736 | tf_op jit(solution)/shard_map/ppermute | solution.py:23
  1.4 5.3 %collective-permute-start.2 = (bf16[512,256]{1,0:T(8,128)(2,1)}, bf16[512,256]{1,0:T(8,128)(2,1)S(1)}, u32[]{:S(2)}, u32[]{:S(2)}) collective-permute-start(bf16[512,256]{1,0:T(8,128)(2,1)} %own_tgt.1), channel_id=1, source_target_pairs={{1,0},{0,1},{3,2},{2,3},{5,4},{4,5},{7,6},{6,7},{9,8},{8,9},{11,10... | collective-permute-start | bytes 786440 | tf_op jit(solution)/shard_map/ppermute | solution.py:23
  1.4 5.1 %collective-permute-start.1 = (s32[1,128]{1,0:T(1,128)}, s32[1,128]{1,0:T(1,128)S(1)}, u32[]{:S(2)}, u32[]{:S(2)}) collective-permute-start(s32[1,128]{1,0:T(1,128)} %param.6), channel_id=1, source_target_pairs={{2,0},{0,2},{3,1},{1,3},{6,4},{4,6},{7,5},{5,7},{10,8},{8,10},{11,... | collective-permute-start | bytes 1544 | tf_op jit(solution)/shard_map/ppermute | solution.py:23
  5.2 1.5 %copy-start = (bf16[512,256]{1,0:T(8,128)(2,1)S(1)}, bf16[512,256]{1,0:T(8,128)(2,1)}, u32[]{:S(2)}) copy-start(bf16[512,256]{1,0:T(8,128)(2,1)} %own_tgt.1) | copy-start | bytes 786436
  8.2 9.8 %collective-permute-start.3 = (bf16[128,1280]{1,0:T(8,128)(2,1)S(1)}, bf16[128,1280]{1,0:T(8,128)(2,1)S(1)}, u32[]{:S(2)}, u32[]{:S(2)}) collective-permute-start(bf16[128,1280]{1,0:T(8,128)(2,1)S(1)} %get-tuple-element.24), channel_id=1, source_target_pairs={{2,0},{0,2},{3,1},{1,3},{6,4},{4,6},{7,5},{5,7},{10,8},{8,10},{11,... | collective-permute-start | bytes 983048 | tf_op jit(solution)/shard_map/ppermute | solution.py:23
  18.1 7.4 %collective-permute-start.5 = (bf16[128,1280]{1,0:T(8,128)(2,1)S(1)}, bf16[128,1280]{1,0:T(8,128)(2,1)S(1)}, u32[]{:S(2)}, u32[]{:S(2)}) collective-permute-start(bf16[128,1280]{1,0:T(8,128)(2,1)S(1)} %add.68), channel_id=1, source_target_pairs={{4,0},{0,4},{5,1},{1,5},{6,2},{2,6},{7,3},{3,7},{12,8},{8,12},{13,... | collective-permute-start | bytes 983048 | tf_op jit(solution)/shard_map/ppermute | solution.py:23
  18.3 9.6 %collective-permute-start.10 = (bf16[128,1280]{1,0:T(8,128)(2,1)S(1)}, bf16[128,1280]{1,0:T(8,128)(2,1)S(1)}, u32[]{:S(2)}, u32[]{:S(2)}) collective-permute-start(bf16[128,1280]{1,0:T(8,128)(2,1)S(1)} %add.68), channel_id=1, source_target_pairs={{24,0},{0,8},{8,16},{16,24},{25,1},{1,9},{9,17},{17,25},{26,2},{2,... | collective-permute-start | bytes 983048 | tf_op jit(solution)/shard_map/ppermute | solution.py:23
  19.6 8.4 %collective-permute-start.4 = (bf16[128,1280]{1,0:T(8,128)(2,1)S(1)}, bf16[128,1280]{1,0:T(8,128)(2,1)S(1)}, u32[]{:S(2)}, u32[]{:S(2)}) collective-permute-start(bf16[128,1280]{1,0:T(8,128)(2,1)S(1)} %add.68), channel_id=1, source_target_pairs={{32,0},{64,32},{96,64},{0,96},{33,1},{65,33},{97,65},{1,97},{34,2}... | collective-permute-start | bytes 983048 | tf_op jit(solution)/shard_map/ppermute | solution.py:23
  22.3 6.2 %collective-permute-start.7 = (bf16[128,1280]{1,0:T(8,128)(2,1)S(1)}, bf16[128,1280]{1,0:T(8,128)(2,1)S(1)}, u32[]{:S(2)}, u32[]{:S(2)}) collective-permute-start(bf16[128,1280]{1,0:T(8,128)(2,1)S(1)} %add.68), channel_id=1, source_target_pairs={{8,0},{16,8},{24,16},{0,24},{9,1},{17,9},{25,17},{1,25},{10,2},{18... | collective-permute-start | bytes 983048 | tf_op jit(solution)/shard_map/ppermute | solution.py:23
  23.8 7.1 %collective-permute-start.12 = (bf16[128,1280]{1,0:T(8,128)(2,1)S(1)}, bf16[128,1280]{1,0:T(8,128)(2,1)S(1)}, u32[]{:S(2)}, u32[]{:S(2)}) collective-permute-start(bf16[128,1280]{1,0:T(8,128)(2,1)S(1)} %add.68), channel_id=1, source_target_pairs={{96,0},{0,32},{32,64},{64,96},{97,1},{1,33},{33,65},{65,97},{98,2}... | collective-permute-start | bytes 983048 | tf_op jit(solution)/shard_map/ppermute | solution.py:23
  25.5 11.6 %collective-permute-start.11 = (bf16[128,1280]{1,0:T(8,128)(2,1)S(1)}, bf16[128,1280]{1,0:T(8,128)(2,1)S(1)}, u32[]{:S(2)}, u32[]{:S(2)}) collective-permute-start(bf16[128,1280]{1,0:T(8,128)(2,1)S(1)} %collective-permute-done.5), channel_id=1, source_target_pairs={{24,0},{0,8},{8,16},{16,24},{25,1},{1,9},{9,17},{17,25},{26,2},{2,... | collective-permute-start | bytes 983048 | tf_op jit(solution)/shard_map/ppermute | solution.py:23
  30.9 44.3 %collective-permute-start.22 = (bf16[1024,1024]{1,0:T(8,128)(2,1)S(1)}, bf16[1024,1024]{1,0:T(8,128)(2,1)S(1)}, u32[]{:S(2)}, u32[]{:S(2)}) collective-permute-start(bf16[1024,1024]{1,0:T(8,128)(2,1)S(1)} %constant_dynamic-update-slice_fusion.orb.slab_ref), channel_id=1, source_target_pairs={{2,0},{0,2},{3,1},{1,3},{6,4},{4,6},{7,5},{5,7},{10,8},{8,10},{11,... | collective-permute-start | bytes 6291464 | tf_op jit(solution)/shard_map/ppermute | solution.py:23
  34.0 5.9 %collective-permute-start.6 = (bf16[128,1280]{1,0:T(8,128)(2,1)S(1)}, bf16[128,1280]{1,0:T(8,128)(2,1)S(1)}, u32[]{:S(2)}, u32[]{:S(2)}) collective-permute-start(bf16[128,1280]{1,0:T(8,128)(2,1)S(1)} %collective-permute-done.5), channel_id=1, source_target_pairs={{32,0},{64,32},{96,64},{0,96},{33,1},{65,33},{97,65},{1,97},{34,2}... | collective-permute-start | bytes 983048 | tf_op jit(solution)/shard_map/ppermute | solution.py:23
  34.1 6.0 %collective-permute-start.8 = (bf16[128,1280]{1,0:T(8,128)(2,1)S(1)}, bf16[128,1280]{1,0:T(8,128)(2,1)S(1)}, u32[]{:S(2)}, u32[]{:S(2)}) collective-permute-start(bf16[128,1280]{1,0:T(8,128)(2,1)S(1)} %collective-permute-done.5), channel_id=1, source_target_pairs={{8,0},{16,8},{24,16},{0,24},{9,1},{17,9},{25,17},{1,25},{10,2},{18... | collective-permute-start | bytes 983048 | tf_op jit(solution)/shard_map/ppermute | solution.py:23
  35.6 7.4 %collective-permute-start.13 = (bf16[128,1280]{1,0:T(8,128)(2,1)S(1)}, bf16[128,1280]{1,0:T(8,128)(2,1)S(1)}, u32[]{:S(2)}, u32[]{:S(2)}) collective-permute-start(bf16[128,1280]{1,0:T(8,128)(2,1)S(1)} %collective-permute-done.5), channel_id=1, source_target_pairs={{96,0},{0,32},{32,64},{64,96},{97,1},{1,33},{33,65},{65,97},{98,2}... | collective-permute-start | bytes 983048 | tf_op jit(solution)/shard_map/ppermute | solution.py:23
  43.5 17.4 %collective-permute-start.9 = (bf16[384,1280]{1,0:T(8,128)(2,1)S(1)}, bf16[384,1280]{1,0:T(8,128)(2,1)S(1)}, u32[]{:S(2)}, u32[]{:S(2)}) collective-permute-start(bf16[384,1280]{1,0:T(8,128)(2,1)S(1)} %get-tuple-element.59), channel_id=1, source_target_pairs={{8,0},{16,8},{24,16},{0,24},{9,1},{17,9},{25,17},{1,25},{10,2},{18... | collective-permute-start | bytes 2949128 | tf_op jit(solution)/shard_map/ppermute | solution.py:23
  43.9 18.1 %collective-permute-start.16 = (bf16[384,1280]{1,0:T(8,128)(2,1)S(1)}, bf16[384,1280]{1,0:T(8,128)(2,1)S(1)}, u32[]{:S(2)}, u32[]{:S(2)}) collective-permute-start(bf16[384,1280]{1,0:T(8,128)(2,1)S(1)} %get-tuple-element.61), channel_id=1, source_target_pairs={{24,0},{0,8},{8,16},{16,24},{25,1},{1,9},{9,17},{17,25},{26,2},{2,... | collective-permute-start | bytes 2949128 | tf_op jit(solution)/shard_map/ppermute | solution.py:23
  45.2 18.0 %collective-permute-start.14 = (bf16[384,1280]{1,0:T(8,128)(2,1)S(1)}, bf16[384,1280]{1,0:T(8,128)(2,1)S(1)}, u32[]{:S(2)}, u32[]{:S(2)}) collective-permute-start(bf16[384,1280]{1,0:T(8,128)(2,1)S(1)} %get-tuple-element.60), channel_id=1, source_target_pairs={{32,0},{64,32},{96,64},{0,96},{33,1},{65,33},{97,65},{1,97},{34,2}... | collective-permute-start | bytes 2949128 | tf_op jit(solution)/shard_map/ppermute | solution.py:23
  45.2 19.9 %collective-permute-start.20 = (bf16[384,1280]{1,0:T(8,128)(2,1)S(1)}, bf16[384,1280]{1,0:T(8,128)(2,1)S(1)}, u32[]{:S(2)}, u32[]{:S(2)}) collective-permute-start(bf16[384,1280]{1,0:T(8,128)(2,1)S(1)} %get-tuple-element.58), channel_id=1, source_target_pairs={{96,0},{0,32},{32,64},{64,96},{97,1},{1,33},{33,65},{65,97},{98,2}... | collective-permute-start | bytes 2949128 | tf_op jit(solution)/shard_map/ppermute | solution.py:23
  62.1 31.2 %collective-permute-start.17 = (bf16[384,1280]{1,0:T(8,128)(2,1)S(1)}, bf16[384,1280]{1,0:T(8,128)(2,1)S(1)}, u32[]{:S(2)}, u32[]{:S(2)}) collective-permute-start(bf16[384,1280]{1,0:T(8,128)(2,1)S(1)} %pad_maximum_fusion.4), channel_id=1, source_target_pairs={{96,0},{0,32},{32,64},{64,96},{97,1},{1,33},{33,65},{65,97},{98,2}... | collective-permute-start | bytes 2949128 | tf_op jit(solution)/shard_map/ppermute | solution.py:23
  63.3 30.0 %collective-permute-start.15 = (bf16[384,1280]{1,0:T(8,128)(2,1)S(1)}, bf16[384,1280]{1,0:T(8,128)(2,1)S(1)}, u32[]{:S(2)}, u32[]{:S(2)}) collective-permute-start(bf16[384,1280]{1,0:T(8,128)(2,1)S(1)} %pad_maximum_fusion.2), channel_id=1, source_target_pairs={{32,0},{64,32},{96,64},{0,96},{33,1},{65,33},{97,65},{1,97},{34,2}... | collective-permute-start | bytes 2949128 | tf_op jit(solution)/shard_map/ppermute | solution.py:23
  65.1 28.2 %collective-permute-start.21 = (bf16[256,1280]{1,0:T(8,128)(2,1)S(1)}, bf16[256,1280]{1,0:T(8,128)(2,1)S(1)}, u32[]{:S(2)}, u32[]{:S(2)}) collective-permute-start(bf16[256,1280]{1,0:T(8,128)(2,1)S(1)} %pad_maximum_fusion.11.refs_10_.refs_5_), channel_id=1, source_target_pairs={{16,0},{24,8},{0,16},{8,24},{17,1},{25,9},{1,17},{9,25},{18,2},{26... | collective-permute-start | bytes 1966088 | tf_op jit(solution)/shard_map/ppermute | solution.py:23
  65.8 27.4 %collective-permute-start.18 = (bf16[128,1280]{1,0:T(8,128)(2,1)S(1)}, bf16[128,1280]{1,0:T(8,128)(2,1)S(1)}, u32[]{:S(2)}, u32[]{:S(2)}) collective-permute-start(bf16[128,1280]{1,0:T(8,128)(2,1)S(1)} %get-tuple-element.44), channel_id=1, source_target_pairs={{8,0},{16,8},{24,16},{0,24},{9,1},{17,9},{25,17},{1,25},{10,2},{18... | collective-permute-start | bytes 983048 | tf_op jit(solution)/shard_map/ppermute | solution.py:23
  75.2 18.1 %collective-permute-start.19 = (bf16[128,1280]{1,0:T(8,128)(2,1)S(1)}, bf16[128,1280]{1,0:T(8,128)(2,1)S(1)}, u32[]{:S(2)}, u32[]{:S(2)}) collective-permute-start(bf16[128,1280]{1,0:T(8,128)(2,1)S(1)} %get-tuple-element.42), channel_id=1, source_target_pairs={{24,0},{0,8},{8,16},{16,24},{25,1},{1,9},{9,17},{17,25},{26,2},{2,... | collective-permute-start | bytes 983048 | tf_op jit(solution)/shard_map/ppermute | solution.py:23
  99.5 7.0 %collective-permute-start.23 = (bf16[512,256]{1,0:T(8,128)(2,1)S(1)}, bf16[512,256]{1,0:T(8,128)(2,1)S(1)}, u32[]{:S(2)}, u32[]{:S(2)}) collective-permute-start(bf16[512,256]{1,0:T(8,128)(2,1)S(1)} %get-tuple-element.37), channel_id=1, source_target_pairs={{1,0},{0,1},{3,2},{2,3},{5,4},{4,5},{7,6},{6,7},{9,8},{8,9},{11,10... | collective-permute-start | bytes 786440 | tf_op jit(solution)/shard_map/ppermute | solution.py:23
  106.5 11.1 %collective-permute-start.25 = (bf16[528,256]{1,0:T(8,128)(2,1)S(1)}, bf16[528,256]{1,0:T(8,128)(2,1)S(1)}, u32[]{:S(2)}, u32[]{:S(2)}) collective-permute-start(bf16[528,256]{1,0:T(8,128)(2,1)S(1)} %pad_maximum_fusion.13), channel_id=1, source_target_pairs={{2,0},{0,2},{3,1},{1,3},{6,4},{4,6},{7,5},{5,7},{10,8},{8,10},{11,... | collective-permute-start | bytes 811016 | tf_op jit(solution)/shard_map/ppermute | solution.py:23
  115.7 1.9 %collective-permute-start.24 = (bf16[512,256]{1,0:T(8,128)(2,1)S(1)}, bf16[512,256]{1,0:T(8,128)(2,1)S(1)}, u32[]{:S(2)}, u32[]{:S(2)}) collective-permute-start(bf16[512,256]{1,0:T(8,128)(2,1)S(1)} %get-tuple-element.40), channel_id=1, source_target_pairs={{1,0},{0,1},{3,2},{2,3},{5,4},{4,5},{7,6},{6,7},{9,8},{8,9},{11,10... | collective-permute-start | bytes 786440 | tf_op jit(solution)/shard_map/ppermute | solution.py:23
